TPU v7x, 32 devices: a whole 2x2x4 slice. The times are simulated.
32 devices in a mesh: groups: 2 (over x), seq: 16 (over z, y, core).
Axes of the slice: x: 2, y: 2, z: 4, core: 2. Of those that a mesh axis runs over, the one named last changes fastest.
Arguments:
- x_true: float32 [3, 4096], P(None, ('groups', 'seq')), parts along dimension 1, may hold values from -96 to 96
- noise: float32 [8, 3, 2048], P('groups', None, 'seq'), parts along dimension 0, may hold values from -6 to 6
- noise_level: int32 [8], P('groups'), parts along dimension 0, may hold values from 0 to 199
- atom_single: bfloat16 [4096, 128], P(('groups', 'seq')), parts along dimension 0, may hold values from -6 to 6
- atom_token: int32 [4096], P(('groups', 'seq')), parts along dimension 0, may hold values from 0 to 255, as said below
- window_edges: int32 [128, 2], P(('groups', 'seq')), parts along dimension 0, may hold values from 0 to 2048, as said below
- atom_pair_bias: float32 [128, 4, 32, 128], P(('groups', 'seq')), parts along dimension 0, may hold values from -6 to 300
- token_single: float32 [512, 768], P(('groups', 'seq')), parts along dimension 0, may hold values from -6 to 6
- pair_bias: float32 [32, 256, 256], P('groups', 'seq'), parts along dimension 0, may hold values from -6 to 300
- w_coord: float32 [3, 128], replicated, may hold values from -3.5 to 3.5
- w_atom_qkv: bfloat16 [4, 128, 384], replicated, may hold values from -0.5 to 0.5
- w_atom_out: bfloat16 [4, 128, 128], replicated, may hold values from -0.5 to 0.5
- w_atom_up: bfloat16 [4, 128, 512], replicated, may hold values from -0.5 to 0.5
- w_atom_down: bfloat16 [4, 256, 128], replicated, may hold values from -0.375 to 0.375
- w_pool: bfloat16 [128, 768], replicated, may hold values from -0.5 to 0.5
- w_token_qkv: bfloat16 [768, 2304], replicated, may hold values from -0.21875 to 0.21875
- w_token_out: bfloat16 [768, 768], replicated, may hold values from -0.21875 to 0.21875
- w_back: bfloat16 [768, 128], replicated, may hold values from -0.21875 to 0.21875
- w_final: bfloat16 [3, 128], replicated, may hold values from -0.5 to 0.5
Outputs:
- denoised: float32 [8, 3, 2048], P('groups', None, 'seq'), parts along dimension 0
- token_state: float32 [8, 256, 768], P('groups', 'seq'), parts along dimension 0
There are 2 independent parts, one for each index of `groups`. A program takes and returns all parts, laid end to end along the dimension named above; an argument that names none is the same for every part. Nothing has to cross between parts.
Inputs may be any that keep to these rules, and one draw needn't show every extreme that they name: `atom_token`: never falls along the atoms; every token has one or more atoms; the atoms of token t lie at or after atom 128 * (t // 16) - 48 and before atom 128 * (t // 16) + 128 + 128 * 3 // 8, so the atoms of shard d of the atoms name tokens of token shards d - 1, d and d + 1 only. For block b: max(0, 32 * b - 48) <= window_edges[b, 0] <= max(0, 32 * b - 48 + 48 // 3) and min(2048, 32 * b + 80 - 48 // 3) <= window_edges[b, 1] <= min(2048, 32 * b + 80).
All inputs are finite; a program needn't handle non-finite values.
Results may differ from a plain program's by a relative error of at most 0.008.
Values may be sent and summed in bfloat16 or wider, within the bound.
No kernel may reach another device: no remote copies, remote signals or barrier semaphores. Data moves between devices by JAX's collectives and lax.ppermute only.
A program may use at most 128 MiB of HBM per device.

v0:
```python
import jax
import jax.numpy as jnp
from jax import lax
from jax.sharding import PartitionSpec as P

QUERY_BLOCK = 32
KEY_WINDOW = 128
ENC_LAYERS = 2
LEVELS = 200
RIM = 48
LAYERS = 4


EPS = 1e-05
SIGMA_DATA = 16.0
HIGH = lax.Precision.HIGHEST


def padded_2(block, sides, width):
    for axis, dim in sides:
        count = lax.axis_size(axis)
        forward = [(i, i + 1) for i in range(count - 1)]
        backward = [(target, source) for source, target in forward]
        low = lax.ppermute(
            lax.slice_in_dim(block, block.shape[dim] - width, None, axis=dim), axis, forward
        )
        high = lax.ppermute(lax.slice_in_dim(block, 0, width, axis=dim), axis, backward)
        block = jnp.concatenate([low, block, high], axis=dim)
    return block


def from_behind(x, axis, by):
    devices = lax.axis_size(axis)
    pairs = [(i, i + by) for i in range(devices) if 0 <= i + by < devices]
    return lax.ppermute(x, axis, pairs)


def normed(values):
    centre = jnp.mean(values, -1, keepdims=True)
    centred = values - centre
    spread = jnp.mean(centred * centred, -1, keepdims=True)
    return centred * lax.rsqrt(spread + EPS)


def noise_scale(noise_level):
    upper_root = 160.0 ** (1.0 / 7.0)
    lower_root = 0.0004 ** (1.0 / 7.0)
    fraction = noise_level.astype(jnp.float32) / (LEVELS - 1)
    return SIGMA_DATA * (upper_root + fraction * (lower_root - upper_root)) ** 7


def atom_layer(stream, layer_index, weight_set, atom_pair_bias, window_edges, first_atom):
    w_atom_qkv, w_atom_out, w_atom_up, w_atom_down = weight_set
    samples, atom_rows, channels = stream.shape
    head_count = atom_pair_bias.shape[1]
    head_size = channels // head_count
    block_count = atom_rows // QUERY_BLOCK
    layer_qkv = w_atom_qkv[layer_index]
    normal_in = normed(stream).astype(jnp.bfloat16)
    projected = jnp.einsum("sac,cf->saf", normal_in, layer_qkv, preferred_element_type=jnp.float32)
    queries = projected[..., :channels].astype(jnp.bfloat16)
    key_value = jnp.stack(
        [projected[..., channels : 2 * channels], projected[..., 2 * channels :]], 0
    ).astype(jnp.bfloat16)
    padded = padded_2(key_value, (("seq", 2),), RIM)
    key_rows = padded[0]
    value_rows = padded[1]
    key_win = jnp.stack(
        [
            key_rows[:, QUERY_BLOCK * block : QUERY_BLOCK * block + KEY_WINDOW]
            for block in range(block_count)
        ],
        1,
    )
    value_win = jnp.stack(
        [
            value_rows[:, QUERY_BLOCK * block : QUERY_BLOCK * block + KEY_WINDOW]
            for block in range(block_count)
        ],
        1,
    )
    key_win = key_win.reshape(samples, block_count, KEY_WINDOW, head_count, head_size)
    value_win = value_win.reshape(samples, block_count, KEY_WINDOW, head_count, head_size)
    query_blocks = queries.reshape(samples, block_count, QUERY_BLOCK, head_count, head_size)
    scores = jnp.einsum(
        "sbqhd,sbkhd->sbhqk", query_blocks, key_win, preferred_element_type=jnp.float32
    )
    scores = scores * head_size ** (-0.5) + atom_pair_bias[None]
    position = (
        first_atom
        - RIM
        + QUERY_BLOCK * jnp.arange(block_count)[:, None]
        + jnp.arange(KEY_WINDOW)[None, :]
    )
    allowed = (position >= window_edges[:, 0:1]) & (position < window_edges[:, 1:2])
    allowed_mask = allowed[None, :, None, None, :]
    row_max = jnp.max(jnp.where(allowed_mask, scores, -jnp.inf), -1, keepdims=True)
    expo = jnp.where(allowed_mask, jnp.exp(scores - row_max), 0.0)
    attend = (expo / jnp.sum(expo, -1, keepdims=True)).astype(jnp.bfloat16)
    mixed = jnp.einsum("sbhqk,sbkhd->sbqhd", attend, value_win, preferred_element_type=jnp.float32)
    mixed = mixed.reshape(samples, atom_rows, channels).astype(jnp.bfloat16)
    stream = stream + jnp.einsum(
        "sac,cd->sad", mixed, w_atom_out[layer_index], preferred_element_type=jnp.float32
    )
    normal_mid = normed(stream).astype(jnp.bfloat16)
    gated = jnp.einsum(
        "sac,cf->saf", normal_mid, w_atom_up[layer_index], preferred_element_type=jnp.float32
    )
    hidden = (jax.nn.silu(gated[..., : 2 * channels]) * gated[..., 2 * channels :]).astype(
        jnp.bfloat16
    )
    return stream + jnp.einsum(
        "saf,fc->sac", hidden, w_atom_down[layer_index], preferred_element_type=jnp.float32
    )


def shards(
    x_true,
    noise,
    noise_level,
    atom_single,
    atom_token,
    window_edges,
    atom_pair_bias,
    token_single,
    pair_bias,
    w_coord,
    w_atom_qkv,
    w_atom_out,
    w_atom_up,
    w_atom_down,
    w_pool,
    w_token_qkv,
    w_token_out,
    w_back,
    w_final,
):
    samples = noise.shape[0]
    atom_rows = atom_single.shape[0]
    token_rows = token_single.shape[0]
    channels = token_single.shape[1]
    head_count = pair_bias.shape[0]
    head_size = channels // head_count
    device = lax.axis_index("seq")
    first_atom = device * atom_rows
    weight_set = (w_atom_qkv, w_atom_out, w_atom_up, w_atom_down)
    sigma = noise_scale(noise_level)[:, None, None]
    total = sigma * sigma + SIGMA_DATA * SIGMA_DATA
    noisy = x_true[None] + sigma * noise
    scaled = noisy * lax.rsqrt(total)
    stream = (
        atom_single.astype(jnp.float32)[None]
        + scaled[:, 0, :, None] * w_coord[0]
        + scaled[:, 1, :, None] * w_coord[1]
        + scaled[:, 2, :, None] * w_coord[2]
    )
    for layer_index in range(ENC_LAYERS):
        stream = atom_layer(
            stream, layer_index, weight_set, atom_pair_bias, window_edges, first_atom
        )
    encoded = stream
    pooled_atoms = jax.nn.relu(
        jnp.einsum(
            "sac,cf->saf",
            normed(encoded).astype(jnp.bfloat16),
            w_pool,
            preferred_element_type=jnp.float32,
        )
    )
    relative = atom_token - (device - 1) * token_rows
    selector = (jnp.arange(3 * token_rows)[:, None] == relative[None, :]).astype(jnp.float32)
    partial_value = jnp.einsum("ra,saf->srf", selector, pooled_atoms, precision=HIGH)
    counted = jnp.sum(selector, 1)
    from_lower = (
        from_behind(partial_value[:, 2 * token_rows :].astype(jnp.bfloat16), "seq", 1).astype(
            jnp.float32
        ),
        from_behind(counted[2 * token_rows :].astype(jnp.bfloat16), "seq", 1).astype(jnp.float32),
    )
    from_upper = (
        from_behind(partial_value[:, :token_rows].astype(jnp.bfloat16), "seq", -1).astype(
            jnp.float32
        ),
        from_behind(counted[:token_rows].astype(jnp.bfloat16), "seq", -1).astype(jnp.float32),
    )
    token_sums = partial_value[:, token_rows : 2 * token_rows] + from_lower[0] + from_upper[0]
    token_counts = counted[token_rows : 2 * token_rows] + from_lower[1] + from_upper[1]
    token_in = token_sums / token_counts[None, :, None] + token_single[None]
    normal_tok = normed(token_in).astype(jnp.bfloat16)
    projected = jnp.einsum(
        "stc,cf->stf", normal_tok, w_token_qkv, preferred_element_type=jnp.float32
    ).astype(jnp.bfloat16)
    scale = head_size ** (-0.5)
    repeat_count = lax.axis_size("seq") // head_count
    items = projected.reshape(samples, token_rows, 3, head_count, head_size).transpose(
        3, 0, 1, 2, 4
    )
    items = items.reshape(head_count * samples, token_rows, 3 * head_size)
    spread_bias = jnp.repeat(pair_bias, repeat_count, 0)
    got_items = lax.all_to_all(items, "seq", split_axis=0, concat_axis=1, tiled=True)
    got_bias = lax.all_to_all(spread_bias, "seq", split_axis=0, concat_axis=1, tiled=True)
    item_queries = got_items[..., :head_size]
    item_keys = got_items[..., head_size : 2 * head_size]
    item_values = got_items[..., 2 * head_size :].astype(jnp.float32)
    scores = (
        jnp.einsum("gqd,gkd->gqk", item_queries, item_keys, preferred_element_type=jnp.float32)
        * scale
        + got_bias
    )
    row_max = jnp.max(scores, -1, keepdims=True)
    expo = jnp.exp(scores - row_max)
    attend = expo / jnp.sum(expo, -1, keepdims=True)
    item_out = jnp.einsum("gqk,gkd->gqd", attend, item_values, precision=HIGH).astype(jnp.bfloat16)
    returned = lax.all_to_all(item_out, "seq", split_axis=1, concat_axis=0, tiled=True)
    mixed = (
        returned.reshape(head_count, samples, token_rows, head_size)
        .transpose(1, 2, 0, 3)
        .reshape(samples, token_rows, channels)
    )
    token_state = token_in + jnp.einsum(
        "stc,cd->std", mixed, w_token_out, preferred_element_type=jnp.float32
    )
    back_proj = jnp.einsum(
        "stc,cf->stf",
        normed(token_state).astype(jnp.bfloat16),
        w_back,
        preferred_element_type=jnp.float32,
    )
    padded_back = padded_2(back_proj.astype(jnp.bfloat16), (("seq", 1),), token_rows).astype(
        back_proj.dtype
    )
    picked = jnp.einsum("ra,srf->saf", selector, padded_back, precision=HIGH)
    stream = encoded + picked
    for layer_index in range(ENC_LAYERS, LAYERS):
        stream = atom_layer(
            stream, layer_index, weight_set, atom_pair_bias, window_edges, first_atom
        )
    update = jnp.einsum(
        "sac,kc->ska",
        normed(stream).astype(jnp.bfloat16),
        w_final,
        preferred_element_type=jnp.float32,
    )
    denoised = (
        SIGMA_DATA * SIGMA_DATA / total * noisy + sigma * SIGMA_DATA * lax.rsqrt(total) * update
    ) / SIGMA_DATA
    return (denoised, token_state)


def solution(mesh):
    in_specs = (
        P(None, ("groups", "seq")),
        P("groups", None, "seq"),
        P("groups"),
        P(("groups", "seq"), None),
        P(("groups", "seq")),
        P(("groups", "seq"), None),
        P(("groups", "seq"), None, None, None),
        P(("groups", "seq"), None),
        P("groups", "seq", None),
        P(),
        P(),
        P(),
        P(),
        P(),
        P(),
        P(),
        P(),
        P(),
        P(),
    )
    out_specs = (P("groups", None, "seq"), P("groups", "seq", None))
    return jax.shard_map(shards, mesh=mesh, in_specs=in_specs, out_specs=out_specs, check_vma=False)
```

profile of v0, /device:TPU:7, one launch (start us, length us, event | category | flops | bytes accessed | tf_op | source)
XLA Modules:
  0.0 273.3 jit_solution(568885372386257276)
XLA Ops:
  11.6 3.7 %collective-permute-start = (bf16[2,4,48,128]{3,2,1,0:T(8,128)(2,1)}, bf16[2,4,48,128]{3,2,1,0:T(8,128)(2,1)}, u32[]{:S(2)}, u32[]{:S(2)}) collective-permute-start(bf16[2,4,48,128]{3,2,1,0:T(8,128)(2,1)} %get-tuple-element.40), channel_id=1, source_target_pairs={{0,1},{1,2},{2,3},{3,4},{4,5},{5,6},{6,7},{7,8},{8,9},{9,10},{10,1... | collective-permute-start | bytes 294920 | tf_op jit(solution)/shard_map/ppermute | solution.py:24
  15.3 1.9 collective-permute-start.1
  17.3 1.9 reshape.339
  42.5 2.1 copy.201
  44.6 2.0 convert_element_type.146
  54.3 4.5 %collective-permute-start.2 = (bf16[2,4,48,128]{3,2,1,0:T(8,128)(2,1)}, bf16[2,4,48,128]{3,2,1,0:T(8,128)(2,1)}, u32[]{:S(2)}, u32[]{:S(2)}) collective-permute-start(bf16[2,4,48,128]{3,2,1,0:T(8,128)(2,1)} %get-tuple-element.38), channel_id=1, source_target_pairs={{0,1},{1,2},{2,3},{3,4},{4,5},{5,6},{6,7},{7,8},{8,9},{9,10},{10,1... | collective-permute-start | bytes 294920 | tf_op jit(solution)/shard_map/ppermute | solution.py:24
  58.8 1.9 collective-permute-start.3
  61.4 4.5 %collective-permute-start.6 = (bf16[16]{0:T(256)(128)(2,1)}, bf16[16]{0:T(256)(128)(2,1)S(1)}, u32[]{:S(2)}, u32[]{:S(2)}) collective-permute-start(bf16[16]{0:T(256)(128)(2,1)} %get-tuple-element.85), channel_id=1, source_target_pairs={{0,1},{1,2},{2,3},{3,4},{4,5},{5,6},{6,7},{7,8},{8,9},{9,10},{10,1... | collective-permute-start | bytes 104 | tf_op jit(solution)/shard_map/ppermute | solution.py:35
  65.9 1.9 collective-permute-start.7
  67.8 6.5 %all-to-all-start.1 = ((f32[16,16,256]{2,1,0:T(8,128)}), f32[16,16,256]{2,1,0:T(8,128)}, u32[]{:S(2)}, u32[]{:S(2)}) async-start(f32[16,16,256]{2,1,0:T(8,128)} %param.27), calls=%async_computation.1 | async-start | bytes 524288 | tf_op jit(solution)/shard_map/all_to_all | solution.py:201
  74.4 1.9 reshape.340
  87.2 2.0 fusion.284
  96.6 2.8 %fusion.52 = bf16[4,4,32,4,32]{2,4,3,1,0:T(8,128)(2,1)} fusion(f32[4,4,4,32,128]{4,3,2,1,0:T(8,128)} %get-tuple-element.94, bf16[4,1,128,4,32]{2,4,3,1,0:T(8,128)(2,1)} %bitcast.328, bf16[4,1,128,4,32]{2,4,3,1,0:T(8,128)(2,1)} %bitcast.319, bf16[4,1,128,4,32]{2,4,3,1,0:T(8,128)(2,1)} %bitcast.315, bf16[4,1,128,4,32]{2,4,3,1,0:T(8,128)(2,1)} %bitcast.312, ...), kind=kOutput, calls=%fused_computation.49 | convolution fusion | flops 18153472 | bytes 1712128 | tf_op jit(solution)/shard_map/sbhqk,sbkhd->sbqhd/dot_general | solution.py:100
  99.4 2.1 copy.223
  101.4 2.0 convert_element_type.153
  109.2 3.4 %collective-permute-start.4 = (bf16[4,16,768]{2,1,0:T(8,128)(2,1)S(1)}, bf16[4,16,768]{2,1,0:T(8,128)(2,1)S(1)}, u32[]{:S(2)}, u32[]{:S(2)}) collective-permute-start(bf16[4,16,768]{2,1,0:T(8,128)(2,1)S(1)} %get-tuple-element.32), channel_id=1, source_target_pairs={{0,1},{1,2},{2,3},{3,4},{4,5},{5,6},{6,7},{7,8},{8,9},{9,10},{10,1... | collective-permute-start | bytes 294920 | tf_op jit(solution)/shard_map/ppermute | solution.py:35
  112.6 2.1 collective-permute-start.5
  115.5 3.9 %collective-permute-done.5 = bf16[4,16,768]{2,1,0:T(8,128)(2,1)S(1)} collective-permute-done((bf16[4,16,768]{2,1,0:T(8,128)(2,1)S(1)}, bf16[4,16,768]{2,1,0:T(8,128)(2,1)S(1)}, u32[]{:S(2)}, u32[]{:S(2)}) %collective-permute-start.5) | collective-permute-done | bytes 98336 | tf_op jit(solution)/shard_map/ppermute | solution.py:35
  121.8 2.9 %reshape.341 = bf16[4,16,3,16,48]{4,3,2,1,0:T(8,128)(2,1)} reshape(bf16[4,16,2304]{2,1,0:T(8,128)(2,1)} %fusion.6) | data formatting | bytes 589824 | tf_op jit(solution)/shard_map/reshape | solution.py:195
  124.7 2.7 copy.322
  127.4 3.1 %reshape.342 = bf16[64,16,144]{2,1,0:T(8,128)(2,1)} reshape(bf16[16,4,16,3,48]{4,3,2,1,0:T(4,128)(2,1)} %bitcast.298) | data formatting | bytes 589824 | tf_op jit(solution)/shard_map/reshape | solution.py:198
  130.6 4.8 %all-to-all-start = ((bf16[64,16,144]{2,1,0:T(8,128)(2,1)}), bf16[64,16,144]{2,1,0:T(8,128)(2,1)}, u32[]{:S(2)}, u32[]{:S(2)}) async-start(bf16[64,16,144]{2,1,0:T(8,128)(2,1)} %reshape.342), calls=%async_computation | async-start | bytes 1048576 | tf_op jit(solution)/shard_map/all_to_all | solution.py:200
  135.4 1.8 copy.232
  137.2 12.0 %all-to-all-done = bf16[64,16,144]{2,1,0:T(8,128)(2,1)} async-done(((bf16[64,16,144]{2,1,0:T(8,128)(2,1)}), bf16[64,16,144]{2,1,0:T(8,128)(2,1)}, u32[]{:S(2)}, u32[]{:S(2)}) %all-to-all-start) | async-done | bytes 294944 | tf_op jit(solution)/shard_map/all_to_all | solution.py:200
  154.9 2.0 reshape.368
  156.9 10.4 %all_to_all.39 = bf16[16,2,1536]{2,1,0:T(2,128)(2,1)} all-to-all(bf16[16,2,1536]{2,1,0:T(2,128)(2,1)} %reshape.368), channel_id=1, replica_groups=mesh['groups'=2,'seq'=16] {'seq'}, dimensions={0} | all-to-all | bytes 196608 | tf_op jit(solution)/shard_map/all_to_all | solution.py:214
  167.2 1.9 reshape.369
  170.8 1.9 reshape.343
  172.7 1.8 fusion.289
  174.9 3.2 %collective-permute-start.8 = (bf16[4,16,128]{2,1,0:T(8,128)(2,1)S(1)}, bf16[4,16,128]{2,1,0:T(8,128)(2,1)S(1)}, u32[]{:S(2)}, u32[]{:S(2)}) collective-permute-start(bf16[4,16,128]{2,1,0:T(8,128)(2,1)S(1)} %convolution_convert_fusion.9), channel_id=1, source_target_pairs={{0,1},{1,2},{2,3},{3,4},{4,5},{5,6},{6,7},{7,8},{8,9},{9,10},{10,1... | collective-permute-start | bytes 49160 | tf_op jit(solution)/shard_map/ppermute | solution.py:24
  178.1 1.9 collective-permute-start.9
  180.1 4.0 %collective-permute-done.9 = bf16[4,16,128]{2,1,0:T(8,128)(2,1)S(1)} collective-permute-done((bf16[4,16,128]{2,1,0:T(8,128)(2,1)S(1)}, bf16[4,16,128]{2,1,0:T(8,128)(2,1)S(1)}, u32[]{:S(2)}, u32[]{:S(2)}) %collective-permute-start.9) | collective-permute-done | bytes 16416 | tf_op jit(solution)/shard_map/ppermute | solution.py:27
  188.3 1.9 collective-permute-start.10
  190.2 2.4 collective-permute-start.11
  192.6 1.9 reshape.344
  194.5 2.8 %collective-permute-done.11 = bf16[2,4,48,128]{3,2,1,0:T(8,128)(2,1)} collective-permute-done((bf16[2,4,48,128]{3,2,1,0:T(8,128)(2,1)}, bf16[2,4,48,128]{3,2,1,0:T(8,128)(2,1)}, u32[]{:S(2)}, u32[]{:S(2)}) %collective-permute-start.11) | collective-permute-done | bytes 98336 | tf_op jit(solution)/shard_map/ppermute | solution.py:27
  208.2 2.0 fusion.291
  217.7 2.8 %fusion.53 = bf16[4,4,32,4,32]{2,4,3,1,0:T(8,128)(2,1)} fusion(f32[4,4,4,32,128]{4,3,2,1,0:T(8,128)} %get-tuple-element.108, bf16[4,1,128,4,32]{2,4,3,1,0:T(8,128)(2,1)} %bitcast.330, bf16[4,1,128,4,32]{2,4,3,1,0:T(8,128)(2,1)} %bitcast.321, bf16[4,1,128,4,32]{2,4,3,1,0:T(8,128)(2,1)} %bitcast.316, bf16[4,1,128,4,32]{2,4,3,1,0:T(8,128)(2,1)} %bitcast.313, ...), kind=kOutput, calls=%fused_computation.50 | convolution fusion | flops 18153472 | bytes 1712128 | tf_op jit(solution)/shard_map/sbhqk,sbkhd->sbqhd/dot_general | solution.py:100
  220.5 2.1 copy.256
  222.6 2.0 convert_element_type.171
  232.3 1.9 collective-permute-start.12
  234.2 2.6 collective-permute-start.13
  236.9 1.9 reshape.345
  238.8 2.6 collective-permute-done.13
  252.3 2.0 fusion.294
  261.7 2.8 %fusion.54 = bf16[4,4,32,4,32]{2,4,3,1,0:T(8,128)(2,1)} fusion(f32[4,4,4,32,128]{4,3,2,1,0:T(8,128)} %get-tuple-element.114, bf16[4,1,128,4,32]{2,4,3,1,0:T(8,128)(2,1)} %bitcast.332, bf16[4,1,128,4,32]{2,4,3,1,0:T(8,128)(2,1)} %bitcast.323, bf16[4,1,128,4,32]{2,4,3,1,0:T(8,128)(2,1)} %bitcast.317, bf16[4,1,128,4,32]{2,4,3,1,0:T(8,128)(2,1)} %bitcast.314, ...), kind=kOutput, calls=%fused_computation.51 | convolution fusion | flops 18153472 | bytes 1712128 | tf_op jit(solution)/shard_map/sbhqk,sbkhd->sbqhd/dot_general | solution.py:100
  264.5 2.1 copy.278
  266.6 2.0 convert_element_type.178
  (233 shorter events, 130.2 us)
Async XLA Ops:
  0.6 119.7 %copy-start = (bf16[768,2304]{1,0:T(8,128)(2,1)S(1)}, bf16[768,2304]{1,0:T(8,128)(2,1)}, u32[]{:S(2)}) copy-start(bf16[768,2304]{1,0:T(8,128)(2,1)} %param.34) | copy-start | bytes 10616836
  2.5 0.8 copy-start.29
  4.7 17.0 %copy-start.28 = (f32[128]{0:T(128)}, f32[128]{0:T(128)S(1)}, u32[]{:S(2)}) copy-start(f32[128]{0:T(128)S(1)} %get-tuple-element.77) | copy-start | bytes 1540
  10.3 1.3 copy-start.12
  11.6 11.5 %collective-permute-start = (bf16[2,4,48,128]{3,2,1,0:T(8,128)(2,1)}, bf16[2,4,48,128]{3,2,1,0:T(8,128)(2,1)}, u32[]{:S(2)}, u32[]{:S(2)}) collective-permute-start(bf16[2,4,48,128]{3,2,1,0:T(8,128)(2,1)} %get-tuple-element.40), channel_id=1, source_target_pairs={{0,1},{1,2},{2,3},{3,4},{4,5},{5,6},{6,7},{7,8},{8,9},{9,10},{10,1... | collective-permute-start | bytes 294920 | tf_op jit(solution)/shard_map/ppermute | solution.py:24
  15.3 7.8 %collective-permute-start.1 = (bf16[2,4,48,128]{3,2,1,0:T(8,128)(2,1)}, bf16[2,4,48,128]{3,2,1,0:T(8,128)(2,1)}, u32[]{:S(2)}, u32[]{:S(2)}) collective-permute-start(bf16[2,4,48,128]{3,2,1,0:T(8,128)(2,1)} %get-tuple-element.41), channel_id=1, source_target_pairs={{1,0},{2,1},{3,2},{4,3},{5,4},{6,5},{7,6},{8,7},{9,8},{10,9},{11,1... | collective-permute-start | bytes 294920 | tf_op jit(solution)/shard_map/ppermute | solution.py:27
  21.7 1.4 copy-start.33
  40.1 1.1 copy-start.21
  40.1 1.1 copy-start.22
  40.1 1.1 copy-start.23
  40.1 1.1 copy-start.24
  50.3 0.7 copy-start.6
  50.3 10.4 %copy-start.32 = (bf16[48]{0:T(256)(128)(2,1)S(1)}, bf16[48]{0:T(256)(128)(2,1)}, u32[]{:S(2)}) copy-start(bf16[48]{0:T(256)(128)(2,1)} %convert.47) | copy-start | bytes 292
  53.0 1.3 copy-start.14
  54.3 22.0 %collective-permute-start.2 = (bf16[2,4,48,128]{3,2,1,0:T(8,128)(2,1)}, bf16[2,4,48,128]{3,2,1,0:T(8,128)(2,1)}, u32[]{:S(2)}, u32[]{:S(2)}) collective-permute-start(bf16[2,4,48,128]{3,2,1,0:T(8,128)(2,1)} %get-tuple-element.38), channel_id=1, source_target_pairs={{0,1},{1,2},{2,3},{3,4},{4,5},{5,6},{6,7},{7,8},{8,9},{9,10},{10,1... | collective-permute-start | bytes 294920 | tf_op jit(solution)/shard_map/ppermute | solution.py:24
  58.8 17.4 %collective-permute-start.3 = (bf16[2,4,48,128]{3,2,1,0:T(8,128)(2,1)}, bf16[2,4,48,128]{3,2,1,0:T(8,128)(2,1)}, u32[]{:S(2)}, u32[]{:S(2)}) collective-permute-start(bf16[2,4,48,128]{3,2,1,0:T(8,128)(2,1)} %get-tuple-element.39), channel_id=1, source_target_pairs={{1,0},{2,1},{3,2},{4,3},{5,4},{6,5},{7,6},{8,7},{9,8},{10,9},{11,1... | collective-permute-start | bytes 294920 | tf_op jit(solution)/shard_map/ppermute | solution.py:27
  61.4 53.3 %collective-permute-start.6 = (bf16[16]{0:T(256)(128)(2,1)}, bf16[16]{0:T(256)(128)(2,1)S(1)}, u32[]{:S(2)}, u32[]{:S(2)}) collective-permute-start(bf16[16]{0:T(256)(128)(2,1)} %get-tuple-element.85), channel_id=1, source_target_pairs={{0,1},{1,2},{2,3},{3,4},{4,5},{5,6},{6,7},{7,8},{8,9},{9,10},{10,1... | collective-permute-start | bytes 104 | tf_op jit(solution)/shard_map/ppermute | solution.py:35
  65.9 48.8 %collective-permute-start.7 = (bf16[16]{0:T(256)(128)(2,1)}, bf16[16]{0:T(256)(128)(2,1)}, u32[]{:S(2)}, u32[]{:S(2)}) collective-permute-start(bf16[16]{0:T(256)(128)(2,1)} %get-tuple-element.86), channel_id=1, source_target_pairs={{1,0},{2,1},{3,2},{4,3},{5,4},{6,5},{7,6},{8,7},{9,8},{10,9},{11,1... | collective-permute-start | bytes 104 | tf_op jit(solution)/shard_map/ppermute | solution.py:35
  67.8 62.7 %all-to-all-start.1 = ((f32[16,16,256]{2,1,0:T(8,128)}), f32[16,16,256]{2,1,0:T(8,128)}, u32[]{:S(2)}, u32[]{:S(2)}) async-start(f32[16,16,256]{2,1,0:T(8,128)} %param.27), calls=%async_computation.1 | async-start | bytes 524288 | tf_op jit(solution)/shard_map/all_to_all | solution.py:201
  87.1 2.0 copy-start.4
  106.1 1.9 copy-start.20
  107.3 0.7 copy-start.8
  107.3 1.1 copy-start.34
  108.4 6.3 %copy-start.38 = (f32[48]{0:T(128)S(1)}, f32[48]{0:T(128)}, u32[]{:S(2)}) copy-start(f32[48]{0:T(128)} %copy-done.37) | copy-start | bytes 580
  108.4 11.0 %copy-start.25 = (f32[16,768]{1,0:T(8,128)S(1)}, f32[16,768]{1,0:T(8,128)}, u32[]{:S(2)}) copy-start(f32[16,768]{1,0:T(8,128)} %param.26) | copy-start | bytes 147460
  109.2 6.3 %collective-permute-start.4 = (bf16[4,16,768]{2,1,0:T(8,128)(2,1)S(1)}, bf16[4,16,768]{2,1,0:T(8,128)(2,1)S(1)}, u32[]{:S(2)}, u32[]{:S(2)}) collective-permute-start(bf16[4,16,768]{2,1,0:T(8,128)(2,1)S(1)} %get-tuple-element.32), channel_id=1, source_target_pairs={{0,1},{1,2},{2,3},{3,4},{4,5},{5,6},{6,7},{7,8},{8,9},{9,10},{10,1... | collective-permute-start | bytes 294920 | tf_op jit(solution)/shard_map/ppermute | solution.py:35
  112.6 6.8 %collective-permute-start.5 = (bf16[4,16,768]{2,1,0:T(8,128)(2,1)S(1)}, bf16[4,16,768]{2,1,0:T(8,128)(2,1)S(1)}, u32[]{:S(2)}, u32[]{:S(2)}) collective-permute-start(bf16[4,16,768]{2,1,0:T(8,128)(2,1)S(1)} %get-tuple-element.33), channel_id=1, source_target_pairs={{1,0},{2,1},{3,2},{4,3},{5,4},{6,5},{7,6},{8,7},{9,8},{10,9},{11,1... | collective-permute-start | bytes 294920 | tf_op jit(solution)/shard_map/ppermute | solution.py:35
  130.6 18.6 %all-to-all-start = ((bf16[64,16,144]{2,1,0:T(8,128)(2,1)}), bf16[64,16,144]{2,1,0:T(8,128)(2,1)}, u32[]{:S(2)}, u32[]{:S(2)}) async-start(bf16[64,16,144]{2,1,0:T(8,128)(2,1)} %reshape.342), calls=%async_computation | async-start | bytes 1048576 | tf_op jit(solution)/shard_map/all_to_all | solution.py:200
  172.7 2.0 copy-start.19
  172.7 11.4 %copy-start.9 = (f32[4,128,128]{1,2,0:T(8,128)S(1)}, f32[4,128,128]{1,2,0:T(8,128)}, u32[]{:S(2)}) copy-start(f32[4,128,128]{1,2,0:T(8,128)} %copy-done.8) | copy-start | bytes 786436
  174.5 5.6 %copy-start.10 = (f32[4,16,768]{2,1,0:T(8,128)}, f32[4,16,768]{2,1,0:T(8,128)S(1)}, u32[]{:S(2)}) copy-start(f32[4,16,768]{2,1,0:T(8,128)S(1)} %get-tuple-element.104) | copy-start | bytes 589828
  174.9 5.1 %collective-permute-start.8 = (bf16[4,16,128]{2,1,0:T(8,128)(2,1)S(1)}, bf16[4,16,128]{2,1,0:T(8,128)(2,1)S(1)}, u32[]{:S(2)}, u32[]{:S(2)}) collective-permute-start(bf16[4,16,128]{2,1,0:T(8,128)(2,1)S(1)} %convolution_convert_fusion.9), channel_id=1, source_target_pairs={{0,1},{1,2},{2,3},{3,4},{4,5},{5,6},{6,7},{7,8},{8,9},{9,10},{10,1... | collective-permute-start | bytes 49160 | tf_op jit(solution)/shard_map/ppermute | solution.py:24
  178.1 6.0 %collective-permute-start.9 = (bf16[4,16,128]{2,1,0:T(8,128)(2,1)S(1)}, bf16[4,16,128]{2,1,0:T(8,128)(2,1)S(1)}, u32[]{:S(2)}, u32[]{:S(2)}) collective-permute-start(bf16[4,16,128]{2,1,0:T(8,128)(2,1)S(1)} %convolution_convert_fusion.9), channel_id=1, source_target_pairs={{1,0},{2,1},{3,2},{4,3},{5,4},{6,5},{7,6},{8,7},{9,8},{10,9},{11,1... | collective-permute-start | bytes 49160 | tf_op jit(solution)/shard_map/ppermute | solution.py:27
  184.3 0.7 copy-start.1
  186.9 1.3 copy-start.16
  188.3 6.3 %collective-permute-start.10 = (bf16[2,4,48,128]{3,2,1,0:T(8,128)(2,1)}, bf16[2,4,48,128]{3,2,1,0:T(8,128)(2,1)}, u32[]{:S(2)}, u32[]{:S(2)}) collective-permute-start(bf16[2,4,48,128]{3,2,1,0:T(8,128)(2,1)} %get-tuple-element.36), channel_id=1, source_target_pairs={{0,1},{1,2},{2,3},{3,4},{4,5},{5,6},{6,7},{7,8},{8,9},{9,10},{10,1... | collective-permute-start | bytes 294920 | tf_op jit(solution)/shard_map/ppermute | solution.py:24
  190.2 7.2 %collective-permute-start.11 = (bf16[2,4,48,128]{3,2,1,0:T(8,128)(2,1)}, bf16[2,4,48,128]{3,2,1,0:T(8,128)(2,1)}, u32[]{:S(2)}, u32[]{:S(2)}) collective-permute-start(bf16[2,4,48,128]{3,2,1,0:T(8,128)(2,1)} %get-tuple-element.37), channel_id=1, source_target_pairs={{1,0},{2,1},{3,2},{4,3},{5,4},{6,5},{7,6},{8,7},{9,8},{10,9},{11,1... | collective-permute-start | bytes 294920 | tf_op jit(solution)/shard_map/ppermute | solution.py:27
  208.2 2.0 copy-start.5
  231.0 1.3 copy-start.18
  232.3 6.5 %collective-permute-start.12 = (bf16[2,4,48,128]{3,2,1,0:T(8,128)(2,1)}, bf16[2,4,48,128]{3,2,1,0:T(8,128)(2,1)}, u32[]{:S(2)}, u32[]{:S(2)}) collective-permute-start(bf16[2,4,48,128]{3,2,1,0:T(8,128)(2,1)} %get-tuple-element.34), channel_id=1, source_target_pairs={{0,1},{1,2},{2,3},{3,4},{4,5},{5,6},{6,7},{7,8},{8,9},{9,10},{10,1... | collective-permute-start | bytes 294920 | tf_op jit(solution)/shard_map/ppermute | solution.py:24
  234.2 7.2 %collective-permute-start.13 = (bf16[2,4,48,128]{3,2,1,0:T(8,128)(2,1)}, bf16[2,4,48,128]{3,2,1,0:T(8,128)(2,1)}, u32[]{:S(2)}, u32[]{:S(2)}) collective-permute-start(bf16[2,4,48,128]{3,2,1,0:T(8,128)(2,1)} %get-tuple-element.35), channel_id=1, source_target_pairs={{1,0},{2,1},{3,2},{4,3},{5,4},{6,5},{7,6},{8,7},{9,8},{10,9},{11,1... | collective-permute-start | bytes 294920 | tf_op jit(solution)/shard_map/ppermute | solution.py:27
  252.3 2.0 copy-start.3
  271.2 1.3 copy-start.26
  271.2 1.3 copy-start.27
  271.3 1.3 copy-start.30
  271.3 1.3 copy-start.31
  271.3 1.3 copy-start.35
  271.3 1.3 copy-start.36
  (7 other events, 4.5 us)
where the time goes:
time: 277 us; the launch traced here: 273 us
  local copies, waits for them, and re-layouts  120 us (43%)
  starting transfers between devices  49.3 us (18%)
  matrix products  43.1 us (16%)
  waiting for transfers between devices  25.3 us (9%)
  other arithmetic  23.3 us (8%)
  blocking collectives  10.4 us (4%)
    slice x20, local copies, waits for them, and re-layouts, atom_layer(): value_rows[:, QUERY_BLOCK * block:QUERY_BLOCK * block + KEY_WINDOW]  30 us
    slice x19, local copies, waits for them, and re-layouts, atom_layer(): key_rows[:, QUERY_BLOCK * block:QUERY_BLOCK * block + KEY_WINDOW]  29 us
    convert_element_type x8, local copies, waits for them, and re-layouts, atom_layer(): mixed = mixed.reshape(samples, atom_rows, channels).astype(jnp.bfloat16)  16.6 us
    ppermute x5, starting transfers between devices, padded_2(): lax.ppermute(lax.slice_in_dim(block, block.shape[dim] - width, None, axis...  15.3 us
    all_to_all x1, waiting for transfers between devices, shards(): lax.all_to_all(items, 'seq', split_axis=0, concat_axis=1, tiled=True)  12 us
    ppermute x4, starting transfers between devices, from_behind(): return lax.ppermute(x, axis, pairs)  11.9 us
    ppermute x5, starting transfers between devices, padded_2(): lax.ppermute(lax.slice_in_dim(block, 0, width, axis=dim), axis, backward)  10.8 us
    all_to_all x1, blocking collectives, shards(): lax.all_to_all(item_out, 'seq', split_axis=1, concat_axis=0, tiled=True)  10.4 us
  transfers between devices with their start and end apart: 16, of which 5 were waited for; matrix products, arithmetic and copies ran while one was open for 21% of the time, Pallas kernels for 0%

commit v1 on v0

v1 whole, which is shorter than its diff:
```python
import functools

import jax
import jax.numpy as jnp
from jax import lax
from jax.experimental import pallas as pl
from jax.experimental.pallas import tpu as pltpu
from jax.sharding import Mesh
from jax.sharding import PartitionSpec as P

QUERY_BLOCK = 32
KEY_WINDOW = 128
ENC_LAYERS = 2
LEVELS = 200
RIM = 48
LAYERS = 4

EPS = 1e-05
SIGMA_DATA = 16.0
BF = jnp.bfloat16
F32 = jnp.float32
SEQ = ("z", "p")
VM = pl.BlockSpec(memory_space=pltpu.VMEM)
SM = pl.BlockSpec(memory_space=pltpu.SMEM)
COUNT_LANES = 128


def normed(values):
    centre = jnp.mean(values, -1, keepdims=True)
    centred = values - centre
    spread = jnp.mean(centred * centred, -1, keepdims=True)
    return centred * lax.rsqrt(spread + EPS)


def dot(a, b):
    return jnp.dot(a, b, preferred_element_type=F32)


def dot_nt(a, b):
    return lax.dot_general(a, b, (((1,), (1,)), ((), ())), preferred_element_type=F32)


def noise_scale(noise_level):
    upper_root = 160.0 ** (1.0 / 7.0)
    lower_root = 0.0004 ** (1.0 / 7.0)
    fraction = noise_level.astype(F32) / (LEVELS - 1)
    root = upper_root + fraction * (lower_root - upper_root)
    square = root * root
    return SIGMA_DATA * (square * square * square * root)


def struct(shape, dtype):
    return jax.ShapeDtypeStruct(shape, dtype)


def call(kernel, name, out_shape, specs, args, scratch=()):
    return pl.pallas_call(
        kernel,
        name=name,
        out_shape=out_shape,
        in_specs=specs,
        out_specs=jax.tree.map(lambda _: VM, out_shape),
        scratch_shapes=scratch,
        compiler_params=pltpu.CompilerParams(vmem_limit_bytes=48 * 1024 * 1024),
    )(*args)


def emit_qkv(stream, weight, odd, samples, rows, q_ref, kv_ref, first_ref, second_ref):
    channels = stream.shape[-1]
    projected = dot(normed(stream).astype(BF), weight)
    q_ref[...] = projected[:, :channels].astype(BF)
    kv_ref[...] = projected[:, channels:].astype(BF)
    upper = rows - RIM
    for s in range(samples):
        first = pl.multiple_of(s * rows + jnp.where(odd == 0, upper, 0), 16)
        second = pl.multiple_of(s * rows + jnp.where(odd == 0, 0, upper), 16)
        first_ref[s * RIM : (s + 1) * RIM] = kv_ref[pl.ds(first, RIM)]
        second_ref[s * RIM : (s + 1) * RIM] = kv_ref[pl.ds(second, RIM)]


def block_body(
    meta, edges, q_ref, kv_ref, first_ref, second_ref, stream, bias_ref, weights, layer,
    samples, rows, padded, mixed_ref,
):
    w_out, w_up, w_down = weights
    channels = q_ref.shape[-1]
    heads = bias_ref.shape[1]
    head_size = channels // heads
    blocks = rows // QUERY_BLOCK
    odd = meta[0]
    first_atom = meta[1]
    first = pl.multiple_of(jnp.where(odd == 0, RIM + rows, 0), 16)
    second = pl.multiple_of(jnp.where(odd == 0, 0, RIM + rows), 16)
    for s in range(samples):
        padded[s, RIM : RIM + rows] = kv_ref[s * rows : (s + 1) * rows]
        padded[s, pl.ds(first, RIM)] = first_ref[s * RIM : (s + 1) * RIM]
        padded[s, pl.ds(second, RIM)] = second_ref[s * RIM : (s + 1) * RIM]
    lane = lax.broadcasted_iota(jnp.int32, (QUERY_BLOCK, channels), 1)
    head_masks = [(lane // head_size == h).astype(F32) for h in range(heads)]
    head_bits = [m.astype(BF) for m in head_masks]
    scale = head_size ** (-0.5)
    stacked = heads * QUERY_BLOCK
    for b in range(blocks):
        position = (
            first_atom
            - RIM
            + QUERY_BLOCK * b
            + lax.broadcasted_iota(jnp.int32, (stacked, KEY_WINDOW), 1)
        )
        allowed = (position >= edges[b, 0]) & (position < edges[b, 1])
        bias = jnp.where(
            allowed, bias_ref[b].reshape(stacked, KEY_WINDOW), -jnp.inf
        )
        for s in range(samples):
            at = s * rows + b * QUERY_BLOCK
            query = q_ref[at : at + QUERY_BLOCK]
            spread = jnp.concatenate([query * bit for bit in head_bits], 0)
            window = slice(QUERY_BLOCK * b, QUERY_BLOCK * b + KEY_WINDOW)
            keys = padded[s, window, :channels]
            values = padded[s, window, channels:]
            scores = dot_nt(spread, keys) * scale + bias
            expo = jnp.exp(scores - jnp.max(scores, -1, keepdims=True))
            total = jnp.sum(expo, -1, keepdims=True)
            attend = (expo * (1.0 / total)).astype(BF)
            out = dot(attend, values)
            mixed = out[:QUERY_BLOCK] * head_masks[0]
            for h in range(1, heads):
                mixed += out[h * QUERY_BLOCK : (h + 1) * QUERY_BLOCK] * head_masks[h]
            mixed_ref[at : at + QUERY_BLOCK] = mixed.astype(BF)
    stream = stream + dot(mixed_ref[...], w_out[layer])
    gated = dot(normed(stream).astype(BF), w_up[layer])
    half = gated.shape[-1] // 2
    gate = gated[:, :half]
    hidden = (gate * (1.0 / (1.0 + jnp.exp(-gate))) * gated[:, half:]).astype(BF)
    return stream + dot(hidden, w_down[layer])


def embed_kernel(
    meta, level, x_true, noise, single, w_coord, w_qkv,
    stream_ref, q_ref, kv_ref, first_ref, second_ref, *, samples, rows,
):
    sigma = noise_scale(level[...])
    inverse = lax.rsqrt(sigma * sigma + SIGMA_DATA * SIGMA_DATA)
    base = single[...].astype(F32)
    for s in range(samples):
        scaled = (x_true[...] + sigma[s : s + 1] * noise[s]) * inverse[s : s + 1]
        stream_ref[s * rows : (s + 1) * rows] = base + lax.dot_general(
            scaled, w_coord[...], (((0,), (0,)), ((), ())),
            precision=lax.Precision.HIGHEST, preferred_element_type=F32,
        )
    emit_qkv(stream_ref[...], w_qkv[0], meta[0], samples, rows, q_ref, kv_ref, first_ref, second_ref)


def block_kernel(
    meta, edges, q, kv, first, second, stream, bias, w_out, w_up, w_down, w_qkv,
    stream_ref, q_ref, kv_ref, first_ref, second_ref, padded, mixed, *, layer, samples, rows,
):
    after = block_body(
        meta, edges, q, kv, first, second, stream[...], bias, (w_out, w_up, w_down), layer,
        samples, rows, padded, mixed,
    )
    stream_ref[...] = after
    emit_qkv(after, w_qkv[layer + 1], meta[0], samples, rows, q_ref, kv_ref, first_ref, second_ref)


def selector_of(meta, atom_token, tokens):
    rows = atom_token.shape[-1]
    relative = atom_token[...] - (meta[2] - 1) * tokens
    row = lax.broadcasted_iota(jnp.int32, (3 * tokens, rows), 0)
    return (row == relative).astype(F32)


def pool_kernel(
    meta, edges, q, kv, first, second, stream, bias, w_out, w_up, w_down, w_pool, atom_token,
    stream_ref, own_ref, *rest, layer, samples, rows, tokens,
):
    send_refs, (padded, mixed, sums) = rest[: samples - 1], rest[samples - 1 :]
    after = block_body(
        meta, edges, q, kv, first, second, stream[...], bias, (w_out, w_up, w_down), layer,
        samples, rows, padded, mixed,
    )
    stream_ref[...] = after
    selector = selector_of(meta, atom_token, tokens)
    counts = jnp.sum(selector, -1, keepdims=True)
    selector = selector.astype(BF)
    normal = normed(after).astype(BF)
    width = w_pool.shape[-1]
    for s in range(samples):
        pooled = jnp.maximum(dot(normal[s * rows : (s + 1) * rows], w_pool[...]), 0.0)
        upper = pooled.astype(BF)
        lower = (pooled - upper.astype(F32)).astype(BF)
        sums[s, :, :width] = dot(selector, upper) + dot(selector, lower)
        sums[s, :, width:] = jnp.broadcast_to(counts, (3 * tokens, COUNT_LANES))
    mine = meta[3]
    own_ref[...] = sums[mine]
    for k in range(1, samples):
        send_refs[k - 1][...] = sums[lax.bitwise_xor(mine, k)].astype(BF)


def plane_kernel(meta, own, *rest, samples, tokens):
    got = rest[: samples - 1]
    mid_ref, low_ref, high_ref, total = rest[samples - 1 :]
    mine = meta[3]
    total[...] = jnp.zeros_like(total)
    at = pl.multiple_of(mine * tokens, tokens)
    total[pl.ds(at, 3 * tokens)] += own[...]
    for k in range(1, samples):
        at = pl.multiple_of(lax.bitwise_xor(mine, k) * tokens, tokens)
        total[pl.ds(at, 3 * tokens)] += got[k - 1][...].astype(F32)
    low_ref[...] = total[:tokens].astype(BF)
    high_ref[...] = total[(samples + 1) * tokens :].astype(BF)
    mid_ref[...] = total[tokens : (samples + 1) * tokens]


def token_in_kernel(
    meta, mid, from_low, from_high, single, *rest, samples, tokens
):
    got = rest[: samples - 1]
    state_ref, normal_ref, total = rest[samples - 1 :]
    width = single.shape[-1]
    total[...] = mid[...]
    total[:tokens] += from_low[...].astype(F32)
    total[(samples - 1) * tokens :] += from_high[...].astype(F32)
    state_ref[...] = total[:, :width] / total[:, width : width + 1]
    mine = meta[3]
    at = pl.multiple_of(mine * tokens, tokens)
    state_ref[pl.ds(at, tokens)] += single[...]
    for k in range(1, samples):
        at = pl.multiple_of(lax.bitwise_xor(mine, k) * tokens, tokens)
        state_ref[pl.ds(at, tokens)] += got[k - 1][...]
    normal_ref[...] = normed(state_ref[...]).astype(BF)


def token_kernel(
    meta, state, normal, *rest, samples, tokens, planes, heads
):
    gathered, rest = rest[: planes - 1], rest[planes - 1 :]
    biases, rest = rest[:samples], rest[samples:]
    w_qkv, w_out, w_back = rest[:3]
    out_ref, back_ref, low_ref, high_ref = rest[3:7]
    everyone, bias_all, q_all, k_all, v_all, mixed_all = rest[7:]
    rows = samples * tokens
    width = state.shape[-1]
    head_size = width // heads
    mine = meta[3]
    plane = meta[4]
    everyone[pl.ds(pl.multiple_of(plane * rows, rows), rows)] = normal[...]
    for k in range(1, planes):
        origin = plane - k + jnp.where(plane < k, planes, 0)
        everyone[pl.ds(pl.multiple_of(origin * rows, rows), rows)] = gathered[k - 1][...]
    for k in range(samples):
        at = pl.multiple_of(lax.bitwise_xor(mine, k) * tokens, tokens)
        bias_all[:, pl.ds(at, tokens)] = biases[k][...]
    q_all[...] = dot(normal[...], w_qkv[:, :width]).astype(BF)
    k_all[...] = dot(everyone[...], w_qkv[:, width : 2 * width]).astype(BF)
    v_all[...] = dot(everyone[...], w_qkv[:, 2 * width :]).astype(BF)
    scale = head_size ** (-0.5)
    mixed_all[...] = jnp.zeros_like(mixed_all)
    for h in range(heads):
        start = h * head_size // 128 * 128
        stop = -(-(h + 1) * head_size // 128) * 128
        lane = lax.broadcasted_iota(jnp.int32, (rows, stop - start), 1) + start
        mask = ((lane >= h * head_size) & (lane < (h + 1) * head_size)).astype(F32)
        query = q_all[:, start:stop] * mask.astype(BF)
        scores = dot_nt(query, k_all[:, start:stop]) * scale + bias_all[h]
        expo = jnp.exp(scores - jnp.max(scores, -1, keepdims=True))
        total = jnp.sum(expo, -1, keepdims=True)
        attend = expo * (1.0 / total)
        upper = attend.astype(BF)
        lower = (attend - upper.astype(F32)).astype(BF)
        values = v_all[:, start:stop]
        out = dot(upper, values) + dot(lower, values)
        mixed_all[:, start:stop] += out * mask
    after = state[...] + dot(mixed_all[...].astype(BF), w_out[...])
    out_ref[...] = after
    back = dot(normed(after).astype(BF), w_back[...]).astype(BF)
    back_ref[...] = back
    low_ref[...] = back[:tokens]
    high_ref[...] = back[rows - tokens :]


def back_kernel(meta, back, from_low, from_high, *rest, samples, tokens):
    own_ref, send_refs, padded = rest[0], rest[1:samples], rest[samples]
    padded[:tokens] = from_low[...]
    padded[tokens : (samples + 1) * tokens] = back[...]
    padded[(samples + 1) * tokens :] = from_high[...]
    mine = meta[3]
    own_ref[...] = padded[pl.ds(pl.multiple_of(mine * tokens, tokens), 3 * tokens)]
    for k in range(1, samples):
        at = pl.multiple_of(lax.bitwise_xor(mine, k) * tokens, tokens)
        send_refs[k - 1][...] = padded[pl.ds(at, 3 * tokens)]


def unpool_kernel(meta, stream, atom_token, w_qkv, *rest, samples, rows, tokens):
    backs, rest = rest[:samples], rest[samples:]
    stream_ref, q_ref, kv_ref, first_ref, second_ref, picked = rest
    selector = selector_of(meta, atom_token, tokens).astype(BF)
    mine = meta[3]
    for k in range(samples):
        picked[lax.bitwise_xor(mine, k)] = lax.dot_general(
            selector, backs[k][...], (((0,), (0,)), ((), ())), preferred_element_type=F32
        )
    after = stream[...] + picked[...].reshape(stream.shape)
    stream_ref[...] = after
    emit_qkv(after, w_qkv[ENC_LAYERS], meta[0], samples, rows, q_ref, kv_ref, first_ref, second_ref)


def final_kernel(
    meta, edges, q, kv, first, second, stream, bias, w_out, w_up, w_down, w_final,
    level, x_true, noise, *rest, layer, samples, rows,
):
    states, rest = rest[:samples], rest[samples:]
    denoised_ref, state_ref, padded, mixed = rest
    after = block_body(
        meta, edges, q, kv, first, second, stream[...], bias, (w_out, w_up, w_down), layer,
        samples, rows, padded, mixed,
    )
    mine = meta[3]
    for k in range(samples):
        state_ref[lax.bitwise_xor(mine, k)] = states[k][...]
    normal = normed(after).astype(BF)
    sigma = noise_scale(level[...])
    total = sigma * sigma + SIGMA_DATA * SIGMA_DATA
    keep = SIGMA_DATA * SIGMA_DATA / total
    move = sigma * SIGMA_DATA * lax.rsqrt(total)
    for s in range(samples):
        update = dot_nt(w_final[...], normal[s * rows : (s + 1) * rows])
        noisy = x_true[...] + sigma[s : s + 1] * noise[s]
        denoised_ref[s] = (keep[s : s + 1] * noisy + move[s : s + 1] * update) / SIGMA_DATA


def swap_rims(pair, count):
    first, second = pair
    lower = [(i, i ^ 1) for i in range(count) if (i ^ 1) < count]
    upper = [(i, i + 1) for i in range(1, count - 1, 2)]
    upper += [(j, i) for i, j in upper]
    return lax.ppermute(first, SEQ, lower), lax.ppermute(second, SEQ, upper)


def across(arrays, count):
    return [
        lax.ppermute(a, "p", [(i, i ^ k) for i in range(count)])
        for k, a in enumerate(arrays, 1)
    ]


def shards(
    x_true, noise, noise_level, atom_single, atom_token, window_edges, atom_pair_bias,
    token_single, pair_bias, w_coord, w_atom_qkv, w_atom_out, w_atom_up, w_atom_down,
    w_pool, w_token_qkv, w_token_out, w_back, w_final,
):
    samples = noise.shape[0]
    rows, channels = atom_single.shape
    tokens, width = token_single.shape
    heads = pair_bias.shape[0]
    planes = lax.axis_size("z")
    count = planes * samples
    mine = lax.axis_index("p")
    plane = lax.axis_index("z")
    device = plane * samples + mine
    meta = jnp.stack([device % 2, device * rows, device, mine, plane]).astype(jnp.int32)
    level = noise_level[:, None]
    atom_token = atom_token[None, :]
    whole = samples * rows
    rim = struct((samples * RIM, 2 * channels), BF)
    atom_outs = (
        struct((whole, channels), F32),
        struct((whole, channels), BF),
        struct((whole, 2 * channels), BF),
        rim,
        rim,
    )
    scratch = [
        pltpu.VMEM((samples, rows + 2 * RIM, 2 * channels), BF),
        pltpu.VMEM((whole, channels), BF),
    ]
    sizes = dict(samples=samples, rows=rows)
    biases = across([pair_bias] * (samples - 1), samples)
    singles = across([token_single] * (samples - 1), samples)

    stream, q, kv, first, second = call(
        functools.partial(embed_kernel, **sizes), "embed", atom_outs, [SM] + [VM] * 6,
        (meta, level, x_true, noise, atom_single, w_coord, w_atom_qkv),
    )
    stacks = (w_atom_out, w_atom_up, w_atom_down)
    for layer in range(ENC_LAYERS - 1):
        first, second = swap_rims((first, second), count)
        stream, q, kv, first, second = call(
            functools.partial(block_kernel, layer=layer, **sizes), f"block{layer}", atom_outs,
            [SM, SM] + [VM] * 10,
            (meta, window_edges, q, kv, first, second, stream, atom_pair_bias, *stacks, w_atom_qkv),
            scratch,
        )
    first, second = swap_rims((first, second), count)
    lanes = width + COUNT_LANES
    encoded, own, *sends = call(
        functools.partial(pool_kernel, layer=ENC_LAYERS - 1, tokens=tokens, **sizes), "pool",
        (atom_outs[0], struct((3 * tokens, lanes), F32))
        + (struct((3 * tokens, lanes), BF),) * (samples - 1),
        [SM, SM] + [VM] * 11,
        (meta, window_edges, q, kv, first, second, stream, atom_pair_bias, *stacks, w_pool, atom_token),
        scratch + [pltpu.VMEM((samples, 3 * tokens, lanes), F32)],
    )
    got = across(sends, samples)
    mid, low, high = call(
        functools.partial(plane_kernel, samples=samples, tokens=tokens), "plane",
        (
            struct((samples * tokens, lanes), F32),
            struct((tokens, lanes), BF),
            struct((tokens, lanes), BF),
        ),
        [SM] + [VM] * samples, (meta, own, *got),
        [pltpu.VMEM(((samples + 2) * tokens, lanes), F32)],
    )
    forward = [(i, i + 1) for i in range(planes - 1)]
    backward = [(j, i) for i, j in forward]
    from_low = lax.ppermute(high, "z", forward)
    from_high = lax.ppermute(low, "z", backward)
    state, normal = call(
        functools.partial(token_in_kernel, samples=samples, tokens=tokens), "token_in",
        (struct((samples * tokens, width), F32), struct((samples * tokens, width), BF)),
        [SM] + [VM] * (4 + samples - 1),
        (meta, mid, from_low, from_high, token_single, *singles),
        [pltpu.VMEM((samples * tokens, lanes), F32)],
    )
    gathered = [
        lax.ppermute(normal, "z", [(i, (i + k) % planes) for i in range(planes)])
        for k in range(1, planes)
    ]
    every = planes * samples * tokens
    held = samples * tokens
    state, back, low, high = call(
        functools.partial(
            token_kernel, samples=samples, tokens=tokens, planes=planes, heads=heads
        ),
        "token",
        (
            struct((held, width), F32),
            struct((held, channels), BF),
            struct((tokens, channels), BF),
            struct((tokens, channels), BF),
        ),
        [SM] + [VM] * (2 + planes - 1 + samples + 3),
        (meta, state, normal, *gathered, pair_bias, *biases, w_token_qkv, w_token_out, w_back),
        [
            pltpu.VMEM((every, width), BF),
            pltpu.VMEM((heads, held, every), F32),
            pltpu.VMEM((held, width), BF),
            pltpu.VMEM((every, width), BF),
            pltpu.VMEM((every, width), BF),
            pltpu.VMEM((held, width), F32),
        ],
    )
    from_low = lax.ppermute(high, "z", forward)
    from_high = lax.ppermute(low, "z", backward)
    own, *sends = call(
        functools.partial(back_kernel, samples=samples, tokens=tokens), "back",
        (struct((3 * tokens, channels), BF),) * samples,
        [SM] + [VM] * 3, (meta, back, from_low, from_high),
        [pltpu.VMEM(((samples + 2) * tokens, channels), BF)],
    )
    got = across(sends, samples)
    state = state.reshape(samples, tokens, width)
    pieces = [
        lax.dynamic_index_in_dim(state, lax.bitwise_xor(mine, k), 0, keepdims=False)
        for k in range(samples)
    ]
    states = [pieces[0]] + across(pieces[1:], samples)
    stream, q, kv, first, second = call(
        functools.partial(unpool_kernel, tokens=tokens, **sizes), "unpool", atom_outs,
        [SM] + [VM] * (3 + samples), (meta, encoded, atom_token, w_atom_qkv, own, *got),
        [pltpu.VMEM((samples, rows, channels), F32)],
    )
    for layer in range(ENC_LAYERS, LAYERS - 1):
        first, second = swap_rims((first, second), count)
        stream, q, kv, first, second = call(
            functools.partial(block_kernel, layer=layer, **sizes), f"block{layer}", atom_outs,
            [SM, SM] + [VM] * 10,
            (meta, window_edges, q, kv, first, second, stream, atom_pair_bias, *stacks, w_atom_qkv),
            scratch,
        )
    first, second = swap_rims((first, second), count)
    return call(
        functools.partial(final_kernel, layer=LAYERS - 1, **sizes), "final",
        (struct(noise.shape, F32), struct((samples, tokens, width), F32)),
        [SM, SM] + [VM] * (13 + samples),
        (
            meta, window_edges, q, kv, first, second, stream, atom_pair_bias, *stacks, w_final,
            level, x_true, noise, *states,
        ),
        scratch,
    )


def solution(mesh):
    def step(*args):
        groups, seq = mesh.devices.shape
        samples = args[1].shape[0] // groups
        split = Mesh(
            mesh.devices.reshape(groups, seq // samples, samples), ("groups",) + SEQ
        )
        both = ("groups",) + SEQ
        in_specs = (
            P(None, both),
            P("groups", None, SEQ),
            P("groups"),
            P(both, None),
            P(both),
            P(both, None),
            P(both, None, None, None),
            P(both, None),
            P("groups", SEQ, None),
        ) + (P(),) * 10
        out_specs = (P("groups", None, SEQ), P("groups", SEQ, None))
        return jax.shard_map(
            shards, mesh=split, in_specs=in_specs, out_specs=out_specs, check_vma=False
        )(*args)

    return step
```

time: 277 us -> 141 us (0.51)
  local copies, waits for them, and re-layouts: 120 us -> 16.3 us
  matrix products: 43.1 us -> 0 us
  Pallas kernels: 0 us -> 39.5 us
  other arithmetic: 23.3 us -> 0 us
  waiting for transfers between devices: 25.3 us -> 40.9 us
  blocking collectives: 10.4 us -> 0 us
  starting transfers between devices: 49.3 us -> 41.1 us
    slice x46 -> x0, local copies, waits for them, and re-layouts: 62.6 us -> none  [the longest x20 30 us: atom_layer(): value_rows[:, QUERY_BLOCK * block:QUERY_BLOCK * block + KEY_WINDOW]]
    dot_general x33 -> x0, matrix products: 43.1 us -> none  [the longest x4 9.67 us: atom_layer(): jnp.einsum('sbhqk,sbkhd->sbqhd', attend, value_win, preferred_element_typ...]
    pallas_call x0 -> x10, Pallas kernels: none -> 39.5 us  [call(): pl.pallas_call(kernel, name=name, out_shape=out_shape, in_specs=specs, ou...]
    ppermute x14 -> x30, waiting for transfers between devices: 13.4 us -> 40.9 us  [the longest x15 18 us: across(): lax.ppermute(a, 'p', [(i, i ^ k) for i in range(count)])]
    convert_element_type x10 -> x0, local copies, waits for them, and re-layouts: 19.8 us -> none  [the longest x8 16.6 us: atom_layer(): mixed = mixed.reshape(samples, atom_rows, channels).astype(jnp.bfloat16)]
    reshape x8 -> x0, local copies, waits for them, and re-layouts: 18.4 us -> none  [the longest x4 7.74 us: atom_layer(): queries.reshape(samples, block_count, QUERY_BLOCK, head_count, head_size)]
    all_to_all x2 -> x0, waiting for transfers between devices: 12 us -> none  [the longest x1 12 us: shards(): lax.all_to_all(items, 'seq', split_axis=0, concat_axis=1, tiled=True)]
    all_to_all x2 -> x0, starting transfers between devices: 11.4 us -> none  [the longest x1 6.52 us: shards(): lax.all_to_all(spread_bias, 'seq', split_axis=0, concat_axis=1, tiled=True)]
  transfers between devices with their start and end apart: 16 -> 30, of which waited for: 5 -> 14; matrix products, arithmetic and copies ran while one was open for 21% -> 1% of each run, Pallas kernels for 0% -> 7%
where the time goes in v1:
time: 141 us; the launch traced here: 139 us
  starting transfers between devices  41.1 us (29%)
  waiting for transfers between devices  40.9 us (29%)
  Pallas kernels  39.5 us (28%)
  local copies, waits for them, and re-layouts  16.3 us (12%)
    pallas_call x10, Pallas kernels, call(): pl.pallas_call(kernel, name=name, out_shape=out_shape, in_specs=specs, ou...  39.5 us
    ppermute x15, waiting for transfers between devices, across(): lax.ppermute(a, 'p', [(i, i ^ k) for i in range(count)])  18 us
    unnamed x54, local copies, waits for them, and re-layouts  14.9 us
    ppermute x8, starting transfers between devices, swap_rims(): return (lax.ppermute(first, SEQ, lower), lax.ppermute(second, SEQ, upper))  13.6 us
    ppermute x15, starting transfers between devices, across(): lax.ppermute(a, 'p', [(i, i ^ k) for i in range(count)])  12.9 us
    ppermute x8, waiting for transfers between devices, swap_rims(): return (lax.ppermute(first, SEQ, lower), lax.ppermute(second, SEQ, upper))  10.2 us
    ppermute x2, starting transfers between devices, shards(): from_low = lax.ppermute(high, 'z', forward)  7.83 us
    ppermute x3, waiting for transfers between devices, shards(): lax.ppermute(normal, 'z', [(i, (i + k) % planes) for i in range(planes)])  6.38 us
  transfers between devices with their start and end apart: 30, of which 14 were waited for; matrix products, arithmetic and copies ran while one was open for 1% of the time, Pallas kernels for 7%

profile of v1, /device:TPU:7, one launch (start us, length us, event | category | flops | bytes accessed | tf_op | source)
XLA Modules:
  0.0 138.9 jit_solution(14021867647208046504)
XLA Ops:
  2.2 1.0 copy-done.3
  5.3 1.5 %embed.1 = (f32[512,128]{1,0:T(8,128)S(1)}, bf16[512,128]{1,0:T(8,128)(2,1)S(1)}, bf16[512,256]{1,0:T(8,128)(2,1)S(1)}, bf16[192,256]{1,0:T(8,128)(2,1)S(1)}, bf16[192,256]{1,0:T(8,128)(2,1)S(1)}) custom-call(s32[5]{0:T(128)S(1)} %stack.23.meta, s32[4,1]{1,0:T(4,128)S(1)} %copy.21.level, f32[3,128]{1,0:T(4,128)S(1)} %copy-done.21, ...), custom_call_target="tpu_custom_call" | custom-call | tf_op jit(solution)/shard_map/embed/pallas_call | solution.py:57
  7.5 3.0 %collective-permute-start.1 = (bf16[192,256]{1,0:T(8,128)(2,1)S(1)}, bf16[192,256]{1,0:T(8,128)(2,1)S(1)}, u32[]{:S(2)}, u32[]{:S(2)}) collective-permute-start(bf16[192,256]{1,0:T(8,128)(2,1)S(1)} %get-tuple-element.43), channel_id=1, source_target_pairs={{1,2},{3,4},{5,6},{7,8},{9,10},{11,12},{13,14},{2,1},{4,3},{6,5},{... | collective-permute-start | bytes 294920 | tf_op jit(solution)/shard_map/ppermute | solution.py:337
  11.3 3.0 %collective-permute-done.1.second = bf16[192,256]{1,0:T(8,128)(2,1)S(1)} collective-permute-done((bf16[192,256]{1,0:T(8,128)(2,1)S(1)}, bf16[192,256]{1,0:T(8,128)(2,1)S(1)}, u32[]{:S(2)}, u32[]{:S(2)}) %collective-permute-start.1) | collective-permute-done | bytes 98336 | tf_op jit(solution)/shard_map/ppermute | solution.py:337
  14.3 1.0 copy-done
  15.4 1.0 copy-done.4
  16.4 0.9 copy-done.6
  17.3 0.9 copy-done.9
  18.3 0.9 copy-done.12
  19.2 7.0 %block0.1 = (f32[512,128]{1,0:T(8,128)S(1)}, bf16[512,128]{1,0:T(8,128)(2,1)S(1)}, bf16[512,256]{1,0:T(8,128)(2,1)S(1)}, bf16[192,256]{1,0:T(8,128)(2,1)S(1)}, bf16[192,256]{1,0:T(8,128)(2,1)S(1)}) custom-call(s32[5]{0:T(128)S(1)} %stack.23.meta, s32[4,2]{1,0:T(4,128)S(1)} %copy.26.edges, bf16[512,128]{1,0:T(8,128)(2,1)S(1)} %get-tuple-element.40.q, ...), custom_call_target="tpu_custom_call" | custom-call | tf_op jit(solution)/shard_map/block0/pallas_call | solution.py:57
  26.2 3.7 %collective-permute-start.3 = (bf16[192,256]{1,0:T(8,128)(2,1)S(1)}, bf16[192,256]{1,0:T(8,128)(2,1)S(1)}, u32[]{:S(2)}, u32[]{:S(2)}) collective-permute-start(bf16[192,256]{1,0:T(8,128)(2,1)S(1)} %get-tuple-element.48), channel_id=1, source_target_pairs={{1,2},{3,4},{5,6},{7,8},{9,10},{11,12},{13,14},{2,1},{4,3},{6,5},{... | collective-permute-start | bytes 294920 | tf_op jit(solution)/shard_map/ppermute | solution.py:337
  30.0 3.1 %collective-permute-done.3.second = bf16[192,256]{1,0:T(8,128)(2,1)S(1)} collective-permute-done((bf16[192,256]{1,0:T(8,128)(2,1)S(1)}, bf16[192,256]{1,0:T(8,128)(2,1)S(1)}, u32[]{:S(2)}, u32[]{:S(2)}) %collective-permute-start.3) | collective-permute-done | bytes 98336 | tf_op jit(solution)/shard_map/ppermute | solution.py:337
  33.1 1.0 copy-done.1
  34.1 0.9 copy-done.7
  35.1 0.9 copy-done.10
  36.0 0.9 copy-done.13
  36.9 0.9 copy-done.17
  38.5 7.7 %pool.1 = (f32[512,128]{1,0:T(8,128)S(1)}, f32[48,896]{1,0:T(8,128)S(1)}, bf16[48,896]{1,0:T(8,128)(2,1)S(1)}, bf16[48,896]{1,0:T(8,128)(2,1)S(1)}, bf16[48,896]{1,0:T(8,128)(2,1)S(1)}) custom-call(s32[5]{0:T(128)S(1)} %stack.23.meta, s32[4,2]{1,0:T(4,128)S(1)} %copy.26.edges, bf16[512,128]{1,0:T(8,128)(2,1)S(1)} %get-tuple-element.45.q, ...), custom_call_target="tpu_custom_call" | custom-call | tf_op jit(solution)/shard_map/pool/pallas_call | solution.py:57
  46.4 1.5 %collective-permute-start.5 = (bf16[48,896]{1,0:T(8,128)(2,1)S(1)}, bf16[48,896]{1,0:T(8,128)(2,1)S(1)}, u32[]{:S(2)}, u32[]{:S(2)}) collective-permute-start(bf16[48,896]{1,0:T(8,128)(2,1)S(1)} %get-tuple-element.53), channel_id=1, source_target_pairs={{0,2},{1,3},{2,0},{3,1},{4,6},{5,7},{6,4},{7,5},{8,10},{9,11},{10,... | collective-permute-start | bytes 258056 | tf_op jit(solution)/shard_map/ppermute | solution.py:342
  48.4 0.9 collective-permute-done.10.rest_1_
  49.3 0.9 collective-permute-start.16
  50.2 2.9 %collective-permute-start.17 = (f32[16,16,256]{2,1,0:T(8,128)S(1)}, f32[16,16,256]{2,1,0:T(8,128)S(1)}, u32[]{:S(2)}, u32[]{:S(2)}) collective-permute-start(f32[16,16,256]{2,1,0:T(8,128)S(1)} %copy-done.16), channel_id=1, source_target_pairs={{0,3},{1,2},{2,1},{3,0},{4,7},{5,6},{6,5},{7,4},{8,11},{9,10},{10,... | collective-permute-start | bytes 786440 | tf_op jit(solution)/shard_map/ppermute | solution.py:342
  54.7 11.1 %collective-permute-done.11.rest_2_ = f32[16,768]{1,0:T(8,128)S(1)} collective-permute-done((f32[16,768]{1,0:T(8,128)S(1)}, f32[16,768]{1,0:T(8,128)S(1)}, u32[]{:S(2)}, u32[]{:S(2)}) %collective-permute-start.11) | collective-permute-done | bytes 49184 | tf_op jit(solution)/shard_map/ppermute | solution.py:342
  65.8 3.5 %collective-permute-start.7 = (bf16[16,896]{1,0:T(8,128)(2,1)S(1)}, bf16[16,896]{1,0:T(8,128)(2,1)S(1)}, u32[]{:S(2)}, u32[]{:S(2)}) collective-permute-start(bf16[16,896]{1,0:T(8,128)(2,1)S(1)} %get-tuple-element.56), channel_id=1, source_target_pairs={{0,4},{4,8},{8,12},{1,5},{5,9},{9,13},{2,6},{6,10},{10,14},{3,7},{... | collective-permute-start | bytes 86024 | tf_op jit(solution)/shard_map/ppermute | solution.py:417
  69.3 1.3 collective-permute-start.8
  70.7 3.3 %collective-permute-done.8.from_high = bf16[16,896]{1,0:T(8,128)(2,1)S(1)} collective-permute-done((bf16[16,896]{1,0:T(8,128)(2,1)S(1)}, bf16[16,896]{1,0:T(8,128)(2,1)S(1)}, u32[]{:S(2)}, u32[]{:S(2)}) %collective-permute-start.8) | collective-permute-done | bytes 28704 | tf_op jit(solution)/shard_map/ppermute | solution.py:418
  74.0 0.8 token_in.1
  74.8 1.4 collective-permute-start.12
  76.7 2.3 %collective-permute-start.14 = (bf16[64,768]{1,0:T(8,128)(2,1)S(1)}, bf16[64,768]{1,0:T(8,128)(2,1)S(1)}, u32[]{:S(2)}, u32[]{:S(2)}) collective-permute-start(bf16[64,768]{1,0:T(8,128)(2,1)S(1)} %get-tuple-element.59.normal), channel_id=1, source_target_pairs={{0,12},{4,0},{8,4},{12,8},{1,13},{5,1},{9,5},{13,9},{2,14},{6,2},{... | collective-permute-start | bytes 294920 | tf_op jit(solution)/shard_map/ppermute | solution.py:427
  79.0 1.3 collective-permute-done.12.rest_0_
  80.3 5.1 %collective-permute-done.13.rest_1_ = bf16[64,768]{1,0:T(8,128)(2,1)S(1)} collective-permute-done((bf16[64,768]{1,0:T(8,128)(2,1)S(1)}, bf16[64,768]{1,0:T(8,128)(2,1)S(1)}, u32[]{:S(2)}, u32[]{:S(2)}) %collective-permute-start.13) | collective-permute-done | bytes 98336 | tf_op jit(solution)/shard_map/ppermute | solution.py:427
  85.5 5.6 %token_.1 = (f32[64,768]{1,0:T(8,128)S(1)}, bf16[64,128]{1,0:T(8,128)(2,1)S(1)}, bf16[16,128]{1,0:T(8,128)(2,1)S(1)}, bf16[16,128]{1,0:T(8,128)(2,1)S(1)}) custom-call(s32[5]{0:T(128)S(1)} %stack.23.meta, f32[64,768]{1,0:T(8,128)S(1)} %get-tuple-element.58.state, bf16[64,768]{1,0:T(8,128)(2,1)S(1)} %get-tuple-element.59.normal, ...), custom_call_target="tpu_custom_call" | custom-call | tf_op jit(solution)/shard_map/token/pallas_call | solution.py:57
  91.2 4.3 %collective-permute-start.18 = (bf16[16,128]{1,0:T(8,128)(2,1)S(1)}, bf16[16,128]{1,0:T(8,128)(2,1)S(1)}, u32[]{:S(2)}, u32[]{:S(2)}) collective-permute-start(bf16[16,128]{1,0:T(8,128)(2,1)S(1)} %get-tuple-element.61), channel_id=1, source_target_pairs={{0,4},{4,8},{8,12},{1,5},{5,9},{9,13},{2,6},{6,10},{10,14},{3,7},{... | collective-permute-start | bytes 12296 | tf_op jit(solution)/shard_map/ppermute | solution.py:454
  95.4 1.3 collective-permute-start.19
  96.7 3.0 %collective-permute-done.19.from_high = bf16[16,128]{1,0:T(8,128)(2,1)S(1)} collective-permute-done((bf16[16,128]{1,0:T(8,128)(2,1)S(1)}, bf16[16,128]{1,0:T(8,128)(2,1)S(1)}, u32[]{:S(2)}, u32[]{:S(2)}) %collective-permute-start.19) | collective-permute-done | bytes 4128 | tf_op jit(solution)/shard_map/ppermute | solution.py:455
  100.3 2.2 %collective-permute-start.20 = (bf16[48,128]{1,0:T(8,128)(2,1)S(1)}, bf16[48,128]{1,0:T(8,128)(2,1)S(1)}, u32[]{:S(2)}, u32[]{:S(2)}) collective-permute-start(bf16[48,128]{1,0:T(8,128)(2,1)S(1)} %get-tuple-element.64), channel_id=1, source_target_pairs={{0,1},{1,0},{2,3},{3,2},{4,5},{5,4},{6,7},{7,6},{8,9},{9,8},{10,11... | collective-permute-start | bytes 36872 | tf_op jit(solution)/shard_map/ppermute | solution.py:342
  103.1 1.2 collective-permute-start.22
  105.1 1.1 collective-permute-done.22.rest_3_
  106.2 1.2 unpool.1
  107.8 2.6 %collective-permute-start.24 = (bf16[192,256]{1,0:T(8,128)(2,1)S(1)}, bf16[192,256]{1,0:T(8,128)(2,1)S(1)}, u32[]{:S(2)}, u32[]{:S(2)}) collective-permute-start(bf16[192,256]{1,0:T(8,128)(2,1)S(1)} %get-tuple-element.70), channel_id=1, source_target_pairs={{1,2},{3,4},{5,6},{7,8},{9,10},{11,12},{13,14},{2,1},{4,3},{6,5},{... | collective-permute-start | bytes 294920 | tf_op jit(solution)/shard_map/ppermute | solution.py:337
  110.5 4.2 %collective-permute-done.24.second = bf16[192,256]{1,0:T(8,128)(2,1)S(1)} collective-permute-done((bf16[192,256]{1,0:T(8,128)(2,1)S(1)}, bf16[192,256]{1,0:T(8,128)(2,1)S(1)}, u32[]{:S(2)}, u32[]{:S(2)}) %collective-permute-start.24) | collective-permute-done | bytes 98336 | tf_op jit(solution)/shard_map/ppermute | solution.py:337
  114.7 7.0 %block2.1 = (f32[512,128]{1,0:T(8,128)S(1)}, bf16[512,128]{1,0:T(8,128)(2,1)S(1)}, bf16[512,256]{1,0:T(8,128)(2,1)S(1)}, bf16[192,256]{1,0:T(8,128)(2,1)S(1)}, bf16[192,256]{1,0:T(8,128)(2,1)S(1)}) custom-call(s32[5]{0:T(128)S(1)} %stack.23.meta, s32[4,2]{1,0:T(4,128)S(1)} %copy.26.edges, bf16[512,128]{1,0:T(8,128)(2,1)S(1)} %get-tuple-element.67.q, ...), custom_call_target="tpu_custom_call" | custom-call | tf_op jit(solution)/shard_map/block2/pallas_call | solution.py:57
  121.8 2.9 %collective-permute-start.26 = (bf16[192,256]{1,0:T(8,128)(2,1)S(1)}, bf16[192,256]{1,0:T(8,128)(2,1)S(1)}, u32[]{:S(2)}, u32[]{:S(2)}) collective-permute-start(bf16[192,256]{1,0:T(8,128)(2,1)S(1)} %get-tuple-element.75), channel_id=1, source_target_pairs={{1,2},{3,4},{5,6},{7,8},{9,10},{11,12},{13,14},{2,1},{4,3},{6,5},{... | collective-permute-start | bytes 294920 | tf_op jit(solution)/shard_map/ppermute | solution.py:337
  124.8 0.9 collective-permute-start.28
  125.7 1.3 collective-permute-start.29
  127.0 2.8 %collective-permute-done.28.rest_2_ = f32[16,768]{1,0:T(8,128)S(1)} collective-permute-done((f32[16,768]{1,0:T(8,128)S(1)}, f32[16,768]{1,0:T(8,128)S(1)}, u32[]{:S(2)}, u32[]{:S(2)}) %collective-permute-start.28) | collective-permute-done | bytes 49184 | tf_op jit(solution)/shard_map/ppermute | solution.py:342
  129.7 1.1 collective-permute-done.29.rest_3_
  130.8 7.4 %final.1 = (f32[4,3,128]{2,1,0:T(4,128)S(1)}, f32[4,16,768]{2,1,0:T(8,128)}) custom-call(s32[5]{0:T(128)S(1)} %stack.23.meta, s32[4,2]{1,0:T(4,128)S(1)} %copy.26.edges, bf16[512,128]{1,0:T(8,128)(2,1)S(1)} %get-tuple-element.72.q, bf16[512,256]{1,0:T(8,128)(2,1)S(1)} %get-tuple-element.73.kv, bf16[192,256]{1,0:T(8,128)(2,1)S(1)} %collective-permute-done.25.first, ...), custom_call_target="tpu_custom_call" | custom-call | tf_op jit(solution)/shard_map/final/pallas_call | solution.py:57
  (80 shorter events, 12.2 us)
Async XLA Ops:
  0.6 45.6 %copy-start.19 = (f32[16,768]{1,0:T(8,128)S(1)}, f32[16,768]{1,0:T(8,128)}, u32[]{:S(2)}) copy-start(f32[16,768]{1,0:T(8,128)} %single.3) | copy-start | bytes 147460
  2.2 1.0 copy-start.3
  5.3 44.0 %copy-start.16 = (f32[16,16,256]{2,1,0:T(8,128)S(1)}, f32[16,16,256]{2,1,0:T(8,128)}, u32[]{:S(2)}) copy-start(f32[16,16,256]{2,1,0:T(8,128)} %rest_3_.1) | copy-start | bytes 786436
  6.8 4.6 %collective-permute-start = (bf16[192,256]{1,0:T(8,128)(2,1)S(1)}, bf16[192,256]{1,0:T(8,128)(2,1)S(1)}, u32[]{:S(2)}, u32[]{:S(2)}) collective-permute-start(bf16[192,256]{1,0:T(8,128)(2,1)S(1)} %get-tuple-element.42), channel_id=1, source_target_pairs={{0,1},{1,0},{2,3},{3,2},{4,5},{5,4},{6,7},{7,6},{8,9},{9,8},{10,11... | collective-permute-start | bytes 294920 | tf_op jit(solution)/shard_map/ppermute | solution.py:337
  7.5 6.8 %collective-permute-start.1 = (bf16[192,256]{1,0:T(8,128)(2,1)S(1)}, bf16[192,256]{1,0:T(8,128)(2,1)S(1)}, u32[]{:S(2)}, u32[]{:S(2)}) collective-permute-start(bf16[192,256]{1,0:T(8,128)(2,1)S(1)} %get-tuple-element.43), channel_id=1, source_target_pairs={{1,2},{3,4},{5,6},{7,8},{9,10},{11,12},{13,14},{2,1},{4,3},{6,5},{... | collective-permute-start | bytes 294920 | tf_op jit(solution)/shard_map/ppermute | solution.py:337
  14.3 1.0 copy-start
  15.4 1.0 copy-start.4
  16.4 0.9 copy-start.6
  17.3 0.9 copy-start.9
  19.2 66.3 %copy-start.15 = (bf16[768,768]{1,0:T(8,128)(2,1)S(1)}, bf16[768,768]{1,0:T(8,128)(2,1)}, u32[]{:S(2)}) copy-start(bf16[768,768]{1,0:T(8,128)(2,1)} %rest_8_.1) | copy-start | bytes 3538948
  19.2 66.3 %copy-start.18 = (bf16[768,128]{1,0:T(8,128)(2,1)S(1)}, bf16[768,128]{1,0:T(8,128)(2,1)}, u32[]{:S(2)}) copy-start(bf16[768,128]{1,0:T(8,128)(2,1)} %rest_9_.1) | copy-start | bytes 589828
  26.2 3.8 %collective-permute-start.2 = (bf16[192,256]{1,0:T(8,128)(2,1)S(1)}, bf16[192,256]{1,0:T(8,128)(2,1)S(1)}, u32[]{:S(2)}, u32[]{:S(2)}) collective-permute-start(bf16[192,256]{1,0:T(8,128)(2,1)S(1)} %get-tuple-element.47), channel_id=1, source_target_pairs={{0,1},{1,0},{2,3},{3,2},{4,5},{5,4},{6,7},{7,6},{8,9},{9,8},{10,11... | collective-permute-start | bytes 294920 | tf_op jit(solution)/shard_map/ppermute | solution.py:337
  26.2 6.8 %collective-permute-start.3 = (bf16[192,256]{1,0:T(8,128)(2,1)S(1)}, bf16[192,256]{1,0:T(8,128)(2,1)S(1)}, u32[]{:S(2)}, u32[]{:S(2)}) collective-permute-start(bf16[192,256]{1,0:T(8,128)(2,1)S(1)} %get-tuple-element.48), channel_id=1, source_target_pairs={{1,2},{3,4},{5,6},{7,8},{9,10},{11,12},{13,14},{2,1},{4,3},{6,5},{... | collective-permute-start | bytes 294920 | tf_op jit(solution)/shard_map/ppermute | solution.py:337
  29.9 46.8 %collective-permute-start.15 = (f32[16,16,256]{2,1,0:T(8,128)}, f32[16,16,256]{2,1,0:T(8,128)S(1)}, u32[]{:S(2)}, u32[]{:S(2)}) collective-permute-start(f32[16,16,256]{2,1,0:T(8,128)} %rest_3_.1), channel_id=1, source_target_pairs={{0,1},{1,0},{2,3},{3,2},{4,5},{5,4},{6,7},{7,6},{8,9},{9,8},{10,11... | collective-permute-start | bytes 786440 | tf_op jit(solution)/shard_map/ppermute | solution.py:342
  33.1 1.0 copy-start.1
  34.1 0.9 copy-start.7
  46.2 4.0 %collective-permute-start.4 = (bf16[48,896]{1,0:T(8,128)(2,1)S(1)}, bf16[48,896]{1,0:T(8,128)(2,1)S(1)}, u32[]{:S(2)}, u32[]{:S(2)}) collective-permute-start(bf16[48,896]{1,0:T(8,128)(2,1)S(1)} %get-tuple-element.52), channel_id=1, source_target_pairs={{0,1},{1,0},{2,3},{3,2},{4,5},{5,4},{6,7},{7,6},{8,9},{9,8},{10,11... | collective-permute-start | bytes 258056 | tf_op jit(solution)/shard_map/ppermute | solution.py:342
  46.3 3.0 %collective-permute-start.10 = (f32[16,768]{1,0:T(8,128)S(1)}, f32[16,768]{1,0:T(8,128)S(1)}, u32[]{:S(2)}, u32[]{:S(2)}) collective-permute-start(f32[16,768]{1,0:T(8,128)S(1)} %copy-done.19), channel_id=1, source_target_pairs={{0,2},{1,3},{2,0},{3,1},{4,6},{5,7},{6,4},{7,5},{8,10},{9,11},{10,... | collective-permute-start | bytes 147464 | tf_op jit(solution)/shard_map/ppermute | solution.py:342
  46.4 6.7 %collective-permute-start.5 = (bf16[48,896]{1,0:T(8,128)(2,1)S(1)}, bf16[48,896]{1,0:T(8,128)(2,1)S(1)}, u32[]{:S(2)}, u32[]{:S(2)}) collective-permute-start(bf16[48,896]{1,0:T(8,128)(2,1)S(1)} %get-tuple-element.53), channel_id=1, source_target_pairs={{0,2},{1,3},{2,0},{3,1},{4,6},{5,7},{6,4},{7,5},{8,10},{9,11},{10,... | collective-permute-start | bytes 258056 | tf_op jit(solution)/shard_map/ppermute | solution.py:342
  47.8 6.2 %collective-permute-start.6 = (bf16[48,896]{1,0:T(8,128)(2,1)S(1)}, bf16[48,896]{1,0:T(8,128)(2,1)S(1)}, u32[]{:S(2)}, u32[]{:S(2)}) collective-permute-start(bf16[48,896]{1,0:T(8,128)(2,1)S(1)} %get-tuple-element.54), channel_id=1, source_target_pairs={{0,3},{1,2},{2,1},{3,0},{4,7},{5,6},{6,5},{7,4},{8,11},{9,10},{10,... | collective-permute-start | bytes 258056 | tf_op jit(solution)/shard_map/ppermute | solution.py:342
  49.3 29.8 %collective-permute-start.16 = (f32[16,16,256]{2,1,0:T(8,128)S(1)}, f32[16,16,256]{2,1,0:T(8,128)S(1)}, u32[]{:S(2)}, u32[]{:S(2)}) collective-permute-start(f32[16,16,256]{2,1,0:T(8,128)S(1)} %copy-done.16), channel_id=1, source_target_pairs={{0,2},{1,3},{2,0},{3,1},{4,6},{5,7},{6,4},{7,5},{8,10},{9,11},{10,... | collective-permute-start | bytes 786440 | tf_op jit(solution)/shard_map/ppermute | solution.py:342
  50.2 28.9 %collective-permute-start.17 = (f32[16,16,256]{2,1,0:T(8,128)S(1)}, f32[16,16,256]{2,1,0:T(8,128)S(1)}, u32[]{:S(2)}, u32[]{:S(2)}) collective-permute-start(f32[16,16,256]{2,1,0:T(8,128)S(1)} %copy-done.16), channel_id=1, source_target_pairs={{0,3},{1,2},{2,1},{3,0},{4,7},{5,6},{6,5},{7,4},{8,11},{9,10},{10,... | collective-permute-start | bytes 786440 | tf_op jit(solution)/shard_map/ppermute | solution.py:342
  53.0 12.8 %collective-permute-start.11 = (f32[16,768]{1,0:T(8,128)S(1)}, f32[16,768]{1,0:T(8,128)S(1)}, u32[]{:S(2)}, u32[]{:S(2)}) collective-permute-start(f32[16,768]{1,0:T(8,128)S(1)} %copy-done.19), channel_id=1, source_target_pairs={{0,3},{1,2},{2,1},{3,0},{4,7},{5,6},{6,5},{7,4},{8,11},{9,10},{10,... | collective-permute-start | bytes 147464 | tf_op jit(solution)/shard_map/ppermute | solution.py:342
  54.1 15.3 %collective-permute-start.9 = (f32[16,768]{1,0:T(8,128)S(1)}, f32[16,768]{1,0:T(8,128)S(1)}, u32[]{:S(2)}, u32[]{:S(2)}) collective-permute-start(f32[16,768]{1,0:T(8,128)S(1)} %copy-done.19), channel_id=1, source_target_pairs={{0,1},{1,0},{2,3},{3,2},{4,5},{5,4},{6,7},{7,6},{8,9},{9,8},{10,11... | collective-permute-start | bytes 147464 | tf_op jit(solution)/shard_map/ppermute | solution.py:342
  65.8 4.9 %collective-permute-start.7 = (bf16[16,896]{1,0:T(8,128)(2,1)S(1)}, bf16[16,896]{1,0:T(8,128)(2,1)S(1)}, u32[]{:S(2)}, u32[]{:S(2)}) collective-permute-start(bf16[16,896]{1,0:T(8,128)(2,1)S(1)} %get-tuple-element.56), channel_id=1, source_target_pairs={{0,4},{4,8},{8,12},{1,5},{5,9},{9,13},{2,6},{6,10},{10,14},{3,7},{... | collective-permute-start | bytes 86024 | tf_op jit(solution)/shard_map/ppermute | solution.py:417
  69.3 4.6 %collective-permute-start.8 = (bf16[16,896]{1,0:T(8,128)(2,1)S(1)}, bf16[16,896]{1,0:T(8,128)(2,1)S(1)}, u32[]{:S(2)}, u32[]{:S(2)}) collective-permute-start(bf16[16,896]{1,0:T(8,128)(2,1)S(1)} %get-tuple-element.57), channel_id=1, source_target_pairs={{4,0},{8,4},{12,8},{5,1},{9,5},{13,9},{6,2},{10,6},{14,10},{7,3},{... | collective-permute-start | bytes 86024 | tf_op jit(solution)/shard_map/ppermute | solution.py:418
  74.0 32.2 %copy-start.5 = (bf16[4,128,384]{2,1,0:T(8,128)(2,1)S(1)}, bf16[4,128,384]{2,1,0:T(8,128)(2,1)}, u32[]{:S(2)}) copy-start(bf16[4,128,384]{2,1,0:T(8,128)(2,1)} %w_qkv.7) | copy-start | bytes 1179652
  74.8 5.5 %collective-permute-start.12 = (bf16[64,768]{1,0:T(8,128)(2,1)S(1)}, bf16[64,768]{1,0:T(8,128)(2,1)S(1)}, u32[]{:S(2)}, u32[]{:S(2)}) collective-permute-start(bf16[64,768]{1,0:T(8,128)(2,1)S(1)} %get-tuple-element.59.normal), channel_id=1, source_target_pairs={{0,4},{4,8},{8,12},{12,0},{1,5},{5,9},{9,13},{13,1},{2,6},{6,10},{... | collective-permute-start | bytes 294920 | tf_op jit(solution)/shard_map/ppermute | solution.py:427
  76.2 9.2 %collective-permute-start.13 = (bf16[64,768]{1,0:T(8,128)(2,1)S(1)}, bf16[64,768]{1,0:T(8,128)(2,1)S(1)}, u32[]{:S(2)}, u32[]{:S(2)}) collective-permute-start(bf16[64,768]{1,0:T(8,128)(2,1)S(1)} %get-tuple-element.59.normal), channel_id=1, source_target_pairs={{0,8},{4,12},{8,0},{12,4},{1,9},{5,13},{9,1},{13,5},{2,10},{6,14},... | collective-permute-start | bytes 294920 | tf_op jit(solution)/shard_map/ppermute | solution.py:427
  76.7 8.7 %collective-permute-start.14 = (bf16[64,768]{1,0:T(8,128)(2,1)S(1)}, bf16[64,768]{1,0:T(8,128)(2,1)S(1)}, u32[]{:S(2)}, u32[]{:S(2)}) collective-permute-start(bf16[64,768]{1,0:T(8,128)(2,1)S(1)} %get-tuple-element.59.normal), channel_id=1, source_target_pairs={{0,12},{4,0},{8,4},{12,8},{1,13},{5,1},{9,5},{13,9},{2,14},{6,2},{... | collective-permute-start | bytes 294920 | tf_op jit(solution)/shard_map/ppermute | solution.py:427
  85.4 29.2 %copy-start.2 = (bf16[4,128,512]{2,1,0:T(8,128)(2,1)S(1)}, bf16[4,128,512]{2,1,0:T(8,128)(2,1)}, u32[]{:S(2)}) copy-start(bf16[4,128,512]{2,1,0:T(8,128)(2,1)} %w_up.7) | copy-start | bytes 1572868
  85.4 29.2 %copy-start.8 = (f32[4,4,32,128]{3,2,1,0:T(8,128)S(1)}, f32[4,4,32,128]{3,2,1,0:T(8,128)}, u32[]{:S(2)}) copy-start(f32[4,4,32,128]{3,2,1,0:T(8,128)} %bias.7) | copy-start | bytes 786436
  85.5 29.2 %copy-start.11 = (bf16[4,256,128]{2,1,0:T(8,128)(2,1)S(1)}, bf16[4,256,128]{2,1,0:T(8,128)(2,1)}, u32[]{:S(2)}) copy-start(bf16[4,256,128]{2,1,0:T(8,128)(2,1)} %w_down.7) | copy-start | bytes 786436
  85.5 29.2 %copy-start.14 = (bf16[4,128,128]{2,1,0:T(8,128)(2,1)S(1)}, bf16[4,128,128]{2,1,0:T(8,128)(2,1)}, u32[]{:S(2)}) copy-start(bf16[4,128,128]{2,1,0:T(8,128)(2,1)} %w_out.7) | copy-start | bytes 393220
  85.5 45.3 %copy-start.22 = (f32[3,128]{1,0:T(4,128)S(1)}, f32[3,128]{1,0:T(4,128)}, u32[]{:S(2)}) copy-start(f32[3,128]{1,0:T(4,128)} %x_true.3) | copy-start | bytes 4612
  85.5 45.3 %copy-start.25 = (bf16[3,128]{1,0:T(4,128)(2,1)S(1)}, bf16[3,128]{1,0:T(4,128)(2,1)}, u32[]{:S(2)}) copy-start(bf16[3,128]{1,0:T(4,128)(2,1)} %w_final.1) | copy-start | bytes 2308
  91.2 5.6 %collective-permute-start.18 = (bf16[16,128]{1,0:T(8,128)(2,1)S(1)}, bf16[16,128]{1,0:T(8,128)(2,1)S(1)}, u32[]{:S(2)}, u32[]{:S(2)}) collective-permute-start(bf16[16,128]{1,0:T(8,128)(2,1)S(1)} %get-tuple-element.61), channel_id=1, source_target_pairs={{0,4},{4,8},{8,12},{1,5},{5,9},{9,13},{2,6},{6,10},{10,14},{3,7},{... | collective-permute-start | bytes 12296 | tf_op jit(solution)/shard_map/ppermute | solution.py:454
  95.4 4.4 %collective-permute-start.19 = (bf16[16,128]{1,0:T(8,128)(2,1)S(1)}, bf16[16,128]{1,0:T(8,128)(2,1)S(1)}, u32[]{:S(2)}, u32[]{:S(2)}) collective-permute-start(bf16[16,128]{1,0:T(8,128)(2,1)S(1)} %get-tuple-element.62), channel_id=1, source_target_pairs={{4,0},{8,4},{12,8},{5,1},{9,5},{13,9},{6,2},{10,6},{14,10},{7,3},{... | collective-permute-start | bytes 12296 | tf_op jit(solution)/shard_map/ppermute | solution.py:455
  100.3 3.9 %collective-permute-start.20 = (bf16[48,128]{1,0:T(8,128)(2,1)S(1)}, bf16[48,128]{1,0:T(8,128)(2,1)S(1)}, u32[]{:S(2)}, u32[]{:S(2)}) collective-permute-start(bf16[48,128]{1,0:T(8,128)(2,1)S(1)} %get-tuple-element.64), channel_id=1, source_target_pairs={{0,1},{1,0},{2,3},{3,2},{4,5},{5,4},{6,7},{7,6},{8,9},{9,8},{10,11... | collective-permute-start | bytes 36872 | tf_op jit(solution)/shard_map/ppermute | solution.py:342
  102.5 2.5 %collective-permute-start.21 = (bf16[48,128]{1,0:T(8,128)(2,1)S(1)}, bf16[48,128]{1,0:T(8,128)(2,1)S(1)}, u32[]{:S(2)}, u32[]{:S(2)}) collective-permute-start(bf16[48,128]{1,0:T(8,128)(2,1)S(1)} %get-tuple-element.65), channel_id=1, source_target_pairs={{0,2},{1,3},{2,0},{3,1},{4,6},{5,7},{6,4},{7,5},{8,10},{9,11},{10,... | collective-permute-start | bytes 36872 | tf_op jit(solution)/shard_map/ppermute | solution.py:342
  103.1 3.1 %collective-permute-start.22 = (bf16[48,128]{1,0:T(8,128)(2,1)S(1)}, bf16[48,128]{1,0:T(8,128)(2,1)S(1)}, u32[]{:S(2)}, u32[]{:S(2)}) collective-permute-start(bf16[48,128]{1,0:T(8,128)(2,1)S(1)} %get-tuple-element.66), channel_id=1, source_target_pairs={{0,3},{1,2},{2,1},{3,0},{4,7},{5,6},{6,5},{7,4},{8,11},{9,10},{10,... | collective-permute-start | bytes 36872 | tf_op jit(solution)/shard_map/ppermute | solution.py:342
  107.4 3.1 %collective-permute-start.23 = (bf16[192,256]{1,0:T(8,128)(2,1)S(1)}, bf16[192,256]{1,0:T(8,128)(2,1)S(1)}, u32[]{:S(2)}, u32[]{:S(2)}) collective-permute-start(bf16[192,256]{1,0:T(8,128)(2,1)S(1)} %get-tuple-element.69), channel_id=1, source_target_pairs={{0,1},{1,0},{2,3},{3,2},{4,5},{5,4},{6,7},{7,6},{8,9},{9,8},{10,11... | collective-permute-start | bytes 294920 | tf_op jit(solution)/shard_map/ppermute | solution.py:337
  107.8 6.8 %collective-permute-start.24 = (bf16[192,256]{1,0:T(8,128)(2,1)S(1)}, bf16[192,256]{1,0:T(8,128)(2,1)S(1)}, u32[]{:S(2)}, u32[]{:S(2)}) collective-permute-start(bf16[192,256]{1,0:T(8,128)(2,1)S(1)} %get-tuple-element.70), channel_id=1, source_target_pairs={{1,2},{3,4},{5,6},{7,8},{9,10},{11,12},{13,14},{2,1},{4,3},{6,5},{... | collective-permute-start | bytes 294920 | tf_op jit(solution)/shard_map/ppermute | solution.py:337
  121.7 9.1 %collective-permute-start.25 = (bf16[192,256]{1,0:T(8,128)(2,1)S(1)}, bf16[192,256]{1,0:T(8,128)(2,1)S(1)}, u32[]{:S(2)}, u32[]{:S(2)}) collective-permute-start(bf16[192,256]{1,0:T(8,128)(2,1)S(1)} %get-tuple-element.74), channel_id=1, source_target_pairs={{0,1},{1,0},{2,3},{3,2},{4,5},{5,4},{6,7},{7,6},{8,9},{9,8},{10,11... | collective-permute-start | bytes 294920 | tf_op jit(solution)/shard_map/ppermute | solution.py:337
  121.8 9.0 %collective-permute-start.26 = (bf16[192,256]{1,0:T(8,128)(2,1)S(1)}, bf16[192,256]{1,0:T(8,128)(2,1)S(1)}, u32[]{:S(2)}, u32[]{:S(2)}) collective-permute-start(bf16[192,256]{1,0:T(8,128)(2,1)S(1)} %get-tuple-element.75), channel_id=1, source_target_pairs={{1,2},{3,4},{5,6},{7,8},{9,10},{11,12},{13,14},{2,1},{4,3},{6,5},{... | collective-permute-start | bytes 294920 | tf_op jit(solution)/shard_map/ppermute | solution.py:337
  124.8 2.2 %collective-permute-start.27 = (f32[16,768]{1,0:T(8,128)S(1)}, f32[16,768]{1,0:T(8,128)S(1)}, u32[]{:S(2)}, u32[]{:S(2)}) collective-permute-start(f32[16,768]{1,0:T(8,128)S(1)} %get-tuple-element.82), channel_id=1, source_target_pairs={{0,1},{1,0},{2,3},{3,2},{4,5},{5,4},{6,7},{7,6},{8,9},{9,8},{10,11... | collective-permute-start | bytes 147464 | tf_op jit(solution)/shard_map/ppermute | solution.py:342
  124.8 4.9 %collective-permute-start.28 = (f32[16,768]{1,0:T(8,128)S(1)}, f32[16,768]{1,0:T(8,128)S(1)}, u32[]{:S(2)}, u32[]{:S(2)}) collective-permute-start(f32[16,768]{1,0:T(8,128)S(1)} %get-tuple-element.81), channel_id=1, source_target_pairs={{0,2},{1,3},{2,0},{3,1},{4,6},{5,7},{6,4},{7,5},{8,10},{9,11},{10,... | collective-permute-start | bytes 147464 | tf_op jit(solution)/shard_map/ppermute | solution.py:342
  125.7 5.1 %collective-permute-start.29 = (f32[16,768]{1,0:T(8,128)S(1)}, f32[16,768]{1,0:T(8,128)S(1)}, u32[]{:S(2)}, u32[]{:S(2)}) collective-permute-start(f32[16,768]{1,0:T(8,128)S(1)} %get-tuple-element.80), channel_id=1, source_target_pairs={{0,3},{1,2},{2,1},{3,0},{4,7},{5,6},{6,5},{7,4},{8,11},{9,10},{10,... | collective-permute-start | bytes 147464 | tf_op jit(solution)/shard_map/ppermute | solution.py:342
  (8 other events, 6.5 us)

commit v2 on v1

v2 whole, which is shorter than its diff:
```python
import functools

import jax
import jax.numpy as jnp
from jax import lax
from jax.experimental import pallas as pl
from jax.experimental.pallas import tpu as pltpu
from jax.sharding import Mesh
from jax.sharding import PartitionSpec as P

QUERY_BLOCK = 32
KEY_WINDOW = 128
ENC_LAYERS = 2
LEVELS = 200
RIM = 48
LAYERS = 4

EPS = 1e-05
SIGMA_DATA = 16.0
BF = jnp.bfloat16
F32 = jnp.float32
SEQ = ("z", "p")
VM = pl.BlockSpec(memory_space=pltpu.VMEM)
SM = pl.BlockSpec(memory_space=pltpu.SMEM)
HB = pl.BlockSpec(memory_space=pltpu.HBM)
COUNT_LANES = 128
PLACES = 5
LOG2E = 1.4426950408889634


def normed(values):
    centre = jnp.mean(values, -1, keepdims=True)
    centred = values - centre
    spread = jnp.mean(centred * centred, -1, keepdims=True)
    return centred * lax.rsqrt(spread + EPS)


def dot(a, b):
    return jnp.dot(a, b, preferred_element_type=F32)


def dot_nt(a, b):
    return lax.dot_general(a, b, (((1,), (1,)), ((), ())), preferred_element_type=F32)


def noise_scale(noise_level):
    upper_root = 160.0 ** (1.0 / 7.0)
    lower_root = 0.0004 ** (1.0 / 7.0)
    fraction = noise_level.astype(F32) / (LEVELS - 1)
    root = upper_root + fraction * (lower_root - upper_root)
    square = root * root
    return SIGMA_DATA * (square * square * square * root)


def struct(shape, dtype):
    return jax.ShapeDtypeStruct(shape, dtype)


def call(kernel, out_shape, specs, args, scratch=()):
    return pl.pallas_call(
        kernel,
        out_shape=out_shape,
        in_specs=specs,
        out_specs=jax.tree.map(lambda _: VM, out_shape),
        scratch_shapes=scratch,
        compiler_params=pltpu.CompilerParams(vmem_limit_bytes=48 * 1024 * 1024),
    )(
        *[
            pltpu.with_memory_space_constraint(arg, pltpu.HBM) if spec is HB else arg
            for spec, arg in zip(specs, args)
        ]
    )


def halves(odd, lower, upper):
    first = jnp.where(odd == 0, upper, lower)
    second = jnp.where(odd == 0, lower, upper)
    return pl.multiple_of(first, 16), pl.multiple_of(second, 16)


def emit_rims(kv_ref, odd, samples, rows, first_ref, second_ref):
    for s in range(samples):
        first, second = halves(odd, s * rows, (s + 1) * rows - RIM)
        first_ref[s * RIM : (s + 1) * RIM] = kv_ref[pl.ds(first, RIM)]
        second_ref[s * RIM : (s + 1) * RIM] = kv_ref[pl.ds(second, RIM)]


def block_rows(b, samples, rows):
    return [slice(s * rows + b * QUERY_BLOCK, s * rows + (b + 1) * QUERY_BLOCK) for s in range(samples)]


def load_rows(ref, b, samples, rows):
    return jnp.concatenate([ref[at] for at in block_rows(b, samples, rows)], 0)


def store_rows(ref, b, samples, rows, values):
    for s, at in enumerate(block_rows(b, samples, rows)):
        ref[at] = values[s * QUERY_BLOCK : (s + 1) * QUERY_BLOCK]


def run_stages(stages, count):
    held = {}
    for step in range(count + len(stages) - 1):
        for place in reversed(range(len(stages))):
            unit = step - place
            if 0 <= unit < count:
                held[unit] = stages[place](unit, held.get(unit))


def fetch(pairs, sems):
    copies = [
        pltpu.make_async_copy(source, target, sems.at[i])
        for i, (source, target) in enumerate(pairs)
    ]
    for copy in copies:
        copy.start()
    return copies


def run_block(
    meta, q_ref, kv_ref, first_ref, second_ref, stream_ref, bias_ref, weights, copies,
    samples, rows, padded, out_ref, finish,
):
    w_out, w_up, w_down = weights
    channels = q_ref.shape[-1]
    heads = bias_ref.shape[1] // QUERY_BLOCK
    head_size = channels // heads
    blocks = rows // QUERY_BLOCK
    first, second = halves(meta[0], 0, RIM + rows)
    for s in range(samples):
        padded[s, RIM : RIM + rows] = kv_ref[s * rows : (s + 1) * rows]
        padded[s, pl.ds(first, RIM)] = first_ref[s * RIM : (s + 1) * RIM]
        padded[s, pl.ds(second, RIM)] = second_ref[s * RIM : (s + 1) * RIM]
    lane = lax.broadcasted_iota(jnp.int32, (QUERY_BLOCK, channels), 1)
    head_masks = [(lane // head_size == h).astype(F32) for h in range(heads)]
    head_bits = [m.astype(BF) for m in head_masks]
    head_masks = [jnp.concatenate([m, m], 1) for m in head_masks]
    scale = head_size ** (-0.5) * LOG2E
    ones = jnp.ones((KEY_WINDOW, channels), BF)

    def score(b, _):
        bias = bias_ref[b]
        scores = []
        for s, at in enumerate(block_rows(b, samples, rows)):
            query = q_ref[at]
            spread = jnp.concatenate([query * bit for bit in head_bits], 0)
            keys = padded[s, QUERY_BLOCK * b : QUERY_BLOCK * b + KEY_WINDOW, :channels]
            scores.append(dot_nt(spread, keys) * scale + bias)
        return scores

    def soften(b, scores):
        tops = [jnp.max(score, -1, keepdims=True) for score in scores]
        return [jnp.exp2(score - top).astype(BF) for score, top in zip(scores, tops)]

    def mix(b, expos):
        parts = []
        for s, expo in enumerate(expos):
            values = padded[s, QUERY_BLOCK * b : QUERY_BLOCK * b + KEY_WINDOW, channels:]
            out = dot(expo, jnp.concatenate([values, ones], 1))
            merged = out[:QUERY_BLOCK] * head_masks[0]
            for h in range(1, heads):
                merged += out[h * QUERY_BLOCK : (h + 1) * QUERY_BLOCK] * head_masks[h]
            parts.append(merged[:, :channels] * (1.0 / merged[:, channels:]))
        return jnp.concatenate(parts, 0).astype(BF)

    def project(b, mixed):
        if b == 0:
            for copy in copies:
                copy.wait()
        stream = load_rows(stream_ref, b, samples, rows) + dot(mixed, w_out[...])
        return stream, normed(stream).astype(BF)

    def widen(b, held):
        stream, normal = held
        gated = dot(normal, w_up[...])
        half = gated.shape[-1] // 2
        gate = gated[:, :half]
        hidden = gate * (1.0 / (1.0 + jnp.exp(-gate))) * gated[:, half:]
        return stream, hidden.astype(BF)

    def narrow(b, held):
        stream, hidden = held
        stream = stream + dot(hidden, w_down[...])
        if out_ref is not None:
            store_rows(out_ref, b, samples, rows, stream)
        return normed(stream).astype(BF)

    run_stages([score, soften, mix, project, widen, narrow, finish], blocks)


def block_scratch(samples, rows, channels, weights):
    return (
        [pltpu.VMEM((samples, rows + 2 * RIM, 2 * channels), BF)]
        + [pltpu.VMEM(w.shape[1:], w.dtype) for w in weights]
        + [pltpu.SemaphoreType.DMA((len(weights),))]
    )


def embed_kernel(
    meta, x_true_hbm, noise_hbm, single_hbm, w_coord_hbm, w_qkv_hbm,
    stream_ref, q_ref, kv_ref, first_ref, second_ref,
    x_true, noise, single, w_coord, w_qkv, sems, *, samples, rows,
):
    copies = fetch(
        [
            (x_true_hbm, x_true),
            (noise_hbm, noise),
            (single_hbm, single),
            (w_coord_hbm, w_coord),
            (w_qkv_hbm.at[0], w_qkv),
        ],
        sems,
    )
    channels = single.shape[-1]
    sigma, total = sigma_of(meta, samples)
    inverse = lax.rsqrt(total)
    for copy in copies:
        copy.wait()
    base = single[...].astype(F32)
    scaled = [
        (x_true[c : c + 1] + sigma * noise[c]) * inverse for c in range(x_true.shape[0])
    ]

    def place(s, _):
        coords = jnp.concatenate([one[s : s + 1] for one in scaled], 0)
        return base + lax.dot_general(
            coords, w_coord[...], (((0,), (0,)), ((), ())),
            precision=lax.Precision.HIGHEST, preferred_element_type=F32,
        )

    def normalise(s, stream):
        stream_ref[s * rows : (s + 1) * rows] = stream
        return normed(stream).astype(BF)

    def project(s, normal):
        projected = dot(normal, w_qkv[...])
        q_ref[s * rows : (s + 1) * rows] = projected[:, :channels].astype(BF)
        kv_ref[s * rows : (s + 1) * rows] = projected[:, channels:].astype(BF)

    run_stages([place, normalise, project], samples)
    emit_rims(kv_ref, meta[0], samples, rows, first_ref, second_ref)


def mask_kernel(meta, edges, bias_hbm, _, out_ref, bias, sems):
    blocks, heads, queries, window = bias.shape
    copies = fetch([(bias_hbm.at[b], bias.at[b]) for b in range(blocks)], sems)
    lane = lax.broadcasted_iota(jnp.int32, (heads * queries, window), 1)
    for b in range(blocks):
        position = meta[1] - RIM + QUERY_BLOCK * b + lane
        allowed = (position >= edges[0, b]) & (position < edges[1, b])
        copies[b].wait()
        values = bias[b].reshape(heads * queries, window) * LOG2E
        out_ref[b] = jnp.where(allowed, values, -jnp.inf)


def sigma_of(meta, samples):
    row = lax.broadcasted_iota(jnp.int32, (samples, 1), 0)
    levels = jnp.zeros((samples, 1), jnp.int32)
    for s in range(samples):
        levels = jnp.where(row == s, meta[PLACES + s], levels)
    sigma = noise_scale(levels)
    return sigma, sigma * sigma + SIGMA_DATA * SIGMA_DATA


def block_kernel(
    meta, q, kv, first, second, stream, bias, w_out, w_up, w_down, w_qkv,
    stream_ref, q_ref, kv_ref, first_ref, second_ref, padded, out, up, down, qkv, sems,
    *, layer, samples, rows,
):
    copies = fetch(
        [
            (w_out.at[layer], out),
            (w_up.at[layer], up),
            (w_down.at[layer], down),
            (w_qkv.at[layer + 1], qkv),
        ],
        sems,
    )
    channels = q.shape[-1]

    def finish(b, normal):
        projected = dot(normal, qkv[...]).astype(BF)
        store_rows(q_ref, b, samples, rows, projected[:, :channels])
        store_rows(kv_ref, b, samples, rows, projected[:, channels:])

    run_block(
        meta, q, kv, first, second, stream, bias, (out, up, down), copies,
        samples, rows, padded, stream_ref, finish,
    )
    emit_rims(kv_ref, meta[0], samples, rows, first_ref, second_ref)


def selector_of(meta, atom_token, tokens):
    rows = atom_token.shape[-1]
    relative = atom_token[...] - (meta[2] - 1) * tokens
    row = lax.broadcasted_iota(jnp.int32, (3 * tokens, rows), 0)
    return (row == relative).astype(F32)


def pool_kernel(
    meta, q, kv, first, second, stream, bias, w_out, w_up, w_down, w_pool, atom_token,
    *rest, layer, samples, rows, tokens,
):
    single_hbm = rest[0]
    (stream_ref, mid_ref, first_ref, second_ref, single_ref,
     padded, out, up, down, sems, normal_all, sums, pooling, owners, late_sems) = rest[-15:]
    copies = fetch(
        [(w_out.at[layer], out), (w_up.at[layer], up), (w_down.at[layer], down)], sems
    )
    late = fetch([(w_pool, pooling), (atom_token, owners), (single_hbm, single_ref)], late_sems)

    def finish(b, normal):
        store_rows(normal_all, b, samples, rows, normal)

    run_block(
        meta, q, kv, first, second, stream, bias, (out, up, down), copies,
        samples, rows, padded, stream_ref, finish,
    )
    for copy in late:
        copy.wait()
    selector = selector_of(meta, owners, tokens)
    counts = jnp.sum(selector, -1, keepdims=True)
    selector = selector.astype(BF)
    width = w_pool.shape[-1]

    def pool(s, _):
        return jnp.maximum(dot(normal_all[s * rows : (s + 1) * rows], pooling[...]), 0.0)

    def gather(s, pooled):
        upper = pooled.astype(BF)
        lower = (pooled - upper.astype(F32)).astype(BF)
        sums[s, :, :width] = dot(selector, upper) + dot(selector, lower)
        sums[s, :, width:] = jnp.broadcast_to(counts, (3 * tokens, COUNT_LANES))

    run_stages([pool, gather], samples)
    for s in range(samples):
        at = slice(s * tokens, (s + 1) * tokens)
        mid_ref[at] = sums[s, tokens : 2 * tokens]
        first_at, second_at = halves(meta[0], 0, 2 * tokens)
        first_ref[at] = sums[s, pl.ds(first_at, tokens)].astype(BF)
        second_ref[at] = sums[s, pl.ds(second_at, tokens)].astype(BF)


def token_in_kernel(
    meta, mid, first, second, single, _, state_ref, *rest, samples, tokens
):
    send_refs, normal_all = rest[:samples], rest[samples]
    width = single.shape[-1]
    total = mid[...] + first[...].astype(F32) + second[...].astype(F32)
    share = total[:, :width] / total[:, width : width + 1]
    for s in range(samples):
        at = slice(s * tokens, (s + 1) * tokens)
        state = share[at] + single[...]
        state_ref[at] = state
        normal_all[s] = normed(state).astype(BF)
    mine = meta[3]
    for k in range(samples):
        send_refs[k][...] = normal_all[lax.bitwise_xor(mine, k)]


def plane_kernel(meta, *rest, samples, tokens):
    parts, out_ref = rest[:samples], rest[samples]
    mine = meta[3]
    for k in range(samples):
        at = pl.multiple_of(lax.bitwise_xor(mine, k) * tokens, tokens)
        out_ref[pl.ds(at, tokens)] = parts[k][...]


def token_kernel(
    meta, normal, *rest, samples, tokens, planes, heads
):
    gathered, rest = rest[: planes - 1], rest[planes - 1 :]
    biases, rest = rest[:samples], rest[samples:]
    w_qkv, rest = rest[0], rest[1:]
    send_refs = rest[:samples]
    everyone, bias_all, q_all, k_all, v_all, mixed_all, sems = rest[samples:]
    rows = samples * tokens
    width = normal.shape[-1]
    head_size = width // heads
    mine = meta[3]
    plane = meta[4]
    copies = fetch(
        [
            (
                biases[k],
                bias_all.at[:, pl.ds(pl.multiple_of(lax.bitwise_xor(mine, k) * tokens, tokens), tokens)],
            )
            for k in range(samples)
        ],
        sems,
    )
    everyone[pl.ds(pl.multiple_of(plane * rows, rows), rows)] = normal[...]
    for k in range(1, planes):
        origin = plane - k + jnp.where(plane < k, planes, 0)
        everyone[pl.ds(pl.multiple_of(origin * rows, rows), rows)] = gathered[k - 1][...]
    q_all[...] = dot(normal[...], w_qkv[:, :width]).astype(BF)
    k_all[...] = dot(everyone[...], w_qkv[:, width : 2 * width]).astype(BF)
    v_all[...] = dot(everyone[...], w_qkv[:, 2 * width :]).astype(BF)
    for copy in copies:
        copy.wait()
    scale = head_size ** (-0.5) * LOG2E
    mixed_all[...] = jnp.zeros_like(mixed_all)

    def lanes_of(h):
        start = h * head_size // 128 * 128
        stop = -(-(h + 1) * head_size // 128) * 128
        lane = lax.broadcasted_iota(jnp.int32, (rows, stop - start), 1) + start
        mask = ((lane >= h * head_size) & (lane < (h + 1) * head_size)).astype(F32)
        return slice(start, stop), mask

    def score(h, _):
        at, mask = lanes_of(h)
        query = q_all[:, at] * mask.astype(BF)
        return dot_nt(query, k_all[:, at]) * scale + bias_all[h] * LOG2E

    def soften(h, scores):
        expo = jnp.exp2(scores - jnp.max(scores, -1, keepdims=True))
        attend = expo * (1.0 / jnp.sum(expo, -1, keepdims=True))
        upper = attend.astype(BF)
        return upper, (attend - upper.astype(F32)).astype(BF)

    def mix(h, attends):
        at, mask = lanes_of(h)
        values = v_all[:, at]
        mixed_all[:, at] += (dot(attends[0], values) + dot(attends[1], values)) * mask

    run_stages([score, soften, mix], heads)
    for k in range(samples):
        at = pl.multiple_of(lax.bitwise_xor(mine, k) * tokens, tokens)
        send_refs[k][...] = mixed_all[pl.ds(at, tokens)].astype(BF)


def token_out_kernel(meta, state, *rest, samples, tokens):
    parts, (w_out, w_back, out_ref, back_ref, mixed) = rest[:samples], rest[samples:]
    mine = meta[3]
    for k in range(samples):
        at = pl.multiple_of(lax.bitwise_xor(mine, k) * tokens, tokens)
        mixed[pl.ds(at, tokens)] = parts[k][...]
    after = state[...] + dot(mixed[...], w_out[...])
    for s in range(samples):
        out_ref[s] = after[s * tokens : (s + 1) * tokens]
    back_ref[...] = dot(normed(after).astype(BF), w_back[...]).astype(BF)


def unpool_kernel(
    meta, stream, atom_token, back, first, second, w_qkv,
    stream_ref, q_ref, kv_ref, first_ref, second_ref, padded, *, samples, rows, tokens,
):
    channels = stream.shape[-1]
    selector = selector_of(meta, atom_token, tokens).astype(BF)
    first_at, second_at = halves(meta[0], 0, 2 * tokens)

    def place(s, _):
        at = slice(s * tokens, (s + 1) * tokens)
        padded[s, tokens : 2 * tokens] = back[at]
        padded[s, pl.ds(first_at, tokens)] = first[at]
        padded[s, pl.ds(second_at, tokens)] = second[at]
        picked = lax.dot_general(
            selector, padded[s], (((0,), (0,)), ((), ())), preferred_element_type=F32
        )
        return stream[s * rows : (s + 1) * rows] + picked

    def normalise(s, after):
        stream_ref[s * rows : (s + 1) * rows] = after
        return normed(after).astype(BF)

    def project(s, normal):
        projected = dot(normal, w_qkv[ENC_LAYERS])
        q_ref[s * rows : (s + 1) * rows] = projected[:, :channels].astype(BF)
        kv_ref[s * rows : (s + 1) * rows] = projected[:, channels:].astype(BF)

    run_stages([place, normalise, project], samples)
    emit_rims(kv_ref, meta[0], samples, rows, first_ref, second_ref)


def final_kernel(
    meta, q, kv, first, second, stream, bias, w_out, w_up, w_down, w_final,
    x_true, noise, denoised_ref, padded, out, up, down, sems, normal_all,
    *, layer, samples, rows,
):
    copies = fetch(
        [(w_out.at[layer], out), (w_up.at[layer], up), (w_down.at[layer], down)], sems
    )

    def finish(b, normal):
        store_rows(normal_all, b, samples, rows, normal)

    run_block(
        meta, q, kv, first, second, stream, bias, (out, up, down), copies,
        samples, rows, padded, None, finish,
    )
    sigma, total = sigma_of(meta, samples)
    keep = SIGMA_DATA * SIGMA_DATA / total
    move = sigma * SIGMA_DATA * lax.rsqrt(total)
    updates = [
        dot_nt(w_final[...], normal_all[s * rows : (s + 1) * rows]) for s in range(samples)
    ]
    for c in range(x_true.shape[0]):
        noisy = x_true[c : c + 1] + sigma * noise[c]
        update = jnp.concatenate([one[c : c + 1] for one in updates], 0)
        denoised_ref[c] = (keep * noisy + move * update) / SIGMA_DATA


def swap(pair, count):
    first, second = pair
    lower = [(i, i ^ 1) for i in range(count)]
    upper = [(i, i + 1) for i in range(1, count - 1, 2)]
    upper += [(j, i) for i, j in upper]
    upper += [(0, count - 1), (count - 1, 0)]
    second = lax.ppermute(second, SEQ, upper)
    first = lax.ppermute(first, SEQ, lower)
    return first, second


def toward(array, k, count):
    return lax.ppermute(array, "p", [(i, i ^ k) for i in range(count)])


def across(arrays, count):
    return [toward(array, k, count) for k, array in enumerate(arrays, 1)]


def shards(
    x_true, noise, noise_level, atom_single, atom_token, window_edges, atom_pair_bias,
    token_single, pair_bias, w_coord, w_atom_qkv, w_atom_out, w_atom_up, w_atom_down,
    w_pool, w_token_qkv, w_token_out, w_back, w_final,
):
    samples = noise.shape[0]
    rows, channels = atom_single.shape
    tokens, width = token_single.shape
    heads = pair_bias.shape[0]
    planes = lax.axis_size("z")
    count = planes * samples
    mine = lax.axis_index("p")
    plane = lax.axis_index("z")
    device = plane * samples + mine
    places = [device % 2, device * rows, device, mine, plane]
    meta = jnp.stack(places + [noise_level[s] for s in range(samples)])
    atom_token = atom_token[None, :]
    edges = window_edges.T
    noise = noise.transpose(1, 0, 2)
    whole = samples * rows
    held = samples * tokens
    rim = struct((samples * RIM, 2 * channels), BF)
    atom_outs = (
        struct((whole, channels), F32),
        struct((whole, channels), BF),
        struct((whole, 2 * channels), BF),
        rim,
        rim,
    )
    stacks = (w_atom_out, w_atom_up, w_atom_down)
    scratch = block_scratch(samples, rows, channels, stacks)
    wide = block_scratch(samples, rows, channels, stacks + (w_atom_qkv,))
    normals = pltpu.VMEM((whole, channels), BF)
    sizes = dict(samples=samples, rows=rows)

    def block(layer, q, kv, rims, stream):
        return call(
            functools.partial(block_kernel, layer=layer, **sizes), atom_outs,
            [SM] + [VM] * 6 + [HB] * 4,
            (meta, q, kv, *rims, stream, bias, *stacks, w_atom_qkv),
            wide,
        )

    stream, q, kv, *rims = call(
        functools.partial(embed_kernel, **sizes), atom_outs, [SM] + [HB] * 5,
        (meta, x_true, noise, atom_single, w_coord, w_atom_qkv),
        [
            pltpu.VMEM(x_true.shape, F32),
            pltpu.VMEM(noise.shape, F32),
            pltpu.VMEM(atom_single.shape, BF),
            pltpu.VMEM(w_coord.shape, F32),
            pltpu.VMEM(w_atom_qkv.shape[1:], BF),
            pltpu.SemaphoreType.DMA((5,)),
        ],
    )
    blocks, atom_heads, queries, window = atom_pair_bias.shape
    bias = call(
        mask_kernel, struct((blocks, atom_heads * queries, window), F32),
        [SM, SM, HB, VM], (meta, edges, atom_pair_bias, stream),
        [pltpu.VMEM(atom_pair_bias.shape, F32), pltpu.SemaphoreType.DMA((blocks,))],
    )
    for layer in range(ENC_LAYERS - 1):
        rims = swap(rims, count)
        if layer == 0:
            held_bias, _ = lax.optimization_barrier((pair_bias, stream))
            biases = [pair_bias]
            for k in (1, 2):
                biases.append(toward(held_bias, k, samples))
        stream, q, kv, *rims = block(layer, q, kv, rims, stream)
        if layer == 0:
            passed, *rims = lax.optimization_barrier((biases[2], *rims))
            biases.append(toward(passed, 1, samples))
    rims = swap(rims, count)
    lanes = width + COUNT_LANES
    edge = struct((held, lanes), BF)
    encoded, mid, first, second, single = call(
        functools.partial(pool_kernel, layer=ENC_LAYERS - 1, tokens=tokens, **sizes),
        (atom_outs[0], struct((held, lanes), F32), edge, edge, struct((tokens, width), F32)),
        [SM] + [VM] * 6 + [HB] * 7,
        (meta, q, kv, *rims, stream, bias, *stacks, w_pool, atom_token, token_single, biases[1]),
        scratch
        + [
            normals,
            pltpu.VMEM((samples, 3 * tokens, lanes), F32),
            pltpu.VMEM(w_pool.shape, BF),
            pltpu.VMEM(atom_token.shape, jnp.int32),
            pltpu.SemaphoreType.DMA((3,)),
        ],
    )
    rims = swap((first, second), count)
    piece = struct((tokens, width), BF)
    state, *sends = call(
        functools.partial(token_in_kernel, samples=samples, tokens=tokens),
        (struct((held, width), F32),) + (piece,) * samples,
        [SM] + [VM] * 4 + [HB], (meta, mid, *rims, single, biases[3]),
        [pltpu.VMEM((samples, tokens, width), BF)],
    )
    got = across(sends[1:], samples)
    normal = call(
        functools.partial(plane_kernel, samples=samples, tokens=tokens),
        struct((held, width), BF), [SM] + [VM] * samples, (meta, sends[0], *got),
    )
    gathered = []
    for k in range(1, planes):
        shift = [(i, (i + k) % planes) for i in range(planes)]
        gathered.append(lax.ppermute(normal, "z", shift))
    every = planes * held
    sends = call(
        functools.partial(
            token_kernel, samples=samples, tokens=tokens, planes=planes, heads=heads
        ),
        (piece,) * samples,
        [SM] + [VM] * planes + [HB] * samples + [VM],
        (meta, normal, *gathered, *biases, w_token_qkv),
        [
            pltpu.VMEM((every, width), BF),
            pltpu.VMEM((heads, held, every), F32),
            pltpu.VMEM((held, width), BF),
            pltpu.VMEM((every, width), BF),
            pltpu.VMEM((every, width), BF),
            pltpu.VMEM((held, width), F32),
            pltpu.SemaphoreType.DMA((samples,)),
        ],
    )
    got = across(sends[1:], samples)
    token_state, back = call(
        functools.partial(token_out_kernel, samples=samples, tokens=tokens),
        (struct((samples, tokens, width), F32), struct((held, channels), BF)),
        [SM] + [VM] * (1 + samples + 2), (meta, state, sends[0], *got, w_token_out, w_back),
        [pltpu.VMEM((held, width), BF)],
    )
    backs = swap((back, back), count)
    stream, q, kv, *rims = call(
        functools.partial(unpool_kernel, tokens=tokens, **sizes), atom_outs,
        [SM] + [VM] * 6, (meta, encoded, atom_token, back, *backs, w_atom_qkv),
        [pltpu.VMEM((samples, 3 * tokens, channels), BF)],
    )
    for layer in range(ENC_LAYERS, LAYERS - 1):
        rims = swap(rims, count)
        stream, q, kv, *rims = block(layer, q, kv, rims, stream)
    rims = swap(rims, count)
    denoised = call(
        functools.partial(final_kernel, layer=LAYERS - 1, **sizes),
        struct(noise.shape, F32), [SM] + [VM] * 6 + [HB] * 3 + [VM] * 3,
        (
            meta, q, kv, *rims, stream, bias, *stacks, w_final, x_true, noise,
        ),
        scratch + [normals],
    )
    return denoised.transpose(1, 0, 2), token_state


def solution(mesh):
    def step(*args):
        groups, seq = mesh.devices.shape
        samples = args[1].shape[0] // groups
        split = Mesh(
            mesh.devices.reshape(groups, seq // samples, samples), ("groups",) + SEQ
        )
        both = ("groups",) + SEQ
        in_specs = (
            P(None, both),
            P("groups", None, SEQ),
            P("groups"),
            P(both, None),
            P(both),
            P(both, None),
            P(both, None, None, None),
            P(both, None),
            P("groups", SEQ, None),
        ) + (P(),) * 10
        out_specs = (P("groups", None, SEQ), P("groups", SEQ, None))
        return jax.shard_map(
            shards, mesh=split, in_specs=in_specs, out_specs=out_specs, check_vma=False
        )(*args)

    return step
```

time: 141 us -> 99.3 us (0.70)
  the two profiles are of different devices: /device:TPU:7 before, /device:TPU:0 now
where the time goes in v2:
time: 99.3 us; the launch traced here: 99 us
  starting transfers between devices  34 us (34%)
  waiting for transfers between devices  31.6 us (32%)
  Pallas kernels  30.2 us (30%)
  local copies, waits for them, and re-layouts  2.17 us (2%)
  between operations  1.03 us (1%)
    pallas_call x11, Pallas kernels, call(): pl.pallas_call(kernel, out_shape=out_shape, in_specs=specs, out_specs=jax...  30.2 us
    ppermute x6, starting transfers between devices, swap(): second = lax.ppermute(second, SEQ, upper)  19.5 us
    ppermute x6, waiting for transfers between devices, swap(): second = lax.ppermute(second, SEQ, upper)  18.9 us
    ppermute x3, waiting for transfers between devices, shards(): gathered.append(lax.ppermute(normal, 'z', shift))  8.55 us
    ppermute x9, starting transfers between devices, toward(): return lax.ppermute(array, 'p', [(i, i ^ k) for i in range(count)])  8.04 us
    ppermute x3, starting transfers between devices, shards(): gathered.append(lax.ppermute(normal, 'z', shift))  5.67 us
    ppermute x9, waiting for transfers between devices, toward(): return lax.ppermute(array, 'p', [(i, i ^ k) for i in range(count)])  4.16 us
  transfers between devices with their start and end apart: 24, of which 10 were waited for; matrix products, arithmetic and copies ran while one was open for 0% of the time, Pallas kernels for 10%

profile of v2, /device:TPU:0, one launch (start us, length us, event | category | flops | bytes accessed | tf_op | source)
XLA Modules:
  0.0 99.0 jit_solution(6010311852615356313)
XLA Ops:
  0.6 0.7 stack.23.meta
  1.4 3.0 %shard_map.194 = (f32[512,128]{1,0:T(8,128)S(1)}, bf16[512,128]{1,0:T(8,128)(2,1)S(1)}, bf16[512,256]{1,0:T(8,128)(2,1)S(1)}, bf16[192,256]{1,0:T(8,128)(2,1)S(1)}, bf16[192,256]{1,0:T(8,128)(2,1)S(1)}) custom-call(s32[9]{0:T(128)S(1)} %stack.23.meta, f32[3,128]{1,0:T(4,128)} %x_true.1, f32[3,4,128]{2,1,0:T(4,128)} %bitcast.9, bf16[128,128]{1,0:T(8,128)(2,1)} %single_hbm.1, ...), custom_call_target="tpu_custom_call" | custom-call | tf_op jit(solution)/shard_map/pallas_call | solution.py:60
  4.4 3.1 %collective-permute-start.2 = (f32[16,16,256]{2,1,0:T(8,128)}, f32[16,16,256]{2,1,0:T(8,128)S(1)}, u32[]{:S(2)}, u32[]{:S(2)}) collective-permute-start(f32[16,16,256]{2,1,0:T(8,128)} %rest_3_.1), channel_id=1, source_target_pairs={{0,2},{1,3},{2,0},{3,1},{4,6},{5,7},{6,4},{7,5},{8,10},{9,11},{10,... | collective-permute-start | bytes 786440 | tf_op jit(solution)/shard_map/ppermute | solution.py:516
  7.5 0.5 collective-permute-start
  8.0 3.2 %collective-permute-start.1 = (bf16[192,256]{1,0:T(8,128)(2,1)S(1)}, bf16[192,256]{1,0:T(8,128)(2,1)S(1)}, u32[]{:S(2)}, u32[]{:S(2)}) collective-permute-start(bf16[192,256]{1,0:T(8,128)(2,1)S(1)} %get-tuple-element.45), channel_id=1, source_target_pairs={{1,2},{3,4},{5,6},{7,8},{9,10},{11,12},{13,14},{2,1},{4,3},{6,5},{... | collective-permute-start | bytes 294920 | tf_op jit(solution)/shard_map/ppermute | solution.py:510
  11.1 0.7 copy-done.8
  11.8 1.5 %shard_map.195.bias = f32[4,128,128]{2,1,0:T(8,128)S(1)} custom-call(s32[9]{0:T(128)S(1)} %stack.23.meta, s32[2,4]{1,0:T(2,128)S(1)} %bitcast.13, f32[4,4,32,128]{3,2,1,0:T(8,128)} %bias_hbm.1, f32[512,128]{1,0:T(8,128)S(1)} %get-tuple-element.46._.stream), custom_call_target="tpu_custom_call" | custom-call | tf_op jit(solution)/shard_map/pallas_call | solution.py:60
  13.4 1.5 %collective-permute-done.1.second = bf16[192,256]{1,0:T(8,128)(2,1)S(1)} collective-permute-done((bf16[192,256]{1,0:T(8,128)(2,1)S(1)}, bf16[192,256]{1,0:T(8,128)(2,1)S(1)}, u32[]{:S(2)}, u32[]{:S(2)}) %collective-permute-start.1) | collective-permute-done | bytes 98336 | tf_op jit(solution)/shard_map/ppermute | solution.py:510
  14.8 3.6 %shard_map.196 = (f32[512,128]{1,0:T(8,128)S(1)}, bf16[512,128]{1,0:T(8,128)(2,1)S(1)}, bf16[512,256]{1,0:T(8,128)(2,1)S(1)}, bf16[192,256]{1,0:T(8,128)(2,1)S(1)}, bf16[192,256]{1,0:T(8,128)(2,1)S(1)}) custom-call(s32[9]{0:T(128)S(1)} %stack.23.meta, bf16[512,128]{1,0:T(8,128)(2,1)S(1)} %get-tuple-element.42.q, bf16[512,256]{1,0:T(8,128)(2,1)S(1)} %get-tuple-element.43.kv, ...), custom_call_target="tpu_custom_call" | custom-call | tf_op jit(solution)/shard_map/pallas_call | solution.py:60
  18.5 1.2 %collective-permute-start.8 = (f32[16,16,256]{2,1,0:T(8,128)S(1)}, f32[16,16,256]{2,1,0:T(8,128)S(1)}, u32[]{:S(2)}, u32[]{:S(2)}) collective-permute-start(f32[16,16,256]{2,1,0:T(8,128)S(1)} %collective-permute-done.2.rest_5_), channel_id=1, source_target_pairs={{0,1},{1,0},{2,3},{3,2},{4,5},{5,4},{6,7},{7,6},{8,9},{9,8},{10,11... | collective-permute-start | bytes 786440 | tf_op jit(solution)/shard_map/ppermute | solution.py:516
  19.6 0.1 collective-permute-start.3
  19.7 5.0 %collective-permute-start.4 = (bf16[192,256]{1,0:T(8,128)(2,1)S(1)}, bf16[192,256]{1,0:T(8,128)(2,1)S(1)}, u32[]{:S(2)}, u32[]{:S(2)}) collective-permute-start(bf16[192,256]{1,0:T(8,128)(2,1)S(1)} %get-tuple-element.53), channel_id=1, source_target_pairs={{1,2},{3,4},{5,6},{7,8},{9,10},{11,12},{13,14},{2,1},{4,3},{6,5},{... | collective-permute-start | bytes 294920 | tf_op jit(solution)/shard_map/ppermute | solution.py:510
  24.7 2.3 %collective-permute-done.4.second = bf16[192,256]{1,0:T(8,128)(2,1)S(1)} collective-permute-done((bf16[192,256]{1,0:T(8,128)(2,1)S(1)}, bf16[192,256]{1,0:T(8,128)(2,1)S(1)}, u32[]{:S(2)}, u32[]{:S(2)}) %collective-permute-start.4) | collective-permute-done | bytes 98336 | tf_op jit(solution)/shard_map/ppermute | solution.py:510
  27.0 4.7 %shard_map.197 = (f32[512,128]{1,0:T(8,128)S(1)}, f32[64,896]{1,0:T(8,128)S(1)}, bf16[64,896]{1,0:T(8,128)(2,1)S(1)}, bf16[64,896]{1,0:T(8,128)(2,1)S(1)}, f32[16,768]{1,0:T(8,128)S(1)}) custom-call(s32[9]{0:T(128)S(1)} %stack.23.meta, bf16[512,128]{1,0:T(8,128)(2,1)S(1)} %get-tuple-element.47.q, bf16[512,256]{1,0:T(8,128)(2,1)S(1)} %get-tuple-element.48.kv, ...), custom_call_target="tpu_custom_call" | custom-call | tf_op jit(solution)/shard_map/pallas_call | solution.py:60
  31.7 0.0 copy-start.2
  31.7 0.0 copy-start.3
  31.7 0.1 collective-permute-start.6
  31.8 4.5 %collective-permute-start.7 = (bf16[64,896]{1,0:T(8,128)(2,1)S(1)}, bf16[64,896]{1,0:T(8,128)(2,1)S(1)}, u32[]{:S(2)}, u32[]{:S(2)}) collective-permute-start(bf16[64,896]{1,0:T(8,128)(2,1)S(1)} %get-tuple-element.58), channel_id=1, source_target_pairs={{1,2},{3,4},{5,6},{7,8},{9,10},{11,12},{13,14},{2,1},{4,3},{6,5},{... | collective-permute-start | bytes 344072 | tf_op jit(solution)/shard_map/ppermute | solution.py:510
  36.3 2.5 %collective-permute-done.7.second = bf16[64,896]{1,0:T(8,128)(2,1)S(1)} collective-permute-done((bf16[64,896]{1,0:T(8,128)(2,1)S(1)}, bf16[64,896]{1,0:T(8,128)(2,1)S(1)}, u32[]{:S(2)}, u32[]{:S(2)}) %collective-permute-start.7) | collective-permute-done | bytes 114720 | tf_op jit(solution)/shard_map/ppermute | solution.py:510
  38.8 0.7 copy-done.10
  39.5 0.8 shard_map.198
  40.3 0.0 copy-start
  40.4 0.1 collective-permute-start.9
  40.4 0.1 collective-permute-start.10
  40.5 1.8 %collective-permute-start.11 = (bf16[16,768]{1,0:T(8,128)(2,1)S(1)}, bf16[16,768]{1,0:T(8,128)(2,1)S(1)}, u32[]{:S(2)}, u32[]{:S(2)}) collective-permute-start(bf16[16,768]{1,0:T(8,128)(2,1)S(1)} %get-tuple-element.65), channel_id=1, source_target_pairs={{0,3},{1,2},{2,1},{3,0},{4,7},{5,6},{6,5},{7,4},{8,11},{9,10},{10,... | collective-permute-start | bytes 73736 | tf_op jit(solution)/shard_map/ppermute | solution.py:516
  42.3 2.0 %collective-permute-done.10.rest_2_ = bf16[16,768]{1,0:T(8,128)(2,1)S(1)} collective-permute-done((bf16[16,768]{1,0:T(8,128)(2,1)S(1)}, bf16[16,768]{1,0:T(8,128)(2,1)S(1)}, u32[]{:S(2)}, u32[]{:S(2)}) %collective-permute-start.10) | collective-permute-done | bytes 24608 | tf_op jit(solution)/shard_map/ppermute | solution.py:516
  44.3 0.6 shard_map.199.normal
  44.9 5.0 %collective-permute-start.14 = (bf16[64,768]{1,0:T(8,128)(2,1)S(1)}, bf16[64,768]{1,0:T(8,128)(2,1)S(1)}, u32[]{:S(2)}, u32[]{:S(2)}) collective-permute-start(bf16[64,768]{1,0:T(8,128)(2,1)S(1)} %shard_map.199.normal), channel_id=1, source_target_pairs={{0,12},{4,0},{8,4},{12,8},{1,13},{5,1},{9,5},{13,9},{2,14},{6,2},{... | collective-permute-start | bytes 294920 | tf_op jit(solution)/shard_map/ppermute | solution.py:628
  49.9 0.6 collective-permute-start.12
  50.6 2.6 %collective-permute-done.14.rest_2_ = bf16[64,768]{1,0:T(8,128)(2,1)S(1)} collective-permute-done((bf16[64,768]{1,0:T(8,128)(2,1)S(1)}, bf16[64,768]{1,0:T(8,128)(2,1)S(1)}, u32[]{:S(2)}, u32[]{:S(2)}) %collective-permute-start.14) | collective-permute-done | bytes 98336 | tf_op jit(solution)/shard_map/ppermute | solution.py:628
  53.2 6.0 %collective-permute-done.13.rest_1_ = bf16[64,768]{1,0:T(8,128)(2,1)S(1)} collective-permute-done((bf16[64,768]{1,0:T(8,128)(2,1)S(1)}, bf16[64,768]{1,0:T(8,128)(2,1)S(1)}, u32[]{:S(2)}, u32[]{:S(2)}) %collective-permute-start.13) | collective-permute-done | bytes 98336 | tf_op jit(solution)/shard_map/ppermute | solution.py:628
  59.1 4.8 %shard_map.200 = (bf16[16,768]{1,0:T(8,128)(2,1)S(1)}, bf16[16,768]{1,0:T(8,128)(2,1)S(1)}, bf16[16,768]{1,0:T(8,128)(2,1)S(1)}, bf16[16,768]{1,0:T(8,128)(2,1)S(1)}) custom-call(s32[9]{0:T(128)S(1)} %stack.23.meta, bf16[64,768]{1,0:T(8,128)(2,1)S(1)} %shard_map.199.normal, bf16[64,768]{1,0:T(8,128)(2,1)S(1)} %collective-permute-done.12.rest_0_, ...), custom_call_target="tpu_custom_call" | custom-call | tf_op jit(solution)/shard_map/pallas_call | solution.py:60
  64.0 0.1 collective-permute-start.15
  64.1 0.4 collective-permute-start.16
  64.5 1.4 %collective-permute-start.17 = (bf16[16,768]{1,0:T(8,128)(2,1)S(1)}, bf16[16,768]{1,0:T(8,128)(2,1)S(1)}, u32[]{:S(2)}, u32[]{:S(2)}) collective-permute-start(bf16[16,768]{1,0:T(8,128)(2,1)S(1)} %get-tuple-element.69), channel_id=1, source_target_pairs={{0,3},{1,2},{2,1},{3,0},{4,7},{5,6},{6,5},{7,4},{8,11},{9,10},{10,... | collective-permute-start | bytes 73736 | tf_op jit(solution)/shard_map/ppermute | solution.py:516
  65.9 2.1 %collective-permute-done.16.rest_2_ = bf16[16,768]{1,0:T(8,128)(2,1)S(1)} collective-permute-done((bf16[16,768]{1,0:T(8,128)(2,1)S(1)}, bf16[16,768]{1,0:T(8,128)(2,1)S(1)}, u32[]{:S(2)}, u32[]{:S(2)}) %collective-permute-start.16) | collective-permute-done | bytes 24608 | tf_op jit(solution)/shard_map/ppermute | solution.py:516
  68.1 1.7 %shard_map.201 = (f32[4,16,768]{2,1,0:T(8,128)}, bf16[64,128]{1,0:T(8,128)(2,1)S(1)}) custom-call(s32[9]{0:T(128)S(1)} %stack.23.meta, f32[64,768]{1,0:T(8,128)S(1)} %get-tuple-element.61.state, bf16[16,768]{1,0:T(8,128)(2,1)S(1)} %get-tuple-element.66.rest_0_, bf16[16,768]{1,0:T(8,128)(2,1)S(1)} %collective-permute-done.15.rest_1_, ...), custom_call_target="tpu_custom_call" | custom-call | tf_op jit(solution)/shard_map/pallas_call | solution.py:60
  69.8 2.2 %collective-permute-start.19 = (bf16[64,128]{1,0:T(8,128)(2,1)S(1)}, bf16[64,128]{1,0:T(8,128)(2,1)S(1)}, u32[]{:S(2)}, u32[]{:S(2)}) collective-permute-start(bf16[64,128]{1,0:T(8,128)(2,1)S(1)} %get-tuple-element.70.back), channel_id=1, source_target_pairs={{1,2},{3,4},{5,6},{7,8},{9,10},{11,12},{13,14},{2,1},{4,3},{6,5},{... | collective-permute-start | bytes 49160 | tf_op jit(solution)/shard_map/ppermute | solution.py:510
  72.0 3.6 %collective-permute-done.19.second = bf16[64,128]{1,0:T(8,128)(2,1)S(1)} collective-permute-done((bf16[64,128]{1,0:T(8,128)(2,1)S(1)}, bf16[64,128]{1,0:T(8,128)(2,1)S(1)}, u32[]{:S(2)}, u32[]{:S(2)}) %collective-permute-start.19) | collective-permute-done | bytes 16416 | tf_op jit(solution)/shard_map/ppermute | solution.py:510
  75.7 1.4 %shard_map.202 = (f32[512,128]{1,0:T(8,128)S(1)}, bf16[512,128]{1,0:T(8,128)(2,1)S(1)}, bf16[512,256]{1,0:T(8,128)(2,1)S(1)}, bf16[192,256]{1,0:T(8,128)(2,1)S(1)}, bf16[192,256]{1,0:T(8,128)(2,1)S(1)}) custom-call(s32[9]{0:T(128)S(1)} %stack.23.meta, f32[512,128]{1,0:T(8,128)S(1)} %get-tuple-element.55.stream, s32[1,128]{1,0:T(1,128)S(1)} %bitcast.12, ...), custom_call_target="tpu_custom_call" | custom-call | tf_op jit(solution)/shard_map/pallas_call | solution.py:60
  77.1 0.1 collective-permute-start.20
  77.2 2.3 %collective-permute-start.21 = (bf16[192,256]{1,0:T(8,128)(2,1)S(1)}, bf16[192,256]{1,0:T(8,128)(2,1)S(1)}, u32[]{:S(2)}, u32[]{:S(2)}) collective-permute-start(bf16[192,256]{1,0:T(8,128)(2,1)S(1)} %get-tuple-element.74), channel_id=1, source_target_pairs={{1,2},{3,4},{5,6},{7,8},{9,10},{11,12},{13,14},{2,1},{4,3},{6,5},{... | collective-permute-start | bytes 294920 | tf_op jit(solution)/shard_map/ppermute | solution.py:510
  79.5 4.5 %collective-permute-done.21.second = bf16[192,256]{1,0:T(8,128)(2,1)S(1)} collective-permute-done((bf16[192,256]{1,0:T(8,128)(2,1)S(1)}, bf16[192,256]{1,0:T(8,128)(2,1)S(1)}, u32[]{:S(2)}, u32[]{:S(2)}) %collective-permute-start.21) | collective-permute-done | bytes 98336 | tf_op jit(solution)/shard_map/ppermute | solution.py:510
  84.0 3.6 %shard_map.203 = (f32[512,128]{1,0:T(8,128)S(1)}, bf16[512,128]{1,0:T(8,128)(2,1)S(1)}, bf16[512,256]{1,0:T(8,128)(2,1)S(1)}, bf16[192,256]{1,0:T(8,128)(2,1)S(1)}, bf16[192,256]{1,0:T(8,128)(2,1)S(1)}) custom-call(s32[9]{0:T(128)S(1)} %stack.23.meta, bf16[512,128]{1,0:T(8,128)(2,1)S(1)} %get-tuple-element.71.q, bf16[512,256]{1,0:T(8,128)(2,1)S(1)} %get-tuple-element.72.kv, ...), custom_call_target="tpu_custom_call" | custom-call | tf_op jit(solution)/shard_map/pallas_call | solution.py:60
  87.6 0.1 collective-permute-start.22
  87.7 2.3 %collective-permute-start.23 = (bf16[192,256]{1,0:T(8,128)(2,1)S(1)}, bf16[192,256]{1,0:T(8,128)(2,1)S(1)}, u32[]{:S(2)}, u32[]{:S(2)}) collective-permute-start(bf16[192,256]{1,0:T(8,128)(2,1)S(1)} %get-tuple-element.79), channel_id=1, source_target_pairs={{1,2},{3,4},{5,6},{7,8},{9,10},{11,12},{13,14},{2,1},{4,3},{6,5},{... | collective-permute-start | bytes 294920 | tf_op jit(solution)/shard_map/ppermute | solution.py:510
  90.0 4.5 %collective-permute-done.23.second = bf16[192,256]{1,0:T(8,128)(2,1)S(1)} collective-permute-done((bf16[192,256]{1,0:T(8,128)(2,1)S(1)}, bf16[192,256]{1,0:T(8,128)(2,1)S(1)}, u32[]{:S(2)}, u32[]{:S(2)}) %collective-permute-start.23) | collective-permute-done | bytes 98336 | tf_op jit(solution)/shard_map/ppermute | solution.py:510
  94.5 4.3 %shard_map.204 = f32[3,4,128]{2,1,0:T(4,128)} custom-call(s32[9]{0:T(128)S(1)} %stack.23.meta, bf16[512,128]{1,0:T(8,128)(2,1)S(1)} %get-tuple-element.76.q, bf16[512,256]{1,0:T(8,128)(2,1)S(1)} %get-tuple-element.77.kv, bf16[192,256]{1,0:T(8,128)(2,1)S(1)} %collective-permute-done.22.first, bf16[192,256]{1,0:T(8,128)(2,1)S(1)} %collective-permute-done.23.second, ...), custom_call_target="tpu_custom_call" | custom-call | tf_op jit(solution)/shard_map/pallas_call | solution.py:60
  (36 shorter events, 0.1 us)
Async XLA Ops:
  1.4 57.7 %copy-start.1 = (bf16[768,2304]{1,0:T(8,128)(2,1)S(1)}, bf16[768,2304]{1,0:T(8,128)(2,1)}, u32[]{:S(2)}) copy-start(bf16[768,2304]{1,0:T(8,128)(2,1)} %rest_7_.1) | copy-start | bytes 10616836
  4.4 14.0 %collective-permute-start.2 = (f32[16,16,256]{2,1,0:T(8,128)}, f32[16,16,256]{2,1,0:T(8,128)S(1)}, u32[]{:S(2)}, u32[]{:S(2)}) collective-permute-start(f32[16,16,256]{2,1,0:T(8,128)} %rest_3_.1), channel_id=1, source_target_pairs={{0,2},{1,3},{2,0},{3,1},{4,6},{5,7},{6,4},{7,5},{8,10},{9,11},{10,... | collective-permute-start | bytes 786440 | tf_op jit(solution)/shard_map/ppermute | solution.py:516
  7.5 17.2 %collective-permute-start.5 = (f32[16,16,256]{2,1,0:T(8,128)}, f32[16,16,256]{2,1,0:T(8,128)S(1)}, u32[]{:S(2)}, u32[]{:S(2)}) collective-permute-start(f32[16,16,256]{2,1,0:T(8,128)} %rest_3_.1), channel_id=1, source_target_pairs={{0,1},{1,0},{2,3},{3,2},{4,5},{5,4},{6,7},{7,6},{8,9},{9,8},{10,11... | collective-permute-start | bytes 786440 | tf_op jit(solution)/shard_map/ppermute | solution.py:516
  7.5 5.9 %collective-permute-start = (bf16[192,256]{1,0:T(8,128)(2,1)S(1)}, bf16[192,256]{1,0:T(8,128)(2,1)S(1)}, u32[]{:S(2)}, u32[]{:S(2)}) collective-permute-start(bf16[192,256]{1,0:T(8,128)(2,1)S(1)} %get-tuple-element.44), channel_id=1, source_target_pairs={{0,1},{1,0},{2,3},{3,2},{4,5},{5,4},{6,7},{7,6},{8,9},{9,8},{10,11... | collective-permute-start | bytes 294920 | tf_op jit(solution)/shard_map/ppermute | solution.py:511
  8.0 6.8 %collective-permute-start.1 = (bf16[192,256]{1,0:T(8,128)(2,1)S(1)}, bf16[192,256]{1,0:T(8,128)(2,1)S(1)}, u32[]{:S(2)}, u32[]{:S(2)}) collective-permute-start(bf16[192,256]{1,0:T(8,128)(2,1)S(1)} %get-tuple-element.45), channel_id=1, source_target_pairs={{1,2},{3,4},{5,6},{7,8},{9,10},{11,12},{13,14},{2,1},{4,3},{6,5},{... | collective-permute-start | bytes 294920 | tf_op jit(solution)/shard_map/ppermute | solution.py:510
  11.1 0.7 copy-start.8
  18.4 40.7 %copy-start.11 = (f32[16,16,256]{2,1,0:T(8,128)}, f32[16,16,256]{2,1,0:T(8,128)S(1)}, u32[]{:S(2)}) copy-start(f32[16,16,256]{2,1,0:T(8,128)S(1)} %collective-permute-done.2.rest_5_) | copy-start | bytes 786436
  18.5 20.4 %collective-permute-start.8 = (f32[16,16,256]{2,1,0:T(8,128)S(1)}, f32[16,16,256]{2,1,0:T(8,128)S(1)}, u32[]{:S(2)}, u32[]{:S(2)}) collective-permute-start(f32[16,16,256]{2,1,0:T(8,128)S(1)} %collective-permute-done.2.rest_5_), channel_id=1, source_target_pairs={{0,1},{1,0},{2,3},{3,2},{4,5},{5,4},{6,7},{7,6},{8,9},{9,8},{10,11... | collective-permute-start | bytes 786440 | tf_op jit(solution)/shard_map/ppermute | solution.py:516
  19.6 5.1 %collective-permute-start.3 = (bf16[192,256]{1,0:T(8,128)(2,1)S(1)}, bf16[192,256]{1,0:T(8,128)(2,1)S(1)}, u32[]{:S(2)}, u32[]{:S(2)}) collective-permute-start(bf16[192,256]{1,0:T(8,128)(2,1)S(1)} %get-tuple-element.52), channel_id=1, source_target_pairs={{0,1},{1,0},{2,3},{3,2},{4,5},{5,4},{6,7},{7,6},{8,9},{9,8},{10,11... | collective-permute-start | bytes 294920 | tf_op jit(solution)/shard_map/ppermute | solution.py:511
  19.7 7.3 %collective-permute-start.4 = (bf16[192,256]{1,0:T(8,128)(2,1)S(1)}, bf16[192,256]{1,0:T(8,128)(2,1)S(1)}, u32[]{:S(2)}, u32[]{:S(2)}) collective-permute-start(bf16[192,256]{1,0:T(8,128)(2,1)S(1)} %get-tuple-element.53), channel_id=1, source_target_pairs={{1,2},{3,4},{5,6},{7,8},{9,10},{11,12},{13,14},{2,1},{4,3},{6,5},{... | collective-permute-start | bytes 294920 | tf_op jit(solution)/shard_map/ppermute | solution.py:510
  24.7 2.3 %copy-start.9 = (f32[16,16,256]{2,1,0:T(8,128)}, f32[16,16,256]{2,1,0:T(8,128)S(1)}, u32[]{:S(2)}) copy-start(f32[16,16,256]{2,1,0:T(8,128)S(1)} %collective-permute-done.5.rest_1_.rest_4_) | copy-start | bytes 786436
  31.7 36.3 %copy-start.2 = (bf16[768,768]{1,0:T(8,128)(2,1)S(1)}, bf16[768,768]{1,0:T(8,128)(2,1)}, u32[]{:S(2)}) copy-start(bf16[768,768]{1,0:T(8,128)(2,1)} %rest_4_.1) | copy-start | bytes 3538948
  31.7 36.3 %copy-start.3 = (bf16[768,128]{1,0:T(8,128)(2,1)S(1)}, bf16[768,128]{1,0:T(8,128)(2,1)}, u32[]{:S(2)}) copy-start(bf16[768,128]{1,0:T(8,128)(2,1)} %rest_5_.1) | copy-start | bytes 589828
  31.7 4.6 %collective-permute-start.6 = (bf16[64,896]{1,0:T(8,128)(2,1)S(1)}, bf16[64,896]{1,0:T(8,128)(2,1)S(1)}, u32[]{:S(2)}, u32[]{:S(2)}) collective-permute-start(bf16[64,896]{1,0:T(8,128)(2,1)S(1)} %get-tuple-element.57), channel_id=1, source_target_pairs={{0,1},{1,0},{2,3},{3,2},{4,5},{5,4},{6,7},{7,6},{8,9},{9,8},{10,11... | collective-permute-start | bytes 344072 | tf_op jit(solution)/shard_map/ppermute | solution.py:511
  31.8 7.0 %collective-permute-start.7 = (bf16[64,896]{1,0:T(8,128)(2,1)S(1)}, bf16[64,896]{1,0:T(8,128)(2,1)S(1)}, u32[]{:S(2)}, u32[]{:S(2)}) collective-permute-start(bf16[64,896]{1,0:T(8,128)(2,1)S(1)} %get-tuple-element.58), channel_id=1, source_target_pairs={{1,2},{3,4},{5,6},{7,8},{9,10},{11,12},{13,14},{2,1},{4,3},{6,5},{... | collective-permute-start | bytes 344072 | tf_op jit(solution)/shard_map/ppermute | solution.py:510
  38.8 0.7 copy-start.10
  40.3 35.3 %copy-start = (bf16[4,128,384]{2,1,0:T(8,128)(2,1)S(1)}, bf16[4,128,384]{2,1,0:T(8,128)(2,1)}, u32[]{:S(2)}) copy-start(bf16[4,128,384]{2,1,0:T(8,128)(2,1)} %w_qkv.5) | copy-start | bytes 1179652
  40.3 35.3 %copy-start.6 = (s32[128]{0:T(128)S(1)}, s32[128]{0:T(128)}, u32[]{:S(2)}) copy-start(s32[128]{0:T(128)} %param.23) | copy-start | bytes 1540
  40.4 1.9 %collective-permute-start.9 = (bf16[16,768]{1,0:T(8,128)(2,1)S(1)}, bf16[16,768]{1,0:T(8,128)(2,1)S(1)}, u32[]{:S(2)}, u32[]{:S(2)}) collective-permute-start(bf16[16,768]{1,0:T(8,128)(2,1)S(1)} %get-tuple-element.63), channel_id=1, source_target_pairs={{0,1},{1,0},{2,3},{3,2},{4,5},{5,4},{6,7},{7,6},{8,9},{9,8},{10,11... | collective-permute-start | bytes 73736 | tf_op jit(solution)/shard_map/ppermute | solution.py:516
  40.4 3.9 %collective-permute-start.10 = (bf16[16,768]{1,0:T(8,128)(2,1)S(1)}, bf16[16,768]{1,0:T(8,128)(2,1)S(1)}, u32[]{:S(2)}, u32[]{:S(2)}) collective-permute-start(bf16[16,768]{1,0:T(8,128)(2,1)S(1)} %get-tuple-element.64), channel_id=1, source_target_pairs={{0,2},{1,3},{2,0},{3,1},{4,6},{5,7},{6,4},{7,5},{8,10},{9,11},{10,... | collective-permute-start | bytes 73736 | tf_op jit(solution)/shard_map/ppermute | solution.py:516
  40.5 3.8 %collective-permute-start.11 = (bf16[16,768]{1,0:T(8,128)(2,1)S(1)}, bf16[16,768]{1,0:T(8,128)(2,1)S(1)}, u32[]{:S(2)}, u32[]{:S(2)}) collective-permute-start(bf16[16,768]{1,0:T(8,128)(2,1)S(1)} %get-tuple-element.65), channel_id=1, source_target_pairs={{0,3},{1,2},{2,1},{3,0},{4,7},{5,6},{6,5},{7,4},{8,11},{9,10},{10,... | collective-permute-start | bytes 73736 | tf_op jit(solution)/shard_map/ppermute | solution.py:516
  44.9 8.3 %collective-permute-start.14 = (bf16[64,768]{1,0:T(8,128)(2,1)S(1)}, bf16[64,768]{1,0:T(8,128)(2,1)S(1)}, u32[]{:S(2)}, u32[]{:S(2)}) collective-permute-start(bf16[64,768]{1,0:T(8,128)(2,1)S(1)} %shard_map.199.normal), channel_id=1, source_target_pairs={{0,12},{4,0},{8,4},{12,8},{1,13},{5,1},{9,5},{13,9},{2,14},{6,2},{... | collective-permute-start | bytes 294920 | tf_op jit(solution)/shard_map/ppermute | solution.py:628
  49.9 9.2 %collective-permute-start.13 = (bf16[64,768]{1,0:T(8,128)(2,1)S(1)}, bf16[64,768]{1,0:T(8,128)(2,1)S(1)}, u32[]{:S(2)}, u32[]{:S(2)}) collective-permute-start(bf16[64,768]{1,0:T(8,128)(2,1)S(1)} %shard_map.199.normal), channel_id=1, source_target_pairs={{0,8},{4,12},{8,0},{12,4},{1,9},{5,13},{9,1},{13,5},{2,10},{6,14},... | collective-permute-start | bytes 294920 | tf_op jit(solution)/shard_map/ppermute | solution.py:628
  49.9 9.2 %collective-permute-start.12 = (bf16[64,768]{1,0:T(8,128)(2,1)S(1)}, bf16[64,768]{1,0:T(8,128)(2,1)S(1)}, u32[]{:S(2)}, u32[]{:S(2)}) collective-permute-start(bf16[64,768]{1,0:T(8,128)(2,1)S(1)} %shard_map.199.normal), channel_id=1, source_target_pairs={{0,4},{4,8},{8,12},{12,0},{1,5},{5,9},{9,13},{13,1},{2,6},{6,10},{... | collective-permute-start | bytes 294920 | tf_op jit(solution)/shard_map/ppermute | solution.py:628
  64.0 30.5 %copy-start.4 = (f32[4,3,128]{2,0,1:T(4,128)S(1)}, f32[4,3,128]{2,0,1:T(4,128)}, u32[]{:S(2)}) copy-start(f32[4,3,128]{2,0,1:T(4,128)} %param.20) | copy-start | bytes 18436
  64.0 30.5 %copy-start.5 = (f32[3,128]{1,0:T(4,128)S(1)}, f32[3,128]{1,0:T(4,128)}, u32[]{:S(2)}) copy-start(f32[3,128]{1,0:T(4,128)} %x_true.1) | copy-start | bytes 4612
  64.0 30.5 %copy-start.7 = (bf16[3,128]{1,0:T(4,128)(2,1)S(1)}, bf16[3,128]{1,0:T(4,128)(2,1)}, u32[]{:S(2)}) copy-start(bf16[3,128]{1,0:T(4,128)(2,1)} %w_final.1) | copy-start | bytes 2308
  64.0 1.9 %collective-permute-start.15 = (bf16[16,768]{1,0:T(8,128)(2,1)S(1)}, bf16[16,768]{1,0:T(8,128)(2,1)S(1)}, u32[]{:S(2)}, u32[]{:S(2)}) collective-permute-start(bf16[16,768]{1,0:T(8,128)(2,1)S(1)} %get-tuple-element.67), channel_id=1, source_target_pairs={{0,1},{1,0},{2,3},{3,2},{4,5},{5,4},{6,7},{7,6},{8,9},{9,8},{10,11... | collective-permute-start | bytes 73736 | tf_op jit(solution)/shard_map/ppermute | solution.py:516
  64.1 4.0 %collective-permute-start.16 = (bf16[16,768]{1,0:T(8,128)(2,1)S(1)}, bf16[16,768]{1,0:T(8,128)(2,1)S(1)}, u32[]{:S(2)}, u32[]{:S(2)}) collective-permute-start(bf16[16,768]{1,0:T(8,128)(2,1)S(1)} %get-tuple-element.68), channel_id=1, source_target_pairs={{0,2},{1,3},{2,0},{3,1},{4,6},{5,7},{6,4},{7,5},{8,10},{9,11},{10,... | collective-permute-start | bytes 73736 | tf_op jit(solution)/shard_map/ppermute | solution.py:516
  64.5 3.5 %collective-permute-start.17 = (bf16[16,768]{1,0:T(8,128)(2,1)S(1)}, bf16[16,768]{1,0:T(8,128)(2,1)S(1)}, u32[]{:S(2)}, u32[]{:S(2)}) collective-permute-start(bf16[16,768]{1,0:T(8,128)(2,1)S(1)} %get-tuple-element.69), channel_id=1, source_target_pairs={{0,3},{1,2},{2,1},{3,0},{4,7},{5,6},{6,5},{7,4},{8,11},{9,10},{10,... | collective-permute-start | bytes 73736 | tf_op jit(solution)/shard_map/ppermute | solution.py:516
  69.8 5.9 %collective-permute-start.19 = (bf16[64,128]{1,0:T(8,128)(2,1)S(1)}, bf16[64,128]{1,0:T(8,128)(2,1)S(1)}, u32[]{:S(2)}, u32[]{:S(2)}) collective-permute-start(bf16[64,128]{1,0:T(8,128)(2,1)S(1)} %get-tuple-element.70.back), channel_id=1, source_target_pairs={{1,2},{3,4},{5,6},{7,8},{9,10},{11,12},{13,14},{2,1},{4,3},{6,5},{... | collective-permute-start | bytes 49160 | tf_op jit(solution)/shard_map/ppermute | solution.py:510
  72.0 3.6 %collective-permute-start.18 = (bf16[64,128]{1,0:T(8,128)(2,1)S(1)}, bf16[64,128]{1,0:T(8,128)(2,1)S(1)}, u32[]{:S(2)}, u32[]{:S(2)}) collective-permute-start(bf16[64,128]{1,0:T(8,128)(2,1)S(1)} %get-tuple-element.70.back), channel_id=1, source_target_pairs={{0,1},{1,0},{2,3},{3,2},{4,5},{5,4},{6,7},{7,6},{8,9},{9,8},{10,11... | collective-permute-start | bytes 49160 | tf_op jit(solution)/shard_map/ppermute | solution.py:511
  77.1 2.4 %collective-permute-start.20 = (bf16[192,256]{1,0:T(8,128)(2,1)S(1)}, bf16[192,256]{1,0:T(8,128)(2,1)S(1)}, u32[]{:S(2)}, u32[]{:S(2)}) collective-permute-start(bf16[192,256]{1,0:T(8,128)(2,1)S(1)} %get-tuple-element.73), channel_id=1, source_target_pairs={{0,1},{1,0},{2,3},{3,2},{4,5},{5,4},{6,7},{7,6},{8,9},{9,8},{10,11... | collective-permute-start | bytes 294920 | tf_op jit(solution)/shard_map/ppermute | solution.py:511
  77.2 6.8 %collective-permute-start.21 = (bf16[192,256]{1,0:T(8,128)(2,1)S(1)}, bf16[192,256]{1,0:T(8,128)(2,1)S(1)}, u32[]{:S(2)}, u32[]{:S(2)}) collective-permute-start(bf16[192,256]{1,0:T(8,128)(2,1)S(1)} %get-tuple-element.74), channel_id=1, source_target_pairs={{1,2},{3,4},{5,6},{7,8},{9,10},{11,12},{13,14},{2,1},{4,3},{6,5},{... | collective-permute-start | bytes 294920 | tf_op jit(solution)/shard_map/ppermute | solution.py:510
  87.6 2.4 %collective-permute-start.22 = (bf16[192,256]{1,0:T(8,128)(2,1)S(1)}, bf16[192,256]{1,0:T(8,128)(2,1)S(1)}, u32[]{:S(2)}, u32[]{:S(2)}) collective-permute-start(bf16[192,256]{1,0:T(8,128)(2,1)S(1)} %get-tuple-element.78), channel_id=1, source_target_pairs={{0,1},{1,0},{2,3},{3,2},{4,5},{5,4},{6,7},{7,6},{8,9},{9,8},{10,11... | collective-permute-start | bytes 294920 | tf_op jit(solution)/shard_map/ppermute | solution.py:511
  87.7 6.8 %collective-permute-start.23 = (bf16[192,256]{1,0:T(8,128)(2,1)S(1)}, bf16[192,256]{1,0:T(8,128)(2,1)S(1)}, u32[]{:S(2)}, u32[]{:S(2)}) collective-permute-start(bf16[192,256]{1,0:T(8,128)(2,1)S(1)} %get-tuple-element.79), channel_id=1, source_target_pairs={{1,2},{3,4},{5,6},{7,8},{9,10},{11,12},{13,14},{2,1},{4,3},{6,5},{... | collective-permute-start | bytes 294920 | tf_op jit(solution)/shard_map/ppermute | solution.py:510

commit v3 on v2

--- a/solution.py
+++ b/solution.py
@@ -302,12 +302,12 @@
     *rest, layer, samples, rows, tokens,
 ):
     single_hbm = rest[0]
-    (stream_ref, mid_ref, first_ref, second_ref, single_ref,
-     padded, out, up, down, sems, normal_all, sums, pooling, owners, late_sems) = rest[-15:]
+    (stream_ref, mid_ref, first_ref, second_ref,
+     padded, out, up, down, sems, normal_all, sums, pooling, owners, single, late_sems) = rest[-15:]
     copies = fetch(
         [(w_out.at[layer], out), (w_up.at[layer], up), (w_down.at[layer], down)], sems
     )
-    late = fetch([(w_pool, pooling), (atom_token, owners), (single_hbm, single_ref)], late_sems)
+    late = fetch([(w_pool, pooling), (atom_token, owners), (single_hbm, single)], late_sems)
 
     def finish(b, normal):
         store_rows(normal_all, b, samples, rows, normal)
@@ -333,6 +333,8 @@
         sums[s, :, width:] = jnp.broadcast_to(counts, (3 * tokens, COUNT_LANES))
 
     run_stages([pool, gather], samples)
+    mid_ref[samples * tokens :, :width] = single[...]
+    mid_ref[samples * tokens :, width:] = jnp.zeros((tokens, COUNT_LANES), F32)
     for s in range(samples):
         at = slice(s * tokens, (s + 1) * tokens)
         mid_ref[at] = sums[s, tokens : 2 * tokens]
@@ -342,15 +344,17 @@
 
 
 def token_in_kernel(
-    meta, mid, first, second, single, _, state_ref, *rest, samples, tokens
+    meta, mid, first, second, _, state_ref, *rest, samples, tokens
 ):
     send_refs, normal_all = rest[:samples], rest[samples]
-    width = single.shape[-1]
-    total = mid[...] + first[...].astype(F32) + second[...].astype(F32)
+    width = state_ref.shape[-1]
+    held = samples * tokens
+    single = mid[held:, :width]
+    total = mid[:held] + first[...].astype(F32) + second[...].astype(F32)
     share = total[:, :width] / total[:, width : width + 1]
     for s in range(samples):
         at = slice(s * tokens, (s + 1) * tokens)
-        state = share[at] + single[...]
+        state = share[at] + single
         state_ref[at] = state
         normal_all[s] = normed(state).astype(BF)
     mine = meta[3]
@@ -366,38 +370,38 @@
         out_ref[pl.ds(at, tokens)] = parts[k][...]
 
 
-def token_kernel(
-    meta, normal, *rest, samples, tokens, planes, heads
-):
-    gathered, rest = rest[: planes - 1], rest[planes - 1 :]
-    biases, rest = rest[:samples], rest[samples:]
-    w_qkv, rest = rest[0], rest[1:]
-    send_refs = rest[:samples]
-    everyone, bias_all, q_all, k_all, v_all, mixed_all, sems = rest[samples:]
+def token_own_kernel(meta, normal, *rest, samples, tokens):
+    biases, (w_qkv, q_ref, kv_ref, bias_ref, sems) = rest[:samples], rest[samples:]
+    mine = meta[3]
+    starts = [
+        pl.multiple_of(lax.bitwise_xor(mine, k) * tokens, tokens) for k in range(samples)
+    ]
+    copies = fetch(
+        [(biases[k], bias_ref.at[:, pl.ds(starts[k], tokens)]) for k in range(samples)], sems
+    )
+    width = normal.shape[-1]
+    projected = dot(normal[...], w_qkv[...]).astype(BF)
+    q_ref[...] = projected[:, :width]
+    kv_ref[...] = projected[:, width:]
+    for copy in copies:
+        copy.wait()
+
+
+def token_kernel(meta, q_own, kv_own, bias_all, *rest, samples, tokens, planes, heads):
+    gathered, w_qkv, rest = rest[: planes - 1], rest[planes - 1], rest[planes:]
+    send_refs, (kv_all, mixed_all) = rest[:samples], rest[samples:]
     rows = samples * tokens
-    width = normal.shape[-1]
+    width = q_own.shape[-1]
     head_size = width // heads
     mine = meta[3]
     plane = meta[4]
-    copies = fetch(
-        [
-            (
-                biases[k],
-                bias_all.at[:, pl.ds(pl.multiple_of(lax.bitwise_xor(mine, k) * tokens, tokens), tokens)],
-            )
-            for k in range(samples)
-        ],
-        sems,
-    )
-    everyone[pl.ds(pl.multiple_of(plane * rows, rows), rows)] = normal[...]
+    kv_all[pl.ds(pl.multiple_of(plane * rows, rows), rows)] = kv_own[...]
+    others = jnp.concatenate([one[...] for one in gathered], 0)
+    others = dot(others, w_qkv[:, width:]).astype(BF)
     for k in range(1, planes):
         origin = plane - k + jnp.where(plane < k, planes, 0)
-        everyone[pl.ds(pl.multiple_of(origin * rows, rows), rows)] = gathered[k - 1][...]
-    q_all[...] = dot(normal[...], w_qkv[:, :width]).astype(BF)
-    k_all[...] = dot(everyone[...], w_qkv[:, width : 2 * width]).astype(BF)
-    v_all[...] = dot(everyone[...], w_qkv[:, 2 * width :]).astype(BF)
-    for copy in copies:
-        copy.wait()
+        at = pl.multiple_of(origin * rows, rows)
+        kv_all[pl.ds(at, rows)] = others[(k - 1) * rows : k * rows]
     scale = head_size ** (-0.5) * LOG2E
     mixed_all[...] = jnp.zeros_like(mixed_all)
 
@@ -410,8 +414,8 @@
 
     def score(h, _):
         at, mask = lanes_of(h)
-        query = q_all[:, at] * mask.astype(BF)
-        return dot_nt(query, k_all[:, at]) * scale + bias_all[h] * LOG2E
+        query = q_own[:, at] * mask.astype(BF)
+        return dot_nt(query, kv_all[:, at]) * scale + bias_all[h] * LOG2E
 
     def soften(h, scores):
         expo = jnp.exp2(scores - jnp.max(scores, -1, keepdims=True))
@@ -421,7 +425,7 @@
 
     def mix(h, attends):
         at, mask = lanes_of(h)
-        values = v_all[:, at]
+        values = kv_all[:, width + at.start : width + at.stop]
         mixed_all[:, at] += (dot(attends[0], values) + dot(attends[1], values)) * mask
 
     run_stages([score, soften, mix], heads)
@@ -503,11 +507,16 @@
 
 def swap(pair, count):
     first, second = pair
+    groups = lax.axis_size("groups")
     lower = [(i, i ^ 1) for i in range(count)]
-    upper = [(i, i + 1) for i in range(1, count - 1, 2)]
-    upper += [(j, i) for i, j in upper]
-    upper += [(0, count - 1), (count - 1, 0)]
-    second = lax.ppermute(second, SEQ, upper)
+    upper = []
+    for g in range(groups):
+        inner = [(g * count + i, g * count + i + 1) for i in range(1, count - 1, 2)]
+        upper += inner + [(j, i) for i, j in inner]
+        for end in (0, count - 1):
+            other = (g ^ 1) * count + end if groups % 2 == 0 else (g + 1) * count - 1 - end
+            upper.append((g * count + end, other))
+    second = lax.ppermute(second, ("groups",) + SEQ, upper)
     first = lax.ppermute(first, SEQ, lower)
     return first, second
 
@@ -595,9 +604,9 @@
     rims = swap(rims, count)
     lanes = width + COUNT_LANES
     edge = struct((held, lanes), BF)
-    encoded, mid, first, second, single = call(
+    encoded, mid, *rims = call(
         functools.partial(pool_kernel, layer=ENC_LAYERS - 1, tokens=tokens, **sizes),
-        (atom_outs[0], struct((held, lanes), F32), edge, edge, struct((tokens, width), F32)),
+        (atom_outs[0], struct((held + tokens, lanes), F32), edge, edge),
         [SM] + [VM] * 6 + [HB] * 7,
         (meta, q, kv, *rims, stream, bias, *stacks, w_pool, atom_token, token_single, biases[1]),
         scratch
@@ -606,15 +615,16 @@
             pltpu.VMEM((samples, 3 * tokens, lanes), F32),
             pltpu.VMEM(w_pool.shape, BF),
             pltpu.VMEM(atom_token.shape, jnp.int32),
+            pltpu.VMEM(token_single.shape, F32),
             pltpu.SemaphoreType.DMA((3,)),
         ],
     )
-    rims = swap((first, second), count)
+    rims = swap(rims, count)
     piece = struct((tokens, width), BF)
     state, *sends = call(
         functools.partial(token_in_kernel, samples=samples, tokens=tokens),
         (struct((held, width), F32),) + (piece,) * samples,
-        [SM] + [VM] * 4 + [HB], (meta, mid, *rims, single, biases[3]),
+        [SM] + [VM] * 3 + [HB], (meta, mid, *rims, biases[3]),
         [pltpu.VMEM((samples, tokens, width), BF)],
     )
     got = across(sends[1:], samples)
@@ -627,22 +637,23 @@
         shift = [(i, (i + k) % planes) for i in range(planes)]
         gathered.append(lax.ppermute(normal, "z", shift))
     every = planes * held
+    q_own, kv_own, bias_all = call(
+        functools.partial(token_own_kernel, samples=samples, tokens=tokens),
+        (
+            struct((held, width), BF),
+            struct((held, 2 * width), BF),
+            struct((heads, held, every), F32),
+        ),
+        [SM, VM] + [HB] * samples + [VM], (meta, normal, *biases, w_token_qkv),
+        [pltpu.SemaphoreType.DMA((samples,))],
+    )
     sends = call(
         functools.partial(
             token_kernel, samples=samples, tokens=tokens, planes=planes, heads=heads
         ),
-        (piece,) * samples,
-        [SM] + [VM] * planes + [HB] * samples + [VM],
-        (meta, normal, *gathered, *biases, w_token_qkv),
-        [
-            pltpu.VMEM((every, width), BF),
-            pltpu.VMEM((heads, held, every), F32),
-            pltpu.VMEM((held, width), BF),
-            pltpu.VMEM((every, width), BF),
-            pltpu.VMEM((every, width), BF),
-            pltpu.VMEM((held, width), F32),
-            pltpu.SemaphoreType.DMA((samples,)),
-        ],
+        (piece,) * samples, [SM] + [VM] * (3 + planes),
+        (meta, q_own, kv_own, bias_all, *gathered, w_token_qkv),
+        [pltpu.VMEM((every, 2 * width), BF), pltpu.VMEM((held, width), F32)],
     )
     got = across(sends[1:], samples)
     token_state, back = call(

time: 99.3 us -> 87.9 us (0.89)
  the two profiles are of different devices: /device:TPU:0 before, /device:TPU:7 now
where the time goes in v3:
time: 87.9 us; the launch traced here: 86.3 us
  Pallas kernels  31.3 us (36%)
  starting transfers between devices  30 us (34%)
  waiting for transfers between devices  21.8 us (25%)
  local copies, waits for them, and re-layouts  2.18 us (2%)
  between operations  1.03 us (1%)
    pallas_call x12, Pallas kernels, call(): pl.pallas_call(kernel, out_shape=out_shape, in_specs=specs, out_specs=jax...  31.3 us
    ppermute x6, waiting for transfers between devices, swap(): second = lax.ppermute(second, ('groups',) + SEQ, upper)  13.7 us
    ppermute x6, starting transfers between devices, swap(): second = lax.ppermute(second, ('groups',) + SEQ, upper)  13.6 us
    ppermute x9, starting transfers between devices, toward(): return lax.ppermute(array, 'p', [(i, i ^ k) for i in range(count)])  10.6 us
    ppermute x3, starting transfers between devices, shards(): gathered.append(lax.ppermute(normal, 'z', shift))  5.16 us
    ppermute x9, waiting for transfers between devices, toward(): return lax.ppermute(array, 'p', [(i, i ^ k) for i in range(count)])  4.34 us
    ppermute x3, waiting for transfers between devices, shards(): gathered.append(lax.ppermute(normal, 'z', shift))  3.58 us
  transfers between devices with their start and end apart: 24, of which 12 were waited for; matrix products, arithmetic and copies ran while one was open for 0% of the time, Pallas kernels for 14%

profile of v3, /device:TPU:7, one launch (start us, length us, event | category | flops | bytes accessed | tf_op | source)
XLA Modules:
  0.0 86.3 jit_solution(9664327015525589939)
XLA Ops:
  0.6 0.7 stack.23.meta
  1.4 3.0 %shard_map.194 = (f32[512,128]{1,0:T(8,128)S(1)}, bf16[512,128]{1,0:T(8,128)(2,1)S(1)}, bf16[512,256]{1,0:T(8,128)(2,1)S(1)}, bf16[192,256]{1,0:T(8,128)(2,1)S(1)}, bf16[192,256]{1,0:T(8,128)(2,1)S(1)}) custom-call(s32[9]{0:T(128)S(1)} %stack.23.meta, f32[3,128]{1,0:T(4,128)} %x_true.1, f32[3,4,128]{2,1,0:T(4,128)} %bitcast.9, bf16[128,128]{1,0:T(8,128)(2,1)} %single_hbm.1, ...), custom_call_target="tpu_custom_call" | custom-call | tf_op jit(solution)/shard_map/pallas_call | solution.py:60
  4.4 0.3 collective-permute-start.2
  4.7 1.0 %collective-permute-start.5 = (f32[16,16,256]{2,1,0:T(8,128)}, f32[16,16,256]{2,1,0:T(8,128)S(1)}, u32[]{:S(2)}, u32[]{:S(2)}) collective-permute-start(f32[16,16,256]{2,1,0:T(8,128)} %rest_0_.3), channel_id=1, source_target_pairs={{0,1},{1,0},{2,3},{3,2},{4,5},{5,4},{6,7},{7,6},{8,9},{9,8},{10,11... | collective-permute-start | bytes 786440 | tf_op jit(solution)/shard_map/ppermute | solution.py:525
  5.7 2.6 %collective-permute-start.1 = (bf16[192,256]{1,0:T(8,128)(2,1)S(1)}, bf16[192,256]{1,0:T(8,128)(2,1)S(1)}, u32[]{:S(2)}, u32[]{:S(2)}) collective-permute-start(bf16[192,256]{1,0:T(8,128)(2,1)S(1)} %get-tuple-element.47), channel_id=1, source_target_pairs={{1,2},{3,4},{5,6},{7,8},{9,10},{11,12},{13,14},{2,1},{4,3},{6,5},{... | collective-permute-start | bytes 294920 | tf_op jit(solution)/shard_map/ppermute | solution.py:519
  8.3 0.7 copy-done.8
  9.0 1.5 %shard_map.195.bias = f32[4,128,128]{2,1,0:T(8,128)S(1)} custom-call(s32[9]{0:T(128)S(1)} %stack.23.meta, s32[2,4]{1,0:T(2,128)S(1)} %bitcast.13, f32[4,4,32,128]{3,2,1,0:T(8,128)} %bias_hbm.1, f32[512,128]{1,0:T(8,128)S(1)} %get-tuple-element.48._.stream), custom_call_target="tpu_custom_call" | custom-call | tf_op jit(solution)/shard_map/pallas_call | solution.py:60
  10.5 0.2 collective-permute-done.1.second
  10.7 3.6 %shard_map.196 = (f32[512,128]{1,0:T(8,128)S(1)}, bf16[512,128]{1,0:T(8,128)(2,1)S(1)}, bf16[512,256]{1,0:T(8,128)(2,1)S(1)}, bf16[192,256]{1,0:T(8,128)(2,1)S(1)}, bf16[192,256]{1,0:T(8,128)(2,1)S(1)}) custom-call(s32[9]{0:T(128)S(1)} %stack.23.meta, bf16[512,128]{1,0:T(8,128)(2,1)S(1)} %get-tuple-element.44.q, bf16[512,256]{1,0:T(8,128)(2,1)S(1)} %get-tuple-element.45.kv, ...), custom_call_target="tpu_custom_call" | custom-call | tf_op jit(solution)/shard_map/pallas_call | solution.py:60
  14.3 4.8 %collective-permute-start.8 = (f32[16,16,256]{2,1,0:T(8,128)S(1)}, f32[16,16,256]{2,1,0:T(8,128)S(1)}, u32[]{:S(2)}, u32[]{:S(2)}) collective-permute-start(f32[16,16,256]{2,1,0:T(8,128)S(1)} %collective-permute-done.2.rest_2_), channel_id=1, source_target_pairs={{0,1},{1,0},{2,3},{3,2},{4,5},{5,4},{6,7},{7,6},{8,9},{9,8},{10,11... | collective-permute-start | bytes 786440 | tf_op jit(solution)/shard_map/ppermute | solution.py:525
  19.1 0.1 collective-permute-start.3
  19.2 1.0 %collective-permute-start.4 = (bf16[192,256]{1,0:T(8,128)(2,1)S(1)}, bf16[192,256]{1,0:T(8,128)(2,1)S(1)}, u32[]{:S(2)}, u32[]{:S(2)}) collective-permute-start(bf16[192,256]{1,0:T(8,128)(2,1)S(1)} %get-tuple-element.55), channel_id=1, source_target_pairs={{1,2},{3,4},{5,6},{7,8},{9,10},{11,12},{13,14},{2,1},{4,3},{6,5},{... | collective-permute-start | bytes 294920 | tf_op jit(solution)/shard_map/ppermute | solution.py:519
  20.2 0.2 collective-permute-done.3.first
  20.4 3.7 %collective-permute-done.4.second = bf16[192,256]{1,0:T(8,128)(2,1)S(1)} collective-permute-done((bf16[192,256]{1,0:T(8,128)(2,1)S(1)}, bf16[192,256]{1,0:T(8,128)(2,1)S(1)}, u32[]{:S(2)}, u32[]{:S(2)}) %collective-permute-start.4) | collective-permute-done | bytes 98336 | tf_op jit(solution)/shard_map/ppermute | solution.py:519
  24.1 4.5 %shard_map.197 = (f32[512,128]{1,0:T(8,128)S(1)}, f32[80,896]{1,0:T(8,128)S(1)}, bf16[64,896]{1,0:T(8,128)(2,1)S(1)}, bf16[64,896]{1,0:T(8,128)(2,1)S(1)}) custom-call(s32[9]{0:T(128)S(1)} %stack.23.meta, bf16[512,128]{1,0:T(8,128)(2,1)S(1)} %get-tuple-element.49.q, bf16[512,256]{1,0:T(8,128)(2,1)S(1)} %get-tuple-element.50.kv, ...), custom_call_target="tpu_custom_call" | custom-call | tf_op jit(solution)/shard_map/pallas_call | solution.py:60
  28.6 0.1 collective-permute-start.6
  28.7 1.6 %collective-permute-start.7 = (bf16[64,896]{1,0:T(8,128)(2,1)S(1)}, bf16[64,896]{1,0:T(8,128)(2,1)S(1)}, u32[]{:S(2)}, u32[]{:S(2)}) collective-permute-start(bf16[64,896]{1,0:T(8,128)(2,1)S(1)} %get-tuple-element.60), channel_id=1, source_target_pairs={{1,2},{3,4},{5,6},{7,8},{9,10},{11,12},{13,14},{2,1},{4,3},{6,5},{... | collective-permute-start | bytes 344072 | tf_op jit(solution)/shard_map/ppermute | solution.py:519
  30.3 3.7 %collective-permute-done.7.second = bf16[64,896]{1,0:T(8,128)(2,1)S(1)} collective-permute-done((bf16[64,896]{1,0:T(8,128)(2,1)S(1)}, bf16[64,896]{1,0:T(8,128)(2,1)S(1)}, u32[]{:S(2)}, u32[]{:S(2)}) %collective-permute-start.7) | collective-permute-done | bytes 114720 | tf_op jit(solution)/shard_map/ppermute | solution.py:519
  34.0 0.7 copy-done.10
  34.7 0.8 shard_map.198
  35.6 0.1 collective-permute-start.10
  35.7 2.0 %collective-permute-start.11 = (bf16[16,768]{1,0:T(8,128)(2,1)S(1)}, bf16[16,768]{1,0:T(8,128)(2,1)S(1)}, u32[]{:S(2)}, u32[]{:S(2)}) collective-permute-start(bf16[16,768]{1,0:T(8,128)(2,1)S(1)} %get-tuple-element.66), channel_id=1, source_target_pairs={{0,3},{1,2},{2,1},{3,0},{4,7},{5,6},{6,5},{7,4},{8,11},{9,10},{10,... | collective-permute-start | bytes 73736 | tf_op jit(solution)/shard_map/ppermute | solution.py:525
  37.7 0.6 collective-permute-done.10.rest_2_
  38.3 1.2 %collective-permute-done.11.rest_3_ = bf16[16,768]{1,0:T(8,128)(2,1)S(1)} collective-permute-done((bf16[16,768]{1,0:T(8,128)(2,1)S(1)}, bf16[16,768]{1,0:T(8,128)(2,1)S(1)}, u32[]{:S(2)}, u32[]{:S(2)}) %collective-permute-start.11) | collective-permute-done | bytes 24608 | tf_op jit(solution)/shard_map/ppermute | solution.py:525
  39.5 0.6 shard_map.199.normal
  40.1 1.8 %collective-permute-start.12 = (bf16[64,768]{1,0:T(8,128)(2,1)S(1)}, bf16[64,768]{1,0:T(8,128)(2,1)S(1)}, u32[]{:S(2)}, u32[]{:S(2)}) collective-permute-start(bf16[64,768]{1,0:T(8,128)(2,1)S(1)} %shard_map.199.normal), channel_id=1, source_target_pairs={{0,4},{4,8},{8,12},{12,0},{1,5},{5,9},{9,13},{13,1},{2,6},{6,10},{... | collective-permute-start | bytes 294920 | tf_op jit(solution)/shard_map/ppermute | solution.py:638
  41.9 2.2 %collective-permute-start.13 = (bf16[64,768]{1,0:T(8,128)(2,1)S(1)}, bf16[64,768]{1,0:T(8,128)(2,1)S(1)}, u32[]{:S(2)}, u32[]{:S(2)}) collective-permute-start(bf16[64,768]{1,0:T(8,128)(2,1)S(1)} %shard_map.199.normal), channel_id=1, source_target_pairs={{0,8},{4,12},{8,0},{12,4},{1,9},{5,13},{9,1},{13,5},{2,10},{6,14},... | collective-permute-start | bytes 294920 | tf_op jit(solution)/shard_map/ppermute | solution.py:638
  44.1 1.2 %collective-permute-start.14 = (bf16[64,768]{1,0:T(8,128)(2,1)S(1)}, bf16[64,768]{1,0:T(8,128)(2,1)S(1)}, u32[]{:S(2)}, u32[]{:S(2)}) collective-permute-start(bf16[64,768]{1,0:T(8,128)(2,1)S(1)} %shard_map.199.normal), channel_id=1, source_target_pairs={{0,12},{4,0},{8,4},{12,8},{1,13},{5,1},{9,5},{13,9},{2,14},{6,2},{... | collective-permute-start | bytes 294920 | tf_op jit(solution)/shard_map/ppermute | solution.py:638
  45.3 2.4 %shard_map.200 = (bf16[64,768]{1,0:T(8,128)(2,1)S(1)}, bf16[64,1536]{1,0:T(8,128)(2,1)S(1)}, f32[16,64,256]{2,1,0:T(8,128)S(1)}) custom-call(s32[9]{0:T(128)S(1)} %stack.23.meta, bf16[64,768]{1,0:T(8,128)(2,1)S(1)} %shard_map.199.normal, f32[16,16,256]{2,1,0:T(8,128)} %rest_0_.3, f32[16,16,256]{2,1,0:T(8,128)} %copy-done.9, f32[16,16,256]{2,1,0:T(8,128)} %copy-done.11, ...), custom_call_target="tpu_custom_call" | custom-call | tf_op jit(solution)/shard_map/pallas_call | solution.py:60
  47.7 3.6 %collective-permute-done.13.rest_1_ = bf16[64,768]{1,0:T(8,128)(2,1)S(1)} collective-permute-done((bf16[64,768]{1,0:T(8,128)(2,1)S(1)}, bf16[64,768]{1,0:T(8,128)(2,1)S(1)}, u32[]{:S(2)}, u32[]{:S(2)}) %collective-permute-start.13) | collective-permute-done | bytes 98336 | tf_op jit(solution)/shard_map/ppermute | solution.py:638
  51.3 3.8 %shard_map.201 = (bf16[16,768]{1,0:T(8,128)(2,1)S(1)}, bf16[16,768]{1,0:T(8,128)(2,1)S(1)}, bf16[16,768]{1,0:T(8,128)(2,1)S(1)}, bf16[16,768]{1,0:T(8,128)(2,1)S(1)}) custom-call(s32[9]{0:T(128)S(1)} %stack.23.meta, bf16[64,768]{1,0:T(8,128)(2,1)S(1)} %get-tuple-element.67.q_own, bf16[64,1536]{1,0:T(8,128)(2,1)S(1)} %get-tuple-element.68.kv_own, ...), custom_call_target="tpu_custom_call" | custom-call | tf_op jit(solution)/shard_map/pallas_call | solution.py:60
  55.1 0.7 collective-permute-start.15
  55.7 1.0 %collective-permute-start.16 = (bf16[16,768]{1,0:T(8,128)(2,1)S(1)}, bf16[16,768]{1,0:T(8,128)(2,1)S(1)}, u32[]{:S(2)}, u32[]{:S(2)}) collective-permute-start(bf16[16,768]{1,0:T(8,128)(2,1)S(1)} %get-tuple-element.72), channel_id=1, source_target_pairs={{0,2},{1,3},{2,0},{3,1},{4,6},{5,7},{6,4},{7,5},{8,10},{9,11},{10,... | collective-permute-start | bytes 73736 | tf_op jit(solution)/shard_map/ppermute | solution.py:525
  56.7 0.7 collective-permute-start.17
  57.4 1.0 %collective-permute-done.16.rest_2_ = bf16[16,768]{1,0:T(8,128)(2,1)S(1)} collective-permute-done((bf16[16,768]{1,0:T(8,128)(2,1)S(1)}, bf16[16,768]{1,0:T(8,128)(2,1)S(1)}, u32[]{:S(2)}, u32[]{:S(2)}) %collective-permute-start.16) | collective-permute-done | bytes 24608 | tf_op jit(solution)/shard_map/ppermute | solution.py:525
  58.4 1.6 %collective-permute-done.17.rest_3_ = bf16[16,768]{1,0:T(8,128)(2,1)S(1)} collective-permute-done((bf16[16,768]{1,0:T(8,128)(2,1)S(1)}, bf16[16,768]{1,0:T(8,128)(2,1)S(1)}, u32[]{:S(2)}, u32[]{:S(2)}) %collective-permute-start.17) | collective-permute-done | bytes 24608 | tf_op jit(solution)/shard_map/ppermute | solution.py:525
  60.0 1.7 %shard_map.202 = (f32[4,16,768]{2,1,0:T(8,128)}, bf16[64,128]{1,0:T(8,128)(2,1)S(1)}) custom-call(s32[9]{0:T(128)S(1)} %stack.23.meta, f32[64,768]{1,0:T(8,128)S(1)} %get-tuple-element.62.state, bf16[16,768]{1,0:T(8,128)(2,1)S(1)} %get-tuple-element.70.rest_0_, bf16[16,768]{1,0:T(8,128)(2,1)S(1)} %collective-permute-done.15.rest_1_, ...), custom_call_target="tpu_custom_call" | custom-call | tf_op jit(solution)/shard_map/pallas_call | solution.py:60
  61.7 0.4 collective-permute-start.18
  62.1 2.6 %collective-permute-start.19 = (bf16[64,128]{1,0:T(8,128)(2,1)S(1)}, bf16[64,128]{1,0:T(8,128)(2,1)S(1)}, u32[]{:S(2)}, u32[]{:S(2)}) collective-permute-start(bf16[64,128]{1,0:T(8,128)(2,1)S(1)} %get-tuple-element.74.back), channel_id=1, source_target_pairs={{1,2},{3,4},{5,6},{7,8},{9,10},{11,12},{13,14},{2,1},{4,3},{6,5},{... | collective-permute-start | bytes 49160 | tf_op jit(solution)/shard_map/ppermute | solution.py:519
  64.7 1.5 %collective-permute-done.19.second = bf16[64,128]{1,0:T(8,128)(2,1)S(1)} collective-permute-done((bf16[64,128]{1,0:T(8,128)(2,1)S(1)}, bf16[64,128]{1,0:T(8,128)(2,1)S(1)}, u32[]{:S(2)}, u32[]{:S(2)}) %collective-permute-start.19) | collective-permute-done | bytes 16416 | tf_op jit(solution)/shard_map/ppermute | solution.py:519
  66.2 1.4 %shard_map.203 = (f32[512,128]{1,0:T(8,128)S(1)}, bf16[512,128]{1,0:T(8,128)(2,1)S(1)}, bf16[512,256]{1,0:T(8,128)(2,1)S(1)}, bf16[192,256]{1,0:T(8,128)(2,1)S(1)}, bf16[192,256]{1,0:T(8,128)(2,1)S(1)}) custom-call(s32[9]{0:T(128)S(1)} %stack.23.meta, f32[512,128]{1,0:T(8,128)S(1)} %get-tuple-element.57.stream, s32[1,128]{1,0:T(1,128)S(1)} %bitcast.12, ...), custom_call_target="tpu_custom_call" | custom-call | tf_op jit(solution)/shard_map/pallas_call | solution.py:60
  67.6 0.1 collective-permute-start.20
  67.7 2.6 %collective-permute-start.21 = (bf16[192,256]{1,0:T(8,128)(2,1)S(1)}, bf16[192,256]{1,0:T(8,128)(2,1)S(1)}, u32[]{:S(2)}, u32[]{:S(2)}) collective-permute-start(bf16[192,256]{1,0:T(8,128)(2,1)S(1)} %get-tuple-element.78), channel_id=1, source_target_pairs={{1,2},{3,4},{5,6},{7,8},{9,10},{11,12},{13,14},{2,1},{4,3},{6,5},{... | collective-permute-start | bytes 294920 | tf_op jit(solution)/shard_map/ppermute | solution.py:519
  70.3 2.4 %collective-permute-done.21.second = bf16[192,256]{1,0:T(8,128)(2,1)S(1)} collective-permute-done((bf16[192,256]{1,0:T(8,128)(2,1)S(1)}, bf16[192,256]{1,0:T(8,128)(2,1)S(1)}, u32[]{:S(2)}, u32[]{:S(2)}) %collective-permute-start.21) | collective-permute-done | bytes 98336 | tf_op jit(solution)/shard_map/ppermute | solution.py:519
  72.7 3.6 %shard_map.204 = (f32[512,128]{1,0:T(8,128)S(1)}, bf16[512,128]{1,0:T(8,128)(2,1)S(1)}, bf16[512,256]{1,0:T(8,128)(2,1)S(1)}, bf16[192,256]{1,0:T(8,128)(2,1)S(1)}, bf16[192,256]{1,0:T(8,128)(2,1)S(1)}) custom-call(s32[9]{0:T(128)S(1)} %stack.23.meta, bf16[512,128]{1,0:T(8,128)(2,1)S(1)} %get-tuple-element.75.q, bf16[512,256]{1,0:T(8,128)(2,1)S(1)} %get-tuple-element.76.kv, ...), custom_call_target="tpu_custom_call" | custom-call | tf_op jit(solution)/shard_map/pallas_call | solution.py:60
  76.4 3.2 %collective-permute-start.23 = (bf16[192,256]{1,0:T(8,128)(2,1)S(1)}, bf16[192,256]{1,0:T(8,128)(2,1)S(1)}, u32[]{:S(2)}, u32[]{:S(2)}) collective-permute-start(bf16[192,256]{1,0:T(8,128)(2,1)S(1)} %get-tuple-element.83), channel_id=1, source_target_pairs={{1,2},{3,4},{5,6},{7,8},{9,10},{11,12},{13,14},{2,1},{4,3},{6,5},{... | collective-permute-start | bytes 294920 | tf_op jit(solution)/shard_map/ppermute | solution.py:519
  79.5 2.3 %collective-permute-done.23.second = bf16[192,256]{1,0:T(8,128)(2,1)S(1)} collective-permute-done((bf16[192,256]{1,0:T(8,128)(2,1)S(1)}, bf16[192,256]{1,0:T(8,128)(2,1)S(1)}, u32[]{:S(2)}, u32[]{:S(2)}) %collective-permute-start.23) | collective-permute-done | bytes 98336 | tf_op jit(solution)/shard_map/ppermute | solution.py:519
  81.8 4.3 %shard_map.205 = f32[3,4,128]{2,1,0:T(4,128)} custom-call(s32[9]{0:T(128)S(1)} %stack.23.meta, bf16[512,128]{1,0:T(8,128)(2,1)S(1)} %get-tuple-element.80.q, bf16[512,256]{1,0:T(8,128)(2,1)S(1)} %get-tuple-element.81.kv, bf16[192,256]{1,0:T(8,128)(2,1)S(1)} %collective-permute-done.22.first, bf16[192,256]{1,0:T(8,128)(2,1)S(1)} %collective-permute-done.23.second, ...), custom_call_target="tpu_custom_call" | custom-call | tf_op jit(solution)/shard_map/pallas_call | solution.py:60
  (37 shorter events, 0.2 us)
Async XLA Ops:
  1.4 43.9 %copy-start = (bf16[768,2304]{1,0:T(8,128)(2,1)S(1)}, bf16[768,2304]{1,0:T(8,128)(2,1)}, u32[]{:S(2)}) copy-start(bf16[768,2304]{1,0:T(8,128)(2,1)} %rest_3_.1) | copy-start | bytes 10616836
  4.4 9.9 %collective-permute-start.2 = (f32[16,16,256]{2,1,0:T(8,128)}, f32[16,16,256]{2,1,0:T(8,128)S(1)}, u32[]{:S(2)}, u32[]{:S(2)}) collective-permute-start(f32[16,16,256]{2,1,0:T(8,128)} %rest_0_.3), channel_id=1, source_target_pairs={{0,2},{1,3},{2,0},{3,1},{4,6},{5,7},{6,4},{7,5},{8,10},{9,11},{10,... | collective-permute-start | bytes 786440 | tf_op jit(solution)/shard_map/ppermute | solution.py:525
  4.7 15.5 %collective-permute-start.5 = (f32[16,16,256]{2,1,0:T(8,128)}, f32[16,16,256]{2,1,0:T(8,128)S(1)}, u32[]{:S(2)}, u32[]{:S(2)}) collective-permute-start(f32[16,16,256]{2,1,0:T(8,128)} %rest_0_.3), channel_id=1, source_target_pairs={{0,1},{1,0},{2,3},{3,2},{4,5},{5,4},{6,7},{7,6},{8,9},{9,8},{10,11... | collective-permute-start | bytes 786440 | tf_op jit(solution)/shard_map/ppermute | solution.py:525
  5.7 4.9 %collective-permute-start = (bf16[192,256]{1,0:T(8,128)(2,1)S(1)}, bf16[192,256]{1,0:T(8,128)(2,1)S(1)}, u32[]{:S(2)}, u32[]{:S(2)}) collective-permute-start(bf16[192,256]{1,0:T(8,128)(2,1)S(1)} %get-tuple-element.46), channel_id=1, source_target_pairs={{0,1},{1,0},{2,3},{3,2},{4,5},{5,4},{6,7},{7,6},{8,9},{9,8},{10,11... | collective-permute-start | bytes 294920 | tf_op jit(solution)/shard_map/ppermute | solution.py:520
  5.7 5.0 %collective-permute-start.1 = (bf16[192,256]{1,0:T(8,128)(2,1)S(1)}, bf16[192,256]{1,0:T(8,128)(2,1)S(1)}, u32[]{:S(2)}, u32[]{:S(2)}) collective-permute-start(bf16[192,256]{1,0:T(8,128)(2,1)S(1)} %get-tuple-element.47), channel_id=1, source_target_pairs={{1,2},{3,4},{5,6},{7,8},{9,10},{11,12},{13,14},{2,1},{4,3},{6,5},{... | collective-permute-start | bytes 294920 | tf_op jit(solution)/shard_map/ppermute | solution.py:519
  8.3 0.7 copy-start.8
  14.3 30.9 %copy-start.11 = (f32[16,16,256]{2,1,0:T(8,128)}, f32[16,16,256]{2,1,0:T(8,128)S(1)}, u32[]{:S(2)}) copy-start(f32[16,16,256]{2,1,0:T(8,128)S(1)} %collective-permute-done.2.rest_2_) | copy-start | bytes 786436
  14.3 19.6 %collective-permute-start.8 = (f32[16,16,256]{2,1,0:T(8,128)S(1)}, f32[16,16,256]{2,1,0:T(8,128)S(1)}, u32[]{:S(2)}, u32[]{:S(2)}) collective-permute-start(f32[16,16,256]{2,1,0:T(8,128)S(1)} %collective-permute-done.2.rest_2_), channel_id=1, source_target_pairs={{0,1},{1,0},{2,3},{3,2},{4,5},{5,4},{6,7},{7,6},{8,9},{9,8},{10,11... | collective-permute-start | bytes 786440 | tf_op jit(solution)/shard_map/ppermute | solution.py:525
  19.1 1.3 %collective-permute-start.3 = (bf16[192,256]{1,0:T(8,128)(2,1)S(1)}, bf16[192,256]{1,0:T(8,128)(2,1)S(1)}, u32[]{:S(2)}, u32[]{:S(2)}) collective-permute-start(bf16[192,256]{1,0:T(8,128)(2,1)S(1)} %get-tuple-element.54), channel_id=1, source_target_pairs={{0,1},{1,0},{2,3},{3,2},{4,5},{5,4},{6,7},{7,6},{8,9},{9,8},{10,11... | collective-permute-start | bytes 294920 | tf_op jit(solution)/shard_map/ppermute | solution.py:520
  19.2 4.9 %collective-permute-start.4 = (bf16[192,256]{1,0:T(8,128)(2,1)S(1)}, bf16[192,256]{1,0:T(8,128)(2,1)S(1)}, u32[]{:S(2)}, u32[]{:S(2)}) collective-permute-start(bf16[192,256]{1,0:T(8,128)(2,1)S(1)} %get-tuple-element.55), channel_id=1, source_target_pairs={{1,2},{3,4},{5,6},{7,8},{9,10},{11,12},{13,14},{2,1},{4,3},{6,5},{... | collective-permute-start | bytes 294920 | tf_op jit(solution)/shard_map/ppermute | solution.py:519
  20.2 3.9 %copy-start.9 = (f32[16,16,256]{2,1,0:T(8,128)}, f32[16,16,256]{2,1,0:T(8,128)S(1)}, u32[]{:S(2)}) copy-start(f32[16,16,256]{2,1,0:T(8,128)S(1)} %collective-permute-done.5.rest_1_) | copy-start | bytes 786436
  28.6 1.7 %collective-permute-start.6 = (bf16[64,896]{1,0:T(8,128)(2,1)S(1)}, bf16[64,896]{1,0:T(8,128)(2,1)S(1)}, u32[]{:S(2)}, u32[]{:S(2)}) collective-permute-start(bf16[64,896]{1,0:T(8,128)(2,1)S(1)} %get-tuple-element.59), channel_id=1, source_target_pairs={{0,1},{1,0},{2,3},{3,2},{4,5},{5,4},{6,7},{7,6},{8,9},{9,8},{10,11... | collective-permute-start | bytes 344072 | tf_op jit(solution)/shard_map/ppermute | solution.py:520
  28.7 5.3 %collective-permute-start.7 = (bf16[64,896]{1,0:T(8,128)(2,1)S(1)}, bf16[64,896]{1,0:T(8,128)(2,1)S(1)}, u32[]{:S(2)}, u32[]{:S(2)}) collective-permute-start(bf16[64,896]{1,0:T(8,128)(2,1)S(1)} %get-tuple-element.60), channel_id=1, source_target_pairs={{1,2},{3,4},{5,6},{7,8},{9,10},{11,12},{13,14},{2,1},{4,3},{6,5},{... | collective-permute-start | bytes 344072 | tf_op jit(solution)/shard_map/ppermute | solution.py:519
  34.0 0.7 copy-start.10
  35.5 2.2 %collective-permute-start.9 = (bf16[16,768]{1,0:T(8,128)(2,1)S(1)}, bf16[16,768]{1,0:T(8,128)(2,1)S(1)}, u32[]{:S(2)}, u32[]{:S(2)}) collective-permute-start(bf16[16,768]{1,0:T(8,128)(2,1)S(1)} %get-tuple-element.64), channel_id=1, source_target_pairs={{0,1},{1,0},{2,3},{3,2},{4,5},{5,4},{6,7},{7,6},{8,9},{9,8},{10,11... | collective-permute-start | bytes 73736 | tf_op jit(solution)/shard_map/ppermute | solution.py:525
  35.6 2.7 %collective-permute-start.10 = (bf16[16,768]{1,0:T(8,128)(2,1)S(1)}, bf16[16,768]{1,0:T(8,128)(2,1)S(1)}, u32[]{:S(2)}, u32[]{:S(2)}) collective-permute-start(bf16[16,768]{1,0:T(8,128)(2,1)S(1)} %get-tuple-element.65), channel_id=1, source_target_pairs={{0,2},{1,3},{2,0},{3,1},{4,6},{5,7},{6,4},{7,5},{8,10},{9,11},{10,... | collective-permute-start | bytes 73736 | tf_op jit(solution)/shard_map/ppermute | solution.py:525
  35.7 3.9 %collective-permute-start.11 = (bf16[16,768]{1,0:T(8,128)(2,1)S(1)}, bf16[16,768]{1,0:T(8,128)(2,1)S(1)}, u32[]{:S(2)}, u32[]{:S(2)}) collective-permute-start(bf16[16,768]{1,0:T(8,128)(2,1)S(1)} %get-tuple-element.66), channel_id=1, source_target_pairs={{0,3},{1,2},{2,1},{3,0},{4,7},{5,6},{6,5},{7,4},{8,11},{9,10},{10,... | collective-permute-start | bytes 73736 | tf_op jit(solution)/shard_map/ppermute | solution.py:525
  40.1 7.6 %collective-permute-start.12 = (bf16[64,768]{1,0:T(8,128)(2,1)S(1)}, bf16[64,768]{1,0:T(8,128)(2,1)S(1)}, u32[]{:S(2)}, u32[]{:S(2)}) collective-permute-start(bf16[64,768]{1,0:T(8,128)(2,1)S(1)} %shard_map.199.normal), channel_id=1, source_target_pairs={{0,4},{4,8},{8,12},{12,0},{1,5},{5,9},{9,13},{13,1},{2,6},{6,10},{... | collective-permute-start | bytes 294920 | tf_op jit(solution)/shard_map/ppermute | solution.py:638
  41.9 9.4 %collective-permute-start.13 = (bf16[64,768]{1,0:T(8,128)(2,1)S(1)}, bf16[64,768]{1,0:T(8,128)(2,1)S(1)}, u32[]{:S(2)}, u32[]{:S(2)}) collective-permute-start(bf16[64,768]{1,0:T(8,128)(2,1)S(1)} %shard_map.199.normal), channel_id=1, source_target_pairs={{0,8},{4,12},{8,0},{12,4},{1,9},{5,13},{9,1},{13,5},{2,10},{6,14},... | collective-permute-start | bytes 294920 | tf_op jit(solution)/shard_map/ppermute | solution.py:638
  44.1 7.2 %collective-permute-start.14 = (bf16[64,768]{1,0:T(8,128)(2,1)S(1)}, bf16[64,768]{1,0:T(8,128)(2,1)S(1)}, u32[]{:S(2)}, u32[]{:S(2)}) collective-permute-start(bf16[64,768]{1,0:T(8,128)(2,1)S(1)} %shard_map.199.normal), channel_id=1, source_target_pairs={{0,12},{4,0},{8,4},{12,8},{1,13},{5,1},{9,5},{13,9},{2,14},{6,2},{... | collective-permute-start | bytes 294920 | tf_op jit(solution)/shard_map/ppermute | solution.py:638
  47.6 12.3 %copy-start.2 = (bf16[768,768]{1,0:T(8,128)(2,1)S(1)}, bf16[768,768]{1,0:T(8,128)(2,1)}, u32[]{:S(2)}) copy-start(bf16[768,768]{1,0:T(8,128)(2,1)} %rest_4_.3) | copy-start | bytes 3538948
  47.6 12.3 %copy-start.3 = (bf16[768,128]{1,0:T(8,128)(2,1)S(1)}, bf16[768,128]{1,0:T(8,128)(2,1)}, u32[]{:S(2)}) copy-start(bf16[768,128]{1,0:T(8,128)(2,1)} %rest_5_.1) | copy-start | bytes 589828
  47.7 18.5 %copy-start.1 = (bf16[4,128,384]{2,1,0:T(8,128)(2,1)S(1)}, bf16[4,128,384]{2,1,0:T(8,128)(2,1)}, u32[]{:S(2)}) copy-start(bf16[4,128,384]{2,1,0:T(8,128)(2,1)} %w_qkv.5) | copy-start | bytes 1179652
  47.7 18.5 %copy-start.6 = (s32[128]{0:T(128)S(1)}, s32[128]{0:T(128)}, u32[]{:S(2)}) copy-start(s32[128]{0:T(128)} %param.23) | copy-start | bytes 1540
  55.0 26.8 %copy-start.4 = (f32[4,3,128]{2,0,1:T(4,128)S(1)}, f32[4,3,128]{2,0,1:T(4,128)}, u32[]{:S(2)}) copy-start(f32[4,3,128]{2,0,1:T(4,128)} %param.20) | copy-start | bytes 18436
  55.0 26.8 %copy-start.5 = (f32[3,128]{1,0:T(4,128)S(1)}, f32[3,128]{1,0:T(4,128)}, u32[]{:S(2)}) copy-start(f32[3,128]{1,0:T(4,128)} %x_true.1) | copy-start | bytes 4612
  55.1 26.8 %copy-start.7 = (bf16[3,128]{1,0:T(4,128)(2,1)S(1)}, bf16[3,128]{1,0:T(4,128)(2,1)}, u32[]{:S(2)}) copy-start(bf16[3,128]{1,0:T(4,128)(2,1)} %w_final.1) | copy-start | bytes 2308
  55.1 2.4 %collective-permute-start.15 = (bf16[16,768]{1,0:T(8,128)(2,1)S(1)}, bf16[16,768]{1,0:T(8,128)(2,1)S(1)}, u32[]{:S(2)}, u32[]{:S(2)}) collective-permute-start(bf16[16,768]{1,0:T(8,128)(2,1)S(1)} %get-tuple-element.71), channel_id=1, source_target_pairs={{0,1},{1,0},{2,3},{3,2},{4,5},{5,4},{6,7},{7,6},{8,9},{9,8},{10,11... | collective-permute-start | bytes 73736 | tf_op jit(solution)/shard_map/ppermute | solution.py:525
  55.7 2.7 %collective-permute-start.16 = (bf16[16,768]{1,0:T(8,128)(2,1)S(1)}, bf16[16,768]{1,0:T(8,128)(2,1)S(1)}, u32[]{:S(2)}, u32[]{:S(2)}) collective-permute-start(bf16[16,768]{1,0:T(8,128)(2,1)S(1)} %get-tuple-element.72), channel_id=1, source_target_pairs={{0,2},{1,3},{2,0},{3,1},{4,6},{5,7},{6,4},{7,5},{8,10},{9,11},{10,... | collective-permute-start | bytes 73736 | tf_op jit(solution)/shard_map/ppermute | solution.py:525
  56.7 3.3 %collective-permute-start.17 = (bf16[16,768]{1,0:T(8,128)(2,1)S(1)}, bf16[16,768]{1,0:T(8,128)(2,1)S(1)}, u32[]{:S(2)}, u32[]{:S(2)}) collective-permute-start(bf16[16,768]{1,0:T(8,128)(2,1)S(1)} %get-tuple-element.73), channel_id=1, source_target_pairs={{0,3},{1,2},{2,1},{3,0},{4,7},{5,6},{6,5},{7,4},{8,11},{9,10},{10,... | collective-permute-start | bytes 73736 | tf_op jit(solution)/shard_map/ppermute | solution.py:525
  61.7 2.9 %collective-permute-start.18 = (bf16[64,128]{1,0:T(8,128)(2,1)S(1)}, bf16[64,128]{1,0:T(8,128)(2,1)S(1)}, u32[]{:S(2)}, u32[]{:S(2)}) collective-permute-start(bf16[64,128]{1,0:T(8,128)(2,1)S(1)} %get-tuple-element.74.back), channel_id=1, source_target_pairs={{0,1},{1,0},{2,3},{3,2},{4,5},{5,4},{6,7},{7,6},{8,9},{9,8},{10,11... | collective-permute-start | bytes 49160 | tf_op jit(solution)/shard_map/ppermute | solution.py:520
  62.1 4.1 %collective-permute-start.19 = (bf16[64,128]{1,0:T(8,128)(2,1)S(1)}, bf16[64,128]{1,0:T(8,128)(2,1)S(1)}, u32[]{:S(2)}, u32[]{:S(2)}) collective-permute-start(bf16[64,128]{1,0:T(8,128)(2,1)S(1)} %get-tuple-element.74.back), channel_id=1, source_target_pairs={{1,2},{3,4},{5,6},{7,8},{9,10},{11,12},{13,14},{2,1},{4,3},{6,5},{... | collective-permute-start | bytes 49160 | tf_op jit(solution)/shard_map/ppermute | solution.py:519
  67.6 2.7 %collective-permute-start.20 = (bf16[192,256]{1,0:T(8,128)(2,1)S(1)}, bf16[192,256]{1,0:T(8,128)(2,1)S(1)}, u32[]{:S(2)}, u32[]{:S(2)}) collective-permute-start(bf16[192,256]{1,0:T(8,128)(2,1)S(1)} %get-tuple-element.77), channel_id=1, source_target_pairs={{0,1},{1,0},{2,3},{3,2},{4,5},{5,4},{6,7},{7,6},{8,9},{9,8},{10,11... | collective-permute-start | bytes 294920 | tf_op jit(solution)/shard_map/ppermute | solution.py:520
  67.7 5.0 %collective-permute-start.21 = (bf16[192,256]{1,0:T(8,128)(2,1)S(1)}, bf16[192,256]{1,0:T(8,128)(2,1)S(1)}, u32[]{:S(2)}, u32[]{:S(2)}) collective-permute-start(bf16[192,256]{1,0:T(8,128)(2,1)S(1)} %get-tuple-element.78), channel_id=1, source_target_pairs={{1,2},{3,4},{5,6},{7,8},{9,10},{11,12},{13,14},{2,1},{4,3},{6,5},{... | collective-permute-start | bytes 294920 | tf_op jit(solution)/shard_map/ppermute | solution.py:519
  76.3 3.2 %collective-permute-start.22 = (bf16[192,256]{1,0:T(8,128)(2,1)S(1)}, bf16[192,256]{1,0:T(8,128)(2,1)S(1)}, u32[]{:S(2)}, u32[]{:S(2)}) collective-permute-start(bf16[192,256]{1,0:T(8,128)(2,1)S(1)} %get-tuple-element.82), channel_id=1, source_target_pairs={{0,1},{1,0},{2,3},{3,2},{4,5},{5,4},{6,7},{7,6},{8,9},{9,8},{10,11... | collective-permute-start | bytes 294920 | tf_op jit(solution)/shard_map/ppermute | solution.py:520
  76.4 5.4 %collective-permute-start.23 = (bf16[192,256]{1,0:T(8,128)(2,1)S(1)}, bf16[192,256]{1,0:T(8,128)(2,1)S(1)}, u32[]{:S(2)}, u32[]{:S(2)}) collective-permute-start(bf16[192,256]{1,0:T(8,128)(2,1)S(1)} %get-tuple-element.83), channel_id=1, source_target_pairs={{1,2},{3,4},{5,6},{7,8},{9,10},{11,12},{13,14},{2,1},{4,3},{6,5},{... | collective-permute-start | bytes 294920 | tf_op jit(solution)/shard_map/ppermute | solution.py:519

commit v4 on v3

--- a/solution.py
+++ b/solution.py
@@ -24,7 +24,6 @@
 SM = pl.BlockSpec(memory_space=pltpu.SMEM)
 HB = pl.BlockSpec(memory_space=pltpu.HBM)
 COUNT_LANES = 128
-PLACES = 5
 LOG2E = 1.4426950408889634
 
 
@@ -197,12 +196,13 @@
 
 
 def embed_kernel(
-    meta, x_true_hbm, noise_hbm, single_hbm, w_coord_hbm, w_qkv_hbm,
+    meta, level_hbm, x_true_hbm, noise_hbm, single_hbm, w_coord_hbm, w_qkv_hbm,
     stream_ref, q_ref, kv_ref, first_ref, second_ref,
-    x_true, noise, single, w_coord, w_qkv, sems, *, samples, rows,
+    level, x_true, noise, single, w_coord, w_qkv, sems, *, samples, rows,
 ):
     copies = fetch(
         [
+            (level_hbm, level),
             (x_true_hbm, x_true),
             (noise_hbm, noise),
             (single_hbm, single),
@@ -212,10 +212,10 @@
         sems,
     )
     channels = single.shape[-1]
-    sigma, total = sigma_of(meta, samples)
-    inverse = lax.rsqrt(total)
     for copy in copies:
         copy.wait()
+    sigma, total = sigma_of(level, samples)
+    inverse = lax.rsqrt(total)
     base = single[...].astype(F32)
     scaled = [
         (x_true[c : c + 1] + sigma * noise[c]) * inverse for c in range(x_true.shape[0])
@@ -253,11 +253,11 @@
         out_ref[b] = jnp.where(allowed, values, -jnp.inf)
 
 
-def sigma_of(meta, samples):
+def sigma_of(level, samples):
     row = lax.broadcasted_iota(jnp.int32, (samples, 1), 0)
     levels = jnp.zeros((samples, 1), jnp.int32)
     for s in range(samples):
-        levels = jnp.where(row == s, meta[PLACES + s], levels)
+        levels = jnp.where(row == s, level[s], levels)
     sigma = noise_scale(levels)
     return sigma, sigma * sigma + SIGMA_DATA * SIGMA_DATA
 
@@ -302,8 +302,8 @@
     *rest, layer, samples, rows, tokens,
 ):
     single_hbm = rest[0]
-    (stream_ref, mid_ref, first_ref, second_ref,
-     padded, out, up, down, sems, normal_all, sums, pooling, owners, single, late_sems) = rest[-15:]
+    (stream_ref, mid_ref, first_ref, second_ref, first_rim, second_rim,
+     padded, out, up, down, sems, normal_all, sums, pooling, owners, single, late_sems) = rest[-17:]
     copies = fetch(
         [(w_out.at[layer], out), (w_up.at[layer], up), (w_down.at[layer], down)], sems
     )
@@ -333,6 +333,14 @@
         sums[s, :, width:] = jnp.broadcast_to(counts, (3 * tokens, COUNT_LANES))
 
     run_stages([pool, gather], samples)
+    ends = [owners[:, :RIM], owners[:, rows - RIM :]]
+    for at, side in ((first_rim, 0), (second_rim, 1)):
+        for s in range(samples):
+            start = halves(meta[0], s * rows, (s + 1) * rows - RIM)[side]
+            at[s * RIM : (s + 1) * RIM] = stream_ref[pl.ds(start, RIM)]
+        named = jnp.where(meta[0] == side, ends[1], ends[0]).astype(F32)
+        at[samples * RIM :] = jnp.zeros((8, at.shape[-1]), F32)
+        at[samples * RIM : samples * RIM + 1, :RIM] = named
     mid_ref[samples * tokens :, :width] = single[...]
     mid_ref[samples * tokens :, width:] = jnp.zeros((tokens, COUNT_LANES), F32)
     for s in range(samples):
@@ -344,7 +352,7 @@
 
 
 def token_in_kernel(
-    meta, mid, first, second, _, state_ref, *rest, samples, tokens
+    meta, mid, first, second, state_ref, *rest, samples, tokens
 ):
     send_refs, normal_all = rest[:samples], rest[samples]
     width = state_ref.shape[-1]
@@ -447,44 +455,61 @@
 
 
 def unpool_kernel(
-    meta, stream, atom_token, back, first, second, w_qkv,
+    meta, stream, atom_token, back, first, second, first_rim, second_rim, w_qkv,
     stream_ref, q_ref, kv_ref, first_ref, second_ref, padded, *, samples, rows, tokens,
 ):
     channels = stream.shape[-1]
+    weight = w_qkv.at[ENC_LAYERS]
     selector = selector_of(meta, atom_token, tokens).astype(BF)
     first_at, second_at = halves(meta[0], 0, 2 * tokens)
+    row = lax.broadcasted_iota(jnp.int32, (3 * tokens, RIM), 0).astype(F32)
+    base = ((meta[2] - 1) * tokens).astype(F32)
+    rims = [
+        (rim, (row == rim[samples * RIM : samples * RIM + 1, :RIM] - base).astype(BF), out)
+        for rim, out in ((first_rim, first_ref), (second_rim, second_ref))
+    ]
+
+    def pick(chosen, s):
+        return lax.dot_general(
+            chosen, padded[s], (((0,), (0,)), ((), ())), preferred_element_type=F32
+        )
 
     def place(s, _):
         at = slice(s * tokens, (s + 1) * tokens)
         padded[s, tokens : 2 * tokens] = back[at]
         padded[s, pl.ds(first_at, tokens)] = first[at]
         padded[s, pl.ds(second_at, tokens)] = second[at]
-        picked = lax.dot_general(
-            selector, padded[s], (((0,), (0,)), ((), ())), preferred_element_type=F32
-        )
-        return stream[s * rows : (s + 1) * rows] + picked
+        own = stream[s * rows : (s + 1) * rows] + pick(selector, s)
+        stream_ref[s * rows : (s + 1) * rows] = own
+        parts = [own]
+        for rim, chosen, _ in rims:
+            parts.append(rim[s * RIM : (s + 1) * RIM] + pick(chosen, s))
+        return jnp.concatenate(parts, 0)
 
     def normalise(s, after):
-        stream_ref[s * rows : (s + 1) * rows] = after
         return normed(after).astype(BF)
 
     def project(s, normal):
-        projected = dot(normal, w_qkv[ENC_LAYERS])
-        q_ref[s * rows : (s + 1) * rows] = projected[:, :channels].astype(BF)
-        kv_ref[s * rows : (s + 1) * rows] = projected[:, channels:].astype(BF)
+        projected = dot(normal, weight[...])
+        q_ref[s * rows : (s + 1) * rows] = projected[:rows, :channels].astype(BF)
+        key_values = projected[:, channels:].astype(BF)
+        kv_ref[s * rows : (s + 1) * rows] = key_values[:rows]
+        for side, (_, _, out) in enumerate(rims):
+            start = rows + side * RIM
+            out[s * RIM : (s + 1) * RIM] = key_values[start : start + RIM]
 
     run_stages([place, normalise, project], samples)
-    emit_rims(kv_ref, meta[0], samples, rows, first_ref, second_ref)
 
 
 def final_kernel(
     meta, q, kv, first, second, stream, bias, w_out, w_up, w_down, w_final,
-    x_true, noise, denoised_ref, padded, out, up, down, sems, normal_all,
-    *, layer, samples, rows,
+    level_hbm, x_true, noise, denoised_ref, padded, out, up, down, sems, normal_all,
+    level, late_sems, *, layer, samples, rows,
 ):
     copies = fetch(
         [(w_out.at[layer], out), (w_up.at[layer], up), (w_down.at[layer], down)], sems
     )
+    late = fetch([(level_hbm, level)], late_sems)
 
     def finish(b, normal):
         store_rows(normal_all, b, samples, rows, normal)
@@ -493,7 +518,8 @@
         meta, q, kv, first, second, stream, bias, (out, up, down), copies,
         samples, rows, padded, None, finish,
     )
-    sigma, total = sigma_of(meta, samples)
+    late[0].wait()
+    sigma, total = sigma_of(level, samples)
     keep = SIGMA_DATA * SIGMA_DATA / total
     move = sigma * SIGMA_DATA * lax.rsqrt(total)
     updates = [
@@ -543,8 +569,7 @@
     mine = lax.axis_index("p")
     plane = lax.axis_index("z")
     device = plane * samples + mine
-    places = [device % 2, device * rows, device, mine, plane]
-    meta = jnp.stack(places + [noise_level[s] for s in range(samples)])
+    meta = jnp.stack([device % 2, device * rows, device, mine, plane]).astype(jnp.int32)
     atom_token = atom_token[None, :]
     edges = window_edges.T
     noise = noise.transpose(1, 0, 2)
@@ -573,15 +598,16 @@
         )
 
     stream, q, kv, *rims = call(
-        functools.partial(embed_kernel, **sizes), atom_outs, [SM] + [HB] * 5,
-        (meta, x_true, noise, atom_single, w_coord, w_atom_qkv),
+        functools.partial(embed_kernel, **sizes), atom_outs, [SM] + [HB] * 6,
+        (meta, noise_level, x_true, noise, atom_single, w_coord, w_atom_qkv),
         [
+            pltpu.SMEM(noise_level.shape, jnp.int32),
             pltpu.VMEM(x_true.shape, F32),
             pltpu.VMEM(noise.shape, F32),
             pltpu.VMEM(atom_single.shape, BF),
             pltpu.VMEM(w_coord.shape, F32),
             pltpu.VMEM(w_atom_qkv.shape[1:], BF),
-            pltpu.SemaphoreType.DMA((5,)),
+            pltpu.SemaphoreType.DMA((6,)),
         ],
     )
     blocks, atom_heads, queries, window = atom_pair_bias.shape
@@ -598,17 +624,18 @@
             for k in (1, 2):
                 biases.append(toward(held_bias, k, samples))
         stream, q, kv, *rims = block(layer, q, kv, rims, stream)
-        if layer == 0:
-            passed, *rims = lax.optimization_barrier((biases[2], *rims))
-            biases.append(toward(passed, 1, samples))
     rims = swap(rims, count)
     lanes = width + COUNT_LANES
     edge = struct((held, lanes), BF)
-    encoded, mid, *rims = call(
+    stream_rim = struct((samples * RIM + 8, channels), F32)
+    encoded, mid, first, second, *stream_rims = call(
         functools.partial(pool_kernel, layer=ENC_LAYERS - 1, tokens=tokens, **sizes),
-        (atom_outs[0], struct((held + tokens, lanes), F32), edge, edge),
-        [SM] + [VM] * 6 + [HB] * 7,
-        (meta, q, kv, *rims, stream, bias, *stacks, w_pool, atom_token, token_single, biases[1]),
+        (atom_outs[0], struct((held + tokens, lanes), F32), edge, edge, stream_rim, stream_rim),
+        [SM] + [VM] * 6 + [HB] * 6 + [VM] * 2,
+        (
+            meta, q, kv, *rims, stream, bias, *stacks, w_pool, atom_token, token_single,
+            *biases[1:3],
+        ),
         scratch
         + [
             normals,
@@ -619,12 +646,14 @@
             pltpu.SemaphoreType.DMA((3,)),
         ],
     )
-    rims = swap(rims, count)
+    passed, _ = lax.optimization_barrier((biases[2], mid))
+    biases.append(toward(passed, 1, samples))
+    rims = swap((first, second), count)
     piece = struct((tokens, width), BF)
     state, *sends = call(
         functools.partial(token_in_kernel, samples=samples, tokens=tokens),
         (struct((held, width), F32),) + (piece,) * samples,
-        [SM] + [VM] * 3 + [HB], (meta, mid, *rims, biases[3]),
+        [SM] + [VM] * 3, (meta, mid, *rims),
         [pltpu.VMEM((samples, tokens, width), BF)],
     )
     got = across(sends[1:], samples)
@@ -636,6 +665,7 @@
     for k in range(1, planes):
         shift = [(i, (i + k) % planes) for i in range(planes)]
         gathered.append(lax.ppermute(normal, "z", shift))
+    stream_rims = swap(stream_rims, count)
     every = planes * held
     q_own, kv_own, bias_all = call(
         functools.partial(token_own_kernel, samples=samples, tokens=tokens),
@@ -644,7 +674,7 @@
             struct((held, 2 * width), BF),
             struct((heads, held, every), F32),
         ),
-        [SM, VM] + [HB] * samples + [VM], (meta, normal, *biases, w_token_qkv),
+        [SM, VM, HB] + [VM] * samples, (meta, normal, *biases, w_token_qkv),
         [pltpu.SemaphoreType.DMA((samples,))],
     )
     sends = call(
@@ -665,20 +695,27 @@
     backs = swap((back, back), count)
     stream, q, kv, *rims = call(
         functools.partial(unpool_kernel, tokens=tokens, **sizes), atom_outs,
-        [SM] + [VM] * 6, (meta, encoded, atom_token, back, *backs, w_atom_qkv),
+        [SM] + [VM] * 8,
+        (meta, encoded, atom_token, back, *backs, *stream_rims, w_atom_qkv),
         [pltpu.VMEM((samples, 3 * tokens, channels), BF)],
     )
     for layer in range(ENC_LAYERS, LAYERS - 1):
-        rims = swap(rims, count)
+        if layer > ENC_LAYERS:
+            rims = swap(rims, count)
         stream, q, kv, *rims = block(layer, q, kv, rims, stream)
     rims = swap(rims, count)
     denoised = call(
         functools.partial(final_kernel, layer=LAYERS - 1, **sizes),
-        struct(noise.shape, F32), [SM] + [VM] * 6 + [HB] * 3 + [VM] * 3,
+        struct(noise.shape, F32), [SM] + [VM] * 6 + [HB] * 3 + [VM, HB, VM, VM],
         (
-            meta, q, kv, *rims, stream, bias, *stacks, w_final, x_true, noise,
+            meta, q, kv, *rims, stream, bias, *stacks, w_final, noise_level, x_true, noise,
         ),
-        scratch + [normals],
+        scratch
+        + [
+            normals,
+            pltpu.SMEM(noise_level.shape, jnp.int32),
+            pltpu.SemaphoreType.DMA((1,)),
+        ],
     )
     return denoised.transpose(1, 0, 2), token_state
 

time: 87.9 us -> 82.7 us (0.941)
  the two profiles are of different devices: /device:TPU:7 before, /device:TPU:11 now
where the time goes in v4:
time: 82.7 us; the launch traced here: 82.4 us
  Pallas kernels  31 us (37%)
  waiting for transfers between devices  29.8 us (36%)
  starting transfers between devices  19.8 us (24%)
  between operations  0.99 us (1%)
    pallas_call x12, Pallas kernels, call(): pl.pallas_call(kernel, out_shape=out_shape, in_specs=specs, out_specs=jax...  31 us
    ppermute x6, waiting for transfers between devices, swap(): second = lax.ppermute(second, ('groups',) + SEQ, upper)  19.6 us
    ppermute x6, starting transfers between devices, swap(): second = lax.ppermute(second, ('groups',) + SEQ, upper)  7.4 us
    ppermute x9, starting transfers between devices, toward(): return lax.ppermute(array, 'p', [(i, i ^ k) for i in range(count)])  6.84 us
    ppermute x3, waiting for transfers between devices, shards(): gathered.append(lax.ppermute(normal, 'z', shift))  5.26 us
    ppermute x9, waiting for transfers between devices, toward(): return lax.ppermute(array, 'p', [(i, i ^ k) for i in range(count)])  4.94 us
    ppermute x6, starting transfers between devices, swap(): first = lax.ppermute(first, SEQ, lower)  2.99 us
    ppermute x3, starting transfers between devices, shards(): gathered.append(lax.ppermute(normal, 'z', shift))  2.61 us
  transfers between devices with their start and end apart: 24, of which 11 were waited for; matrix products, arithmetic and copies ran while one was open for 0% of the time, Pallas kernels for 16%

profile of v4, /device:TPU:11, one launch (start us, length us, event | category | flops | bytes accessed | tf_op | source)
XLA Modules:
  0.0 82.4 jit_solution(14115999435104506984)
XLA Ops:
  0.6 0.1 stack.23.meta
  0.7 3.1 %shard_map.194 = (f32[512,128]{1,0:T(8,128)S(1)}, bf16[512,128]{1,0:T(8,128)(2,1)S(1)}, bf16[512,256]{1,0:T(8,128)(2,1)S(1)}, bf16[192,256]{1,0:T(8,128)(2,1)S(1)}, bf16[192,256]{1,0:T(8,128)(2,1)S(1)}) custom-call(s32[5]{0:T(128)S(1)} %stack.23.meta, s32[4]{0:T(128)} %level_hbm.3, f32[3,128]{1,0:T(4,128)} %x_true.1, f32[3,4,128]{2,1,0:T(4,128)} %bitcast.9, ...), custom_call_target="tpu_custom_call" | custom-call | tf_op jit(solution)/shard_map/pallas_call | solution.py:59
  3.8 0.7 collective-permute-start.4
  4.5 1.2 %collective-permute-start.5 = (f32[16,16,256]{2,1,0:T(8,128)}, f32[16,16,256]{2,1,0:T(8,128)S(1)}, u32[]{:S(2)}, u32[]{:S(2)}) collective-permute-start(f32[16,16,256]{2,1,0:T(8,128)} %rest_0_.3), channel_id=1, source_target_pairs={{0,2},{1,3},{2,0},{3,1},{4,6},{5,7},{6,4},{7,5},{8,10},{9,11},{10,... | collective-permute-start | bytes 786440 | tf_op jit(solution)/shard_map/ppermute | solution.py:551
  5.8 0.4 collective-permute-start
  6.1 0.3 collective-permute-start.1
  6.4 0.7 copy-done.7
  7.1 1.5 %shard_map.195.bias = f32[4,128,128]{2,1,0:T(8,128)S(1)} custom-call(s32[5]{0:T(128)S(1)} %stack.23.meta, s32[2,4]{1,0:T(2,128)S(1)} %bitcast.13, f32[4,4,32,128]{3,2,1,0:T(8,128)} %bias_hbm.1, f32[512,128]{1,0:T(8,128)S(1)} %get-tuple-element.48._.stream), custom_call_target="tpu_custom_call" | custom-call | tf_op jit(solution)/shard_map/pallas_call | solution.py:59
  8.6 6.3 %collective-permute-done.1.second = bf16[192,256]{1,0:T(8,128)(2,1)S(1)} collective-permute-done((bf16[192,256]{1,0:T(8,128)(2,1)S(1)}, bf16[192,256]{1,0:T(8,128)(2,1)S(1)}, u32[]{:S(2)}, u32[]{:S(2)}) %collective-permute-start.1) | collective-permute-done | bytes 98336 | tf_op jit(solution)/shard_map/ppermute | solution.py:545
  14.9 3.6 %shard_map.196 = (f32[512,128]{1,0:T(8,128)S(1)}, bf16[512,128]{1,0:T(8,128)(2,1)S(1)}, bf16[512,256]{1,0:T(8,128)(2,1)S(1)}, bf16[192,256]{1,0:T(8,128)(2,1)S(1)}, bf16[192,256]{1,0:T(8,128)(2,1)S(1)}) custom-call(s32[5]{0:T(128)S(1)} %stack.23.meta, bf16[512,128]{1,0:T(8,128)(2,1)S(1)} %get-tuple-element.44.q, bf16[512,256]{1,0:T(8,128)(2,1)S(1)} %get-tuple-element.45.kv, ...), custom_call_target="tpu_custom_call" | custom-call | tf_op jit(solution)/shard_map/pallas_call | solution.py:59
  18.6 1.9 %collective-permute-start.3 = (bf16[192,256]{1,0:T(8,128)(2,1)S(1)}, bf16[192,256]{1,0:T(8,128)(2,1)S(1)}, u32[]{:S(2)}, u32[]{:S(2)}) collective-permute-start(bf16[192,256]{1,0:T(8,128)(2,1)S(1)} %get-tuple-element.52), channel_id=1, source_target_pairs={{1,2},{3,4},{5,6},{7,8},{9,10},{11,12},{13,14},{2,1},{4,3},{6,5},{... | collective-permute-start | bytes 294920 | tf_op jit(solution)/shard_map/ppermute | solution.py:545
  20.5 3.4 %collective-permute-done.3.second = bf16[192,256]{1,0:T(8,128)(2,1)S(1)} collective-permute-done((bf16[192,256]{1,0:T(8,128)(2,1)S(1)}, bf16[192,256]{1,0:T(8,128)(2,1)S(1)}, u32[]{:S(2)}, u32[]{:S(2)}) %collective-permute-start.3) | collective-permute-done | bytes 98336 | tf_op jit(solution)/shard_map/ppermute | solution.py:545
  23.8 4.7 %shard_map.197 = (f32[512,128]{1,0:T(8,128)S(1)}, f32[80,896]{1,0:T(8,128)S(1)}, bf16[64,896]{1,0:T(8,128)(2,1)S(1)}, bf16[64,896]{1,0:T(8,128)(2,1)S(1)}, f32[2...) custom-call(s32[5]{0:T(128)S(1)} %stack.23.meta, bf16[512,128]{1,0:T(8,128)(2,1)S(1)} %get-tuple-element.49.q, ...), custom_call_target="tpu_custom_call" | custom-call | tf_op jit(solution)/shard_map/pallas_call | solution.py:59
  28.6 0.4 collective-permute-start.11
  28.9 0.2 collective-permute-start.6
  29.1 1.6 %collective-permute-start.7 = (bf16[64,896]{1,0:T(8,128)(2,1)S(1)}, bf16[64,896]{1,0:T(8,128)(2,1)S(1)}, u32[]{:S(2)}, u32[]{:S(2)}) collective-permute-start(bf16[64,896]{1,0:T(8,128)(2,1)S(1)} %get-tuple-element.58), channel_id=1, source_target_pairs={{1,2},{3,4},{5,6},{7,8},{9,10},{11,12},{13,14},{2,1},{4,3},{6,5},{... | collective-permute-start | bytes 344072 | tf_op jit(solution)/shard_map/ppermute | solution.py:545
  30.7 3.9 %collective-permute-done.7.second = bf16[64,896]{1,0:T(8,128)(2,1)S(1)} collective-permute-done((bf16[64,896]{1,0:T(8,128)(2,1)S(1)}, bf16[64,896]{1,0:T(8,128)(2,1)S(1)}, u32[]{:S(2)}, u32[]{:S(2)}) %collective-permute-start.7) | collective-permute-done | bytes 114720 | tf_op jit(solution)/shard_map/ppermute | solution.py:545
  34.6 0.8 %shard_map.198 = (f32[64,768]{1,0:T(8,128)S(1)}, bf16[16,768]{1,0:T(8,128)(2,1)S(1)}, bf16[16,768]{1,0:T(8,128)(2,1)S(1)}, bf16[16,768]{1,0:T(8,128)(2,1)S(1)}, bf16[16,768]{1,0:T(8,128)(2,1)S(1)}) custom-call(s32[5]{0:T(128)S(1)} %stack.23.meta, f32[80,896]{1,0:T(8,128)S(1)} %get-tuple-element.56.mid, bf16[64,896]{1,0:T(8,128)(2,1)S(1)} %collective-permute-done.6.first, ...), custom_call_target="tpu_custom_call" | custom-call | tf_op jit(solution)/shard_map/pallas_call | solution.py:59
  35.4 0.2 collective-permute-start.8
  35.6 1.3 %collective-permute-start.9 = (bf16[16,768]{1,0:T(8,128)(2,1)S(1)}, bf16[16,768]{1,0:T(8,128)(2,1)S(1)}, u32[]{:S(2)}, u32[]{:S(2)}) collective-permute-start(bf16[16,768]{1,0:T(8,128)(2,1)S(1)} %get-tuple-element.62), channel_id=1, source_target_pairs={{0,2},{1,3},{2,0},{3,1},{4,6},{5,7},{6,4},{7,5},{8,10},{9,11},{10,... | collective-permute-start | bytes 73736 | tf_op jit(solution)/shard_map/ppermute | solution.py:551
  36.8 0.8 collective-permute-start.10
  37.6 0.6 collective-permute-done.9.rest_2_
  38.2 2.4 %collective-permute-done.10.rest_3_ = bf16[16,768]{1,0:T(8,128)(2,1)S(1)} collective-permute-done((bf16[16,768]{1,0:T(8,128)(2,1)S(1)}, bf16[16,768]{1,0:T(8,128)(2,1)S(1)}, u32[]{:S(2)}, u32[]{:S(2)}) %collective-permute-start.10) | collective-permute-done | bytes 24608 | tf_op jit(solution)/shard_map/ppermute | solution.py:551
  40.6 0.6 shard_map.199.normal
  41.2 1.4 %collective-permute-start.12 = (bf16[64,768]{1,0:T(8,128)(2,1)S(1)}, bf16[64,768]{1,0:T(8,128)(2,1)S(1)}, u32[]{:S(2)}, u32[]{:S(2)}) collective-permute-start(bf16[64,768]{1,0:T(8,128)(2,1)S(1)} %shard_map.199.normal), channel_id=1, source_target_pairs={{0,4},{4,8},{8,12},{12,0},{1,5},{5,9},{9,13},{13,1},{2,6},{6,10},{... | collective-permute-start | bytes 294920 | tf_op jit(solution)/shard_map/ppermute | solution.py:667
  42.5 1.0 %collective-permute-start.13 = (bf16[64,768]{1,0:T(8,128)(2,1)S(1)}, bf16[64,768]{1,0:T(8,128)(2,1)S(1)}, u32[]{:S(2)}, u32[]{:S(2)}) collective-permute-start(bf16[64,768]{1,0:T(8,128)(2,1)S(1)} %shard_map.199.normal), channel_id=1, source_target_pairs={{0,8},{4,12},{8,0},{12,4},{1,9},{5,13},{9,1},{13,5},{2,10},{6,14},... | collective-permute-start | bytes 294920 | tf_op jit(solution)/shard_map/ppermute | solution.py:667
  43.5 0.3 collective-permute-start.14
  43.8 1.2 %collective-permute-start.20 = (f32[200,128]{1,0:T(8,128)S(1)}, f32[200,128]{1,0:T(8,128)S(1)}, u32[]{:S(2)}, u32[]{:S(2)}) collective-permute-start(f32[200,128]{1,0:T(8,128)S(1)} %get-tuple-element.73), channel_id=1, source_target_pairs={{0,1},{1,0},{2,3},{3,2},{4,5},{5,4},{6,7},{7,6},{8,9},{9,8},{10,11... | collective-permute-start | bytes 307208 | tf_op jit(solution)/shard_map/ppermute | solution.py:546
  45.0 1.3 %collective-permute-start.21 = (f32[200,128]{1,0:T(8,128)S(1)}, f32[200,128]{1,0:T(8,128)S(1)}, u32[]{:S(2)}, u32[]{:S(2)}) collective-permute-start(f32[200,128]{1,0:T(8,128)S(1)} %get-tuple-element.74), channel_id=1, source_target_pairs={{1,2},{3,4},{5,6},{7,8},{9,10},{11,12},{13,14},{2,1},{4,3},{6,5},{... | collective-permute-start | bytes 307208 | tf_op jit(solution)/shard_map/ppermute | solution.py:545
  46.3 1.5 %shard_map.200 = (bf16[64,768]{1,0:T(8,128)(2,1)S(1)}, bf16[64,1536]{1,0:T(8,128)(2,1)S(1)}, f32[16,64,256]{2,1,0:T(8,128)S(1)}) custom-call(s32[5]{0:T(128)S(1)} %stack.23.meta, bf16[64,768]{1,0:T(8,128)(2,1)S(1)} %shard_map.199.normal, f32[16,16,256]{2,1,0:T(8,128)} %rest_0_.3, f32[16,16,256]{2,1,0:T(8,128)S(1)} %collective-permute-done.4.rest_1_, ...), custom_call_target="tpu_custom_call" | custom-call | tf_op jit(solution)/shard_map/pallas_call | solution.py:59
  47.9 2.7 %collective-permute-done.13.rest_1_ = bf16[64,768]{1,0:T(8,128)(2,1)S(1)} collective-permute-done((bf16[64,768]{1,0:T(8,128)(2,1)S(1)}, bf16[64,768]{1,0:T(8,128)(2,1)S(1)}, u32[]{:S(2)}, u32[]{:S(2)}) %collective-permute-start.13) | collective-permute-done | bytes 98336 | tf_op jit(solution)/shard_map/ppermute | solution.py:667
  50.6 2.5 %collective-permute-done.14.rest_2_ = bf16[64,768]{1,0:T(8,128)(2,1)S(1)} collective-permute-done((bf16[64,768]{1,0:T(8,128)(2,1)S(1)}, bf16[64,768]{1,0:T(8,128)(2,1)S(1)}, u32[]{:S(2)}, u32[]{:S(2)}) %collective-permute-start.14) | collective-permute-done | bytes 98336 | tf_op jit(solution)/shard_map/ppermute | solution.py:667
  53.1 3.7 %shard_map.201 = (bf16[16,768]{1,0:T(8,128)(2,1)S(1)}, bf16[16,768]{1,0:T(8,128)(2,1)S(1)}, bf16[16,768]{1,0:T(8,128)(2,1)S(1)}, bf16[16,768]{1,0:T(8,128)(2,1)S(1)}) custom-call(s32[5]{0:T(128)S(1)} %stack.23.meta, bf16[64,768]{1,0:T(8,128)(2,1)S(1)} %get-tuple-element.65.q_own, bf16[64,1536]{1,0:T(8,128)(2,1)S(1)} %get-tuple-element.66.kv_own, ...), custom_call_target="tpu_custom_call" | custom-call | tf_op jit(solution)/shard_map/pallas_call | solution.py:59
  56.9 0.6 collective-permute-start.15
  57.5 0.2 collective-permute-start.16
  57.6 1.6 %collective-permute-start.17 = (bf16[16,768]{1,0:T(8,128)(2,1)S(1)}, bf16[16,768]{1,0:T(8,128)(2,1)S(1)}, u32[]{:S(2)}, u32[]{:S(2)}) collective-permute-start(bf16[16,768]{1,0:T(8,128)(2,1)S(1)} %get-tuple-element.71), channel_id=1, source_target_pairs={{0,3},{1,2},{2,1},{3,0},{4,7},{5,6},{6,5},{7,4},{8,11},{9,10},{10,... | collective-permute-start | bytes 73736 | tf_op jit(solution)/shard_map/ppermute | solution.py:551
  59.2 1.0 %collective-permute-done.16.rest_2_ = bf16[16,768]{1,0:T(8,128)(2,1)S(1)} collective-permute-done((bf16[16,768]{1,0:T(8,128)(2,1)S(1)}, bf16[16,768]{1,0:T(8,128)(2,1)S(1)}, u32[]{:S(2)}, u32[]{:S(2)}) %collective-permute-start.16) | collective-permute-done | bytes 24608 | tf_op jit(solution)/shard_map/ppermute | solution.py:551
  60.1 1.0 %collective-permute-done.17.rest_3_ = bf16[16,768]{1,0:T(8,128)(2,1)S(1)} collective-permute-done((bf16[16,768]{1,0:T(8,128)(2,1)S(1)}, bf16[16,768]{1,0:T(8,128)(2,1)S(1)}, u32[]{:S(2)}, u32[]{:S(2)}) %collective-permute-start.17) | collective-permute-done | bytes 24608 | tf_op jit(solution)/shard_map/ppermute | solution.py:551
  61.1 1.7 %shard_map.202 = (f32[4,16,768]{2,1,0:T(8,128)}, bf16[64,128]{1,0:T(8,128)(2,1)S(1)}) custom-call(s32[5]{0:T(128)S(1)} %stack.23.meta, f32[64,768]{1,0:T(8,128)S(1)} %get-tuple-element.59.state, bf16[16,768]{1,0:T(8,128)(2,1)S(1)} %get-tuple-element.68.rest_0_, bf16[16,768]{1,0:T(8,128)(2,1)S(1)} %collective-permute-done.15.rest_1_, ...), custom_call_target="tpu_custom_call" | custom-call | tf_op jit(solution)/shard_map/pallas_call | solution.py:59
  62.9 0.4 collective-permute-start.18
  63.3 1.1 %collective-permute-start.19 = (bf16[64,128]{1,0:T(8,128)(2,1)S(1)}, bf16[64,128]{1,0:T(8,128)(2,1)S(1)}, u32[]{:S(2)}, u32[]{:S(2)}) collective-permute-start(bf16[64,128]{1,0:T(8,128)(2,1)S(1)} %get-tuple-element.72.back), channel_id=1, source_target_pairs={{1,2},{3,4},{5,6},{7,8},{9,10},{11,12},{13,14},{2,1},{4,3},{6,5},{... | collective-permute-start | bytes 49160 | tf_op jit(solution)/shard_map/ppermute | solution.py:545
  64.3 2.4 %collective-permute-done.19.second = bf16[64,128]{1,0:T(8,128)(2,1)S(1)} collective-permute-done((bf16[64,128]{1,0:T(8,128)(2,1)S(1)}, bf16[64,128]{1,0:T(8,128)(2,1)S(1)}, u32[]{:S(2)}, u32[]{:S(2)}) %collective-permute-start.19) | collective-permute-done | bytes 16416 | tf_op jit(solution)/shard_map/ppermute | solution.py:545
  66.7 1.6 %shard_map.203 = (f32[512,128]{1,0:T(8,128)S(1)}, bf16[512,128]{1,0:T(8,128)(2,1)S(1)}, bf16[512,256]{1,0:T(8,128)(2,1)S(1)}, bf16[192,256]{1,0:T(8,128)(2,1)S(1)}, bf16[192,256]{1,0:T(8,128)(2,1)S(1)}) custom-call(s32[5]{0:T(128)S(1)} %stack.23.meta, f32[512,128]{1,0:T(8,128)S(1)} %get-tuple-element.55.stream, s32[1,128]{1,0:T(1,128)S(1)} %bitcast.12, ...), custom_call_target="tpu_custom_call" | custom-call | tf_op jit(solution)/shard_map/pallas_call | solution.py:59
  68.3 3.6 %shard_map.204 = (f32[512,128]{1,0:T(8,128)S(1)}, bf16[512,128]{1,0:T(8,128)(2,1)S(1)}, bf16[512,256]{1,0:T(8,128)(2,1)S(1)}, bf16[192,256]{1,0:T(8,128)(2,1)S(1)}, bf16[192,256]{1,0:T(8,128)(2,1)S(1)}) custom-call(s32[5]{0:T(128)S(1)} %stack.23.meta, bf16[512,128]{1,0:T(8,128)(2,1)S(1)} %get-tuple-element.75.q, bf16[512,256]{1,0:T(8,128)(2,1)S(1)} %get-tuple-element.76.kv, ...), custom_call_target="tpu_custom_call" | custom-call | tf_op jit(solution)/shard_map/pallas_call | solution.py:59
  71.9 0.8 collective-permute-start.22
  72.7 1.3 %collective-permute-start.23 = (bf16[192,256]{1,0:T(8,128)(2,1)S(1)}, bf16[192,256]{1,0:T(8,128)(2,1)S(1)}, u32[]{:S(2)}, u32[]{:S(2)}) collective-permute-start(bf16[192,256]{1,0:T(8,128)(2,1)S(1)} %get-tuple-element.83), channel_id=1, source_target_pairs={{1,2},{3,4},{5,6},{7,8},{9,10},{11,12},{13,14},{2,1},{4,3},{6,5},{... | collective-permute-start | bytes 294920 | tf_op jit(solution)/shard_map/ppermute | solution.py:545
  74.1 3.8 %collective-permute-done.23.second = bf16[192,256]{1,0:T(8,128)(2,1)S(1)} collective-permute-done((bf16[192,256]{1,0:T(8,128)(2,1)S(1)}, bf16[192,256]{1,0:T(8,128)(2,1)S(1)}, u32[]{:S(2)}, u32[]{:S(2)}) %collective-permute-start.23) | collective-permute-done | bytes 98336 | tf_op jit(solution)/shard_map/ppermute | solution.py:545
  77.8 4.4 %shard_map.205 = f32[3,4,128]{2,1,0:T(4,128)} custom-call(s32[5]{0:T(128)S(1)} %stack.23.meta, bf16[512,128]{1,0:T(8,128)(2,1)S(1)} %get-tuple-element.80.q, bf16[512,256]{1,0:T(8,128)(2,1)S(1)} %get-tuple-element.81.kv, bf16[192,256]{1,0:T(8,128)(2,1)S(1)} %collective-permute-done.22.first, bf16[192,256]{1,0:T(8,128)(2,1)S(1)} %collective-permute-done.23.second, ...), custom_call_target="tpu_custom_call" | custom-call | tf_op jit(solution)/shard_map/pallas_call | solution.py:59
  (31 shorter events, 0.2 us)
Async XLA Ops:
  0.7 45.5 %copy-start = (bf16[768,2304]{1,0:T(8,128)(2,1)S(1)}, bf16[768,2304]{1,0:T(8,128)(2,1)}, u32[]{:S(2)}) copy-start(bf16[768,2304]{1,0:T(8,128)(2,1)} %rest_3_.1) | copy-start | bytes 10616836
  3.8 20.0 %collective-permute-start.4 = (f32[16,16,256]{2,1,0:T(8,128)}, f32[16,16,256]{2,1,0:T(8,128)S(1)}, u32[]{:S(2)}, u32[]{:S(2)}) collective-permute-start(f32[16,16,256]{2,1,0:T(8,128)} %rest_0_.3), channel_id=1, source_target_pairs={{0,1},{1,0},{2,3},{3,2},{4,5},{5,4},{6,7},{7,6},{8,9},{9,8},{10,11... | collective-permute-start | bytes 786440 | tf_op jit(solution)/shard_map/ppermute | solution.py:551
  4.5 19.3 %collective-permute-start.5 = (f32[16,16,256]{2,1,0:T(8,128)}, f32[16,16,256]{2,1,0:T(8,128)S(1)}, u32[]{:S(2)}, u32[]{:S(2)}) collective-permute-start(f32[16,16,256]{2,1,0:T(8,128)} %rest_0_.3), channel_id=1, source_target_pairs={{0,2},{1,3},{2,0},{3,1},{4,6},{5,7},{6,4},{7,5},{8,10},{9,11},{10,... | collective-permute-start | bytes 786440 | tf_op jit(solution)/shard_map/ppermute | solution.py:551
  5.8 2.8 %collective-permute-start = (bf16[192,256]{1,0:T(8,128)(2,1)S(1)}, bf16[192,256]{1,0:T(8,128)(2,1)S(1)}, u32[]{:S(2)}, u32[]{:S(2)}) collective-permute-start(bf16[192,256]{1,0:T(8,128)(2,1)S(1)} %get-tuple-element.46), channel_id=1, source_target_pairs={{0,1},{1,0},{2,3},{3,2},{4,5},{5,4},{6,7},{7,6},{8,9},{9,8},{10,11... | collective-permute-start | bytes 294920 | tf_op jit(solution)/shard_map/ppermute | solution.py:546
  6.1 8.7 %collective-permute-start.1 = (bf16[192,256]{1,0:T(8,128)(2,1)S(1)}, bf16[192,256]{1,0:T(8,128)(2,1)S(1)}, u32[]{:S(2)}, u32[]{:S(2)}) collective-permute-start(bf16[192,256]{1,0:T(8,128)(2,1)S(1)} %get-tuple-element.47), channel_id=1, source_target_pairs={{1,2},{3,4},{5,6},{7,8},{9,10},{11,12},{13,14},{2,1},{4,3},{6,5},{... | collective-permute-start | bytes 294920 | tf_op jit(solution)/shard_map/ppermute | solution.py:545
  6.4 0.7 copy-start.7
  18.5 2.0 %collective-permute-start.2 = (bf16[192,256]{1,0:T(8,128)(2,1)S(1)}, bf16[192,256]{1,0:T(8,128)(2,1)S(1)}, u32[]{:S(2)}, u32[]{:S(2)}) collective-permute-start(bf16[192,256]{1,0:T(8,128)(2,1)S(1)} %get-tuple-element.51), channel_id=1, source_target_pairs={{0,1},{1,0},{2,3},{3,2},{4,5},{5,4},{6,7},{7,6},{8,9},{9,8},{10,11... | collective-permute-start | bytes 294920 | tf_op jit(solution)/shard_map/ppermute | solution.py:546
  18.6 5.2 %collective-permute-start.3 = (bf16[192,256]{1,0:T(8,128)(2,1)S(1)}, bf16[192,256]{1,0:T(8,128)(2,1)S(1)}, u32[]{:S(2)}, u32[]{:S(2)}) collective-permute-start(bf16[192,256]{1,0:T(8,128)(2,1)S(1)} %get-tuple-element.52), channel_id=1, source_target_pairs={{1,2},{3,4},{5,6},{7,8},{9,10},{11,12},{13,14},{2,1},{4,3},{6,5},{... | collective-permute-start | bytes 294920 | tf_op jit(solution)/shard_map/ppermute | solution.py:545
  28.6 16.4 %collective-permute-start.11 = (f32[16,16,256]{2,1,0:T(8,128)S(1)}, f32[16,16,256]{2,1,0:T(8,128)S(1)}, u32[]{:S(2)}, u32[]{:S(2)}) collective-permute-start(f32[16,16,256]{2,1,0:T(8,128)S(1)} %collective-permute-done.5.rest_2_), channel_id=1, source_target_pairs={{0,1},{1,0},{2,3},{3,2},{4,5},{5,4},{6,7},{7,6},{8,9},{9,8},{10,11... | collective-permute-start | bytes 786440 | tf_op jit(solution)/shard_map/ppermute | solution.py:551
  28.9 1.8 %collective-permute-start.6 = (bf16[64,896]{1,0:T(8,128)(2,1)S(1)}, bf16[64,896]{1,0:T(8,128)(2,1)S(1)}, u32[]{:S(2)}, u32[]{:S(2)}) collective-permute-start(bf16[64,896]{1,0:T(8,128)(2,1)S(1)} %get-tuple-element.57), channel_id=1, source_target_pairs={{0,1},{1,0},{2,3},{3,2},{4,5},{5,4},{6,7},{7,6},{8,9},{9,8},{10,11... | collective-permute-start | bytes 344072 | tf_op jit(solution)/shard_map/ppermute | solution.py:546
  29.1 5.4 %collective-permute-start.7 = (bf16[64,896]{1,0:T(8,128)(2,1)S(1)}, bf16[64,896]{1,0:T(8,128)(2,1)S(1)}, u32[]{:S(2)}, u32[]{:S(2)}) collective-permute-start(bf16[64,896]{1,0:T(8,128)(2,1)S(1)} %get-tuple-element.58), channel_id=1, source_target_pairs={{1,2},{3,4},{5,6},{7,8},{9,10},{11,12},{13,14},{2,1},{4,3},{6,5},{... | collective-permute-start | bytes 344072 | tf_op jit(solution)/shard_map/ppermute | solution.py:545
  35.4 2.2 %collective-permute-start.8 = (bf16[16,768]{1,0:T(8,128)(2,1)S(1)}, bf16[16,768]{1,0:T(8,128)(2,1)S(1)}, u32[]{:S(2)}, u32[]{:S(2)}) collective-permute-start(bf16[16,768]{1,0:T(8,128)(2,1)S(1)} %get-tuple-element.61), channel_id=1, source_target_pairs={{0,1},{1,0},{2,3},{3,2},{4,5},{5,4},{6,7},{7,6},{8,9},{9,8},{10,11... | collective-permute-start | bytes 73736 | tf_op jit(solution)/shard_map/ppermute | solution.py:551
  35.6 2.7 %collective-permute-start.9 = (bf16[16,768]{1,0:T(8,128)(2,1)S(1)}, bf16[16,768]{1,0:T(8,128)(2,1)S(1)}, u32[]{:S(2)}, u32[]{:S(2)}) collective-permute-start(bf16[16,768]{1,0:T(8,128)(2,1)S(1)} %get-tuple-element.62), channel_id=1, source_target_pairs={{0,2},{1,3},{2,0},{3,1},{4,6},{5,7},{6,4},{7,5},{8,10},{9,11},{10,... | collective-permute-start | bytes 73736 | tf_op jit(solution)/shard_map/ppermute | solution.py:551
  36.8 3.8 %collective-permute-start.10 = (bf16[16,768]{1,0:T(8,128)(2,1)S(1)}, bf16[16,768]{1,0:T(8,128)(2,1)S(1)}, u32[]{:S(2)}, u32[]{:S(2)}) collective-permute-start(bf16[16,768]{1,0:T(8,128)(2,1)S(1)} %get-tuple-element.63), channel_id=1, source_target_pairs={{0,3},{1,2},{2,1},{3,0},{4,7},{5,6},{6,5},{7,4},{8,11},{9,10},{10,... | collective-permute-start | bytes 73736 | tf_op jit(solution)/shard_map/ppermute | solution.py:551
  41.2 6.7 %collective-permute-start.12 = (bf16[64,768]{1,0:T(8,128)(2,1)S(1)}, bf16[64,768]{1,0:T(8,128)(2,1)S(1)}, u32[]{:S(2)}, u32[]{:S(2)}) collective-permute-start(bf16[64,768]{1,0:T(8,128)(2,1)S(1)} %shard_map.199.normal), channel_id=1, source_target_pairs={{0,4},{4,8},{8,12},{12,0},{1,5},{5,9},{9,13},{13,1},{2,6},{6,10},{... | collective-permute-start | bytes 294920 | tf_op jit(solution)/shard_map/ppermute | solution.py:667
  42.5 8.1 %collective-permute-start.13 = (bf16[64,768]{1,0:T(8,128)(2,1)S(1)}, bf16[64,768]{1,0:T(8,128)(2,1)S(1)}, u32[]{:S(2)}, u32[]{:S(2)}) collective-permute-start(bf16[64,768]{1,0:T(8,128)(2,1)S(1)} %shard_map.199.normal), channel_id=1, source_target_pairs={{0,8},{4,12},{8,0},{12,4},{1,9},{5,13},{9,1},{13,5},{2,10},{6,14},... | collective-permute-start | bytes 294920 | tf_op jit(solution)/shard_map/ppermute | solution.py:667
  43.5 9.6 %collective-permute-start.14 = (bf16[64,768]{1,0:T(8,128)(2,1)S(1)}, bf16[64,768]{1,0:T(8,128)(2,1)S(1)}, u32[]{:S(2)}, u32[]{:S(2)}) collective-permute-start(bf16[64,768]{1,0:T(8,128)(2,1)S(1)} %shard_map.199.normal), channel_id=1, source_target_pairs={{0,12},{4,0},{8,4},{12,8},{1,13},{5,1},{9,5},{13,9},{2,14},{6,2},{... | collective-permute-start | bytes 294920 | tf_op jit(solution)/shard_map/ppermute | solution.py:667
  43.8 20.5 %collective-permute-start.20 = (f32[200,128]{1,0:T(8,128)S(1)}, f32[200,128]{1,0:T(8,128)S(1)}, u32[]{:S(2)}, u32[]{:S(2)}) collective-permute-start(f32[200,128]{1,0:T(8,128)S(1)} %get-tuple-element.73), channel_id=1, source_target_pairs={{0,1},{1,0},{2,3},{3,2},{4,5},{5,4},{6,7},{7,6},{8,9},{9,8},{10,11... | collective-permute-start | bytes 307208 | tf_op jit(solution)/shard_map/ppermute | solution.py:546
  45.0 19.4 %collective-permute-start.21 = (f32[200,128]{1,0:T(8,128)S(1)}, f32[200,128]{1,0:T(8,128)S(1)}, u32[]{:S(2)}, u32[]{:S(2)}) collective-permute-start(f32[200,128]{1,0:T(8,128)S(1)} %get-tuple-element.74), channel_id=1, source_target_pairs={{1,2},{3,4},{5,6},{7,8},{9,10},{11,12},{13,14},{2,1},{4,3},{6,5},{... | collective-permute-start | bytes 307208 | tf_op jit(solution)/shard_map/ppermute | solution.py:545
  47.8 13.3 %copy-start.2 = (bf16[768,768]{1,0:T(8,128)(2,1)S(1)}, bf16[768,768]{1,0:T(8,128)(2,1)}, u32[]{:S(2)}) copy-start(bf16[768,768]{1,0:T(8,128)(2,1)} %rest_4_.3) | copy-start | bytes 3538948
  47.8 13.3 %copy-start.3 = (bf16[768,128]{1,0:T(8,128)(2,1)S(1)}, bf16[768,128]{1,0:T(8,128)(2,1)}, u32[]{:S(2)}) copy-start(bf16[768,128]{1,0:T(8,128)(2,1)} %rest_5_.1) | copy-start | bytes 589828
  47.8 18.9 %copy-start.1 = (bf16[4,128,384]{2,1,0:T(8,128)(2,1)S(1)}, bf16[4,128,384]{2,1,0:T(8,128)(2,1)}, u32[]{:S(2)}) copy-start(bf16[4,128,384]{2,1,0:T(8,128)(2,1)} %w_qkv.5) | copy-start | bytes 1179652
  47.8 18.9 %copy-start.6 = (s32[128]{0:T(128)S(1)}, s32[128]{0:T(128)}, u32[]{:S(2)}) copy-start(s32[128]{0:T(128)} %param.23) | copy-start | bytes 1540
  56.9 21.0 %copy-start.4 = (f32[4,3,128]{2,0,1:T(4,128)S(1)}, f32[4,3,128]{2,0,1:T(4,128)}, u32[]{:S(2)}) copy-start(f32[4,3,128]{2,0,1:T(4,128)} %param.20) | copy-start | bytes 18436
  56.9 20.9 %copy-start.5 = (f32[3,128]{1,0:T(4,128)S(1)}, f32[3,128]{1,0:T(4,128)}, u32[]{:S(2)}) copy-start(f32[3,128]{1,0:T(4,128)} %x_true.1) | copy-start | bytes 4612
  56.9 20.9 %copy-start.8 = (bf16[3,128]{1,0:T(4,128)(2,1)S(1)}, bf16[3,128]{1,0:T(4,128)(2,1)}, u32[]{:S(2)}) copy-start(bf16[3,128]{1,0:T(4,128)(2,1)} %w_final.1) | copy-start | bytes 2308
  56.9 2.3 %collective-permute-start.15 = (bf16[16,768]{1,0:T(8,128)(2,1)S(1)}, bf16[16,768]{1,0:T(8,128)(2,1)S(1)}, u32[]{:S(2)}, u32[]{:S(2)}) collective-permute-start(bf16[16,768]{1,0:T(8,128)(2,1)S(1)} %get-tuple-element.69), channel_id=1, source_target_pairs={{0,1},{1,0},{2,3},{3,2},{4,5},{5,4},{6,7},{7,6},{8,9},{9,8},{10,11... | collective-permute-start | bytes 73736 | tf_op jit(solution)/shard_map/ppermute | solution.py:551
  57.5 2.7 %collective-permute-start.16 = (bf16[16,768]{1,0:T(8,128)(2,1)S(1)}, bf16[16,768]{1,0:T(8,128)(2,1)S(1)}, u32[]{:S(2)}, u32[]{:S(2)}) collective-permute-start(bf16[16,768]{1,0:T(8,128)(2,1)S(1)} %get-tuple-element.70), channel_id=1, source_target_pairs={{0,2},{1,3},{2,0},{3,1},{4,6},{5,7},{6,4},{7,5},{8,10},{9,11},{10,... | collective-permute-start | bytes 73736 | tf_op jit(solution)/shard_map/ppermute | solution.py:551
  57.6 3.5 %collective-permute-start.17 = (bf16[16,768]{1,0:T(8,128)(2,1)S(1)}, bf16[16,768]{1,0:T(8,128)(2,1)S(1)}, u32[]{:S(2)}, u32[]{:S(2)}) collective-permute-start(bf16[16,768]{1,0:T(8,128)(2,1)S(1)} %get-tuple-element.71), channel_id=1, source_target_pairs={{0,3},{1,2},{2,1},{3,0},{4,7},{5,6},{6,5},{7,4},{8,11},{9,10},{10,... | collective-permute-start | bytes 73736 | tf_op jit(solution)/shard_map/ppermute | solution.py:551
  62.9 1.5 %collective-permute-start.18 = (bf16[64,128]{1,0:T(8,128)(2,1)S(1)}, bf16[64,128]{1,0:T(8,128)(2,1)S(1)}, u32[]{:S(2)}, u32[]{:S(2)}) collective-permute-start(bf16[64,128]{1,0:T(8,128)(2,1)S(1)} %get-tuple-element.72.back), channel_id=1, source_target_pairs={{0,1},{1,0},{2,3},{3,2},{4,5},{5,4},{6,7},{7,6},{8,9},{9,8},{10,11... | collective-permute-start | bytes 49160 | tf_op jit(solution)/shard_map/ppermute | solution.py:546
  63.3 3.5 %collective-permute-start.19 = (bf16[64,128]{1,0:T(8,128)(2,1)S(1)}, bf16[64,128]{1,0:T(8,128)(2,1)S(1)}, u32[]{:S(2)}, u32[]{:S(2)}) collective-permute-start(bf16[64,128]{1,0:T(8,128)(2,1)S(1)} %get-tuple-element.72.back), channel_id=1, source_target_pairs={{1,2},{3,4},{5,6},{7,8},{9,10},{11,12},{13,14},{2,1},{4,3},{6,5},{... | collective-permute-start | bytes 49160 | tf_op jit(solution)/shard_map/ppermute | solution.py:545
  71.9 2.1 %collective-permute-start.22 = (bf16[192,256]{1,0:T(8,128)(2,1)S(1)}, bf16[192,256]{1,0:T(8,128)(2,1)S(1)}, u32[]{:S(2)}, u32[]{:S(2)}) collective-permute-start(bf16[192,256]{1,0:T(8,128)(2,1)S(1)} %get-tuple-element.82), channel_id=1, source_target_pairs={{0,1},{1,0},{2,3},{3,2},{4,5},{5,4},{6,7},{7,6},{8,9},{9,8},{10,11... | collective-permute-start | bytes 294920 | tf_op jit(solution)/shard_map/ppermute | solution.py:546
  72.7 5.1 %collective-permute-start.23 = (bf16[192,256]{1,0:T(8,128)(2,1)S(1)}, bf16[192,256]{1,0:T(8,128)(2,1)S(1)}, u32[]{:S(2)}, u32[]{:S(2)}) collective-permute-start(bf16[192,256]{1,0:T(8,128)(2,1)S(1)} %get-tuple-element.83), channel_id=1, source_target_pairs={{1,2},{3,4},{5,6},{7,8},{9,10},{11,12},{13,14},{2,1},{4,3},{6,5},{... | collective-permute-start | bytes 294920 | tf_op jit(solution)/shard_map/ppermute | solution.py:545

commit v5 on v4

--- a/solution.py
+++ b/solution.py
@@ -55,12 +55,12 @@
     return jax.ShapeDtypeStruct(shape, dtype)
 
 
-def call(kernel, out_shape, specs, args, scratch=()):
+def call(kernel, out_shape, specs, args, scratch=(), out_specs=None):
     return pl.pallas_call(
         kernel,
         out_shape=out_shape,
         in_specs=specs,
-        out_specs=jax.tree.map(lambda _: VM, out_shape),
+        out_specs=out_specs or jax.tree.map(lambda _: VM, out_shape),
         scratch_shapes=scratch,
         compiler_params=pltpu.CompilerParams(vmem_limit_bytes=48 * 1024 * 1024),
     )(
@@ -84,26 +84,15 @@
         second_ref[s * RIM : (s + 1) * RIM] = kv_ref[pl.ds(second, RIM)]
 
 
-def block_rows(b, samples, rows):
-    return [slice(s * rows + b * QUERY_BLOCK, s * rows + (b + 1) * QUERY_BLOCK) for s in range(samples)]
-
-
-def load_rows(ref, b, samples, rows):
-    return jnp.concatenate([ref[at] for at in block_rows(b, samples, rows)], 0)
-
-
-def store_rows(ref, b, samples, rows, values):
-    for s, at in enumerate(block_rows(b, samples, rows)):
-        ref[at] = values[s * QUERY_BLOCK : (s + 1) * QUERY_BLOCK]
-
-
-def run_stages(stages, count):
-    held = {}
-    for step in range(count + len(stages) - 1):
-        for place in reversed(range(len(stages))):
-            unit = step - place
-            if 0 <= unit < count:
-                held[unit] = stages[place](unit, held.get(unit))
+def unit_rows(samples, rows):
+    starts = [(b, s, s * rows + b * QUERY_BLOCK) for b in range(rows // QUERY_BLOCK) for s in range(samples)]
+    return [(b, s, slice(at, at + QUERY_BLOCK)) for b, s, at in starts]
+
+
+def in_stages(stages, units):
+    held = [None] * len(units)
+    for stage in stages:
+        held = [stage(unit, before) for unit, before in zip(units, held)]
 
 
 def fetch(pairs, sems):
@@ -118,13 +107,12 @@
 
 def run_block(
     meta, q_ref, kv_ref, first_ref, second_ref, stream_ref, bias_ref, weights, copies,
-    samples, rows, padded, out_ref, finish,
+    samples, rows, padded, mixed, out_ref,
 ):
     w_out, w_up, w_down = weights
     channels = q_ref.shape[-1]
     heads = bias_ref.shape[1] // QUERY_BLOCK
     head_size = channels // heads
-    blocks = rows // QUERY_BLOCK
     first, second = halves(meta[0], 0, RIM + rows)
     for s in range(samples):
         padded[s, RIM : RIM + rows] = kv_ref[s * rows : (s + 1) * rows]
@@ -137,59 +125,49 @@
     scale = head_size ** (-0.5) * LOG2E
     ones = jnp.ones((KEY_WINDOW, channels), BF)
 
-    def score(b, _):
-        bias = bias_ref[b]
-        scores = []
-        for s, at in enumerate(block_rows(b, samples, rows)):
-            query = q_ref[at]
-            spread = jnp.concatenate([query * bit for bit in head_bits], 0)
-            keys = padded[s, QUERY_BLOCK * b : QUERY_BLOCK * b + KEY_WINDOW, :channels]
-            scores.append(dot_nt(spread, keys) * scale + bias)
-        return scores
-
-    def soften(b, scores):
-        tops = [jnp.max(score, -1, keepdims=True) for score in scores]
-        return [jnp.exp2(score - top).astype(BF) for score, top in zip(scores, tops)]
-
-    def mix(b, expos):
-        parts = []
-        for s, expo in enumerate(expos):
-            values = padded[s, QUERY_BLOCK * b : QUERY_BLOCK * b + KEY_WINDOW, channels:]
-            out = dot(expo, jnp.concatenate([values, ones], 1))
-            merged = out[:QUERY_BLOCK] * head_masks[0]
-            for h in range(1, heads):
-                merged += out[h * QUERY_BLOCK : (h + 1) * QUERY_BLOCK] * head_masks[h]
-            parts.append(merged[:, :channels] * (1.0 / merged[:, channels:]))
-        return jnp.concatenate(parts, 0).astype(BF)
-
-    def project(b, mixed):
-        if b == 0:
-            for copy in copies:
-                copy.wait()
-        stream = load_rows(stream_ref, b, samples, rows) + dot(mixed, w_out[...])
-        return stream, normed(stream).astype(BF)
-
-    def widen(b, held):
-        stream, normal = held
-        gated = dot(normal, w_up[...])
-        half = gated.shape[-1] // 2
-        gate = gated[:, :half]
-        hidden = gate * (1.0 / (1.0 + jnp.exp(-gate))) * gated[:, half:]
-        return stream, hidden.astype(BF)
-
-    def narrow(b, held):
-        stream, hidden = held
-        stream = stream + dot(hidden, w_down[...])
-        if out_ref is not None:
-            store_rows(out_ref, b, samples, rows, stream)
-        return normed(stream).astype(BF)
-
-    run_stages([score, soften, mix, project, widen, narrow, finish], blocks)
+    units = unit_rows(samples, rows)
+
+    def window(b):
+        return slice(QUERY_BLOCK * b, QUERY_BLOCK * b + KEY_WINDOW)
+
+    def score(unit, _):
+        b, s, at = unit
+        query = q_ref[at]
+        spread = jnp.concatenate([query * bit for bit in head_bits], 0)
+        return dot_nt(spread, padded[s, window(b), :channels]) * scale + bias_ref[b]
+
+    def soften(_, scores):
+        return jnp.exp2(scores - jnp.max(scores, -1, keepdims=True)).astype(BF)
+
+    def mix(unit, expo):
+        b, s, at = unit
+        values = padded[s, window(b), channels:]
+        out = dot(expo, jnp.concatenate([values, ones], 1))
+        merged = out[:QUERY_BLOCK] * head_masks[0]
+        for h in range(1, heads):
+            merged += out[h * QUERY_BLOCK : (h + 1) * QUERY_BLOCK] * head_masks[h]
+        mixed[at] = (merged[:, :channels] * (1.0 / merged[:, channels:])).astype(BF)
+
+    in_stages([score, soften, mix], units)
+    for copy in copies:
+        copy.wait()
+    stream = stream_ref[...] + dot(mixed[...], w_out[...])
+    gated = dot(normed(stream).astype(BF), w_up[...])
+    half = gated.shape[-1] // 2
+    gate = gated[:, :half]
+    hidden = (gate * (1.0 / (1.0 + jnp.exp(-gate))) * gated[:, half:]).astype(BF)
+    stream = stream + dot(hidden, w_down[...])
+    if out_ref is not None:
+        out_ref[...] = stream
+    return normed(stream).astype(BF)
 
 
 def block_scratch(samples, rows, channels, weights):
     return (
-        [pltpu.VMEM((samples, rows + 2 * RIM, 2 * channels), BF)]
+        [
+            pltpu.VMEM((samples, rows + 2 * RIM, 2 * channels), BF),
+            pltpu.VMEM((samples * rows, channels), BF),
+        ]
         + [pltpu.VMEM(w.shape[1:], w.dtype) for w in weights]
         + [pltpu.SemaphoreType.DMA((len(weights),))]
     )
@@ -237,7 +215,7 @@
         q_ref[s * rows : (s + 1) * rows] = projected[:, :channels].astype(BF)
         kv_ref[s * rows : (s + 1) * rows] = projected[:, channels:].astype(BF)
 
-    run_stages([place, normalise, project], samples)
+    in_stages([place, normalise, project], range(samples))
     emit_rims(kv_ref, meta[0], samples, rows, first_ref, second_ref)
 
 
@@ -264,7 +242,7 @@
 
 def block_kernel(
     meta, q, kv, first, second, stream, bias, w_out, w_up, w_down, w_qkv,
-    stream_ref, q_ref, kv_ref, first_ref, second_ref, padded, out, up, down, qkv, sems,
+    stream_ref, q_ref, kv_ref, first_ref, second_ref, padded, mixed, out, up, down, qkv, sems,
     *, layer, samples, rows,
 ):
     copies = fetch(
@@ -278,15 +256,13 @@
     )
     channels = q.shape[-1]
 
-    def finish(b, normal):
-        projected = dot(normal, qkv[...]).astype(BF)
-        store_rows(q_ref, b, samples, rows, projected[:, :channels])
-        store_rows(kv_ref, b, samples, rows, projected[:, channels:])
-
-    run_block(
+    normal = run_block(
         meta, q, kv, first, second, stream, bias, (out, up, down), copies,
-        samples, rows, padded, stream_ref, finish,
-    )
+        samples, rows, padded, mixed, stream_ref,
+    )
+    projected = dot(normal, qkv[...]).astype(BF)
+    q_ref[...] = projected[:, :channels]
+    kv_ref[...] = projected[:, channels:]
     emit_rims(kv_ref, meta[0], samples, rows, first_ref, second_ref)
 
 
@@ -303,18 +279,15 @@
 ):
     single_hbm = rest[0]
     (stream_ref, mid_ref, first_ref, second_ref, first_rim, second_rim,
-     padded, out, up, down, sems, normal_all, sums, pooling, owners, single, late_sems) = rest[-17:]
+     padded, mixed, out, up, down, sems, sums, pooling, owners, single, late_sems) = rest[-17:]
     copies = fetch(
         [(w_out.at[layer], out), (w_up.at[layer], up), (w_down.at[layer], down)], sems
     )
     late = fetch([(w_pool, pooling), (atom_token, owners), (single_hbm, single)], late_sems)
 
-    def finish(b, normal):
-        store_rows(normal_all, b, samples, rows, normal)
-
-    run_block(
+    normal = run_block(
         meta, q, kv, first, second, stream, bias, (out, up, down), copies,
-        samples, rows, padded, stream_ref, finish,
+        samples, rows, padded, mixed, stream_ref,
     )
     for copy in late:
         copy.wait()
@@ -324,7 +297,7 @@
     width = w_pool.shape[-1]
 
     def pool(s, _):
-        return jnp.maximum(dot(normal_all[s * rows : (s + 1) * rows], pooling[...]), 0.0)
+        return jnp.maximum(dot(normal[s * rows : (s + 1) * rows], pooling[...]), 0.0)
 
     def gather(s, pooled):
         upper = pooled.astype(BF)
@@ -332,7 +305,7 @@
         sums[s, :, :width] = dot(selector, upper) + dot(selector, lower)
         sums[s, :, width:] = jnp.broadcast_to(counts, (3 * tokens, COUNT_LANES))
 
-    run_stages([pool, gather], samples)
+    in_stages([pool, gather], range(samples))
     ends = [owners[:, :RIM], owners[:, rows - RIM :]]
     for at, side in ((first_rim, 0), (second_rim, 1)):
         for s in range(samples):
@@ -436,7 +409,7 @@
         values = kv_all[:, width + at.start : width + at.stop]
         mixed_all[:, at] += (dot(attends[0], values) + dot(attends[1], values)) * mask
 
-    run_stages([score, soften, mix], heads)
+    in_stages([score, soften, mix], range(heads))
     for k in range(samples):
         at = pl.multiple_of(lax.bitwise_xor(mine, k) * tokens, tokens)
         send_refs[k][...] = mixed_all[pl.ds(at, tokens)].astype(BF)
@@ -498,37 +471,35 @@
             start = rows + side * RIM
             out[s * RIM : (s + 1) * RIM] = key_values[start : start + RIM]
 
-    run_stages([place, normalise, project], samples)
+    in_stages([place, normalise, project], range(samples))
 
 
 def final_kernel(
     meta, q, kv, first, second, stream, bias, w_out, w_up, w_down, w_final,
-    level_hbm, x_true, noise, denoised_ref, padded, out, up, down, sems, normal_all,
+    level_hbm, x_true, noise, state, denoised_ref, state_ref, padded, mixed, out, up, down, sems,
     level, late_sems, *, layer, samples, rows,
 ):
     copies = fetch(
         [(w_out.at[layer], out), (w_up.at[layer], up), (w_down.at[layer], down)], sems
     )
-    late = fetch([(level_hbm, level)], late_sems)
-
-    def finish(b, normal):
-        store_rows(normal_all, b, samples, rows, normal)
-
-    run_block(
+    late = fetch([(level_hbm, level), (state, state_ref)], late_sems)
+
+    normal = run_block(
         meta, q, kv, first, second, stream, bias, (out, up, down), copies,
-        samples, rows, padded, None, finish,
+        samples, rows, padded, mixed, None,
     )
     late[0].wait()
     sigma, total = sigma_of(level, samples)
     keep = SIGMA_DATA * SIGMA_DATA / total
     move = sigma * SIGMA_DATA * lax.rsqrt(total)
     updates = [
-        dot_nt(w_final[...], normal_all[s * rows : (s + 1) * rows]) for s in range(samples)
+        dot_nt(w_final[...], normal[s * rows : (s + 1) * rows]) for s in range(samples)
     ]
     for c in range(x_true.shape[0]):
         noisy = x_true[c : c + 1] + sigma * noise[c]
         update = jnp.concatenate([one[c : c + 1] for one in updates], 0)
         denoised_ref[c] = (keep * noisy + move * update) / SIGMA_DATA
+    late[1].wait()
 
 
 def swap(pair, count):
@@ -586,7 +557,6 @@
     stacks = (w_atom_out, w_atom_up, w_atom_down)
     scratch = block_scratch(samples, rows, channels, stacks)
     wide = block_scratch(samples, rows, channels, stacks + (w_atom_qkv,))
-    normals = pltpu.VMEM((whole, channels), BF)
     sizes = dict(samples=samples, rows=rows)
 
     def block(layer, q, kv, rims, stream):
@@ -638,7 +608,6 @@
         ),
         scratch
         + [
-            normals,
             pltpu.VMEM((samples, 3 * tokens, lanes), F32),
             pltpu.VMEM(w_pool.shape, BF),
             pltpu.VMEM(atom_token.shape, jnp.int32),
@@ -686,7 +655,7 @@
         [pltpu.VMEM((every, 2 * width), BF), pltpu.VMEM((held, width), F32)],
     )
     got = across(sends[1:], samples)
-    token_state, back = call(
+    after, back = call(
         functools.partial(token_out_kernel, samples=samples, tokens=tokens),
         (struct((samples, tokens, width), F32), struct((held, channels), BF)),
         [SM] + [VM] * (1 + samples + 2), (meta, state, sends[0], *got, w_token_out, w_back),
@@ -704,18 +673,20 @@
             rims = swap(rims, count)
         stream, q, kv, *rims = block(layer, q, kv, rims, stream)
     rims = swap(rims, count)
-    denoised = call(
+    denoised, token_state = call(
         functools.partial(final_kernel, layer=LAYERS - 1, **sizes),
-        struct(noise.shape, F32), [SM] + [VM] * 6 + [HB] * 3 + [VM, HB, VM, VM],
+        (struct(noise.shape, F32), struct((samples, tokens, width), F32)),
+        [SM] + [VM] * 6 + [HB] * 3 + [VM, HB, VM, VM, VM],
         (
             meta, q, kv, *rims, stream, bias, *stacks, w_final, noise_level, x_true, noise,
+            after,
         ),
         scratch
         + [
-            normals,
             pltpu.SMEM(noise_level.shape, jnp.int32),
-            pltpu.SemaphoreType.DMA((1,)),
+            pltpu.SemaphoreType.DMA((2,)),
         ],
+        (VM, HB),
     )
     return denoised.transpose(1, 0, 2), token_state
 

time: 82.7 us -> 77.6 us (0.938)
  Pallas kernels: 31 us -> 25.8 us
    pallas_call x12, Pallas kernels: 31 us -> 25.8 us  [call(): pl.pallas_call(kernel, out_shape=out_shape, in_specs=specs, out_specs=out...]
  transfers between devices with their start and end apart: 24 -> 24, of which waited for: 11 -> 11; matrix products, arithmetic and copies ran while one was open for 0% -> 0% of each run, Pallas kernels for 16% -> 15%
where the time goes in v5:
time: 77.6 us; the launch traced here: 77.3 us
  waiting for transfers between devices  29.8 us (38%)
  Pallas kernels  25.8 us (33%)
  starting transfers between devices  19.9 us (26%)
  between operations  0.99 us (1%)
  local copies, waits for them, and re-layouts  0.81 us (1%)
    pallas_call x12, Pallas kernels, call(): pl.pallas_call(kernel, out_shape=out_shape, in_specs=specs, out_specs=out...  25.8 us
    ppermute x6, waiting for transfers between devices, swap(): second = lax.ppermute(second, ('groups',) + SEQ, upper)  19.6 us
    ppermute x6, starting transfers between devices, swap(): second = lax.ppermute(second, ('groups',) + SEQ, upper)  7.43 us
    ppermute x9, starting transfers between devices, toward(): return lax.ppermute(array, 'p', [(i, i ^ k) for i in range(count)])  6.8 us
    ppermute x3, waiting for transfers between devices, shards(): gathered.append(lax.ppermute(normal, 'z', shift))  5.27 us
    ppermute x9, waiting for transfers between devices, toward(): return lax.ppermute(array, 'p', [(i, i ^ k) for i in range(count)])  4.93 us
    ppermute x6, starting transfers between devices, swap(): first = lax.ppermute(first, SEQ, lower)  3.07 us
    ppermute x3, starting transfers between devices, shards(): gathered.append(lax.ppermute(normal, 'z', shift))  2.59 us
  transfers between devices with their start and end apart: 24, of which 11 were waited for; matrix products, arithmetic and copies ran while one was open for 0% of the time, Pallas kernels for 15%

profile of v5, /device:TPU:11, one launch (start us, length us, event | category | flops | bytes accessed | tf_op | source)
XLA Modules:
  0.0 77.3 jit_solution(7005127098471409837)
XLA Ops:
  0.6 0.1 stack.23.meta
  0.7 2.7 %shard_map.194 = (f32[512,128]{1,0:T(8,128)S(1)}, bf16[512,128]{1,0:T(8,128)(2,1)S(1)}, bf16[512,256]{1,0:T(8,128)(2,1)S(1)}, bf16[192,256]{1,0:T(8,128)(2,1)S(1)}, bf16[192,256]{1,0:T(8,128)(2,1)S(1)}) custom-call(s32[5]{0:T(128)S(1)} %stack.23.meta, s32[4]{0:T(128)} %level_hbm.3, f32[3,128]{1,0:T(4,128)} %x_true.1, f32[3,4,128]{2,1,0:T(4,128)} %bitcast.9, ...), custom_call_target="tpu_custom_call" | custom-call | tf_op jit(solution)/shard_map/pallas_call | solution.py:59
  3.4 0.7 collective-permute-start.4
  4.1 1.2 %collective-permute-start.5 = (f32[16,16,256]{2,1,0:T(8,128)}, f32[16,16,256]{2,1,0:T(8,128)S(1)}, u32[]{:S(2)}, u32[]{:S(2)}) collective-permute-start(f32[16,16,256]{2,1,0:T(8,128)} %rest_0_.3), channel_id=1, source_target_pairs={{0,2},{1,3},{2,0},{3,1},{4,6},{5,7},{6,4},{7,5},{8,10},{9,11},{10,... | collective-permute-start | bytes 786440 | tf_op jit(solution)/shard_map/ppermute | solution.py:522
  5.4 0.4 collective-permute-start
  5.7 0.3 collective-permute-start.1
  6.0 0.7 copy-done.8
  6.7 1.5 %shard_map.195.bias = f32[4,128,128]{2,1,0:T(8,128)S(1)} custom-call(s32[5]{0:T(128)S(1)} %stack.23.meta, s32[2,4]{1,0:T(2,128)S(1)} %bitcast.13, f32[4,4,32,128]{3,2,1,0:T(8,128)} %bias_hbm.1, f32[512,128]{1,0:T(8,128)S(1)} %get-tuple-element.50._.stream), custom_call_target="tpu_custom_call" | custom-call | tf_op jit(solution)/shard_map/pallas_call | solution.py:59
  8.2 6.3 %collective-permute-done.1.second = bf16[192,256]{1,0:T(8,128)(2,1)S(1)} collective-permute-done((bf16[192,256]{1,0:T(8,128)(2,1)S(1)}, bf16[192,256]{1,0:T(8,128)(2,1)S(1)}, u32[]{:S(2)}, u32[]{:S(2)}) %collective-permute-start.1) | collective-permute-done | bytes 98336 | tf_op jit(solution)/shard_map/ppermute | solution.py:516
  14.5 3.4 %shard_map.196 = (f32[512,128]{1,0:T(8,128)S(1)}, bf16[512,128]{1,0:T(8,128)(2,1)S(1)}, bf16[512,256]{1,0:T(8,128)(2,1)S(1)}, bf16[192,256]{1,0:T(8,128)(2,1)S(1)}, bf16[192,256]{1,0:T(8,128)(2,1)S(1)}) custom-call(s32[5]{0:T(128)S(1)} %stack.23.meta, bf16[512,128]{1,0:T(8,128)(2,1)S(1)} %get-tuple-element.46.q, bf16[512,256]{1,0:T(8,128)(2,1)S(1)} %get-tuple-element.47.kv, ...), custom_call_target="tpu_custom_call" | custom-call | tf_op jit(solution)/shard_map/pallas_call | solution.py:59
  18.0 1.9 %collective-permute-start.3 = (bf16[192,256]{1,0:T(8,128)(2,1)S(1)}, bf16[192,256]{1,0:T(8,128)(2,1)S(1)}, u32[]{:S(2)}, u32[]{:S(2)}) collective-permute-start(bf16[192,256]{1,0:T(8,128)(2,1)S(1)} %get-tuple-element.54), channel_id=1, source_target_pairs={{1,2},{3,4},{5,6},{7,8},{9,10},{11,12},{13,14},{2,1},{4,3},{6,5},{... | collective-permute-start | bytes 294920 | tf_op jit(solution)/shard_map/ppermute | solution.py:516
  19.8 3.4 %collective-permute-done.3.second = bf16[192,256]{1,0:T(8,128)(2,1)S(1)} collective-permute-done((bf16[192,256]{1,0:T(8,128)(2,1)S(1)}, bf16[192,256]{1,0:T(8,128)(2,1)S(1)}, u32[]{:S(2)}, u32[]{:S(2)}) %collective-permute-start.3) | collective-permute-done | bytes 98336 | tf_op jit(solution)/shard_map/ppermute | solution.py:516
  23.2 3.7 %shard_map.197 = (f32[512,128]{1,0:T(8,128)S(1)}, f32[80,896]{1,0:T(8,128)S(1)}, bf16[64,896]{1,0:T(8,128)(2,1)S(1)}, bf16[64,896]{1,0:T(8,128)(2,1)S(1)}, f32[2...) custom-call(s32[5]{0:T(128)S(1)} %stack.23.meta, bf16[512,128]{1,0:T(8,128)(2,1)S(1)} %get-tuple-element.51.q, ...), custom_call_target="tpu_custom_call" | custom-call | tf_op jit(solution)/shard_map/pallas_call | solution.py:59
  26.9 0.3 collective-permute-start.11
  27.2 0.2 collective-permute-start.6
  27.4 1.6 %collective-permute-start.7 = (bf16[64,896]{1,0:T(8,128)(2,1)S(1)}, bf16[64,896]{1,0:T(8,128)(2,1)S(1)}, u32[]{:S(2)}, u32[]{:S(2)}) collective-permute-start(bf16[64,896]{1,0:T(8,128)(2,1)S(1)} %get-tuple-element.60), channel_id=1, source_target_pairs={{1,2},{3,4},{5,6},{7,8},{9,10},{11,12},{13,14},{2,1},{4,3},{6,5},{... | collective-permute-start | bytes 344072 | tf_op jit(solution)/shard_map/ppermute | solution.py:516
  29.0 3.9 %collective-permute-done.7.second = bf16[64,896]{1,0:T(8,128)(2,1)S(1)} collective-permute-done((bf16[64,896]{1,0:T(8,128)(2,1)S(1)}, bf16[64,896]{1,0:T(8,128)(2,1)S(1)}, u32[]{:S(2)}, u32[]{:S(2)}) %collective-permute-start.7) | collective-permute-done | bytes 114720 | tf_op jit(solution)/shard_map/ppermute | solution.py:516
  32.9 0.8 %shard_map.198 = (f32[64,768]{1,0:T(8,128)S(1)}, bf16[16,768]{1,0:T(8,128)(2,1)S(1)}, bf16[16,768]{1,0:T(8,128)(2,1)S(1)}, bf16[16,768]{1,0:T(8,128)(2,1)S(1)}, bf16[16,768]{1,0:T(8,128)(2,1)S(1)}) custom-call(s32[5]{0:T(128)S(1)} %stack.23.meta, f32[80,896]{1,0:T(8,128)S(1)} %get-tuple-element.58.mid, bf16[64,896]{1,0:T(8,128)(2,1)S(1)} %collective-permute-done.6.first, ...), custom_call_target="tpu_custom_call" | custom-call | tf_op jit(solution)/shard_map/pallas_call | solution.py:59
  33.7 0.1 collective-permute-start.8
  33.8 1.3 %collective-permute-start.9 = (bf16[16,768]{1,0:T(8,128)(2,1)S(1)}, bf16[16,768]{1,0:T(8,128)(2,1)S(1)}, u32[]{:S(2)}, u32[]{:S(2)}) collective-permute-start(bf16[16,768]{1,0:T(8,128)(2,1)S(1)} %get-tuple-element.64), channel_id=1, source_target_pairs={{0,2},{1,3},{2,0},{3,1},{4,6},{5,7},{6,4},{7,5},{8,10},{9,11},{10,... | collective-permute-start | bytes 73736 | tf_op jit(solution)/shard_map/ppermute | solution.py:522
  35.2 0.8 collective-permute-start.10
  35.9 0.6 collective-permute-done.9.rest_2_
  36.5 2.4 %collective-permute-done.10.rest_3_ = bf16[16,768]{1,0:T(8,128)(2,1)S(1)} collective-permute-done((bf16[16,768]{1,0:T(8,128)(2,1)S(1)}, bf16[16,768]{1,0:T(8,128)(2,1)S(1)}, u32[]{:S(2)}, u32[]{:S(2)}) %collective-permute-start.10) | collective-permute-done | bytes 24608 | tf_op jit(solution)/shard_map/ppermute | solution.py:522
  38.9 0.6 shard_map.199.normal
  39.5 1.3 %collective-permute-start.12 = (bf16[64,768]{1,0:T(8,128)(2,1)S(1)}, bf16[64,768]{1,0:T(8,128)(2,1)S(1)}, u32[]{:S(2)}, u32[]{:S(2)}) collective-permute-start(bf16[64,768]{1,0:T(8,128)(2,1)S(1)} %shard_map.199.normal), channel_id=1, source_target_pairs={{0,4},{4,8},{8,12},{12,0},{1,5},{5,9},{9,13},{13,1},{2,6},{6,10},{... | collective-permute-start | bytes 294920 | tf_op jit(solution)/shard_map/ppermute | solution.py:636
  40.8 1.0 %collective-permute-start.13 = (bf16[64,768]{1,0:T(8,128)(2,1)S(1)}, bf16[64,768]{1,0:T(8,128)(2,1)S(1)}, u32[]{:S(2)}, u32[]{:S(2)}) collective-permute-start(bf16[64,768]{1,0:T(8,128)(2,1)S(1)} %shard_map.199.normal), channel_id=1, source_target_pairs={{0,8},{4,12},{8,0},{12,4},{1,9},{5,13},{9,1},{13,5},{2,10},{6,14},... | collective-permute-start | bytes 294920 | tf_op jit(solution)/shard_map/ppermute | solution.py:636
  41.8 0.3 collective-permute-start.14
  42.1 1.2 %collective-permute-start.20 = (f32[200,128]{1,0:T(8,128)S(1)}, f32[200,128]{1,0:T(8,128)S(1)}, u32[]{:S(2)}, u32[]{:S(2)}) collective-permute-start(f32[200,128]{1,0:T(8,128)S(1)} %get-tuple-element.75), channel_id=1, source_target_pairs={{0,1},{1,0},{2,3},{3,2},{4,5},{5,4},{6,7},{7,6},{8,9},{9,8},{10,11... | collective-permute-start | bytes 307208 | tf_op jit(solution)/shard_map/ppermute | solution.py:517
  43.3 1.3 %collective-permute-start.21 = (f32[200,128]{1,0:T(8,128)S(1)}, f32[200,128]{1,0:T(8,128)S(1)}, u32[]{:S(2)}, u32[]{:S(2)}) collective-permute-start(f32[200,128]{1,0:T(8,128)S(1)} %get-tuple-element.76), channel_id=1, source_target_pairs={{1,2},{3,4},{5,6},{7,8},{9,10},{11,12},{13,14},{2,1},{4,3},{6,5},{... | collective-permute-start | bytes 307208 | tf_op jit(solution)/shard_map/ppermute | solution.py:516
  44.5 1.5 %shard_map.200 = (bf16[64,768]{1,0:T(8,128)(2,1)S(1)}, bf16[64,1536]{1,0:T(8,128)(2,1)S(1)}, f32[16,64,256]{2,1,0:T(8,128)S(1)}) custom-call(s32[5]{0:T(128)S(1)} %stack.23.meta, bf16[64,768]{1,0:T(8,128)(2,1)S(1)} %shard_map.199.normal, f32[16,16,256]{2,1,0:T(8,128)} %rest_0_.3, f32[16,16,256]{2,1,0:T(8,128)S(1)} %collective-permute-done.4.rest_1_, ...), custom_call_target="tpu_custom_call" | custom-call | tf_op jit(solution)/shard_map/pallas_call | solution.py:59
  46.1 2.7 %collective-permute-done.13.rest_1_ = bf16[64,768]{1,0:T(8,128)(2,1)S(1)} collective-permute-done((bf16[64,768]{1,0:T(8,128)(2,1)S(1)}, bf16[64,768]{1,0:T(8,128)(2,1)S(1)}, u32[]{:S(2)}, u32[]{:S(2)}) %collective-permute-start.13) | collective-permute-done | bytes 98336 | tf_op jit(solution)/shard_map/ppermute | solution.py:636
  48.9 2.5 %collective-permute-done.14.rest_2_ = bf16[64,768]{1,0:T(8,128)(2,1)S(1)} collective-permute-done((bf16[64,768]{1,0:T(8,128)(2,1)S(1)}, bf16[64,768]{1,0:T(8,128)(2,1)S(1)}, u32[]{:S(2)}, u32[]{:S(2)}) %collective-permute-start.14) | collective-permute-done | bytes 98336 | tf_op jit(solution)/shard_map/ppermute | solution.py:636
  51.4 2.4 %shard_map.201 = (bf16[16,768]{1,0:T(8,128)(2,1)S(1)}, bf16[16,768]{1,0:T(8,128)(2,1)S(1)}, bf16[16,768]{1,0:T(8,128)(2,1)S(1)}, bf16[16,768]{1,0:T(8,128)(2,1)S(1)}) custom-call(s32[5]{0:T(128)S(1)} %stack.23.meta, bf16[64,768]{1,0:T(8,128)(2,1)S(1)} %get-tuple-element.67.q_own, bf16[64,1536]{1,0:T(8,128)(2,1)S(1)} %get-tuple-element.68.kv_own, ...), custom_call_target="tpu_custom_call" | custom-call | tf_op jit(solution)/shard_map/pallas_call | solution.py:59
  53.8 0.6 collective-permute-start.15
  54.4 0.1 collective-permute-start.16
  54.5 1.6 %collective-permute-start.17 = (bf16[16,768]{1,0:T(8,128)(2,1)S(1)}, bf16[16,768]{1,0:T(8,128)(2,1)S(1)}, u32[]{:S(2)}, u32[]{:S(2)}) collective-permute-start(bf16[16,768]{1,0:T(8,128)(2,1)S(1)} %get-tuple-element.73), channel_id=1, source_target_pairs={{0,3},{1,2},{2,1},{3,0},{4,7},{5,6},{6,5},{7,4},{8,11},{9,10},{10,... | collective-permute-start | bytes 73736 | tf_op jit(solution)/shard_map/ppermute | solution.py:522
  56.1 1.0 %collective-permute-done.16.rest_2_ = bf16[16,768]{1,0:T(8,128)(2,1)S(1)} collective-permute-done((bf16[16,768]{1,0:T(8,128)(2,1)S(1)}, bf16[16,768]{1,0:T(8,128)(2,1)S(1)}, u32[]{:S(2)}, u32[]{:S(2)}) %collective-permute-start.16) | collective-permute-done | bytes 24608 | tf_op jit(solution)/shard_map/ppermute | solution.py:522
  57.0 0.9 %collective-permute-done.17.rest_3_ = bf16[16,768]{1,0:T(8,128)(2,1)S(1)} collective-permute-done((bf16[16,768]{1,0:T(8,128)(2,1)S(1)}, bf16[16,768]{1,0:T(8,128)(2,1)S(1)}, u32[]{:S(2)}, u32[]{:S(2)}) %collective-permute-start.17) | collective-permute-done | bytes 24608 | tf_op jit(solution)/shard_map/ppermute | solution.py:522
  58.0 1.2 %shard_map.202 = (f32[4,16,768]{2,1,0:T(8,128)S(1)}, bf16[64,128]{1,0:T(8,128)(2,1)S(1)}) custom-call(s32[5]{0:T(128)S(1)} %stack.23.meta, f32[64,768]{1,0:T(8,128)S(1)} %get-tuple-element.61.state, bf16[16,768]{1,0:T(8,128)(2,1)S(1)} %get-tuple-element.70.rest_0_, bf16[16,768]{1,0:T(8,128)(2,1)S(1)} %collective-permute-done.15.rest_1_, ...), custom_call_target="tpu_custom_call" | custom-call | tf_op jit(solution)/shard_map/pallas_call | solution.py:59
  59.2 0.5 collective-permute-start.18
  59.7 1.1 %collective-permute-start.19 = (bf16[64,128]{1,0:T(8,128)(2,1)S(1)}, bf16[64,128]{1,0:T(8,128)(2,1)S(1)}, u32[]{:S(2)}, u32[]{:S(2)}) collective-permute-start(bf16[64,128]{1,0:T(8,128)(2,1)S(1)} %get-tuple-element.74.back), channel_id=1, source_target_pairs={{1,2},{3,4},{5,6},{7,8},{9,10},{11,12},{13,14},{2,1},{4,3},{6,5},{... | collective-permute-start | bytes 49160 | tf_op jit(solution)/shard_map/ppermute | solution.py:516
  60.8 2.4 %collective-permute-done.19.second = bf16[64,128]{1,0:T(8,128)(2,1)S(1)} collective-permute-done((bf16[64,128]{1,0:T(8,128)(2,1)S(1)}, bf16[64,128]{1,0:T(8,128)(2,1)S(1)}, u32[]{:S(2)}, u32[]{:S(2)}) %collective-permute-start.19) | collective-permute-done | bytes 16416 | tf_op jit(solution)/shard_map/ppermute | solution.py:516
  63.1 1.3 %shard_map.203 = (f32[512,128]{1,0:T(8,128)S(1)}, bf16[512,128]{1,0:T(8,128)(2,1)S(1)}, bf16[512,256]{1,0:T(8,128)(2,1)S(1)}, bf16[192,256]{1,0:T(8,128)(2,1)S(1)}, bf16[192,256]{1,0:T(8,128)(2,1)S(1)}) custom-call(s32[5]{0:T(128)S(1)} %stack.23.meta, f32[512,128]{1,0:T(8,128)S(1)} %get-tuple-element.57.stream, s32[1,128]{1,0:T(1,128)S(1)} %bitcast.12, ...), custom_call_target="tpu_custom_call" | custom-call | tf_op jit(solution)/shard_map/pallas_call | solution.py:59
  64.4 3.4 %shard_map.204 = (f32[512,128]{1,0:T(8,128)S(1)}, bf16[512,128]{1,0:T(8,128)(2,1)S(1)}, bf16[512,256]{1,0:T(8,128)(2,1)S(1)}, bf16[192,256]{1,0:T(8,128)(2,1)S(1)}, bf16[192,256]{1,0:T(8,128)(2,1)S(1)}) custom-call(s32[5]{0:T(128)S(1)} %stack.23.meta, bf16[512,128]{1,0:T(8,128)(2,1)S(1)} %get-tuple-element.77.q, bf16[512,256]{1,0:T(8,128)(2,1)S(1)} %get-tuple-element.78.kv, ...), custom_call_target="tpu_custom_call" | custom-call | tf_op jit(solution)/shard_map/pallas_call | solution.py:59
  67.8 0.8 %collective-permute-start.22 = (bf16[192,256]{1,0:T(8,128)(2,1)S(1)}, bf16[192,256]{1,0:T(8,128)(2,1)S(1)}, u32[]{:S(2)}, u32[]{:S(2)}) collective-permute-start(bf16[192,256]{1,0:T(8,128)(2,1)S(1)} %get-tuple-element.84), channel_id=1, source_target_pairs={{0,1},{1,0},{2,3},{3,2},{4,5},{5,4},{6,7},{7,6},{8,9},{9,8},{10,11... | collective-permute-start | bytes 294920 | tf_op jit(solution)/shard_map/ppermute | solution.py:517
  68.6 1.3 %collective-permute-start.23 = (bf16[192,256]{1,0:T(8,128)(2,1)S(1)}, bf16[192,256]{1,0:T(8,128)(2,1)S(1)}, u32[]{:S(2)}, u32[]{:S(2)}) collective-permute-start(bf16[192,256]{1,0:T(8,128)(2,1)S(1)} %get-tuple-element.85), channel_id=1, source_target_pairs={{1,2},{3,4},{5,6},{7,8},{9,10},{11,12},{13,14},{2,1},{4,3},{6,5},{... | collective-permute-start | bytes 294920 | tf_op jit(solution)/shard_map/ppermute | solution.py:516
  70.0 3.8 %collective-permute-done.23.second = bf16[192,256]{1,0:T(8,128)(2,1)S(1)} collective-permute-done((bf16[192,256]{1,0:T(8,128)(2,1)S(1)}, bf16[192,256]{1,0:T(8,128)(2,1)S(1)}, u32[]{:S(2)}, u32[]{:S(2)}) %collective-permute-start.23) | collective-permute-done | bytes 98336 | tf_op jit(solution)/shard_map/ppermute | solution.py:516
  73.7 3.4 %shard_map.205 = (f32[3,4,128]{2,1,0:T(4,128)}, f32[4,16,768]{2,1,0:T(8,128)}) custom-call(s32[5]{0:T(128)S(1)} %stack.23.meta, bf16[512,128]{1,0:T(8,128)(2,1)S(1)} %get-tuple-element.82.q, bf16[512,256]{1,0:T(8,128)(2,1)S(1)} %get-tuple-element.83.kv, bf16[192,256]{1,0:T(8,128)(2,1)S(1)} %collective-permute-done.22.first, ...), custom_call_target="tpu_custom_call" | custom-call | tf_op jit(solution)/shard_map/pallas_call | solution.py:59
  (31 shorter events, 0.2 us)
Async XLA Ops:
  0.7 43.8 %copy-start = (bf16[768,2304]{1,0:T(8,128)(2,1)S(1)}, bf16[768,2304]{1,0:T(8,128)(2,1)}, u32[]{:S(2)}) copy-start(bf16[768,2304]{1,0:T(8,128)(2,1)} %rest_3_.1) | copy-start | bytes 10616836
  3.4 19.8 %collective-permute-start.4 = (f32[16,16,256]{2,1,0:T(8,128)}, f32[16,16,256]{2,1,0:T(8,128)S(1)}, u32[]{:S(2)}, u32[]{:S(2)}) collective-permute-start(f32[16,16,256]{2,1,0:T(8,128)} %rest_0_.3), channel_id=1, source_target_pairs={{0,1},{1,0},{2,3},{3,2},{4,5},{5,4},{6,7},{7,6},{8,9},{9,8},{10,11... | collective-permute-start | bytes 786440 | tf_op jit(solution)/shard_map/ppermute | solution.py:522
  4.1 19.1 %collective-permute-start.5 = (f32[16,16,256]{2,1,0:T(8,128)}, f32[16,16,256]{2,1,0:T(8,128)S(1)}, u32[]{:S(2)}, u32[]{:S(2)}) collective-permute-start(f32[16,16,256]{2,1,0:T(8,128)} %rest_0_.3), channel_id=1, source_target_pairs={{0,2},{1,3},{2,0},{3,1},{4,6},{5,7},{6,4},{7,5},{8,10},{9,11},{10,... | collective-permute-start | bytes 786440 | tf_op jit(solution)/shard_map/ppermute | solution.py:522
  5.4 2.8 %collective-permute-start = (bf16[192,256]{1,0:T(8,128)(2,1)S(1)}, bf16[192,256]{1,0:T(8,128)(2,1)S(1)}, u32[]{:S(2)}, u32[]{:S(2)}) collective-permute-start(bf16[192,256]{1,0:T(8,128)(2,1)S(1)} %get-tuple-element.48), channel_id=1, source_target_pairs={{0,1},{1,0},{2,3},{3,2},{4,5},{5,4},{6,7},{7,6},{8,9},{9,8},{10,11... | collective-permute-start | bytes 294920 | tf_op jit(solution)/shard_map/ppermute | solution.py:517
  5.7 8.7 %collective-permute-start.1 = (bf16[192,256]{1,0:T(8,128)(2,1)S(1)}, bf16[192,256]{1,0:T(8,128)(2,1)S(1)}, u32[]{:S(2)}, u32[]{:S(2)}) collective-permute-start(bf16[192,256]{1,0:T(8,128)(2,1)S(1)} %get-tuple-element.49), channel_id=1, source_target_pairs={{1,2},{3,4},{5,6},{7,8},{9,10},{11,12},{13,14},{2,1},{4,3},{6,5},{... | collective-permute-start | bytes 294920 | tf_op jit(solution)/shard_map/ppermute | solution.py:516
  6.0 0.7 copy-start.8
  17.9 2.0 %collective-permute-start.2 = (bf16[192,256]{1,0:T(8,128)(2,1)S(1)}, bf16[192,256]{1,0:T(8,128)(2,1)S(1)}, u32[]{:S(2)}, u32[]{:S(2)}) collective-permute-start(bf16[192,256]{1,0:T(8,128)(2,1)S(1)} %get-tuple-element.53), channel_id=1, source_target_pairs={{0,1},{1,0},{2,3},{3,2},{4,5},{5,4},{6,7},{7,6},{8,9},{9,8},{10,11... | collective-permute-start | bytes 294920 | tf_op jit(solution)/shard_map/ppermute | solution.py:517
  18.0 5.2 %collective-permute-start.3 = (bf16[192,256]{1,0:T(8,128)(2,1)S(1)}, bf16[192,256]{1,0:T(8,128)(2,1)S(1)}, u32[]{:S(2)}, u32[]{:S(2)}) collective-permute-start(bf16[192,256]{1,0:T(8,128)(2,1)S(1)} %get-tuple-element.54), channel_id=1, source_target_pairs={{1,2},{3,4},{5,6},{7,8},{9,10},{11,12},{13,14},{2,1},{4,3},{6,5},{... | collective-permute-start | bytes 294920 | tf_op jit(solution)/shard_map/ppermute | solution.py:516
  26.9 16.4 %collective-permute-start.11 = (f32[16,16,256]{2,1,0:T(8,128)S(1)}, f32[16,16,256]{2,1,0:T(8,128)S(1)}, u32[]{:S(2)}, u32[]{:S(2)}) collective-permute-start(f32[16,16,256]{2,1,0:T(8,128)S(1)} %collective-permute-done.5.rest_2_), channel_id=1, source_target_pairs={{0,1},{1,0},{2,3},{3,2},{4,5},{5,4},{6,7},{7,6},{8,9},{9,8},{10,11... | collective-permute-start | bytes 786440 | tf_op jit(solution)/shard_map/ppermute | solution.py:522
  27.2 1.8 %collective-permute-start.6 = (bf16[64,896]{1,0:T(8,128)(2,1)S(1)}, bf16[64,896]{1,0:T(8,128)(2,1)S(1)}, u32[]{:S(2)}, u32[]{:S(2)}) collective-permute-start(bf16[64,896]{1,0:T(8,128)(2,1)S(1)} %get-tuple-element.59), channel_id=1, source_target_pairs={{0,1},{1,0},{2,3},{3,2},{4,5},{5,4},{6,7},{7,6},{8,9},{9,8},{10,11... | collective-permute-start | bytes 344072 | tf_op jit(solution)/shard_map/ppermute | solution.py:517
  27.4 5.4 %collective-permute-start.7 = (bf16[64,896]{1,0:T(8,128)(2,1)S(1)}, bf16[64,896]{1,0:T(8,128)(2,1)S(1)}, u32[]{:S(2)}, u32[]{:S(2)}) collective-permute-start(bf16[64,896]{1,0:T(8,128)(2,1)S(1)} %get-tuple-element.60), channel_id=1, source_target_pairs={{1,2},{3,4},{5,6},{7,8},{9,10},{11,12},{13,14},{2,1},{4,3},{6,5},{... | collective-permute-start | bytes 344072 | tf_op jit(solution)/shard_map/ppermute | solution.py:516
  33.7 2.2 %collective-permute-start.8 = (bf16[16,768]{1,0:T(8,128)(2,1)S(1)}, bf16[16,768]{1,0:T(8,128)(2,1)S(1)}, u32[]{:S(2)}, u32[]{:S(2)}) collective-permute-start(bf16[16,768]{1,0:T(8,128)(2,1)S(1)} %get-tuple-element.63), channel_id=1, source_target_pairs={{0,1},{1,0},{2,3},{3,2},{4,5},{5,4},{6,7},{7,6},{8,9},{9,8},{10,11... | collective-permute-start | bytes 73736 | tf_op jit(solution)/shard_map/ppermute | solution.py:522
  33.8 2.7 %collective-permute-start.9 = (bf16[16,768]{1,0:T(8,128)(2,1)S(1)}, bf16[16,768]{1,0:T(8,128)(2,1)S(1)}, u32[]{:S(2)}, u32[]{:S(2)}) collective-permute-start(bf16[16,768]{1,0:T(8,128)(2,1)S(1)} %get-tuple-element.64), channel_id=1, source_target_pairs={{0,2},{1,3},{2,0},{3,1},{4,6},{5,7},{6,4},{7,5},{8,10},{9,11},{10,... | collective-permute-start | bytes 73736 | tf_op jit(solution)/shard_map/ppermute | solution.py:522
  35.2 3.8 %collective-permute-start.10 = (bf16[16,768]{1,0:T(8,128)(2,1)S(1)}, bf16[16,768]{1,0:T(8,128)(2,1)S(1)}, u32[]{:S(2)}, u32[]{:S(2)}) collective-permute-start(bf16[16,768]{1,0:T(8,128)(2,1)S(1)} %get-tuple-element.65), channel_id=1, source_target_pairs={{0,3},{1,2},{2,1},{3,0},{4,7},{5,6},{6,5},{7,4},{8,11},{9,10},{10,... | collective-permute-start | bytes 73736 | tf_op jit(solution)/shard_map/ppermute | solution.py:522
  39.5 6.6 %collective-permute-start.12 = (bf16[64,768]{1,0:T(8,128)(2,1)S(1)}, bf16[64,768]{1,0:T(8,128)(2,1)S(1)}, u32[]{:S(2)}, u32[]{:S(2)}) collective-permute-start(bf16[64,768]{1,0:T(8,128)(2,1)S(1)} %shard_map.199.normal), channel_id=1, source_target_pairs={{0,4},{4,8},{8,12},{12,0},{1,5},{5,9},{9,13},{13,1},{2,6},{6,10},{... | collective-permute-start | bytes 294920 | tf_op jit(solution)/shard_map/ppermute | solution.py:636
  40.8 8.1 %collective-permute-start.13 = (bf16[64,768]{1,0:T(8,128)(2,1)S(1)}, bf16[64,768]{1,0:T(8,128)(2,1)S(1)}, u32[]{:S(2)}, u32[]{:S(2)}) collective-permute-start(bf16[64,768]{1,0:T(8,128)(2,1)S(1)} %shard_map.199.normal), channel_id=1, source_target_pairs={{0,8},{4,12},{8,0},{12,4},{1,9},{5,13},{9,1},{13,5},{2,10},{6,14},... | collective-permute-start | bytes 294920 | tf_op jit(solution)/shard_map/ppermute | solution.py:636
  41.8 9.6 %collective-permute-start.14 = (bf16[64,768]{1,0:T(8,128)(2,1)S(1)}, bf16[64,768]{1,0:T(8,128)(2,1)S(1)}, u32[]{:S(2)}, u32[]{:S(2)}) collective-permute-start(bf16[64,768]{1,0:T(8,128)(2,1)S(1)} %shard_map.199.normal), channel_id=1, source_target_pairs={{0,12},{4,0},{8,4},{12,8},{1,13},{5,1},{9,5},{13,9},{2,14},{6,2},{... | collective-permute-start | bytes 294920 | tf_op jit(solution)/shard_map/ppermute | solution.py:636
  42.1 18.7 %collective-permute-start.20 = (f32[200,128]{1,0:T(8,128)S(1)}, f32[200,128]{1,0:T(8,128)S(1)}, u32[]{:S(2)}, u32[]{:S(2)}) collective-permute-start(f32[200,128]{1,0:T(8,128)S(1)} %get-tuple-element.75), channel_id=1, source_target_pairs={{0,1},{1,0},{2,3},{3,2},{4,5},{5,4},{6,7},{7,6},{8,9},{9,8},{10,11... | collective-permute-start | bytes 307208 | tf_op jit(solution)/shard_map/ppermute | solution.py:517
  43.3 17.5 %collective-permute-start.21 = (f32[200,128]{1,0:T(8,128)S(1)}, f32[200,128]{1,0:T(8,128)S(1)}, u32[]{:S(2)}, u32[]{:S(2)}) collective-permute-start(f32[200,128]{1,0:T(8,128)S(1)} %get-tuple-element.76), channel_id=1, source_target_pairs={{1,2},{3,4},{5,6},{7,8},{9,10},{11,12},{13,14},{2,1},{4,3},{6,5},{... | collective-permute-start | bytes 307208 | tf_op jit(solution)/shard_map/ppermute | solution.py:516
  46.1 11.9 %copy-start.2 = (bf16[768,768]{1,0:T(8,128)(2,1)S(1)}, bf16[768,768]{1,0:T(8,128)(2,1)}, u32[]{:S(2)}) copy-start(bf16[768,768]{1,0:T(8,128)(2,1)} %rest_4_.3) | copy-start | bytes 3538948
  46.1 11.9 %copy-start.3 = (bf16[768,128]{1,0:T(8,128)(2,1)S(1)}, bf16[768,128]{1,0:T(8,128)(2,1)}, u32[]{:S(2)}) copy-start(bf16[768,128]{1,0:T(8,128)(2,1)} %rest_5_.1) | copy-start | bytes 589828
  46.1 17.0 %copy-start.1 = (bf16[4,128,384]{2,1,0:T(8,128)(2,1)S(1)}, bf16[4,128,384]{2,1,0:T(8,128)(2,1)}, u32[]{:S(2)}) copy-start(bf16[4,128,384]{2,1,0:T(8,128)(2,1)} %w_qkv.5) | copy-start | bytes 1179652
  46.1 17.0 %copy-start.6 = (s32[128]{0:T(128)S(1)}, s32[128]{0:T(128)}, u32[]{:S(2)}) copy-start(s32[128]{0:T(128)} %param.23) | copy-start | bytes 1540
  53.8 20.0 %copy-start.4 = (f32[4,3,128]{2,0,1:T(4,128)S(1)}, f32[4,3,128]{2,0,1:T(4,128)}, u32[]{:S(2)}) copy-start(f32[4,3,128]{2,0,1:T(4,128)} %param.20) | copy-start | bytes 18436
  53.8 19.9 %copy-start.5 = (f32[3,128]{1,0:T(4,128)S(1)}, f32[3,128]{1,0:T(4,128)}, u32[]{:S(2)}) copy-start(f32[3,128]{1,0:T(4,128)} %x_true.1) | copy-start | bytes 4612
  53.8 19.9 %copy-start.7 = (bf16[3,128]{1,0:T(4,128)(2,1)S(1)}, bf16[3,128]{1,0:T(4,128)(2,1)}, u32[]{:S(2)}) copy-start(bf16[3,128]{1,0:T(4,128)(2,1)} %w_final.1) | copy-start | bytes 2308
  53.8 2.3 %collective-permute-start.15 = (bf16[16,768]{1,0:T(8,128)(2,1)S(1)}, bf16[16,768]{1,0:T(8,128)(2,1)S(1)}, u32[]{:S(2)}, u32[]{:S(2)}) collective-permute-start(bf16[16,768]{1,0:T(8,128)(2,1)S(1)} %get-tuple-element.71), channel_id=1, source_target_pairs={{0,1},{1,0},{2,3},{3,2},{4,5},{5,4},{6,7},{7,6},{8,9},{9,8},{10,11... | collective-permute-start | bytes 73736 | tf_op jit(solution)/shard_map/ppermute | solution.py:522
  54.4 2.7 %collective-permute-start.16 = (bf16[16,768]{1,0:T(8,128)(2,1)S(1)}, bf16[16,768]{1,0:T(8,128)(2,1)S(1)}, u32[]{:S(2)}, u32[]{:S(2)}) collective-permute-start(bf16[16,768]{1,0:T(8,128)(2,1)S(1)} %get-tuple-element.72), channel_id=1, source_target_pairs={{0,2},{1,3},{2,0},{3,1},{4,6},{5,7},{6,4},{7,5},{8,10},{9,11},{10,... | collective-permute-start | bytes 73736 | tf_op jit(solution)/shard_map/ppermute | solution.py:522
  54.5 3.5 %collective-permute-start.17 = (bf16[16,768]{1,0:T(8,128)(2,1)S(1)}, bf16[16,768]{1,0:T(8,128)(2,1)S(1)}, u32[]{:S(2)}, u32[]{:S(2)}) collective-permute-start(bf16[16,768]{1,0:T(8,128)(2,1)S(1)} %get-tuple-element.73), channel_id=1, source_target_pairs={{0,3},{1,2},{2,1},{3,0},{4,7},{5,6},{6,5},{7,4},{8,11},{9,10},{10,... | collective-permute-start | bytes 73736 | tf_op jit(solution)/shard_map/ppermute | solution.py:522
  59.2 1.6 %collective-permute-start.18 = (bf16[64,128]{1,0:T(8,128)(2,1)S(1)}, bf16[64,128]{1,0:T(8,128)(2,1)S(1)}, u32[]{:S(2)}, u32[]{:S(2)}) collective-permute-start(bf16[64,128]{1,0:T(8,128)(2,1)S(1)} %get-tuple-element.74.back), channel_id=1, source_target_pairs={{0,1},{1,0},{2,3},{3,2},{4,5},{5,4},{6,7},{7,6},{8,9},{9,8},{10,11... | collective-permute-start | bytes 49160 | tf_op jit(solution)/shard_map/ppermute | solution.py:517
  59.7 3.5 %collective-permute-start.19 = (bf16[64,128]{1,0:T(8,128)(2,1)S(1)}, bf16[64,128]{1,0:T(8,128)(2,1)S(1)}, u32[]{:S(2)}, u32[]{:S(2)}) collective-permute-start(bf16[64,128]{1,0:T(8,128)(2,1)S(1)} %get-tuple-element.74.back), channel_id=1, source_target_pairs={{1,2},{3,4},{5,6},{7,8},{9,10},{11,12},{13,14},{2,1},{4,3},{6,5},{... | collective-permute-start | bytes 49160 | tf_op jit(solution)/shard_map/ppermute | solution.py:516
  67.8 2.1 %collective-permute-start.22 = (bf16[192,256]{1,0:T(8,128)(2,1)S(1)}, bf16[192,256]{1,0:T(8,128)(2,1)S(1)}, u32[]{:S(2)}, u32[]{:S(2)}) collective-permute-start(bf16[192,256]{1,0:T(8,128)(2,1)S(1)} %get-tuple-element.84), channel_id=1, source_target_pairs={{0,1},{1,0},{2,3},{3,2},{4,5},{5,4},{6,7},{7,6},{8,9},{9,8},{10,11... | collective-permute-start | bytes 294920 | tf_op jit(solution)/shard_map/ppermute | solution.py:517
  68.6 5.1 %collective-permute-start.23 = (bf16[192,256]{1,0:T(8,128)(2,1)S(1)}, bf16[192,256]{1,0:T(8,128)(2,1)S(1)}, u32[]{:S(2)}, u32[]{:S(2)}) collective-permute-start(bf16[192,256]{1,0:T(8,128)(2,1)S(1)} %get-tuple-element.85), channel_id=1, source_target_pairs={{1,2},{3,4},{5,6},{7,8},{9,10},{11,12},{13,14},{2,1},{4,3},{6,5},{... | collective-permute-start | bytes 294920 | tf_op jit(solution)/shard_map/ppermute | solution.py:516

commit v6 on v5

--- a/solution.py
+++ b/solution.py
@@ -106,7 +106,7 @@
 
 
 def run_block(
-    meta, q_ref, kv_ref, first_ref, second_ref, stream_ref, bias_ref, weights, copies,
+    meta, q_ref, kv_ref, first_ref, second_ref, stream_ref, bias_ref, weights, layer,
     samples, rows, padded, mixed, out_ref,
 ):
     w_out, w_up, w_down = weights
@@ -149,28 +149,22 @@
         mixed[at] = (merged[:, :channels] * (1.0 / merged[:, channels:])).astype(BF)
 
     in_stages([score, soften, mix], units)
-    for copy in copies:
-        copy.wait()
-    stream = stream_ref[...] + dot(mixed[...], w_out[...])
-    gated = dot(normed(stream).astype(BF), w_up[...])
+    stream = stream_ref[...] + dot(mixed[...], w_out[layer])
+    gated = dot(normed(stream).astype(BF), w_up[layer])
     half = gated.shape[-1] // 2
     gate = gated[:, :half]
     hidden = (gate * (1.0 / (1.0 + jnp.exp(-gate))) * gated[:, half:]).astype(BF)
-    stream = stream + dot(hidden, w_down[...])
+    stream = stream + dot(hidden, w_down[layer])
     if out_ref is not None:
         out_ref[...] = stream
     return normed(stream).astype(BF)
 
 
-def block_scratch(samples, rows, channels, weights):
-    return (
-        [
-            pltpu.VMEM((samples, rows + 2 * RIM, 2 * channels), BF),
-            pltpu.VMEM((samples * rows, channels), BF),
-        ]
-        + [pltpu.VMEM(w.shape[1:], w.dtype) for w in weights]
-        + [pltpu.SemaphoreType.DMA((len(weights),))]
-    )
+def block_scratch(samples, rows, channels):
+    return [
+        pltpu.VMEM((samples, rows + 2 * RIM, 2 * channels), BF),
+        pltpu.VMEM((samples * rows, channels), BF),
+    ]
 
 
 def embed_kernel(
@@ -219,9 +213,14 @@
     emit_rims(kv_ref, meta[0], samples, rows, first_ref, second_ref)
 
 
-def mask_kernel(meta, edges, bias_hbm, _, out_ref, bias, sems):
+def prepare_kernel(meta, edges_hbm, bias_hbm, _, *rest):
+    moved = (len(rest) - 4) // 2
+    sources, out_ref, targets = rest[:moved], rest[moved], rest[moved + 1 : 2 * moved + 1]
+    bias, edges, sems = rest[2 * moved + 1 :]
     blocks, heads, queries, window = bias.shape
-    copies = fetch([(bias_hbm.at[b], bias.at[b]) for b in range(blocks)], sems)
+    pieces = [(bias_hbm.at[b], bias.at[b]) for b in range(blocks)]
+    copies = fetch(pieces + list(zip(sources, targets)) + [(edges_hbm, edges)], sems)
+    copies.pop().wait()
     lane = lax.broadcasted_iota(jnp.int32, (heads * queries, window), 1)
     for b in range(blocks):
         position = meta[1] - RIM + QUERY_BLOCK * b + lane
@@ -229,6 +228,8 @@
         copies[b].wait()
         values = bias[b].reshape(heads * queries, window) * LOG2E
         out_ref[b] = jnp.where(allowed, values, -jnp.inf)
+    for copy in copies[blocks:]:
+        copy.wait()
 
 
 def sigma_of(level, samples):
@@ -242,25 +243,14 @@
 
 def block_kernel(
     meta, q, kv, first, second, stream, bias, w_out, w_up, w_down, w_qkv,
-    stream_ref, q_ref, kv_ref, first_ref, second_ref, padded, mixed, out, up, down, qkv, sems,
-    *, layer, samples, rows,
-):
-    copies = fetch(
-        [
-            (w_out.at[layer], out),
-            (w_up.at[layer], up),
-            (w_down.at[layer], down),
-            (w_qkv.at[layer + 1], qkv),
-        ],
-        sems,
-    )
+    stream_ref, q_ref, kv_ref, first_ref, second_ref, padded, mixed, *, layer, samples, rows,
+):
     channels = q.shape[-1]
-
     normal = run_block(
-        meta, q, kv, first, second, stream, bias, (out, up, down), copies,
+        meta, q, kv, first, second, stream, bias, (w_out, w_up, w_down), layer,
         samples, rows, padded, mixed, stream_ref,
     )
-    projected = dot(normal, qkv[...]).astype(BF)
+    projected = dot(normal, w_qkv[layer + 1]).astype(BF)
     q_ref[...] = projected[:, :channels]
     kv_ref[...] = projected[:, channels:]
     emit_rims(kv_ref, meta[0], samples, rows, first_ref, second_ref)
@@ -274,27 +264,19 @@
 
 
 def pool_kernel(
-    meta, q, kv, first, second, stream, bias, w_out, w_up, w_down, w_pool, atom_token,
+    meta, q, kv, first, second, stream, bias, w_out, w_up, w_down, pooling, owners, single,
     *rest, layer, samples, rows, tokens,
 ):
-    single_hbm = rest[0]
     (stream_ref, mid_ref, first_ref, second_ref, first_rim, second_rim,
-     padded, mixed, out, up, down, sems, sums, pooling, owners, single, late_sems) = rest[-17:]
-    copies = fetch(
-        [(w_out.at[layer], out), (w_up.at[layer], up), (w_down.at[layer], down)], sems
-    )
-    late = fetch([(w_pool, pooling), (atom_token, owners), (single_hbm, single)], late_sems)
-
+     padded, mixed, sums) = rest[-9:]
     normal = run_block(
-        meta, q, kv, first, second, stream, bias, (out, up, down), copies,
+        meta, q, kv, first, second, stream, bias, (w_out, w_up, w_down), layer,
         samples, rows, padded, mixed, stream_ref,
     )
-    for copy in late:
-        copy.wait()
     selector = selector_of(meta, owners, tokens)
     counts = jnp.sum(selector, -1, keepdims=True)
     selector = selector.astype(BF)
-    width = w_pool.shape[-1]
+    width = pooling.shape[-1]
 
     def pool(s, _):
         return jnp.maximum(dot(normal[s * rows : (s + 1) * rows], pooling[...]), 0.0)
@@ -476,16 +458,13 @@
 
 def final_kernel(
     meta, q, kv, first, second, stream, bias, w_out, w_up, w_down, w_final,
-    level_hbm, x_true, noise, state, denoised_ref, state_ref, padded, mixed, out, up, down, sems,
+    level_hbm, x_true, noise, state, denoised_ref, state_ref, padded, mixed,
     level, late_sems, *, layer, samples, rows,
 ):
-    copies = fetch(
-        [(w_out.at[layer], out), (w_up.at[layer], up), (w_down.at[layer], down)], sems
-    )
     late = fetch([(level_hbm, level), (state, state_ref)], late_sems)
 
     normal = run_block(
-        meta, q, kv, first, second, stream, bias, (out, up, down), copies,
+        meta, q, kv, first, second, stream, bias, (w_out, w_up, w_down), layer,
         samples, rows, padded, mixed, None,
     )
     late[0].wait()
@@ -555,17 +534,8 @@
         rim,
     )
     stacks = (w_atom_out, w_atom_up, w_atom_down)
-    scratch = block_scratch(samples, rows, channels, stacks)
-    wide = block_scratch(samples, rows, channels, stacks + (w_atom_qkv,))
+    scratch = block_scratch(samples, rows, channels)
     sizes = dict(samples=samples, rows=rows)
-
-    def block(layer, q, kv, rims, stream):
-        return call(
-            functools.partial(block_kernel, layer=layer, **sizes), atom_outs,
-            [SM] + [VM] * 6 + [HB] * 4,
-            (meta, q, kv, *rims, stream, bias, *stacks, w_atom_qkv),
-            wide,
-        )
 
     stream, q, kv, *rims = call(
         functools.partial(embed_kernel, **sizes), atom_outs, [SM] + [HB] * 6,
@@ -581,11 +551,27 @@
         ],
     )
     blocks, atom_heads, queries, window = atom_pair_bias.shape
-    bias = call(
-        mask_kernel, struct((blocks, atom_heads * queries, window), F32),
-        [SM, SM, HB, VM], (meta, edges, atom_pair_bias, stream),
-        [pltpu.VMEM(atom_pair_bias.shape, F32), pltpu.SemaphoreType.DMA((blocks,))],
-    )
+    moved = (*stacks, w_atom_qkv, w_pool, atom_token, token_single)
+    bias, *stacks, w_atom_qkv, w_pool, atom_token, token_single = call(
+        prepare_kernel,
+        (struct((blocks, atom_heads * queries, window), F32),)
+        + tuple(struct(array.shape, array.dtype) for array in moved),
+        [SM, HB, HB, VM] + [HB] * len(moved), (meta, edges, atom_pair_bias, stream, *moved),
+        [
+            pltpu.VMEM(atom_pair_bias.shape, F32),
+            pltpu.SMEM(edges.shape, jnp.int32),
+            pltpu.SemaphoreType.DMA((blocks + len(moved) + 1,)),
+        ],
+    )
+
+    def block(layer, q, kv, rims, stream):
+        return call(
+            functools.partial(block_kernel, layer=layer, **sizes), atom_outs,
+            [SM] + [VM] * 10,
+            (meta, q, kv, *rims, stream, bias, *stacks, w_atom_qkv),
+            scratch,
+        )
+
     for layer in range(ENC_LAYERS - 1):
         rims = swap(rims, count)
         if layer == 0:
@@ -601,19 +587,12 @@
     encoded, mid, first, second, *stream_rims = call(
         functools.partial(pool_kernel, layer=ENC_LAYERS - 1, tokens=tokens, **sizes),
         (atom_outs[0], struct((held + tokens, lanes), F32), edge, edge, stream_rim, stream_rim),
-        [SM] + [VM] * 6 + [HB] * 6 + [VM] * 2,
+        [SM] + [VM] * 14,
         (
             meta, q, kv, *rims, stream, bias, *stacks, w_pool, atom_token, token_single,
             *biases[1:3],
         ),
-        scratch
-        + [
-            pltpu.VMEM((samples, 3 * tokens, lanes), F32),
-            pltpu.VMEM(w_pool.shape, BF),
-            pltpu.VMEM(atom_token.shape, jnp.int32),
-            pltpu.VMEM(token_single.shape, F32),
-            pltpu.SemaphoreType.DMA((3,)),
-        ],
+        scratch + [pltpu.VMEM((samples, 3 * tokens, lanes), F32)],
     )
     passed, _ = lax.optimization_barrier((biases[2], mid))
     biases.append(toward(passed, 1, samples))
@@ -676,7 +655,7 @@
     denoised, token_state = call(
         functools.partial(final_kernel, layer=LAYERS - 1, **sizes),
         (struct(noise.shape, F32), struct((samples, tokens, width), F32)),
-        [SM] + [VM] * 6 + [HB] * 3 + [VM, HB, VM, VM, VM],
+        [SM] + [VM] * 10 + [HB, VM, VM, VM],
         (
             meta, q, kv, *rims, stream, bias, *stacks, w_final, noise_level, x_true, noise,
             after,

time: 77.6 us -> 74.5 us (0.960)
  the two profiles are of different devices: /device:TPU:11 before, /device:TPU:9 now
where the time goes in v6:
time: 74.5 us; the launch traced here: 74.3 us
  waiting for transfers between devices  29.7 us (40%)
  Pallas kernels  23.6 us (32%)
  starting transfers between devices  19.9 us (27%)
  between operations  0.97 us (1%)
    pallas_call x12, Pallas kernels, call(): pl.pallas_call(kernel, out_shape=out_shape, in_specs=specs, out_specs=out...  23.6 us
    ppermute x6, waiting for transfers between devices, swap(): second = lax.ppermute(second, ('groups',) + SEQ, upper)  19.4 us
    ppermute x6, starting transfers between devices, swap(): second = lax.ppermute(second, ('groups',) + SEQ, upper)  7.38 us
    ppermute x9, starting transfers between devices, toward(): return lax.ppermute(array, 'p', [(i, i ^ k) for i in range(count)])  6.82 us
    ppermute x3, waiting for transfers between devices, shards(): gathered.append(lax.ppermute(normal, 'z', shift))  5.28 us
    ppermute x9, waiting for transfers between devices, toward(): return lax.ppermute(array, 'p', [(i, i ^ k) for i in range(count)])  4.94 us
    ppermute x6, starting transfers between devices, swap(): first = lax.ppermute(first, SEQ, lower)  3.07 us
    ppermute x3, starting transfers between devices, shards(): gathered.append(lax.ppermute(normal, 'z', shift))  2.61 us
  transfers between devices with their start and end apart: 24, of which 11 were waited for; matrix products, arithmetic and copies ran while one was open for 0% of the time, Pallas kernels for 15%

profile of v6, /device:TPU:9, one launch (start us, length us, event | category | flops | bytes accessed | tf_op | source)
XLA Modules:
  0.0 74.3 jit_solution(2573442823299258034)
XLA Ops:
  0.6 0.1 stack.23.meta
  0.7 2.4 %shard_map.194 = (f32[512,128]{1,0:T(8,128)S(1)}, bf16[512,128]{1,0:T(8,128)(2,1)S(1)}, bf16[512,256]{1,0:T(8,128)(2,1)S(1)}, bf16[192,256]{1,0:T(8,128)(2,1)S(1)}, bf16[192,256]{1,0:T(8,128)(2,1)S(1)}) custom-call(s32[5]{0:T(128)S(1)} %stack.23.meta, s32[4]{0:T(128)} %level_hbm.3, f32[3,128]{1,0:T(4,128)} %x_true.1, f32[3,4,128]{2,1,0:T(4,128)} %bitcast.9, ...), custom_call_target="tpu_custom_call" | custom-call | tf_op jit(solution)/shard_map/pallas_call | solution.py:59
  3.1 0.7 collective-permute-start.4
  3.9 1.2 %collective-permute-start.5 = (f32[16,16,256]{2,1,0:T(8,128)}, f32[16,16,256]{2,1,0:T(8,128)S(1)}, u32[]{:S(2)}, u32[]{:S(2)}) collective-permute-start(f32[16,16,256]{2,1,0:T(8,128)} %rest_0_.3), channel_id=1, source_target_pairs={{0,2},{1,3},{2,0},{3,1},{4,6},{5,7},{6,4},{7,5},{8,10},{9,11},{10,... | collective-permute-start | bytes 786440 | tf_op jit(solution)/shard_map/ppermute | solution.py:501
  5.1 0.4 collective-permute-start
  5.5 0.3 collective-permute-start.1
  5.7 2.4 %shard_map.195 = (f32[4,128,128]{2,1,0:T(8,128)S(1)}, bf16[4,128,128]{2,1,0:T(8,128)(2,1)S(1)}, bf16[4,128,512]{2,1,0:T(8,128)(2,1)S(1)}, bf16[4,256,128]{2,1,0:...) custom-call(s32[5]{0:T(128)S(1)} %stack.23.meta, ...), custom_call_target="tpu_custom_call" | custom-call | tf_op jit(solution)/shard_map/pallas_call | solution.py:59
  8.1 6.1 %collective-permute-done.1.second = bf16[192,256]{1,0:T(8,128)(2,1)S(1)} collective-permute-done((bf16[192,256]{1,0:T(8,128)(2,1)S(1)}, bf16[192,256]{1,0:T(8,128)(2,1)S(1)}, u32[]{:S(2)}, u32[]{:S(2)}) %collective-permute-start.1) | collective-permute-done | bytes 98336 | tf_op jit(solution)/shard_map/ppermute | solution.py:495
  14.2 2.5 %shard_map.196 = (f32[512,128]{1,0:T(8,128)S(1)}, bf16[512,128]{1,0:T(8,128)(2,1)S(1)}, bf16[512,256]{1,0:T(8,128)(2,1)S(1)}, bf16[192,256]{1,0:T(8,128)(2,1)S(1)}, bf16[192,256]{1,0:T(8,128)(2,1)S(1)}) custom-call(s32[5]{0:T(128)S(1)} %stack.23.meta, bf16[512,128]{1,0:T(8,128)(2,1)S(1)} %get-tuple-element.54.q, bf16[512,256]{1,0:T(8,128)(2,1)S(1)} %get-tuple-element.55.kv, ...), custom_call_target="tpu_custom_call" | custom-call | tf_op jit(solution)/shard_map/pallas_call | solution.py:59
  16.8 0.1 collective-permute-start.2
  16.8 1.9 %collective-permute-start.3 = (bf16[192,256]{1,0:T(8,128)(2,1)S(1)}, bf16[192,256]{1,0:T(8,128)(2,1)S(1)}, u32[]{:S(2)}, u32[]{:S(2)}) collective-permute-start(bf16[192,256]{1,0:T(8,128)(2,1)S(1)} %get-tuple-element.67), channel_id=1, source_target_pairs={{1,2},{3,4},{5,6},{7,8},{9,10},{11,12},{13,14},{2,1},{4,3},{6,5},{... | collective-permute-start | bytes 294920 | tf_op jit(solution)/shard_map/ppermute | solution.py:495
  18.7 3.4 %collective-permute-done.3.second = bf16[192,256]{1,0:T(8,128)(2,1)S(1)} collective-permute-done((bf16[192,256]{1,0:T(8,128)(2,1)S(1)}, bf16[192,256]{1,0:T(8,128)(2,1)S(1)}, u32[]{:S(2)}, u32[]{:S(2)}) %collective-permute-start.3) | collective-permute-done | bytes 98336 | tf_op jit(solution)/shard_map/ppermute | solution.py:495
  22.1 2.9 %shard_map.197 = (f32[512,128]{1,0:T(8,128)S(1)}, f32[80,896]{1,0:T(8,128)S(1)}, bf16[64,896]{1,0:T(8,128)(2,1)S(1)}, bf16[64,896]{1,0:T(8,128)(2,1)S(1)}, f32[2...) custom-call(s32[5]{0:T(128)S(1)} %stack.23.meta, bf16[512,128]{1,0:T(8,128)(2,1)S(1)} %get-tuple-element.64.q, ...), custom_call_target="tpu_custom_call" | custom-call | tf_op jit(solution)/shard_map/pallas_call | solution.py:59
  24.9 0.4 collective-permute-start.11
  25.3 0.2 collective-permute-start.6
  25.5 1.6 %collective-permute-start.7 = (bf16[64,896]{1,0:T(8,128)(2,1)S(1)}, bf16[64,896]{1,0:T(8,128)(2,1)S(1)}, u32[]{:S(2)}, u32[]{:S(2)}) collective-permute-start(bf16[64,896]{1,0:T(8,128)(2,1)S(1)} %get-tuple-element.76), channel_id=1, source_target_pairs={{1,2},{3,4},{5,6},{7,8},{9,10},{11,12},{13,14},{2,1},{4,3},{6,5},{... | collective-permute-start | bytes 344072 | tf_op jit(solution)/shard_map/ppermute | solution.py:495
  27.1 3.9 %collective-permute-done.7.second = bf16[64,896]{1,0:T(8,128)(2,1)S(1)} collective-permute-done((bf16[64,896]{1,0:T(8,128)(2,1)S(1)}, bf16[64,896]{1,0:T(8,128)(2,1)S(1)}, u32[]{:S(2)}, u32[]{:S(2)}) %collective-permute-start.7) | collective-permute-done | bytes 114720 | tf_op jit(solution)/shard_map/ppermute | solution.py:495
  31.0 0.8 %shard_map.198 = (f32[64,768]{1,0:T(8,128)S(1)}, bf16[16,768]{1,0:T(8,128)(2,1)S(1)}, bf16[16,768]{1,0:T(8,128)(2,1)S(1)}, bf16[16,768]{1,0:T(8,128)(2,1)S(1)}, bf16[16,768]{1,0:T(8,128)(2,1)S(1)}) custom-call(s32[5]{0:T(128)S(1)} %stack.23.meta, f32[80,896]{1,0:T(8,128)S(1)} %get-tuple-element.74.mid, bf16[64,896]{1,0:T(8,128)(2,1)S(1)} %collective-permute-done.6.first, ...), custom_call_target="tpu_custom_call" | custom-call | tf_op jit(solution)/shard_map/pallas_call | solution.py:59
  31.8 0.1 collective-permute-start.8
  31.9 1.3 %collective-permute-start.9 = (bf16[16,768]{1,0:T(8,128)(2,1)S(1)}, bf16[16,768]{1,0:T(8,128)(2,1)S(1)}, u32[]{:S(2)}, u32[]{:S(2)}) collective-permute-start(bf16[16,768]{1,0:T(8,128)(2,1)S(1)} %get-tuple-element.80), channel_id=1, source_target_pairs={{0,2},{1,3},{2,0},{3,1},{4,6},{5,7},{6,4},{7,5},{8,10},{9,11},{10,... | collective-permute-start | bytes 73736 | tf_op jit(solution)/shard_map/ppermute | solution.py:501
  33.2 0.8 %collective-permute-start.10 = (bf16[16,768]{1,0:T(8,128)(2,1)S(1)}, bf16[16,768]{1,0:T(8,128)(2,1)S(1)}, u32[]{:S(2)}, u32[]{:S(2)}) collective-permute-start(bf16[16,768]{1,0:T(8,128)(2,1)S(1)} %get-tuple-element.81), channel_id=1, source_target_pairs={{0,3},{1,2},{2,1},{3,0},{4,7},{5,6},{6,5},{7,4},{8,11},{9,10},{10,... | collective-permute-start | bytes 73736 | tf_op jit(solution)/shard_map/ppermute | solution.py:501
  34.0 0.6 collective-permute-done.9.rest_2_
  34.6 2.4 %collective-permute-done.10.rest_3_ = bf16[16,768]{1,0:T(8,128)(2,1)S(1)} collective-permute-done((bf16[16,768]{1,0:T(8,128)(2,1)S(1)}, bf16[16,768]{1,0:T(8,128)(2,1)S(1)}, u32[]{:S(2)}, u32[]{:S(2)}) %collective-permute-start.10) | collective-permute-done | bytes 24608 | tf_op jit(solution)/shard_map/ppermute | solution.py:501
  37.0 0.6 shard_map.199.normal
  37.6 1.4 %collective-permute-start.12 = (bf16[64,768]{1,0:T(8,128)(2,1)S(1)}, bf16[64,768]{1,0:T(8,128)(2,1)S(1)}, u32[]{:S(2)}, u32[]{:S(2)}) collective-permute-start(bf16[64,768]{1,0:T(8,128)(2,1)S(1)} %shard_map.199.normal), channel_id=1, source_target_pairs={{0,4},{4,8},{8,12},{12,0},{1,5},{5,9},{9,13},{13,1},{2,6},{6,10},{... | collective-permute-start | bytes 294920 | tf_op jit(solution)/shard_map/ppermute | solution.py:615
  38.9 1.0 %collective-permute-start.13 = (bf16[64,768]{1,0:T(8,128)(2,1)S(1)}, bf16[64,768]{1,0:T(8,128)(2,1)S(1)}, u32[]{:S(2)}, u32[]{:S(2)}) collective-permute-start(bf16[64,768]{1,0:T(8,128)(2,1)S(1)} %shard_map.199.normal), channel_id=1, source_target_pairs={{0,8},{4,12},{8,0},{12,4},{1,9},{5,13},{9,1},{13,5},{2,10},{6,14},... | collective-permute-start | bytes 294920 | tf_op jit(solution)/shard_map/ppermute | solution.py:615
  39.9 0.3 collective-permute-start.14
  40.2 1.2 %collective-permute-start.20 = (f32[200,128]{1,0:T(8,128)S(1)}, f32[200,128]{1,0:T(8,128)S(1)}, u32[]{:S(2)}, u32[]{:S(2)}) collective-permute-start(f32[200,128]{1,0:T(8,128)S(1)} %get-tuple-element.91), channel_id=1, source_target_pairs={{0,1},{1,0},{2,3},{3,2},{4,5},{5,4},{6,7},{7,6},{8,9},{9,8},{10,11... | collective-permute-start | bytes 307208 | tf_op jit(solution)/shard_map/ppermute | solution.py:496
  41.4 1.3 %collective-permute-start.21 = (f32[200,128]{1,0:T(8,128)S(1)}, f32[200,128]{1,0:T(8,128)S(1)}, u32[]{:S(2)}, u32[]{:S(2)}) collective-permute-start(f32[200,128]{1,0:T(8,128)S(1)} %get-tuple-element.92), channel_id=1, source_target_pairs={{1,2},{3,4},{5,6},{7,8},{9,10},{11,12},{13,14},{2,1},{4,3},{6,5},{... | collective-permute-start | bytes 307208 | tf_op jit(solution)/shard_map/ppermute | solution.py:495
  42.6 1.5 %shard_map.200 = (bf16[64,768]{1,0:T(8,128)(2,1)S(1)}, bf16[64,1536]{1,0:T(8,128)(2,1)S(1)}, f32[16,64,256]{2,1,0:T(8,128)S(1)}) custom-call(s32[5]{0:T(128)S(1)} %stack.23.meta, bf16[64,768]{1,0:T(8,128)(2,1)S(1)} %shard_map.199.normal, f32[16,16,256]{2,1,0:T(8,128)} %rest_0_.3, f32[16,16,256]{2,1,0:T(8,128)S(1)} %collective-permute-done.4.rest_0_.rest_1_, ...), custom_call_target="tpu_custom_call" | custom-call | tf_op jit(solution)/shard_map/pallas_call | solution.py:59
  44.2 2.8 %collective-permute-done.13.rest_1_ = bf16[64,768]{1,0:T(8,128)(2,1)S(1)} collective-permute-done((bf16[64,768]{1,0:T(8,128)(2,1)S(1)}, bf16[64,768]{1,0:T(8,128)(2,1)S(1)}, u32[]{:S(2)}, u32[]{:S(2)}) %collective-permute-start.13) | collective-permute-done | bytes 98336 | tf_op jit(solution)/shard_map/ppermute | solution.py:615
  47.0 2.5 %collective-permute-done.14.rest_2_ = bf16[64,768]{1,0:T(8,128)(2,1)S(1)} collective-permute-done((bf16[64,768]{1,0:T(8,128)(2,1)S(1)}, bf16[64,768]{1,0:T(8,128)(2,1)S(1)}, u32[]{:S(2)}, u32[]{:S(2)}) %collective-permute-start.14) | collective-permute-done | bytes 98336 | tf_op jit(solution)/shard_map/ppermute | solution.py:615
  49.5 2.4 %shard_map.201 = (bf16[16,768]{1,0:T(8,128)(2,1)S(1)}, bf16[16,768]{1,0:T(8,128)(2,1)S(1)}, bf16[16,768]{1,0:T(8,128)(2,1)S(1)}, bf16[16,768]{1,0:T(8,128)(2,1)S(1)}) custom-call(s32[5]{0:T(128)S(1)} %stack.23.meta, bf16[64,768]{1,0:T(8,128)(2,1)S(1)} %get-tuple-element.83.q_own, bf16[64,1536]{1,0:T(8,128)(2,1)S(1)} %get-tuple-element.84.kv_own, ...), custom_call_target="tpu_custom_call" | custom-call | tf_op jit(solution)/shard_map/pallas_call | solution.py:59
  51.9 0.6 collective-permute-start.15
  52.5 0.2 collective-permute-start.16
  52.6 1.5 %collective-permute-start.17 = (bf16[16,768]{1,0:T(8,128)(2,1)S(1)}, bf16[16,768]{1,0:T(8,128)(2,1)S(1)}, u32[]{:S(2)}, u32[]{:S(2)}) collective-permute-start(bf16[16,768]{1,0:T(8,128)(2,1)S(1)} %get-tuple-element.89), channel_id=1, source_target_pairs={{0,3},{1,2},{2,1},{3,0},{4,7},{5,6},{6,5},{7,4},{8,11},{9,10},{10,... | collective-permute-start | bytes 73736 | tf_op jit(solution)/shard_map/ppermute | solution.py:501
  54.2 1.0 %collective-permute-done.16.rest_2_ = bf16[16,768]{1,0:T(8,128)(2,1)S(1)} collective-permute-done((bf16[16,768]{1,0:T(8,128)(2,1)S(1)}, bf16[16,768]{1,0:T(8,128)(2,1)S(1)}, u32[]{:S(2)}, u32[]{:S(2)}) %collective-permute-start.16) | collective-permute-done | bytes 24608 | tf_op jit(solution)/shard_map/ppermute | solution.py:501
  55.1 1.0 %collective-permute-done.17.rest_3_ = bf16[16,768]{1,0:T(8,128)(2,1)S(1)} collective-permute-done((bf16[16,768]{1,0:T(8,128)(2,1)S(1)}, bf16[16,768]{1,0:T(8,128)(2,1)S(1)}, u32[]{:S(2)}, u32[]{:S(2)}) %collective-permute-start.17) | collective-permute-done | bytes 24608 | tf_op jit(solution)/shard_map/ppermute | solution.py:501
  56.1 1.2 %shard_map.202 = (f32[4,16,768]{2,1,0:T(8,128)S(1)}, bf16[64,128]{1,0:T(8,128)(2,1)S(1)}) custom-call(s32[5]{0:T(128)S(1)} %stack.23.meta, f32[64,768]{1,0:T(8,128)S(1)} %get-tuple-element.77.state, bf16[16,768]{1,0:T(8,128)(2,1)S(1)} %get-tuple-element.86.rest_0_, bf16[16,768]{1,0:T(8,128)(2,1)S(1)} %collective-permute-done.15.rest_1_, ...), custom_call_target="tpu_custom_call" | custom-call | tf_op jit(solution)/shard_map/pallas_call | solution.py:59
  57.3 0.5 collective-permute-start.18
  57.8 1.1 %collective-permute-start.19 = (bf16[64,128]{1,0:T(8,128)(2,1)S(1)}, bf16[64,128]{1,0:T(8,128)(2,1)S(1)}, u32[]{:S(2)}, u32[]{:S(2)}) collective-permute-start(bf16[64,128]{1,0:T(8,128)(2,1)S(1)} %get-tuple-element.90.back), channel_id=1, source_target_pairs={{1,2},{3,4},{5,6},{7,8},{9,10},{11,12},{13,14},{2,1},{4,3},{6,5},{... | collective-permute-start | bytes 49160 | tf_op jit(solution)/shard_map/ppermute | solution.py:495
  58.9 2.4 %collective-permute-done.19.second = bf16[64,128]{1,0:T(8,128)(2,1)S(1)} collective-permute-done((bf16[64,128]{1,0:T(8,128)(2,1)S(1)}, bf16[64,128]{1,0:T(8,128)(2,1)S(1)}, u32[]{:S(2)}, u32[]{:S(2)}) %collective-permute-start.19) | collective-permute-done | bytes 16416 | tf_op jit(solution)/shard_map/ppermute | solution.py:495
  61.3 1.3 %shard_map.203 = (f32[512,128]{1,0:T(8,128)S(1)}, bf16[512,128]{1,0:T(8,128)(2,1)S(1)}, bf16[512,256]{1,0:T(8,128)(2,1)S(1)}, bf16[192,256]{1,0:T(8,128)(2,1)S(1)}, bf16[192,256]{1,0:T(8,128)(2,1)S(1)}) custom-call(s32[5]{0:T(128)S(1)} %stack.23.meta, f32[512,128]{1,0:T(8,128)S(1)} %get-tuple-element.73.stream, ...), custom_call_target="tpu_custom_call" | custom-call | tf_op jit(solution)/shard_map/pallas_call | solution.py:59
  62.6 2.6 %shard_map.204 = (f32[512,128]{1,0:T(8,128)S(1)}, bf16[512,128]{1,0:T(8,128)(2,1)S(1)}, bf16[512,256]{1,0:T(8,128)(2,1)S(1)}, bf16[192,256]{1,0:T(8,128)(2,1)S(1)}, bf16[192,256]{1,0:T(8,128)(2,1)S(1)}) custom-call(s32[5]{0:T(128)S(1)} %stack.23.meta, bf16[512,128]{1,0:T(8,128)(2,1)S(1)} %get-tuple-element.93.q, bf16[512,256]{1,0:T(8,128)(2,1)S(1)} %get-tuple-element.94.kv, ...), custom_call_target="tpu_custom_call" | custom-call | tf_op jit(solution)/shard_map/pallas_call | solution.py:59
  65.1 0.8 %collective-permute-start.22 = (bf16[192,256]{1,0:T(8,128)(2,1)S(1)}, bf16[192,256]{1,0:T(8,128)(2,1)S(1)}, u32[]{:S(2)}, u32[]{:S(2)}) collective-permute-start(bf16[192,256]{1,0:T(8,128)(2,1)S(1)} %get-tuple-element.100), channel_id=1, source_target_pairs={{0,1},{1,0},{2,3},{3,2},{4,5},{5,4},{6,7},{7,6},{8,9},{9,8},{10,11... | collective-permute-start | bytes 294920 | tf_op jit(solution)/shard_map/ppermute | solution.py:496
  65.9 1.3 %collective-permute-start.23 = (bf16[192,256]{1,0:T(8,128)(2,1)S(1)}, bf16[192,256]{1,0:T(8,128)(2,1)S(1)}, u32[]{:S(2)}, u32[]{:S(2)}) collective-permute-start(bf16[192,256]{1,0:T(8,128)(2,1)S(1)} %get-tuple-element.101), channel_id=1, source_target_pairs={{1,2},{3,4},{5,6},{7,8},{9,10},{11,12},{13,14},{2,1},{4,3},{6,5},{... | collective-permute-start | bytes 294920 | tf_op jit(solution)/shard_map/ppermute | solution.py:495
  67.2 3.8 %collective-permute-done.23.second = bf16[192,256]{1,0:T(8,128)(2,1)S(1)} collective-permute-done((bf16[192,256]{1,0:T(8,128)(2,1)S(1)}, bf16[192,256]{1,0:T(8,128)(2,1)S(1)}, u32[]{:S(2)}, u32[]{:S(2)}) %collective-permute-start.23) | collective-permute-done | bytes 98336 | tf_op jit(solution)/shard_map/ppermute | solution.py:495
  71.0 3.1 %shard_map.205 = (f32[3,4,128]{2,1,0:T(4,128)}, f32[4,16,768]{2,1,0:T(8,128)}) custom-call(s32[5]{0:T(128)S(1)} %stack.23.meta, bf16[512,128]{1,0:T(8,128)(2,1)S(1)} %get-tuple-element.98.q, bf16[512,256]{1,0:T(8,128)(2,1)S(1)} %get-tuple-element.99.kv, bf16[192,256]{1,0:T(8,128)(2,1)S(1)} %collective-permute-done.22.first, ...), custom_call_target="tpu_custom_call" | custom-call | tf_op jit(solution)/shard_map/pallas_call | solution.py:59
  (25 shorter events, 0.1 us)
Async XLA Ops:
  3.1 19.0 %collective-permute-start.4 = (f32[16,16,256]{2,1,0:T(8,128)}, f32[16,16,256]{2,1,0:T(8,128)S(1)}, u32[]{:S(2)}, u32[]{:S(2)}) collective-permute-start(f32[16,16,256]{2,1,0:T(8,128)} %rest_0_.3), channel_id=1, source_target_pairs={{0,1},{1,0},{2,3},{3,2},{4,5},{5,4},{6,7},{7,6},{8,9},{9,8},{10,11... | collective-permute-start | bytes 786440 | tf_op jit(solution)/shard_map/ppermute | solution.py:501
  3.9 18.2 %collective-permute-start.5 = (f32[16,16,256]{2,1,0:T(8,128)}, f32[16,16,256]{2,1,0:T(8,128)S(1)}, u32[]{:S(2)}, u32[]{:S(2)}) collective-permute-start(f32[16,16,256]{2,1,0:T(8,128)} %rest_0_.3), channel_id=1, source_target_pairs={{0,2},{1,3},{2,0},{3,1},{4,6},{5,7},{6,4},{7,5},{8,10},{9,11},{10,... | collective-permute-start | bytes 786440 | tf_op jit(solution)/shard_map/ppermute | solution.py:501
  5.1 3.0 %collective-permute-start = (bf16[192,256]{1,0:T(8,128)(2,1)S(1)}, bf16[192,256]{1,0:T(8,128)(2,1)S(1)}, u32[]{:S(2)}, u32[]{:S(2)}) collective-permute-start(bf16[192,256]{1,0:T(8,128)(2,1)S(1)} %get-tuple-element.56), channel_id=1, source_target_pairs={{0,1},{1,0},{2,3},{3,2},{4,5},{5,4},{6,7},{7,6},{8,9},{9,8},{10,11... | collective-permute-start | bytes 294920 | tf_op jit(solution)/shard_map/ppermute | solution.py:496
  5.5 8.7 %collective-permute-start.1 = (bf16[192,256]{1,0:T(8,128)(2,1)S(1)}, bf16[192,256]{1,0:T(8,128)(2,1)S(1)}, u32[]{:S(2)}, u32[]{:S(2)}) collective-permute-start(bf16[192,256]{1,0:T(8,128)(2,1)S(1)} %get-tuple-element.57), channel_id=1, source_target_pairs={{1,2},{3,4},{5,6},{7,8},{9,10},{11,12},{13,14},{2,1},{4,3},{6,5},{... | collective-permute-start | bytes 294920 | tf_op jit(solution)/shard_map/ppermute | solution.py:495
  5.7 36.9 %copy-start = (bf16[768,2304]{1,0:T(8,128)(2,1)S(1)}, bf16[768,2304]{1,0:T(8,128)(2,1)}, u32[]{:S(2)}) copy-start(bf16[768,2304]{1,0:T(8,128)(2,1)} %rest_3_.3) | copy-start | bytes 10616836
  16.8 2.0 %collective-permute-start.2 = (bf16[192,256]{1,0:T(8,128)(2,1)S(1)}, bf16[192,256]{1,0:T(8,128)(2,1)S(1)}, u32[]{:S(2)}, u32[]{:S(2)}) collective-permute-start(bf16[192,256]{1,0:T(8,128)(2,1)S(1)} %get-tuple-element.66), channel_id=1, source_target_pairs={{0,1},{1,0},{2,3},{3,2},{4,5},{5,4},{6,7},{7,6},{8,9},{9,8},{10,11... | collective-permute-start | bytes 294920 | tf_op jit(solution)/shard_map/ppermute | solution.py:496
  16.8 5.2 %collective-permute-start.3 = (bf16[192,256]{1,0:T(8,128)(2,1)S(1)}, bf16[192,256]{1,0:T(8,128)(2,1)S(1)}, u32[]{:S(2)}, u32[]{:S(2)}) collective-permute-start(bf16[192,256]{1,0:T(8,128)(2,1)S(1)} %get-tuple-element.67), channel_id=1, source_target_pairs={{1,2},{3,4},{5,6},{7,8},{9,10},{11,12},{13,14},{2,1},{4,3},{6,5},{... | collective-permute-start | bytes 294920 | tf_op jit(solution)/shard_map/ppermute | solution.py:495
  24.9 16.4 %collective-permute-start.11 = (f32[16,16,256]{2,1,0:T(8,128)S(1)}, f32[16,16,256]{2,1,0:T(8,128)S(1)}, u32[]{:S(2)}, u32[]{:S(2)}) collective-permute-start(f32[16,16,256]{2,1,0:T(8,128)S(1)} %collective-permute-done.5.rest_1_.rest_2_), channel_id=1, source_target_pairs={{0,1},{1,0},{2,3},{3,2},{4,5},{5,4},{6,7},{7,6},{8,9},{9,8},{10,11... | collective-permute-start | bytes 786440 | tf_op jit(solution)/shard_map/ppermute | solution.py:501
  25.3 1.8 %collective-permute-start.6 = (bf16[64,896]{1,0:T(8,128)(2,1)S(1)}, bf16[64,896]{1,0:T(8,128)(2,1)S(1)}, u32[]{:S(2)}, u32[]{:S(2)}) collective-permute-start(bf16[64,896]{1,0:T(8,128)(2,1)S(1)} %get-tuple-element.75), channel_id=1, source_target_pairs={{0,1},{1,0},{2,3},{3,2},{4,5},{5,4},{6,7},{7,6},{8,9},{9,8},{10,11... | collective-permute-start | bytes 344072 | tf_op jit(solution)/shard_map/ppermute | solution.py:496
  25.5 5.4 %collective-permute-start.7 = (bf16[64,896]{1,0:T(8,128)(2,1)S(1)}, bf16[64,896]{1,0:T(8,128)(2,1)S(1)}, u32[]{:S(2)}, u32[]{:S(2)}) collective-permute-start(bf16[64,896]{1,0:T(8,128)(2,1)S(1)} %get-tuple-element.76), channel_id=1, source_target_pairs={{1,2},{3,4},{5,6},{7,8},{9,10},{11,12},{13,14},{2,1},{4,3},{6,5},{... | collective-permute-start | bytes 344072 | tf_op jit(solution)/shard_map/ppermute | solution.py:495
  31.8 2.2 %collective-permute-start.8 = (bf16[16,768]{1,0:T(8,128)(2,1)S(1)}, bf16[16,768]{1,0:T(8,128)(2,1)S(1)}, u32[]{:S(2)}, u32[]{:S(2)}) collective-permute-start(bf16[16,768]{1,0:T(8,128)(2,1)S(1)} %get-tuple-element.79), channel_id=1, source_target_pairs={{0,1},{1,0},{2,3},{3,2},{4,5},{5,4},{6,7},{7,6},{8,9},{9,8},{10,11... | collective-permute-start | bytes 73736 | tf_op jit(solution)/shard_map/ppermute | solution.py:501
  31.9 2.7 %collective-permute-start.9 = (bf16[16,768]{1,0:T(8,128)(2,1)S(1)}, bf16[16,768]{1,0:T(8,128)(2,1)S(1)}, u32[]{:S(2)}, u32[]{:S(2)}) collective-permute-start(bf16[16,768]{1,0:T(8,128)(2,1)S(1)} %get-tuple-element.80), channel_id=1, source_target_pairs={{0,2},{1,3},{2,0},{3,1},{4,6},{5,7},{6,4},{7,5},{8,10},{9,11},{10,... | collective-permute-start | bytes 73736 | tf_op jit(solution)/shard_map/ppermute | solution.py:501
  33.2 3.8 %collective-permute-start.10 = (bf16[16,768]{1,0:T(8,128)(2,1)S(1)}, bf16[16,768]{1,0:T(8,128)(2,1)S(1)}, u32[]{:S(2)}, u32[]{:S(2)}) collective-permute-start(bf16[16,768]{1,0:T(8,128)(2,1)S(1)} %get-tuple-element.81), channel_id=1, source_target_pairs={{0,3},{1,2},{2,1},{3,0},{4,7},{5,6},{6,5},{7,4},{8,11},{9,10},{10,... | collective-permute-start | bytes 73736 | tf_op jit(solution)/shard_map/ppermute | solution.py:501
  37.6 6.6 %collective-permute-start.12 = (bf16[64,768]{1,0:T(8,128)(2,1)S(1)}, bf16[64,768]{1,0:T(8,128)(2,1)S(1)}, u32[]{:S(2)}, u32[]{:S(2)}) collective-permute-start(bf16[64,768]{1,0:T(8,128)(2,1)S(1)} %shard_map.199.normal), channel_id=1, source_target_pairs={{0,4},{4,8},{8,12},{12,0},{1,5},{5,9},{9,13},{13,1},{2,6},{6,10},{... | collective-permute-start | bytes 294920 | tf_op jit(solution)/shard_map/ppermute | solution.py:615
  38.9 8.1 %collective-permute-start.13 = (bf16[64,768]{1,0:T(8,128)(2,1)S(1)}, bf16[64,768]{1,0:T(8,128)(2,1)S(1)}, u32[]{:S(2)}, u32[]{:S(2)}) collective-permute-start(bf16[64,768]{1,0:T(8,128)(2,1)S(1)} %shard_map.199.normal), channel_id=1, source_target_pairs={{0,8},{4,12},{8,0},{12,4},{1,9},{5,13},{9,1},{13,5},{2,10},{6,14},... | collective-permute-start | bytes 294920 | tf_op jit(solution)/shard_map/ppermute | solution.py:615
  39.9 9.6 %collective-permute-start.14 = (bf16[64,768]{1,0:T(8,128)(2,1)S(1)}, bf16[64,768]{1,0:T(8,128)(2,1)S(1)}, u32[]{:S(2)}, u32[]{:S(2)}) collective-permute-start(bf16[64,768]{1,0:T(8,128)(2,1)S(1)} %shard_map.199.normal), channel_id=1, source_target_pairs={{0,12},{4,0},{8,4},{12,8},{1,13},{5,1},{9,5},{13,9},{2,14},{6,2},{... | collective-permute-start | bytes 294920 | tf_op jit(solution)/shard_map/ppermute | solution.py:615
  40.2 18.7 %collective-permute-start.20 = (f32[200,128]{1,0:T(8,128)S(1)}, f32[200,128]{1,0:T(8,128)S(1)}, u32[]{:S(2)}, u32[]{:S(2)}) collective-permute-start(f32[200,128]{1,0:T(8,128)S(1)} %get-tuple-element.91), channel_id=1, source_target_pairs={{0,1},{1,0},{2,3},{3,2},{4,5},{5,4},{6,7},{7,6},{8,9},{9,8},{10,11... | collective-permute-start | bytes 307208 | tf_op jit(solution)/shard_map/ppermute | solution.py:496
  41.4 17.5 %collective-permute-start.21 = (f32[200,128]{1,0:T(8,128)S(1)}, f32[200,128]{1,0:T(8,128)S(1)}, u32[]{:S(2)}, u32[]{:S(2)}) collective-permute-start(f32[200,128]{1,0:T(8,128)S(1)} %get-tuple-element.92), channel_id=1, source_target_pairs={{1,2},{3,4},{5,6},{7,8},{9,10},{11,12},{13,14},{2,1},{4,3},{6,5},{... | collective-permute-start | bytes 307208 | tf_op jit(solution)/shard_map/ppermute | solution.py:495
  44.2 11.9 %copy-start.1 = (bf16[768,768]{1,0:T(8,128)(2,1)S(1)}, bf16[768,768]{1,0:T(8,128)(2,1)}, u32[]{:S(2)}) copy-start(bf16[768,768]{1,0:T(8,128)(2,1)} %rest_4_.5) | copy-start | bytes 3538948
  44.2 11.9 %copy-start.2 = (bf16[768,128]{1,0:T(8,128)(2,1)S(1)}, bf16[768,128]{1,0:T(8,128)(2,1)}, u32[]{:S(2)}) copy-start(bf16[768,128]{1,0:T(8,128)(2,1)} %rest_5_.1) | copy-start | bytes 589828
  51.9 19.1 %copy-start.3 = (f32[4,3,128]{2,0,1:T(4,128)S(1)}, f32[4,3,128]{2,0,1:T(4,128)}, u32[]{:S(2)}) copy-start(f32[4,3,128]{2,0,1:T(4,128)} %param.20) | copy-start | bytes 18436
  51.9 19.1 %copy-start.4 = (f32[3,128]{1,0:T(4,128)S(1)}, f32[3,128]{1,0:T(4,128)}, u32[]{:S(2)}) copy-start(f32[3,128]{1,0:T(4,128)} %x_true.1) | copy-start | bytes 4612
  51.9 19.1 %copy-start.5 = (bf16[3,128]{1,0:T(4,128)(2,1)S(1)}, bf16[3,128]{1,0:T(4,128)(2,1)}, u32[]{:S(2)}) copy-start(bf16[3,128]{1,0:T(4,128)(2,1)} %w_final.1) | copy-start | bytes 2308
  51.9 2.3 %collective-permute-start.15 = (bf16[16,768]{1,0:T(8,128)(2,1)S(1)}, bf16[16,768]{1,0:T(8,128)(2,1)S(1)}, u32[]{:S(2)}, u32[]{:S(2)}) collective-permute-start(bf16[16,768]{1,0:T(8,128)(2,1)S(1)} %get-tuple-element.87), channel_id=1, source_target_pairs={{0,1},{1,0},{2,3},{3,2},{4,5},{5,4},{6,7},{7,6},{8,9},{9,8},{10,11... | collective-permute-start | bytes 73736 | tf_op jit(solution)/shard_map/ppermute | solution.py:501
  52.5 2.7 %collective-permute-start.16 = (bf16[16,768]{1,0:T(8,128)(2,1)S(1)}, bf16[16,768]{1,0:T(8,128)(2,1)S(1)}, u32[]{:S(2)}, u32[]{:S(2)}) collective-permute-start(bf16[16,768]{1,0:T(8,128)(2,1)S(1)} %get-tuple-element.88), channel_id=1, source_target_pairs={{0,2},{1,3},{2,0},{3,1},{4,6},{5,7},{6,4},{7,5},{8,10},{9,11},{10,... | collective-permute-start | bytes 73736 | tf_op jit(solution)/shard_map/ppermute | solution.py:501
  52.6 3.5 %collective-permute-start.17 = (bf16[16,768]{1,0:T(8,128)(2,1)S(1)}, bf16[16,768]{1,0:T(8,128)(2,1)S(1)}, u32[]{:S(2)}, u32[]{:S(2)}) collective-permute-start(bf16[16,768]{1,0:T(8,128)(2,1)S(1)} %get-tuple-element.89), channel_id=1, source_target_pairs={{0,3},{1,2},{2,1},{3,0},{4,7},{5,6},{6,5},{7,4},{8,11},{9,10},{10,... | collective-permute-start | bytes 73736 | tf_op jit(solution)/shard_map/ppermute | solution.py:501
  57.3 1.5 %collective-permute-start.18 = (bf16[64,128]{1,0:T(8,128)(2,1)S(1)}, bf16[64,128]{1,0:T(8,128)(2,1)S(1)}, u32[]{:S(2)}, u32[]{:S(2)}) collective-permute-start(bf16[64,128]{1,0:T(8,128)(2,1)S(1)} %get-tuple-element.90.back), channel_id=1, source_target_pairs={{0,1},{1,0},{2,3},{3,2},{4,5},{5,4},{6,7},{7,6},{8,9},{9,8},{10,11... | collective-permute-start | bytes 49160 | tf_op jit(solution)/shard_map/ppermute | solution.py:496
  57.8 3.5 %collective-permute-start.19 = (bf16[64,128]{1,0:T(8,128)(2,1)S(1)}, bf16[64,128]{1,0:T(8,128)(2,1)S(1)}, u32[]{:S(2)}, u32[]{:S(2)}) collective-permute-start(bf16[64,128]{1,0:T(8,128)(2,1)S(1)} %get-tuple-element.90.back), channel_id=1, source_target_pairs={{1,2},{3,4},{5,6},{7,8},{9,10},{11,12},{13,14},{2,1},{4,3},{6,5},{... | collective-permute-start | bytes 49160 | tf_op jit(solution)/shard_map/ppermute | solution.py:495
  65.1 2.1 %collective-permute-start.22 = (bf16[192,256]{1,0:T(8,128)(2,1)S(1)}, bf16[192,256]{1,0:T(8,128)(2,1)S(1)}, u32[]{:S(2)}, u32[]{:S(2)}) collective-permute-start(bf16[192,256]{1,0:T(8,128)(2,1)S(1)} %get-tuple-element.100), channel_id=1, source_target_pairs={{0,1},{1,0},{2,3},{3,2},{4,5},{5,4},{6,7},{7,6},{8,9},{9,8},{10,11... | collective-permute-start | bytes 294920 | tf_op jit(solution)/shard_map/ppermute | solution.py:496
  65.9 5.1 %collective-permute-start.23 = (bf16[192,256]{1,0:T(8,128)(2,1)S(1)}, bf16[192,256]{1,0:T(8,128)(2,1)S(1)}, u32[]{:S(2)}, u32[]{:S(2)}) collective-permute-start(bf16[192,256]{1,0:T(8,128)(2,1)S(1)} %get-tuple-element.101), channel_id=1, source_target_pairs={{1,2},{3,4},{5,6},{7,8},{9,10},{11,12},{13,14},{2,1},{4,3},{6,5},{... | collective-permute-start | bytes 294920 | tf_op jit(solution)/shard_map/ppermute | solution.py:495

commit v7 on v6

--- a/solution.py
+++ b/solution.py
@@ -21,7 +21,6 @@
 F32 = jnp.float32
 SEQ = ("z", "p")
 VM = pl.BlockSpec(memory_space=pltpu.VMEM)
-SM = pl.BlockSpec(memory_space=pltpu.SMEM)
 HB = pl.BlockSpec(memory_space=pltpu.HBM)
 COUNT_LANES = 128
 LOG2E = 1.4426950408889634
@@ -55,9 +54,19 @@
     return jax.ShapeDtypeStruct(shape, dtype)
 
 
+def places():
+    mine = lax.axis_index("p")
+    plane = lax.axis_index("z")
+    device = plane * lax.axis_size("p") + mine
+    return lax.rem(device, 2), device, mine, plane
+
+
 def call(kernel, out_shape, specs, args, scratch=(), out_specs=None):
+    def body(*refs):
+        kernel(places(), *refs)
+
     return pl.pallas_call(
-        kernel,
+        body,
         out_shape=out_shape,
         in_specs=specs,
         out_specs=out_specs or jax.tree.map(lambda _: VM, out_shape),
@@ -223,7 +232,7 @@
     copies.pop().wait()
     lane = lax.broadcasted_iota(jnp.int32, (heads * queries, window), 1)
     for b in range(blocks):
-        position = meta[1] - RIM + QUERY_BLOCK * b + lane
+        position = meta[1] * (blocks * QUERY_BLOCK) - RIM + QUERY_BLOCK * b + lane
         allowed = (position >= edges[0, b]) & (position < edges[1, b])
         copies[b].wait()
         values = bias[b].reshape(heads * queries, window) * LOG2E
@@ -258,7 +267,7 @@
 
 def selector_of(meta, atom_token, tokens):
     rows = atom_token.shape[-1]
-    relative = atom_token[...] - (meta[2] - 1) * tokens
+    relative = atom_token[...] - (meta[1] - 1) * tokens
     row = lax.broadcasted_iota(jnp.int32, (3 * tokens, rows), 0)
     return (row == relative).astype(F32)
 
@@ -320,14 +329,14 @@
         state = share[at] + single
         state_ref[at] = state
         normal_all[s] = normed(state).astype(BF)
-    mine = meta[3]
+    mine = meta[2]
     for k in range(samples):
         send_refs[k][...] = normal_all[lax.bitwise_xor(mine, k)]
 
 
 def plane_kernel(meta, *rest, samples, tokens):
     parts, out_ref = rest[:samples], rest[samples]
-    mine = meta[3]
+    mine = meta[2]
     for k in range(samples):
         at = pl.multiple_of(lax.bitwise_xor(mine, k) * tokens, tokens)
         out_ref[pl.ds(at, tokens)] = parts[k][...]
@@ -335,7 +344,7 @@
 
 def token_own_kernel(meta, normal, *rest, samples, tokens):
     biases, (w_qkv, q_ref, kv_ref, bias_ref, sems) = rest[:samples], rest[samples:]
-    mine = meta[3]
+    mine = meta[2]
     starts = [
         pl.multiple_of(lax.bitwise_xor(mine, k) * tokens, tokens) for k in range(samples)
     ]
@@ -356,8 +365,8 @@
     rows = samples * tokens
     width = q_own.shape[-1]
     head_size = width // heads
-    mine = meta[3]
-    plane = meta[4]
+    mine = meta[2]
+    plane = meta[3]
     kv_all[pl.ds(pl.multiple_of(plane * rows, rows), rows)] = kv_own[...]
     others = jnp.concatenate([one[...] for one in gathered], 0)
     others = dot(others, w_qkv[:, width:]).astype(BF)
@@ -399,7 +408,7 @@
 
 def token_out_kernel(meta, state, *rest, samples, tokens):
     parts, (w_out, w_back, out_ref, back_ref, mixed) = rest[:samples], rest[samples:]
-    mine = meta[3]
+    mine = meta[2]
     for k in range(samples):
         at = pl.multiple_of(lax.bitwise_xor(mine, k) * tokens, tokens)
         mixed[pl.ds(at, tokens)] = parts[k][...]
@@ -418,7 +427,7 @@
     selector = selector_of(meta, atom_token, tokens).astype(BF)
     first_at, second_at = halves(meta[0], 0, 2 * tokens)
     row = lax.broadcasted_iota(jnp.int32, (3 * tokens, RIM), 0).astype(F32)
-    base = ((meta[2] - 1) * tokens).astype(F32)
+    base = ((meta[1] - 1) * tokens).astype(F32)
     rims = [
         (rim, (row == rim[samples * RIM : samples * RIM + 1, :RIM] - base).astype(BF), out)
         for rim, out in ((first_rim, first_ref), (second_rim, second_ref))
@@ -516,10 +525,6 @@
     heads = pair_bias.shape[0]
     planes = lax.axis_size("z")
     count = planes * samples
-    mine = lax.axis_index("p")
-    plane = lax.axis_index("z")
-    device = plane * samples + mine
-    meta = jnp.stack([device % 2, device * rows, device, mine, plane]).astype(jnp.int32)
     atom_token = atom_token[None, :]
     edges = window_edges.T
     noise = noise.transpose(1, 0, 2)
@@ -538,8 +543,8 @@
     sizes = dict(samples=samples, rows=rows)
 
     stream, q, kv, *rims = call(
-        functools.partial(embed_kernel, **sizes), atom_outs, [SM] + [HB] * 6,
-        (meta, noise_level, x_true, noise, atom_single, w_coord, w_atom_qkv),
+        functools.partial(embed_kernel, **sizes), atom_outs, [HB] * 6,
+        (noise_level, x_true, noise, atom_single, w_coord, w_atom_qkv),
         [
             pltpu.SMEM(noise_level.shape, jnp.int32),
             pltpu.VMEM(x_true.shape, F32),
@@ -556,7 +561,7 @@
         prepare_kernel,
         (struct((blocks, atom_heads * queries, window), F32),)
         + tuple(struct(array.shape, array.dtype) for array in moved),
-        [SM, HB, HB, VM] + [HB] * len(moved), (meta, edges, atom_pair_bias, stream, *moved),
+        [HB, HB, VM] + [HB] * len(moved), (edges, atom_pair_bias, stream, *moved),
         [
             pltpu.VMEM(atom_pair_bias.shape, F32),
             pltpu.SMEM(edges.shape, jnp.int32),
@@ -567,8 +572,8 @@
     def block(layer, q, kv, rims, stream):
         return call(
             functools.partial(block_kernel, layer=layer, **sizes), atom_outs,
-            [SM] + [VM] * 10,
-            (meta, q, kv, *rims, stream, bias, *stacks, w_atom_qkv),
+            [VM] * 10,
+            (q, kv, *rims, stream, bias, *stacks, w_atom_qkv),
             scratch,
         )
 
@@ -587,9 +592,9 @@
     encoded, mid, first, second, *stream_rims = call(
         functools.partial(pool_kernel, layer=ENC_LAYERS - 1, tokens=tokens, **sizes),
         (atom_outs[0], struct((held + tokens, lanes), F32), edge, edge, stream_rim, stream_rim),
-        [SM] + [VM] * 14,
+        [VM] * 14,
         (
-            meta, q, kv, *rims, stream, bias, *stacks, w_pool, atom_token, token_single,
+            q, kv, *rims, stream, bias, *stacks, w_pool, atom_token, token_single,
             *biases[1:3],
         ),
         scratch + [pltpu.VMEM((samples, 3 * tokens, lanes), F32)],
@@ -601,13 +606,13 @@
     state, *sends = call(
         functools.partial(token_in_kernel, samples=samples, tokens=tokens),
         (struct((held, width), F32),) + (piece,) * samples,
-        [SM] + [VM] * 3, (meta, mid, *rims),
+        [VM] * 3, (mid, *rims),
         [pltpu.VMEM((samples, tokens, width), BF)],
     )
     got = across(sends[1:], samples)
     normal = call(
         functools.partial(plane_kernel, samples=samples, tokens=tokens),
-        struct((held, width), BF), [SM] + [VM] * samples, (meta, sends[0], *got),
+        struct((held, width), BF), [VM] * samples, (sends[0], *got),
     )
     gathered = []
     for k in range(1, planes):
@@ -622,29 +627,29 @@
             struct((held, 2 * width), BF),
             struct((heads, held, every), F32),
         ),
-        [SM, VM, HB] + [VM] * samples, (meta, normal, *biases, w_token_qkv),
+        [VM, HB] + [VM] * samples, (normal, *biases, w_token_qkv),
         [pltpu.SemaphoreType.DMA((samples,))],
     )
     sends = call(
         functools.partial(
             token_kernel, samples=samples, tokens=tokens, planes=planes, heads=heads
         ),
-        (piece,) * samples, [SM] + [VM] * (3 + planes),
-        (meta, q_own, kv_own, bias_all, *gathered, w_token_qkv),
+        (piece,) * samples, [VM] * (3 + planes),
+        (q_own, kv_own, bias_all, *gathered, w_token_qkv),
         [pltpu.VMEM((every, 2 * width), BF), pltpu.VMEM((held, width), F32)],
     )
     got = across(sends[1:], samples)
     after, back = call(
         functools.partial(token_out_kernel, samples=samples, tokens=tokens),
         (struct((samples, tokens, width), F32), struct((held, channels), BF)),
-        [SM] + [VM] * (1 + samples + 2), (meta, state, sends[0], *got, w_token_out, w_back),
+        [VM] * (1 + samples + 2), (state, sends[0], *got, w_token_out, w_back),
         [pltpu.VMEM((held, width), BF)],
     )
     backs = swap((back, back), count)
     stream, q, kv, *rims = call(
         functools.partial(unpool_kernel, tokens=tokens, **sizes), atom_outs,
-        [SM] + [VM] * 8,
-        (meta, encoded, atom_token, back, *backs, *stream_rims, w_atom_qkv),
+        [VM] * 8,
+        (encoded, atom_token, back, *backs, *stream_rims, w_atom_qkv),
         [pltpu.VMEM((samples, 3 * tokens, channels), BF)],
     )
     for layer in range(ENC_LAYERS, LAYERS - 1):
@@ -655,9 +660,9 @@
     denoised, token_state = call(
         functools.partial(final_kernel, layer=LAYERS - 1, **sizes),
         (struct(noise.shape, F32), struct((samples, tokens, width), F32)),
-        [SM] + [VM] * 10 + [HB, VM, VM, VM],
+        [VM] * 10 + [HB, VM, VM, VM],
         (
-            meta, q, kv, *rims, stream, bias, *stacks, w_final, noise_level, x_true, noise,
+            q, kv, *rims, stream, bias, *stacks, w_final, noise_level, x_true, noise,
             after,
         ),
         scratch

time: 74.5 us -> 68.9 us (0.925)
  the two profiles are of different devices: /device:TPU:9 before, /device:TPU:11 now
where the time goes in v7:
time: 68.9 us; the launch traced here: 68.7 us
  waiting for transfers between devices  30.9 us (45%)
  starting transfers between devices  19.9 us (29%)
  Pallas kernels  17 us (25%)
  between operations  0.94 us (1%)
    ppermute x6, waiting for transfers between devices, swap(): second = lax.ppermute(second, ('groups',) + SEQ, upper)  20.1 us
    pallas_call x12, Pallas kernels, call(): pl.pallas_call(body, out_shape=out_shape, in_specs=specs, out_specs=out_s...  17 us
    ppermute x6, starting transfers between devices, swap(): second = lax.ppermute(second, ('groups',) + SEQ, upper)  7.4 us
    ppermute x9, starting transfers between devices, toward(): return lax.ppermute(array, 'p', [(i, i ^ k) for i in range(count)])  6.82 us
    ppermute x3, waiting for transfers between devices, shards(): gathered.append(lax.ppermute(normal, 'z', shift))  5.82 us
    ppermute x9, waiting for transfers between devices, toward(): return lax.ppermute(array, 'p', [(i, i ^ k) for i in range(count)])  4.93 us
    ppermute x6, starting transfers between devices, swap(): first = lax.ppermute(first, SEQ, lower)  3.06 us
    ppermute x3, starting transfers between devices, shards(): gathered.append(lax.ppermute(normal, 'z', shift))  2.61 us
  transfers between devices with their start and end apart: 24, of which 11 were waited for; matrix products, arithmetic and copies ran while one was open for 0% of the time, Pallas kernels for 11%

profile of v7, /device:TPU:11, one launch (start us, length us, event | category | flops | bytes accessed | tf_op | source)
XLA Modules:
  0.0 68.7 jit_solution(8674233227550361225)
XLA Ops:
  0.6 1.9 %shard_map.194 = (f32[512,128]{1,0:T(8,128)S(1)}, bf16[512,128]{1,0:T(8,128)(2,1)S(1)}, bf16[512,256]{1,0:T(8,128)(2,1)S(1)}, bf16[192,256]{1,0:T(8,128)(2,1)S(1)}, bf16[192,256]{1,0:T(8,128)(2,1)S(1)}) custom-call(s32[4]{0:T(128)} %refs_10_.1, f32[3,128]{1,0:T(4,128)} %refs_11_.1, f32[3,4,128]{2,1,0:T(4,128)} %bitcast.4, bf16[128,128]{1,0:T(8,128)(2,1)} %refs_3_.2, ...), custom_call_target="tpu_custom_call" | custom-call | tf_op jit(solution)/shard_map/pallas_call | solution.py:68
  2.5 0.7 %collective-permute-start.4 = (f32[16,16,256]{2,1,0:T(8,128)}, f32[16,16,256]{2,1,0:T(8,128)S(1)}, u32[]{:S(2)}, u32[]{:S(2)}) collective-permute-start(f32[16,16,256]{2,1,0:T(8,128)} %refs_1_.5), channel_id=1, source_target_pairs={{0,1},{1,0},{2,3},{3,2},{4,5},{5,4},{6,7},{7,6},{8,9},{9,8},{10,11... | collective-permute-start | bytes 786440 | tf_op jit(solution)/shard_map/ppermute | solution.py:510
  3.2 1.2 %collective-permute-start.5 = (f32[16,16,256]{2,1,0:T(8,128)}, f32[16,16,256]{2,1,0:T(8,128)S(1)}, u32[]{:S(2)}, u32[]{:S(2)}) collective-permute-start(f32[16,16,256]{2,1,0:T(8,128)} %refs_1_.5), channel_id=1, source_target_pairs={{0,2},{1,3},{2,0},{3,1},{4,6},{5,7},{6,4},{7,5},{8,10},{9,11},{10,... | collective-permute-start | bytes 786440 | tf_op jit(solution)/shard_map/ppermute | solution.py:510
  4.5 0.4 collective-permute-start
  4.8 0.3 collective-permute-start.1
  5.1 1.7 %shard_map.195 = (f32[4,128,128]{2,1,0:T(8,128)S(1)}, bf16[4,128,128]{2,1,0:T(8,128)(2,1)S(1)}, bf16[4,128,512]{2,1,0:T(8,128)(2,1)S(1)}, bf16[4,256,128]{2,1,0:...) custom-call(s32[2,4]{1,0:T(2,128)} %bitcast.6, ...), custom_call_target="tpu_custom_call" | custom-call | tf_op jit(solution)/shard_map/pallas_call | solution.py:68
  6.8 6.7 %collective-permute-done.1.refs_3_ = bf16[192,256]{1,0:T(8,128)(2,1)S(1)} collective-permute-done((bf16[192,256]{1,0:T(8,128)(2,1)S(1)}, bf16[192,256]{1,0:T(8,128)(2,1)S(1)}, u32[]{:S(2)}, u32[]{:S(2)}) %collective-permute-start.1) | collective-permute-done | bytes 98336 | tf_op jit(solution)/shard_map/ppermute | solution.py:504
  13.6 2.0 %shard_map.196 = (f32[512,128]{1,0:T(8,128)S(1)}, bf16[512,128]{1,0:T(8,128)(2,1)S(1)}, bf16[512,256]{1,0:T(8,128)(2,1)S(1)}, bf16[192,256]{1,0:T(8,128)(2,1)S(1)}, bf16[192,256]{1,0:T(8,128)(2,1)S(1)}) custom-call(bf16[512,128]{1,0:T(8,128)(2,1)S(1)} %get-tuple-element.54.refs_0_, bf16[512,256]{1,0:T(8,128)(2,1)S(1)} %get-tuple-element.55.refs_1_, ...), custom_call_target="tpu_custom_call" | custom-call | tf_op jit(solution)/shard_map/pallas_call | solution.py:68
  15.6 0.1 collective-permute-start.2
  15.7 1.9 %collective-permute-start.3 = (bf16[192,256]{1,0:T(8,128)(2,1)S(1)}, bf16[192,256]{1,0:T(8,128)(2,1)S(1)}, u32[]{:S(2)}, u32[]{:S(2)}) collective-permute-start(bf16[192,256]{1,0:T(8,128)(2,1)S(1)} %get-tuple-element.67), channel_id=1, source_target_pairs={{1,2},{3,4},{5,6},{7,8},{9,10},{11,12},{13,14},{2,1},{4,3},{6,5},{... | collective-permute-start | bytes 294920 | tf_op jit(solution)/shard_map/ppermute | solution.py:504
  17.5 3.4 %collective-permute-done.3.refs_3_ = bf16[192,256]{1,0:T(8,128)(2,1)S(1)} collective-permute-done((bf16[192,256]{1,0:T(8,128)(2,1)S(1)}, bf16[192,256]{1,0:T(8,128)(2,1)S(1)}, u32[]{:S(2)}, u32[]{:S(2)}) %collective-permute-start.3) | collective-permute-done | bytes 98336 | tf_op jit(solution)/shard_map/ppermute | solution.py:504
  20.9 2.3 %shard_map.197 = (f32[512,128]{1,0:T(8,128)S(1)}, f32[80,896]{1,0:T(8,128)S(1)}, bf16[64,896]{1,0:T(8,128)(2,1)S(1)}, bf16[64,896]{1,0:T(8,128)(2,1)S(1)}, f32[2...) custom-call(bf16[512,128]{1,0:T(8,128)(2,1)S(1)} %get-tuple-element.64.refs_0_, ...), custom_call_target="tpu_custom_call" | custom-call | tf_op jit(solution)/shard_map/pallas_call | solution.py:68
  23.2 0.4 collective-permute-start.11
  23.6 0.2 collective-permute-start.6
  23.8 1.6 %collective-permute-start.7 = (bf16[64,896]{1,0:T(8,128)(2,1)S(1)}, bf16[64,896]{1,0:T(8,128)(2,1)S(1)}, u32[]{:S(2)}, u32[]{:S(2)}) collective-permute-start(bf16[64,896]{1,0:T(8,128)(2,1)S(1)} %get-tuple-element.76), channel_id=1, source_target_pairs={{1,2},{3,4},{5,6},{7,8},{9,10},{11,12},{13,14},{2,1},{4,3},{6,5},{... | collective-permute-start | bytes 344072 | tf_op jit(solution)/shard_map/ppermute | solution.py:504
  25.4 3.9 %collective-permute-done.7.refs_2_ = bf16[64,896]{1,0:T(8,128)(2,1)S(1)} collective-permute-done((bf16[64,896]{1,0:T(8,128)(2,1)S(1)}, bf16[64,896]{1,0:T(8,128)(2,1)S(1)}, u32[]{:S(2)}, u32[]{:S(2)}) %collective-permute-start.7) | collective-permute-done | bytes 114720 | tf_op jit(solution)/shard_map/ppermute | solution.py:504
  29.2 0.3 shard_map.198
  29.5 0.1 collective-permute-start.8
  29.7 1.3 %collective-permute-start.9 = (bf16[16,768]{1,0:T(8,128)(2,1)S(1)}, bf16[16,768]{1,0:T(8,128)(2,1)S(1)}, u32[]{:S(2)}, u32[]{:S(2)}) collective-permute-start(bf16[16,768]{1,0:T(8,128)(2,1)S(1)} %get-tuple-element.80), channel_id=1, source_target_pairs={{0,2},{1,3},{2,0},{3,1},{4,6},{5,7},{6,4},{7,5},{8,10},{9,11},{10,... | collective-permute-start | bytes 73736 | tf_op jit(solution)/shard_map/ppermute | solution.py:510
  31.0 0.8 %collective-permute-start.10 = (bf16[16,768]{1,0:T(8,128)(2,1)S(1)}, bf16[16,768]{1,0:T(8,128)(2,1)S(1)}, u32[]{:S(2)}, u32[]{:S(2)}) collective-permute-start(bf16[16,768]{1,0:T(8,128)(2,1)S(1)} %get-tuple-element.81), channel_id=1, source_target_pairs={{0,3},{1,2},{2,1},{3,0},{4,7},{5,6},{6,5},{7,4},{8,11},{9,10},{10,... | collective-permute-start | bytes 73736 | tf_op jit(solution)/shard_map/ppermute | solution.py:510
  31.7 0.6 collective-permute-done.9.refs_2_
  32.3 2.4 %collective-permute-done.10.refs_3_ = bf16[16,768]{1,0:T(8,128)(2,1)S(1)} collective-permute-done((bf16[16,768]{1,0:T(8,128)(2,1)S(1)}, bf16[16,768]{1,0:T(8,128)(2,1)S(1)}, u32[]{:S(2)}, u32[]{:S(2)}) %collective-permute-start.10) | collective-permute-done | bytes 24608 | tf_op jit(solution)/shard_map/ppermute | solution.py:510
  34.8 1.4 %collective-permute-start.12 = (bf16[64,768]{1,0:T(8,128)(2,1)S(1)}, bf16[64,768]{1,0:T(8,128)(2,1)S(1)}, u32[]{:S(2)}, u32[]{:S(2)}) collective-permute-start(bf16[64,768]{1,0:T(8,128)(2,1)S(1)} %shard_map.199.refs_0_), channel_id=1, source_target_pairs={{0,4},{4,8},{8,12},{12,0},{1,5},{5,9},{9,13},{13,1},{2,6},{6,10},{... | collective-permute-start | bytes 294920 | tf_op jit(solution)/shard_map/ppermute | solution.py:620
  36.1 1.0 %collective-permute-start.13 = (bf16[64,768]{1,0:T(8,128)(2,1)S(1)}, bf16[64,768]{1,0:T(8,128)(2,1)S(1)}, u32[]{:S(2)}, u32[]{:S(2)}) collective-permute-start(bf16[64,768]{1,0:T(8,128)(2,1)S(1)} %shard_map.199.refs_0_), channel_id=1, source_target_pairs={{0,8},{4,12},{8,0},{12,4},{1,9},{5,13},{9,1},{13,5},{2,10},{6,14},... | collective-permute-start | bytes 294920 | tf_op jit(solution)/shard_map/ppermute | solution.py:620
  37.1 0.3 collective-permute-start.14
  37.4 1.2 %collective-permute-start.20 = (f32[200,128]{1,0:T(8,128)S(1)}, f32[200,128]{1,0:T(8,128)S(1)}, u32[]{:S(2)}, u32[]{:S(2)}) collective-permute-start(f32[200,128]{1,0:T(8,128)S(1)} %get-tuple-element.91), channel_id=1, source_target_pairs={{0,1},{1,0},{2,3},{3,2},{4,5},{5,4},{6,7},{7,6},{8,9},{9,8},{10,11... | collective-permute-start | bytes 307208 | tf_op jit(solution)/shard_map/ppermute | solution.py:505
  38.6 1.3 %collective-permute-start.21 = (f32[200,128]{1,0:T(8,128)S(1)}, f32[200,128]{1,0:T(8,128)S(1)}, u32[]{:S(2)}, u32[]{:S(2)}) collective-permute-start(f32[200,128]{1,0:T(8,128)S(1)} %get-tuple-element.92), channel_id=1, source_target_pairs={{1,2},{3,4},{5,6},{7,8},{9,10},{11,12},{13,14},{2,1},{4,3},{6,5},{... | collective-permute-start | bytes 307208 | tf_op jit(solution)/shard_map/ppermute | solution.py:504
  39.8 1.0 %shard_map.200 = (bf16[64,768]{1,0:T(8,128)(2,1)S(1)}, bf16[64,1536]{1,0:T(8,128)(2,1)S(1)}, f32[16,64,256]{2,1,0:T(8,128)S(1)}) custom-call(bf16[64,768]{1,0:T(8,128)(2,1)S(1)} %shard_map.199.refs_0_, f32[16,16,256]{2,1,0:T(8,128)} %refs_1_.5, f32[16,16,256]{2,1,0:T(8,128)S(1)} %collective-permute-done.4.refs_12_.refs_2_, ...), custom_call_target="tpu_custom_call" | custom-call | tf_op jit(solution)/shard_map/pallas_call | solution.py:68
  40.8 0.0 copy-start.2
  40.9 3.3 %collective-permute-done.13.refs_4_ = bf16[64,768]{1,0:T(8,128)(2,1)S(1)} collective-permute-done((bf16[64,768]{1,0:T(8,128)(2,1)S(1)}, bf16[64,768]{1,0:T(8,128)(2,1)S(1)}, u32[]{:S(2)}, u32[]{:S(2)}) %collective-permute-start.13) | collective-permute-done | bytes 98336 | tf_op jit(solution)/shard_map/ppermute | solution.py:620
  44.2 2.5 %collective-permute-done.14.refs_5_ = bf16[64,768]{1,0:T(8,128)(2,1)S(1)} collective-permute-done((bf16[64,768]{1,0:T(8,128)(2,1)S(1)}, bf16[64,768]{1,0:T(8,128)(2,1)S(1)}, u32[]{:S(2)}, u32[]{:S(2)}) %collective-permute-start.14) | collective-permute-done | bytes 98336 | tf_op jit(solution)/shard_map/ppermute | solution.py:620
  46.7 1.8 %shard_map.201 = (bf16[16,768]{1,0:T(8,128)(2,1)S(1)}, bf16[16,768]{1,0:T(8,128)(2,1)S(1)}, bf16[16,768]{1,0:T(8,128)(2,1)S(1)}, bf16[16,768]{1,0:T(8,128)(2,1)S(1)}) custom-call(bf16[64,768]{1,0:T(8,128)(2,1)S(1)} %get-tuple-element.83.refs_0_, bf16[64,1536]{1,0:T(8,128)(2,1)S(1)} %get-tuple-element.84.refs_1_, ...), custom_call_target="tpu_custom_call" | custom-call | tf_op jit(solution)/shard_map/pallas_call | solution.py:68
  48.5 0.0 copy-start.3
  48.5 0.6 collective-permute-start.15
  49.1 0.2 collective-permute-start.16
  49.2 1.6 %collective-permute-start.17 = (bf16[16,768]{1,0:T(8,128)(2,1)S(1)}, bf16[16,768]{1,0:T(8,128)(2,1)S(1)}, u32[]{:S(2)}, u32[]{:S(2)}) collective-permute-start(bf16[16,768]{1,0:T(8,128)(2,1)S(1)} %get-tuple-element.89), channel_id=1, source_target_pairs={{0,3},{1,2},{2,1},{3,0},{4,7},{5,6},{6,5},{7,4},{8,11},{9,10},{10,... | collective-permute-start | bytes 73736 | tf_op jit(solution)/shard_map/ppermute | solution.py:510
  50.8 1.0 %collective-permute-done.16.refs_3_ = bf16[16,768]{1,0:T(8,128)(2,1)S(1)} collective-permute-done((bf16[16,768]{1,0:T(8,128)(2,1)S(1)}, bf16[16,768]{1,0:T(8,128)(2,1)S(1)}, u32[]{:S(2)}, u32[]{:S(2)}) %collective-permute-start.16) | collective-permute-done | bytes 24608 | tf_op jit(solution)/shard_map/ppermute | solution.py:510
  51.7 1.0 %collective-permute-done.17.refs_4_ = bf16[16,768]{1,0:T(8,128)(2,1)S(1)} collective-permute-done((bf16[16,768]{1,0:T(8,128)(2,1)S(1)}, bf16[16,768]{1,0:T(8,128)(2,1)S(1)}, u32[]{:S(2)}, u32[]{:S(2)}) %collective-permute-start.17) | collective-permute-done | bytes 24608 | tf_op jit(solution)/shard_map/ppermute | solution.py:510
  52.7 0.7 shard_map.202
  53.4 0.5 collective-permute-start.18
  53.8 1.1 %collective-permute-start.19 = (bf16[64,128]{1,0:T(8,128)(2,1)S(1)}, bf16[64,128]{1,0:T(8,128)(2,1)S(1)}, u32[]{:S(2)}, u32[]{:S(2)}) collective-permute-start(bf16[64,128]{1,0:T(8,128)(2,1)S(1)} %get-tuple-element.90.refs_2_), channel_id=1, source_target_pairs={{1,2},{3,4},{5,6},{7,8},{9,10},{11,12},{13,14},{2,1},{4,3},{6,5},{... | collective-permute-start | bytes 49160 | tf_op jit(solution)/shard_map/ppermute | solution.py:504
  54.9 2.4 %collective-permute-done.19.refs_4_ = bf16[64,128]{1,0:T(8,128)(2,1)S(1)} collective-permute-done((bf16[64,128]{1,0:T(8,128)(2,1)S(1)}, bf16[64,128]{1,0:T(8,128)(2,1)S(1)}, u32[]{:S(2)}, u32[]{:S(2)}) %collective-permute-start.19) | collective-permute-done | bytes 16416 | tf_op jit(solution)/shard_map/ppermute | solution.py:504
  57.3 0.8 %shard_map.203 = (f32[512,128]{1,0:T(8,128)S(1)}, bf16[512,128]{1,0:T(8,128)(2,1)S(1)}, bf16[512,256]{1,0:T(8,128)(2,1)S(1)}, bf16[192,256]{1,0:T(8,128)(2,1)S(1)}, bf16[192,256]{1,0:T(8,128)(2,1)S(1)}) custom-call(f32[512,128]{1,0:T(8,128)S(1)} %get-tuple-element.73.refs_0_, s32[1,128]{1,0:T(1,128)S(1)} %get-tuple-element.70.refs_10_.refs_1_, ...), custom_call_target="tpu_custom_call" | custom-call | tf_op jit(solution)/shard_map/pallas_call | solution.py:68
  58.1 2.0 %shard_map.204 = (f32[512,128]{1,0:T(8,128)S(1)}, bf16[512,128]{1,0:T(8,128)(2,1)S(1)}, bf16[512,256]{1,0:T(8,128)(2,1)S(1)}, bf16[192,256]{1,0:T(8,128)(2,1)S(1)}, bf16[192,256]{1,0:T(8,128)(2,1)S(1)}) custom-call(bf16[512,128]{1,0:T(8,128)(2,1)S(1)} %get-tuple-element.93.refs_0_, bf16[512,256]{1,0:T(8,128)(2,1)S(1)} %get-tuple-element.94.refs_1_, ...), custom_call_target="tpu_custom_call" | custom-call | tf_op jit(solution)/shard_map/pallas_call | solution.py:68
  60.1 0.8 %collective-permute-start.22 = (bf16[192,256]{1,0:T(8,128)(2,1)S(1)}, bf16[192,256]{1,0:T(8,128)(2,1)S(1)}, u32[]{:S(2)}, u32[]{:S(2)}) collective-permute-start(bf16[192,256]{1,0:T(8,128)(2,1)S(1)} %get-tuple-element.100), channel_id=1, source_target_pairs={{0,1},{1,0},{2,3},{3,2},{4,5},{5,4},{6,7},{7,6},{8,9},{9,8},{10,11... | collective-permute-start | bytes 294920 | tf_op jit(solution)/shard_map/ppermute | solution.py:505
  60.9 1.3 %collective-permute-start.23 = (bf16[192,256]{1,0:T(8,128)(2,1)S(1)}, bf16[192,256]{1,0:T(8,128)(2,1)S(1)}, u32[]{:S(2)}, u32[]{:S(2)}) collective-permute-start(bf16[192,256]{1,0:T(8,128)(2,1)S(1)} %get-tuple-element.101), channel_id=1, source_target_pairs={{1,2},{3,4},{5,6},{7,8},{9,10},{11,12},{13,14},{2,1},{4,3},{6,5},{... | collective-permute-start | bytes 294920 | tf_op jit(solution)/shard_map/ppermute | solution.py:504
  62.2 3.8 %collective-permute-done.23.refs_3_ = bf16[192,256]{1,0:T(8,128)(2,1)S(1)} collective-permute-done((bf16[192,256]{1,0:T(8,128)(2,1)S(1)}, bf16[192,256]{1,0:T(8,128)(2,1)S(1)}, u32[]{:S(2)}, u32[]{:S(2)}) %collective-permute-start.23) | collective-permute-done | bytes 98336 | tf_op jit(solution)/shard_map/ppermute | solution.py:504
  66.0 2.6 %shard_map.205 = (f32[3,4,128]{2,1,0:T(4,128)}, f32[4,16,768]{2,1,0:T(8,128)}) custom-call(bf16[512,128]{1,0:T(8,128)(2,1)S(1)} %get-tuple-element.98.refs_0_, bf16[512,256]{1,0:T(8,128)(2,1)S(1)} %get-tuple-element.99.refs_1_, bf16[192,256]{1,0:T(8,128)(2,1)S(1)} %collective-permute-done.22.refs_2_, bf16[192,256]{1,0:T(8,128)(2,1)S(1)} %collective-permute-done.23.refs_3_, ...), custom_call_target="tpu_custom_call" | custom-call | tf_op jit(solution)/shard_map/pallas_call | solution.py:68
  (24 shorter events, 0.1 us)
Async XLA Ops:
  2.5 18.4 %collective-permute-start.4 = (f32[16,16,256]{2,1,0:T(8,128)}, f32[16,16,256]{2,1,0:T(8,128)S(1)}, u32[]{:S(2)}, u32[]{:S(2)}) collective-permute-start(f32[16,16,256]{2,1,0:T(8,128)} %refs_1_.5), channel_id=1, source_target_pairs={{0,1},{1,0},{2,3},{3,2},{4,5},{5,4},{6,7},{7,6},{8,9},{9,8},{10,11... | collective-permute-start | bytes 786440 | tf_op jit(solution)/shard_map/ppermute | solution.py:510
  3.2 17.7 %collective-permute-start.5 = (f32[16,16,256]{2,1,0:T(8,128)}, f32[16,16,256]{2,1,0:T(8,128)S(1)}, u32[]{:S(2)}, u32[]{:S(2)}) collective-permute-start(f32[16,16,256]{2,1,0:T(8,128)} %refs_1_.5), channel_id=1, source_target_pairs={{0,2},{1,3},{2,0},{3,1},{4,6},{5,7},{6,4},{7,5},{8,10},{9,11},{10,... | collective-permute-start | bytes 786440 | tf_op jit(solution)/shard_map/ppermute | solution.py:510
  4.5 2.4 %collective-permute-start = (bf16[192,256]{1,0:T(8,128)(2,1)S(1)}, bf16[192,256]{1,0:T(8,128)(2,1)S(1)}, u32[]{:S(2)}, u32[]{:S(2)}) collective-permute-start(bf16[192,256]{1,0:T(8,128)(2,1)S(1)} %get-tuple-element.56), channel_id=1, source_target_pairs={{0,1},{1,0},{2,3},{3,2},{4,5},{5,4},{6,7},{7,6},{8,9},{9,8},{10,11... | collective-permute-start | bytes 294920 | tf_op jit(solution)/shard_map/ppermute | solution.py:505
  4.8 8.7 %collective-permute-start.1 = (bf16[192,256]{1,0:T(8,128)(2,1)S(1)}, bf16[192,256]{1,0:T(8,128)(2,1)S(1)}, u32[]{:S(2)}, u32[]{:S(2)}) collective-permute-start(bf16[192,256]{1,0:T(8,128)(2,1)S(1)} %get-tuple-element.57), channel_id=1, source_target_pairs={{1,2},{3,4},{5,6},{7,8},{9,10},{11,12},{13,14},{2,1},{4,3},{6,5},{... | collective-permute-start | bytes 294920 | tf_op jit(solution)/shard_map/ppermute | solution.py:504
  5.1 34.7 %copy-start = (bf16[768,2304]{1,0:T(8,128)(2,1)S(1)}, bf16[768,2304]{1,0:T(8,128)(2,1)}, u32[]{:S(2)}) copy-start(bf16[768,2304]{1,0:T(8,128)(2,1)} %refs_6_.4) | copy-start | bytes 10616836
  15.6 2.0 %collective-permute-start.2 = (bf16[192,256]{1,0:T(8,128)(2,1)S(1)}, bf16[192,256]{1,0:T(8,128)(2,1)S(1)}, u32[]{:S(2)}, u32[]{:S(2)}) collective-permute-start(bf16[192,256]{1,0:T(8,128)(2,1)S(1)} %get-tuple-element.66), channel_id=1, source_target_pairs={{0,1},{1,0},{2,3},{3,2},{4,5},{5,4},{6,7},{7,6},{8,9},{9,8},{10,11... | collective-permute-start | bytes 294920 | tf_op jit(solution)/shard_map/ppermute | solution.py:505
  15.7 5.2 %collective-permute-start.3 = (bf16[192,256]{1,0:T(8,128)(2,1)S(1)}, bf16[192,256]{1,0:T(8,128)(2,1)S(1)}, u32[]{:S(2)}, u32[]{:S(2)}) collective-permute-start(bf16[192,256]{1,0:T(8,128)(2,1)S(1)} %get-tuple-element.67), channel_id=1, source_target_pairs={{1,2},{3,4},{5,6},{7,8},{9,10},{11,12},{13,14},{2,1},{4,3},{6,5},{... | collective-permute-start | bytes 294920 | tf_op jit(solution)/shard_map/ppermute | solution.py:504
  23.2 15.3 %collective-permute-start.11 = (f32[16,16,256]{2,1,0:T(8,128)S(1)}, f32[16,16,256]{2,1,0:T(8,128)S(1)}, u32[]{:S(2)}, u32[]{:S(2)}) collective-permute-start(f32[16,16,256]{2,1,0:T(8,128)S(1)} %collective-permute-done.5.refs_13_.refs_3_), channel_id=1, source_target_pairs={{0,1},{1,0},{2,3},{3,2},{4,5},{5,4},{6,7},{7,6},{8,9},{9,8},{10,11... | collective-permute-start | bytes 786440 | tf_op jit(solution)/shard_map/ppermute | solution.py:510
  23.6 1.8 %collective-permute-start.6 = (bf16[64,896]{1,0:T(8,128)(2,1)S(1)}, bf16[64,896]{1,0:T(8,128)(2,1)S(1)}, u32[]{:S(2)}, u32[]{:S(2)}) collective-permute-start(bf16[64,896]{1,0:T(8,128)(2,1)S(1)} %get-tuple-element.75), channel_id=1, source_target_pairs={{0,1},{1,0},{2,3},{3,2},{4,5},{5,4},{6,7},{7,6},{8,9},{9,8},{10,11... | collective-permute-start | bytes 344072 | tf_op jit(solution)/shard_map/ppermute | solution.py:505
  23.8 5.4 %collective-permute-start.7 = (bf16[64,896]{1,0:T(8,128)(2,1)S(1)}, bf16[64,896]{1,0:T(8,128)(2,1)S(1)}, u32[]{:S(2)}, u32[]{:S(2)}) collective-permute-start(bf16[64,896]{1,0:T(8,128)(2,1)S(1)} %get-tuple-element.76), channel_id=1, source_target_pairs={{1,2},{3,4},{5,6},{7,8},{9,10},{11,12},{13,14},{2,1},{4,3},{6,5},{... | collective-permute-start | bytes 344072 | tf_op jit(solution)/shard_map/ppermute | solution.py:504
  29.5 2.2 %collective-permute-start.8 = (bf16[16,768]{1,0:T(8,128)(2,1)S(1)}, bf16[16,768]{1,0:T(8,128)(2,1)S(1)}, u32[]{:S(2)}, u32[]{:S(2)}) collective-permute-start(bf16[16,768]{1,0:T(8,128)(2,1)S(1)} %get-tuple-element.79), channel_id=1, source_target_pairs={{0,1},{1,0},{2,3},{3,2},{4,5},{5,4},{6,7},{7,6},{8,9},{9,8},{10,11... | collective-permute-start | bytes 73736 | tf_op jit(solution)/shard_map/ppermute | solution.py:510
  29.7 2.7 %collective-permute-start.9 = (bf16[16,768]{1,0:T(8,128)(2,1)S(1)}, bf16[16,768]{1,0:T(8,128)(2,1)S(1)}, u32[]{:S(2)}, u32[]{:S(2)}) collective-permute-start(bf16[16,768]{1,0:T(8,128)(2,1)S(1)} %get-tuple-element.80), channel_id=1, source_target_pairs={{0,2},{1,3},{2,0},{3,1},{4,6},{5,7},{6,4},{7,5},{8,10},{9,11},{10,... | collective-permute-start | bytes 73736 | tf_op jit(solution)/shard_map/ppermute | solution.py:510
  31.0 3.8 %collective-permute-start.10 = (bf16[16,768]{1,0:T(8,128)(2,1)S(1)}, bf16[16,768]{1,0:T(8,128)(2,1)S(1)}, u32[]{:S(2)}, u32[]{:S(2)}) collective-permute-start(bf16[16,768]{1,0:T(8,128)(2,1)S(1)} %get-tuple-element.81), channel_id=1, source_target_pairs={{0,3},{1,2},{2,1},{3,0},{4,7},{5,6},{6,5},{7,4},{8,11},{9,10},{10,... | collective-permute-start | bytes 73736 | tf_op jit(solution)/shard_map/ppermute | solution.py:510
  34.8 6.1 %collective-permute-start.12 = (bf16[64,768]{1,0:T(8,128)(2,1)S(1)}, bf16[64,768]{1,0:T(8,128)(2,1)S(1)}, u32[]{:S(2)}, u32[]{:S(2)}) collective-permute-start(bf16[64,768]{1,0:T(8,128)(2,1)S(1)} %shard_map.199.refs_0_), channel_id=1, source_target_pairs={{0,4},{4,8},{8,12},{12,0},{1,5},{5,9},{9,13},{13,1},{2,6},{6,10},{... | collective-permute-start | bytes 294920 | tf_op jit(solution)/shard_map/ppermute | solution.py:620
  36.1 8.1 %collective-permute-start.13 = (bf16[64,768]{1,0:T(8,128)(2,1)S(1)}, bf16[64,768]{1,0:T(8,128)(2,1)S(1)}, u32[]{:S(2)}, u32[]{:S(2)}) collective-permute-start(bf16[64,768]{1,0:T(8,128)(2,1)S(1)} %shard_map.199.refs_0_), channel_id=1, source_target_pairs={{0,8},{4,12},{8,0},{12,4},{1,9},{5,13},{9,1},{13,5},{2,10},{6,14},... | collective-permute-start | bytes 294920 | tf_op jit(solution)/shard_map/ppermute | solution.py:620
  37.1 9.6 %collective-permute-start.14 = (bf16[64,768]{1,0:T(8,128)(2,1)S(1)}, bf16[64,768]{1,0:T(8,128)(2,1)S(1)}, u32[]{:S(2)}, u32[]{:S(2)}) collective-permute-start(bf16[64,768]{1,0:T(8,128)(2,1)S(1)} %shard_map.199.refs_0_), channel_id=1, source_target_pairs={{0,12},{4,0},{8,4},{12,8},{1,13},{5,1},{9,5},{13,9},{2,14},{6,2},{... | collective-permute-start | bytes 294920 | tf_op jit(solution)/shard_map/ppermute | solution.py:620
  37.4 17.6 %collective-permute-start.20 = (f32[200,128]{1,0:T(8,128)S(1)}, f32[200,128]{1,0:T(8,128)S(1)}, u32[]{:S(2)}, u32[]{:S(2)}) collective-permute-start(f32[200,128]{1,0:T(8,128)S(1)} %get-tuple-element.91), channel_id=1, source_target_pairs={{0,1},{1,0},{2,3},{3,2},{4,5},{5,4},{6,7},{7,6},{8,9},{9,8},{10,11... | collective-permute-start | bytes 307208 | tf_op jit(solution)/shard_map/ppermute | solution.py:505
  38.6 16.4 %collective-permute-start.21 = (f32[200,128]{1,0:T(8,128)S(1)}, f32[200,128]{1,0:T(8,128)S(1)}, u32[]{:S(2)}, u32[]{:S(2)}) collective-permute-start(f32[200,128]{1,0:T(8,128)S(1)} %get-tuple-element.92), channel_id=1, source_target_pairs={{1,2},{3,4},{5,6},{7,8},{9,10},{11,12},{13,14},{2,1},{4,3},{6,5},{... | collective-permute-start | bytes 307208 | tf_op jit(solution)/shard_map/ppermute | solution.py:504
  40.8 11.9 %copy-start.1 = (bf16[768,768]{1,0:T(8,128)(2,1)S(1)}, bf16[768,768]{1,0:T(8,128)(2,1)}, u32[]{:S(2)}) copy-start(bf16[768,768]{1,0:T(8,128)(2,1)} %refs_5_.7) | copy-start | bytes 3538948
  40.8 11.9 %copy-start.2 = (bf16[768,128]{1,0:T(8,128)(2,1)S(1)}, bf16[768,128]{1,0:T(8,128)(2,1)}, u32[]{:S(2)}) copy-start(bf16[768,128]{1,0:T(8,128)(2,1)} %refs_6_.5) | copy-start | bytes 589828
  48.5 17.5 %copy-start.3 = (f32[4,3,128]{2,0,1:T(4,128)S(1)}, f32[4,3,128]{2,0,1:T(4,128)}, u32[]{:S(2)}) copy-start(f32[4,3,128]{2,0,1:T(4,128)} %param.20) | copy-start | bytes 18436
  48.5 17.5 %copy-start.4 = (f32[3,128]{1,0:T(4,128)S(1)}, f32[3,128]{1,0:T(4,128)}, u32[]{:S(2)}) copy-start(f32[3,128]{1,0:T(4,128)} %refs_11_.1) | copy-start | bytes 4612
  48.5 17.5 %copy-start.5 = (bf16[3,128]{1,0:T(4,128)(2,1)S(1)}, bf16[3,128]{1,0:T(4,128)(2,1)}, u32[]{:S(2)}) copy-start(bf16[3,128]{1,0:T(4,128)(2,1)} %refs_9_.3) | copy-start | bytes 2308
  48.5 2.3 %collective-permute-start.15 = (bf16[16,768]{1,0:T(8,128)(2,1)S(1)}, bf16[16,768]{1,0:T(8,128)(2,1)S(1)}, u32[]{:S(2)}, u32[]{:S(2)}) collective-permute-start(bf16[16,768]{1,0:T(8,128)(2,1)S(1)} %get-tuple-element.87), channel_id=1, source_target_pairs={{0,1},{1,0},{2,3},{3,2},{4,5},{5,4},{6,7},{7,6},{8,9},{9,8},{10,11... | collective-permute-start | bytes 73736 | tf_op jit(solution)/shard_map/ppermute | solution.py:510
  49.1 2.7 %collective-permute-start.16 = (bf16[16,768]{1,0:T(8,128)(2,1)S(1)}, bf16[16,768]{1,0:T(8,128)(2,1)S(1)}, u32[]{:S(2)}, u32[]{:S(2)}) collective-permute-start(bf16[16,768]{1,0:T(8,128)(2,1)S(1)} %get-tuple-element.88), channel_id=1, source_target_pairs={{0,2},{1,3},{2,0},{3,1},{4,6},{5,7},{6,4},{7,5},{8,10},{9,11},{10,... | collective-permute-start | bytes 73736 | tf_op jit(solution)/shard_map/ppermute | solution.py:510
  49.2 3.5 %collective-permute-start.17 = (bf16[16,768]{1,0:T(8,128)(2,1)S(1)}, bf16[16,768]{1,0:T(8,128)(2,1)S(1)}, u32[]{:S(2)}, u32[]{:S(2)}) collective-permute-start(bf16[16,768]{1,0:T(8,128)(2,1)S(1)} %get-tuple-element.89), channel_id=1, source_target_pairs={{0,3},{1,2},{2,1},{3,0},{4,7},{5,6},{6,5},{7,4},{8,11},{9,10},{10,... | collective-permute-start | bytes 73736 | tf_op jit(solution)/shard_map/ppermute | solution.py:510
  53.4 1.6 %collective-permute-start.18 = (bf16[64,128]{1,0:T(8,128)(2,1)S(1)}, bf16[64,128]{1,0:T(8,128)(2,1)S(1)}, u32[]{:S(2)}, u32[]{:S(2)}) collective-permute-start(bf16[64,128]{1,0:T(8,128)(2,1)S(1)} %get-tuple-element.90.refs_2_), channel_id=1, source_target_pairs={{0,1},{1,0},{2,3},{3,2},{4,5},{5,4},{6,7},{7,6},{8,9},{9,8},{10,11... | collective-permute-start | bytes 49160 | tf_op jit(solution)/shard_map/ppermute | solution.py:505
  53.8 3.5 %collective-permute-start.19 = (bf16[64,128]{1,0:T(8,128)(2,1)S(1)}, bf16[64,128]{1,0:T(8,128)(2,1)S(1)}, u32[]{:S(2)}, u32[]{:S(2)}) collective-permute-start(bf16[64,128]{1,0:T(8,128)(2,1)S(1)} %get-tuple-element.90.refs_2_), channel_id=1, source_target_pairs={{1,2},{3,4},{5,6},{7,8},{9,10},{11,12},{13,14},{2,1},{4,3},{6,5},{... | collective-permute-start | bytes 49160 | tf_op jit(solution)/shard_map/ppermute | solution.py:504
  60.1 2.1 %collective-permute-start.22 = (bf16[192,256]{1,0:T(8,128)(2,1)S(1)}, bf16[192,256]{1,0:T(8,128)(2,1)S(1)}, u32[]{:S(2)}, u32[]{:S(2)}) collective-permute-start(bf16[192,256]{1,0:T(8,128)(2,1)S(1)} %get-tuple-element.100), channel_id=1, source_target_pairs={{0,1},{1,0},{2,3},{3,2},{4,5},{5,4},{6,7},{7,6},{8,9},{9,8},{10,11... | collective-permute-start | bytes 294920 | tf_op jit(solution)/shard_map/ppermute | solution.py:505
  60.9 5.1 %collective-permute-start.23 = (bf16[192,256]{1,0:T(8,128)(2,1)S(1)}, bf16[192,256]{1,0:T(8,128)(2,1)S(1)}, u32[]{:S(2)}, u32[]{:S(2)}) collective-permute-start(bf16[192,256]{1,0:T(8,128)(2,1)S(1)} %get-tuple-element.101), channel_id=1, source_target_pairs={{1,2},{3,4},{5,6},{7,8},{9,10},{11,12},{13,14},{2,1},{4,3},{6,5},{... | collective-permute-start | bytes 294920 | tf_op jit(solution)/shard_map/ppermute | solution.py:504

commit v8 on v7

--- a/solution.py
+++ b/solution.py
@@ -7,6 +7,7 @@
 from jax.experimental.pallas import tpu as pltpu
 from jax.sharding import Mesh
 from jax.sharding import PartitionSpec as P
+
 
 QUERY_BLOCK = 32
 KEY_WINDOW = 128
@@ -579,11 +580,6 @@
 
     for layer in range(ENC_LAYERS - 1):
         rims = swap(rims, count)
-        if layer == 0:
-            held_bias, _ = lax.optimization_barrier((pair_bias, stream))
-            biases = [pair_bias]
-            for k in (1, 2):
-                biases.append(toward(held_bias, k, samples))
         stream, q, kv, *rims = block(layer, q, kv, rims, stream)
     rims = swap(rims, count)
     lanes = width + COUNT_LANES
@@ -592,15 +588,10 @@
     encoded, mid, first, second, *stream_rims = call(
         functools.partial(pool_kernel, layer=ENC_LAYERS - 1, tokens=tokens, **sizes),
         (atom_outs[0], struct((held + tokens, lanes), F32), edge, edge, stream_rim, stream_rim),
-        [VM] * 14,
-        (
-            q, kv, *rims, stream, bias, *stacks, w_pool, atom_token, token_single,
-            *biases[1:3],
-        ),
+        [VM] * 12,
+        (q, kv, *rims, stream, bias, *stacks, w_pool, atom_token, token_single),
         scratch + [pltpu.VMEM((samples, 3 * tokens, lanes), F32)],
     )
-    passed, _ = lax.optimization_barrier((biases[2], mid))
-    biases.append(toward(passed, 1, samples))
     rims = swap((first, second), count)
     piece = struct((tokens, width), BF)
     state, *sends = call(
@@ -610,6 +601,10 @@
         [pltpu.VMEM((samples, tokens, width), BF)],
     )
     got = across(sends[1:], samples)
+    held_bias, _ = lax.optimization_barrier((pair_bias, state))
+    biases = [pair_bias]
+    for k in (1, 2):
+        biases.append(toward(held_bias, k, samples))
     normal = call(
         functools.partial(plane_kernel, samples=samples, tokens=tokens),
         struct((held, width), BF), [VM] * samples, (sends[0], *got),
@@ -619,6 +614,8 @@
         shift = [(i, (i + k) % planes) for i in range(planes)]
         gathered.append(lax.ppermute(normal, "z", shift))
     stream_rims = swap(stream_rims, count)
+    passed, _ = lax.optimization_barrier((biases[2], normal))
+    biases.append(toward(passed, 1, samples))
     every = planes * held
     q_own, kv_own, bias_all = call(
         functools.partial(token_own_kernel, samples=samples, tokens=tokens),

time: 68.9 us -> 68 us (0.987)
  the two profiles are of different devices: /device:TPU:11 before, /device:TPU:9 now
where the time goes in v8:
time: 68 us; the launch traced here: 67.8 us
  waiting for transfers between devices  31.6 us (46%)
  starting transfers between devices  18.3 us (27%)
  Pallas kernels  17 us (25%)
  between operations  0.95 us (1%)
    pallas_call x12, Pallas kernels, call(): pl.pallas_call(body, out_shape=out_shape, in_specs=specs, out_specs=out_s...  17 us
    ppermute x6, waiting for transfers between devices, swap(): second = lax.ppermute(second, ('groups',) + SEQ, upper)  16.7 us
    ppermute x9, waiting for transfers between devices, toward(): return lax.ppermute(array, 'p', [(i, i ^ k) for i in range(count)])  8.67 us
    ppermute x3, waiting for transfers between devices, shards(): gathered.append(lax.ppermute(normal, 'z', shift))  6.13 us
    ppermute x6, starting transfers between devices, swap(): second = lax.ppermute(second, ('groups',) + SEQ, upper)  5.73 us
    ppermute x9, starting transfers between devices, toward(): return lax.ppermute(array, 'p', [(i, i ^ k) for i in range(count)])  5.31 us
    ppermute x3, starting transfers between devices, shards(): gathered.append(lax.ppermute(normal, 'z', shift))  3.78 us
    ppermute x6, starting transfers between devices, swap(): first = lax.ppermute(first, SEQ, lower)  3.47 us
  transfers between devices with their start and end apart: 24, of which 11 were waited for; matrix products, arithmetic and copies ran while one was open for 0% of the time, Pallas kernels for 8%

profile of v8, /device:TPU:9, one launch (start us, length us, event | category | flops | bytes accessed | tf_op | source)
XLA Modules:
  0.0 67.8 jit_solution(9050536949966601386)
XLA Ops:
  0.6 1.9 %shard_map.194 = (f32[512,128]{1,0:T(8,128)S(1)}, bf16[512,128]{1,0:T(8,128)(2,1)S(1)}, bf16[512,256]{1,0:T(8,128)(2,1)S(1)}, bf16[192,256]{1,0:T(8,128)(2,1)S(1)}, bf16[192,256]{1,0:T(8,128)(2,1)S(1)}) custom-call(s32[4]{0:T(128)} %refs_10_.1, f32[3,128]{1,0:T(4,128)} %refs_11_.1, f32[3,4,128]{2,1,0:T(4,128)} %bitcast.4, bf16[128,128]{1,0:T(8,128)(2,1)} %refs_3_.2, ...), custom_call_target="tpu_custom_call" | custom-call | tf_op jit(solution)/shard_map/pallas_call | solution.py:69
  2.5 0.7 %collective-permute-start = (bf16[192,256]{1,0:T(8,128)(2,1)S(1)}, bf16[192,256]{1,0:T(8,128)(2,1)S(1)}, u32[]{:S(2)}, u32[]{:S(2)}) collective-permute-start(bf16[192,256]{1,0:T(8,128)(2,1)S(1)} %get-tuple-element.56), channel_id=1, source_target_pairs={{0,1},{1,0},{2,3},{3,2},{4,5},{5,4},{6,7},{7,6},{8,9},{9,8},{10,11... | collective-permute-start | bytes 294920 | tf_op jit(solution)/shard_map/ppermute | solution.py:506
  3.2 1.2 %collective-permute-start.1 = (bf16[192,256]{1,0:T(8,128)(2,1)S(1)}, bf16[192,256]{1,0:T(8,128)(2,1)S(1)}, u32[]{:S(2)}, u32[]{:S(2)}) collective-permute-start(bf16[192,256]{1,0:T(8,128)(2,1)S(1)} %get-tuple-element.57), channel_id=1, source_target_pairs={{1,2},{3,4},{5,6},{7,8},{9,10},{11,12},{13,14},{2,1},{4,3},{6,5},{... | collective-permute-start | bytes 294920 | tf_op jit(solution)/shard_map/ppermute | solution.py:505
  4.4 1.7 %shard_map.195 = (f32[4,128,128]{2,1,0:T(8,128)S(1)}, bf16[4,128,128]{2,1,0:T(8,128)(2,1)S(1)}, bf16[4,128,512]{2,1,0:T(8,128)(2,1)S(1)}, bf16[4,256,128]{2,1,0:...) custom-call(s32[2,4]{1,0:T(2,128)} %bitcast.6, ...), custom_call_target="tpu_custom_call" | custom-call | tf_op jit(solution)/shard_map/pallas_call | solution.py:69
  6.2 2.1 %collective-permute-done.1.refs_3_ = bf16[192,256]{1,0:T(8,128)(2,1)S(1)} collective-permute-done((bf16[192,256]{1,0:T(8,128)(2,1)S(1)}, bf16[192,256]{1,0:T(8,128)(2,1)S(1)}, u32[]{:S(2)}, u32[]{:S(2)}) %collective-permute-start.1) | collective-permute-done | bytes 98336 | tf_op jit(solution)/shard_map/ppermute | solution.py:505
  8.3 2.0 %shard_map.196 = (f32[512,128]{1,0:T(8,128)S(1)}, bf16[512,128]{1,0:T(8,128)(2,1)S(1)}, bf16[512,256]{1,0:T(8,128)(2,1)S(1)}, bf16[192,256]{1,0:T(8,128)(2,1)S(1)}, bf16[192,256]{1,0:T(8,128)(2,1)S(1)}) custom-call(bf16[512,128]{1,0:T(8,128)(2,1)S(1)} %get-tuple-element.54.refs_0_, bf16[512,256]{1,0:T(8,128)(2,1)S(1)} %get-tuple-element.55.refs_1_, ...), custom_call_target="tpu_custom_call" | custom-call | tf_op jit(solution)/shard_map/pallas_call | solution.py:69
  10.3 0.1 collective-permute-start.2
  10.4 1.5 %collective-permute-start.3 = (bf16[192,256]{1,0:T(8,128)(2,1)S(1)}, bf16[192,256]{1,0:T(8,128)(2,1)S(1)}, u32[]{:S(2)}, u32[]{:S(2)}) collective-permute-start(bf16[192,256]{1,0:T(8,128)(2,1)S(1)} %get-tuple-element.67), channel_id=1, source_target_pairs={{1,2},{3,4},{5,6},{7,8},{9,10},{11,12},{13,14},{2,1},{4,3},{6,5},{... | collective-permute-start | bytes 294920 | tf_op jit(solution)/shard_map/ppermute | solution.py:505
  11.9 3.7 %collective-permute-done.3.refs_3_ = bf16[192,256]{1,0:T(8,128)(2,1)S(1)} collective-permute-done((bf16[192,256]{1,0:T(8,128)(2,1)S(1)}, bf16[192,256]{1,0:T(8,128)(2,1)S(1)}, u32[]{:S(2)}, u32[]{:S(2)}) %collective-permute-start.3) | collective-permute-done | bytes 98336 | tf_op jit(solution)/shard_map/ppermute | solution.py:505
  15.6 2.3 %shard_map.197 = (f32[512,128]{1,0:T(8,128)S(1)}, f32[80,896]{1,0:T(8,128)S(1)}, bf16[64,896]{1,0:T(8,128)(2,1)S(1)}, bf16[64,896]{1,0:T(8,128)(2,1)S(1)}, f32[2...) custom-call(bf16[512,128]{1,0:T(8,128)(2,1)S(1)} %get-tuple-element.64.refs_0_, ...), custom_call_target="tpu_custom_call" | custom-call | tf_op jit(solution)/shard_map/pallas_call | solution.py:69
  17.9 0.4 collective-permute-start.4
  18.3 0.9 %collective-permute-start.5 = (bf16[64,896]{1,0:T(8,128)(2,1)S(1)}, bf16[64,896]{1,0:T(8,128)(2,1)S(1)}, u32[]{:S(2)}, u32[]{:S(2)}) collective-permute-start(bf16[64,896]{1,0:T(8,128)(2,1)S(1)} %get-tuple-element.75), channel_id=1, source_target_pairs={{1,2},{3,4},{5,6},{7,8},{9,10},{11,12},{13,14},{2,1},{4,3},{6,5},{... | collective-permute-start | bytes 344072 | tf_op jit(solution)/shard_map/ppermute | solution.py:505
  19.3 0.0 collective-permute-done.4.refs_1_
  19.3 4.5 %collective-permute-done.5.refs_2_ = bf16[64,896]{1,0:T(8,128)(2,1)S(1)} collective-permute-done((bf16[64,896]{1,0:T(8,128)(2,1)S(1)}, bf16[64,896]{1,0:T(8,128)(2,1)S(1)}, u32[]{:S(2)}, u32[]{:S(2)}) %collective-permute-start.5) | collective-permute-done | bytes 114720 | tf_op jit(solution)/shard_map/ppermute | solution.py:505
  23.8 0.3 shard_map.198
  24.1 0.4 collective-permute-start.10
  24.5 1.3 %collective-permute-start.7 = (bf16[16,768]{1,0:T(8,128)(2,1)S(1)}, bf16[16,768]{1,0:T(8,128)(2,1)S(1)}, u32[]{:S(2)}, u32[]{:S(2)}) collective-permute-start(bf16[16,768]{1,0:T(8,128)(2,1)S(1)} %get-tuple-element.79), channel_id=1, source_target_pairs={{0,2},{1,3},{2,0},{3,1},{4,6},{5,7},{6,4},{7,5},{8,10},{9,11},{10,... | collective-permute-start | bytes 73736 | tf_op jit(solution)/shard_map/ppermute | solution.py:511
  25.8 0.9 %collective-permute-start.8 = (bf16[16,768]{1,0:T(8,128)(2,1)S(1)}, bf16[16,768]{1,0:T(8,128)(2,1)S(1)}, u32[]{:S(2)}, u32[]{:S(2)}) collective-permute-start(bf16[16,768]{1,0:T(8,128)(2,1)S(1)} %get-tuple-element.80), channel_id=1, source_target_pairs={{0,3},{1,2},{2,1},{3,0},{4,7},{5,6},{6,5},{7,4},{8,11},{9,10},{10,... | collective-permute-start | bytes 73736 | tf_op jit(solution)/shard_map/ppermute | solution.py:511
  26.7 6.0 %collective-permute-done.7.refs_2_ = bf16[16,768]{1,0:T(8,128)(2,1)S(1)} collective-permute-done((bf16[16,768]{1,0:T(8,128)(2,1)S(1)}, bf16[16,768]{1,0:T(8,128)(2,1)S(1)}, u32[]{:S(2)}, u32[]{:S(2)}) %collective-permute-start.7) | collective-permute-done | bytes 24608 | tf_op jit(solution)/shard_map/ppermute | solution.py:511
  32.6 0.6 collective-permute-done.8.refs_3_
  33.3 0.5 collective-permute-start.11
  33.7 1.3 %collective-permute-start.12 = (bf16[64,768]{1,0:T(8,128)(2,1)S(1)}, bf16[64,768]{1,0:T(8,128)(2,1)S(1)}, u32[]{:S(2)}, u32[]{:S(2)}) collective-permute-start(bf16[64,768]{1,0:T(8,128)(2,1)S(1)} %shard_map.199.refs_0_), channel_id=1, source_target_pairs={{0,4},{4,8},{8,12},{12,0},{1,5},{5,9},{9,13},{13,1},{2,6},{6,10},{... | collective-permute-start | bytes 294920 | tf_op jit(solution)/shard_map/ppermute | solution.py:615
  35.0 1.0 %collective-permute-start.13 = (bf16[64,768]{1,0:T(8,128)(2,1)S(1)}, bf16[64,768]{1,0:T(8,128)(2,1)S(1)}, u32[]{:S(2)}, u32[]{:S(2)}) collective-permute-start(bf16[64,768]{1,0:T(8,128)(2,1)S(1)} %shard_map.199.refs_0_), channel_id=1, source_target_pairs={{0,8},{4,12},{8,0},{12,4},{1,9},{5,13},{9,1},{13,5},{2,10},{6,14},... | collective-permute-start | bytes 294920 | tf_op jit(solution)/shard_map/ppermute | solution.py:615
  36.1 1.5 %collective-permute-start.14 = (bf16[64,768]{1,0:T(8,128)(2,1)S(1)}, bf16[64,768]{1,0:T(8,128)(2,1)S(1)}, u32[]{:S(2)}, u32[]{:S(2)}) collective-permute-start(bf16[64,768]{1,0:T(8,128)(2,1)S(1)} %shard_map.199.refs_0_), channel_id=1, source_target_pairs={{0,12},{4,0},{8,4},{12,8},{1,13},{5,1},{9,5},{13,9},{2,14},{6,2},{... | collective-permute-start | bytes 294920 | tf_op jit(solution)/shard_map/ppermute | solution.py:615
  37.5 0.9 %collective-permute-start.20 = (f32[200,128]{1,0:T(8,128)S(1)}, f32[200,128]{1,0:T(8,128)S(1)}, u32[]{:S(2)}, u32[]{:S(2)}) collective-permute-start(f32[200,128]{1,0:T(8,128)S(1)} %get-tuple-element.91), channel_id=1, source_target_pairs={{0,1},{1,0},{2,3},{3,2},{4,5},{5,4},{6,7},{7,6},{8,9},{9,8},{10,11... | collective-permute-start | bytes 307208 | tf_op jit(solution)/shard_map/ppermute | solution.py:506
  38.5 1.0 %shard_map.200 = (bf16[64,768]{1,0:T(8,128)(2,1)S(1)}, bf16[64,1536]{1,0:T(8,128)(2,1)S(1)}, f32[16,64,256]{2,1,0:T(8,128)S(1)}) custom-call(bf16[64,768]{1,0:T(8,128)(2,1)S(1)} %shard_map.199.refs_0_, f32[16,16,256]{2,1,0:T(8,128)} %refs_1_.5, f32[16,16,256]{2,1,0:T(8,128)S(1)} %collective-permute-done.9.refs_2_, ...), custom_call_target="tpu_custom_call" | custom-call | tf_op jit(solution)/shard_map/pallas_call | solution.py:69
  39.5 0.0 copy-start.1
  39.5 0.0 copy-start.2
  39.5 3.9 %collective-permute-done.13.refs_4_ = bf16[64,768]{1,0:T(8,128)(2,1)S(1)} collective-permute-done((bf16[64,768]{1,0:T(8,128)(2,1)S(1)}, bf16[64,768]{1,0:T(8,128)(2,1)S(1)}, u32[]{:S(2)}, u32[]{:S(2)}) %collective-permute-start.13) | collective-permute-done | bytes 98336 | tf_op jit(solution)/shard_map/ppermute | solution.py:615
  43.4 2.3 %collective-permute-done.14.refs_5_ = bf16[64,768]{1,0:T(8,128)(2,1)S(1)} collective-permute-done((bf16[64,768]{1,0:T(8,128)(2,1)S(1)}, bf16[64,768]{1,0:T(8,128)(2,1)S(1)}, u32[]{:S(2)}, u32[]{:S(2)}) %collective-permute-start.14) | collective-permute-done | bytes 98336 | tf_op jit(solution)/shard_map/ppermute | solution.py:615
  45.7 1.8 %shard_map.201 = (bf16[16,768]{1,0:T(8,128)(2,1)S(1)}, bf16[16,768]{1,0:T(8,128)(2,1)S(1)}, bf16[16,768]{1,0:T(8,128)(2,1)S(1)}, bf16[16,768]{1,0:T(8,128)(2,1)S(1)}) custom-call(bf16[64,768]{1,0:T(8,128)(2,1)S(1)} %get-tuple-element.83.refs_0_, bf16[64,1536]{1,0:T(8,128)(2,1)S(1)} %get-tuple-element.84.refs_1_, ...), custom_call_target="tpu_custom_call" | custom-call | tf_op jit(solution)/shard_map/pallas_call | solution.py:69
  47.5 0.0 copy-start.3
  47.5 0.0 copy-start.4
  47.5 0.5 collective-permute-start.15
  48.0 0.5 collective-permute-start.16
  48.5 1.2 %collective-permute-start.17 = (bf16[16,768]{1,0:T(8,128)(2,1)S(1)}, bf16[16,768]{1,0:T(8,128)(2,1)S(1)}, u32[]{:S(2)}, u32[]{:S(2)}) collective-permute-start(bf16[16,768]{1,0:T(8,128)(2,1)S(1)} %get-tuple-element.89), channel_id=1, source_target_pairs={{0,3},{1,2},{2,1},{3,0},{4,7},{5,6},{6,5},{7,4},{8,11},{9,10},{10,... | collective-permute-start | bytes 73736 | tf_op jit(solution)/shard_map/ppermute | solution.py:511
  49.7 1.0 %collective-permute-done.16.refs_3_ = bf16[16,768]{1,0:T(8,128)(2,1)S(1)} collective-permute-done((bf16[16,768]{1,0:T(8,128)(2,1)S(1)}, bf16[16,768]{1,0:T(8,128)(2,1)S(1)}, u32[]{:S(2)}, u32[]{:S(2)}) %collective-permute-start.16) | collective-permute-done | bytes 24608 | tf_op jit(solution)/shard_map/ppermute | solution.py:511
  50.7 1.1 %collective-permute-done.17.refs_4_ = bf16[16,768]{1,0:T(8,128)(2,1)S(1)} collective-permute-done((bf16[16,768]{1,0:T(8,128)(2,1)S(1)}, bf16[16,768]{1,0:T(8,128)(2,1)S(1)}, u32[]{:S(2)}, u32[]{:S(2)}) %collective-permute-start.17) | collective-permute-done | bytes 24608 | tf_op jit(solution)/shard_map/ppermute | solution.py:511
  51.8 0.7 shard_map.202
  52.5 0.5 collective-permute-start.18
  53.0 0.9 %collective-permute-start.19 = (bf16[64,128]{1,0:T(8,128)(2,1)S(1)}, bf16[64,128]{1,0:T(8,128)(2,1)S(1)}, u32[]{:S(2)}, u32[]{:S(2)}) collective-permute-start(bf16[64,128]{1,0:T(8,128)(2,1)S(1)} %get-tuple-element.90.refs_2_), channel_id=1, source_target_pairs={{1,2},{3,4},{5,6},{7,8},{9,10},{11,12},{13,14},{2,1},{4,3},{6,5},{... | collective-permute-start | bytes 49160 | tf_op jit(solution)/shard_map/ppermute | solution.py:505
  53.9 2.5 %collective-permute-done.19.refs_4_ = bf16[64,128]{1,0:T(8,128)(2,1)S(1)} collective-permute-done((bf16[64,128]{1,0:T(8,128)(2,1)S(1)}, bf16[64,128]{1,0:T(8,128)(2,1)S(1)}, u32[]{:S(2)}, u32[]{:S(2)}) %collective-permute-start.19) | collective-permute-done | bytes 16416 | tf_op jit(solution)/shard_map/ppermute | solution.py:505
  56.4 0.8 %shard_map.203 = (f32[512,128]{1,0:T(8,128)S(1)}, bf16[512,128]{1,0:T(8,128)(2,1)S(1)}, bf16[512,256]{1,0:T(8,128)(2,1)S(1)}, bf16[192,256]{1,0:T(8,128)(2,1)S(1)}, bf16[192,256]{1,0:T(8,128)(2,1)S(1)}) custom-call(f32[512,128]{1,0:T(8,128)S(1)} %get-tuple-element.72.refs_0_, s32[1,128]{1,0:T(1,128)S(1)} %get-tuple-element.70.refs_10_.refs_1_, ...), custom_call_target="tpu_custom_call" | custom-call | tf_op jit(solution)/shard_map/pallas_call | solution.py:69
  57.2 2.0 %shard_map.204 = (f32[512,128]{1,0:T(8,128)S(1)}, bf16[512,128]{1,0:T(8,128)(2,1)S(1)}, bf16[512,256]{1,0:T(8,128)(2,1)S(1)}, bf16[192,256]{1,0:T(8,128)(2,1)S(1)}, bf16[192,256]{1,0:T(8,128)(2,1)S(1)}) custom-call(bf16[512,128]{1,0:T(8,128)(2,1)S(1)} %get-tuple-element.93.refs_0_, bf16[512,256]{1,0:T(8,128)(2,1)S(1)} %get-tuple-element.94.refs_1_, ...), custom_call_target="tpu_custom_call" | custom-call | tf_op jit(solution)/shard_map/pallas_call | solution.py:69
  59.2 0.8 %collective-permute-start.22 = (bf16[192,256]{1,0:T(8,128)(2,1)S(1)}, bf16[192,256]{1,0:T(8,128)(2,1)S(1)}, u32[]{:S(2)}, u32[]{:S(2)}) collective-permute-start(bf16[192,256]{1,0:T(8,128)(2,1)S(1)} %get-tuple-element.100), channel_id=1, source_target_pairs={{0,1},{1,0},{2,3},{3,2},{4,5},{5,4},{6,7},{7,6},{8,9},{9,8},{10,11... | collective-permute-start | bytes 294920 | tf_op jit(solution)/shard_map/ppermute | solution.py:506
  60.0 1.2 %collective-permute-start.23 = (bf16[192,256]{1,0:T(8,128)(2,1)S(1)}, bf16[192,256]{1,0:T(8,128)(2,1)S(1)}, u32[]{:S(2)}, u32[]{:S(2)}) collective-permute-start(bf16[192,256]{1,0:T(8,128)(2,1)S(1)} %get-tuple-element.101), channel_id=1, source_target_pairs={{1,2},{3,4},{5,6},{7,8},{9,10},{11,12},{13,14},{2,1},{4,3},{6,5},{... | collective-permute-start | bytes 294920 | tf_op jit(solution)/shard_map/ppermute | solution.py:505
  61.2 3.9 %collective-permute-done.23.refs_3_ = bf16[192,256]{1,0:T(8,128)(2,1)S(1)} collective-permute-done((bf16[192,256]{1,0:T(8,128)(2,1)S(1)}, bf16[192,256]{1,0:T(8,128)(2,1)S(1)}, u32[]{:S(2)}, u32[]{:S(2)}) %collective-permute-start.23) | collective-permute-done | bytes 98336 | tf_op jit(solution)/shard_map/ppermute | solution.py:505
  65.1 2.6 %shard_map.205 = (f32[3,4,128]{2,1,0:T(4,128)}, f32[4,16,768]{2,1,0:T(8,128)}) custom-call(bf16[512,128]{1,0:T(8,128)(2,1)S(1)} %get-tuple-element.98.refs_0_, bf16[512,256]{1,0:T(8,128)(2,1)S(1)} %get-tuple-element.99.refs_1_, bf16[192,256]{1,0:T(8,128)(2,1)S(1)} %collective-permute-done.22.refs_2_, bf16[192,256]{1,0:T(8,128)(2,1)S(1)} %collective-permute-done.23.refs_3_, ...), custom_call_target="tpu_custom_call" | custom-call | tf_op jit(solution)/shard_map/pallas_call | solution.py:69
  (26 shorter events, 0.1 us)
Async XLA Ops:
  2.5 3.7 %collective-permute-start = (bf16[192,256]{1,0:T(8,128)(2,1)S(1)}, bf16[192,256]{1,0:T(8,128)(2,1)S(1)}, u32[]{:S(2)}, u32[]{:S(2)}) collective-permute-start(bf16[192,256]{1,0:T(8,128)(2,1)S(1)} %get-tuple-element.56), channel_id=1, source_target_pairs={{0,1},{1,0},{2,3},{3,2},{4,5},{5,4},{6,7},{7,6},{8,9},{9,8},{10,11... | collective-permute-start | bytes 294920 | tf_op jit(solution)/shard_map/ppermute | solution.py:506
  3.2 5.1 %collective-permute-start.1 = (bf16[192,256]{1,0:T(8,128)(2,1)S(1)}, bf16[192,256]{1,0:T(8,128)(2,1)S(1)}, u32[]{:S(2)}, u32[]{:S(2)}) collective-permute-start(bf16[192,256]{1,0:T(8,128)(2,1)S(1)} %get-tuple-element.57), channel_id=1, source_target_pairs={{1,2},{3,4},{5,6},{7,8},{9,10},{11,12},{13,14},{2,1},{4,3},{6,5},{... | collective-permute-start | bytes 294920 | tf_op jit(solution)/shard_map/ppermute | solution.py:505
  4.4 19.6 %copy-start.6 = (f32[16,16,256]{2,1,0:T(8,128)S(1)}, f32[16,16,256]{2,1,0:T(8,128)}, u32[]{:S(2)}) copy-start(f32[16,16,256]{2,1,0:T(8,128)} %refs_1_.5) | copy-start | bytes 786436
  4.4 34.0 %copy-start = (bf16[768,2304]{1,0:T(8,128)(2,1)S(1)}, bf16[768,2304]{1,0:T(8,128)(2,1)}, u32[]{:S(2)}) copy-start(bf16[768,2304]{1,0:T(8,128)(2,1)} %refs_6_.4) | copy-start | bytes 10616836
  10.3 1.6 %collective-permute-start.2 = (bf16[192,256]{1,0:T(8,128)(2,1)S(1)}, bf16[192,256]{1,0:T(8,128)(2,1)S(1)}, u32[]{:S(2)}, u32[]{:S(2)}) collective-permute-start(bf16[192,256]{1,0:T(8,128)(2,1)S(1)} %get-tuple-element.66), channel_id=1, source_target_pairs={{0,1},{1,0},{2,3},{3,2},{4,5},{5,4},{6,7},{7,6},{8,9},{9,8},{10,11... | collective-permute-start | bytes 294920 | tf_op jit(solution)/shard_map/ppermute | solution.py:506
  10.4 5.1 %collective-permute-start.3 = (bf16[192,256]{1,0:T(8,128)(2,1)S(1)}, bf16[192,256]{1,0:T(8,128)(2,1)S(1)}, u32[]{:S(2)}, u32[]{:S(2)}) collective-permute-start(bf16[192,256]{1,0:T(8,128)(2,1)S(1)} %get-tuple-element.67), channel_id=1, source_target_pairs={{1,2},{3,4},{5,6},{7,8},{9,10},{11,12},{13,14},{2,1},{4,3},{6,5},{... | collective-permute-start | bytes 294920 | tf_op jit(solution)/shard_map/ppermute | solution.py:505
  17.9 1.4 %collective-permute-start.4 = (bf16[64,896]{1,0:T(8,128)(2,1)S(1)}, bf16[64,896]{1,0:T(8,128)(2,1)S(1)}, u32[]{:S(2)}, u32[]{:S(2)}) collective-permute-start(bf16[64,896]{1,0:T(8,128)(2,1)S(1)} %get-tuple-element.74), channel_id=1, source_target_pairs={{0,1},{1,0},{2,3},{3,2},{4,5},{5,4},{6,7},{7,6},{8,9},{9,8},{10,11... | collective-permute-start | bytes 344072 | tf_op jit(solution)/shard_map/ppermute | solution.py:506
  18.3 5.4 %collective-permute-start.5 = (bf16[64,896]{1,0:T(8,128)(2,1)S(1)}, bf16[64,896]{1,0:T(8,128)(2,1)S(1)}, u32[]{:S(2)}, u32[]{:S(2)}) collective-permute-start(bf16[64,896]{1,0:T(8,128)(2,1)S(1)} %get-tuple-element.75), channel_id=1, source_target_pairs={{1,2},{3,4},{5,6},{7,8},{9,10},{11,12},{13,14},{2,1},{4,3},{6,5},{... | collective-permute-start | bytes 344072 | tf_op jit(solution)/shard_map/ppermute | solution.py:505
  24.1 9.2 %collective-permute-start.10 = (f32[16,16,256]{2,1,0:T(8,128)S(1)}, f32[16,16,256]{2,1,0:T(8,128)S(1)}, u32[]{:S(2)}, u32[]{:S(2)}) collective-permute-start(f32[16,16,256]{2,1,0:T(8,128)S(1)} %copy-done.6), channel_id=1, source_target_pairs={{0,2},{1,3},{2,0},{3,1},{4,6},{5,7},{6,4},{7,5},{8,10},{9,11},{10,... | collective-permute-start | bytes 786440 | tf_op jit(solution)/shard_map/ppermute | solution.py:511
  24.5 2.1 %collective-permute-start.6 = (bf16[16,768]{1,0:T(8,128)(2,1)S(1)}, bf16[16,768]{1,0:T(8,128)(2,1)S(1)}, u32[]{:S(2)}, u32[]{:S(2)}) collective-permute-start(bf16[16,768]{1,0:T(8,128)(2,1)S(1)} %get-tuple-element.78), channel_id=1, source_target_pairs={{0,1},{1,0},{2,3},{3,2},{4,5},{5,4},{6,7},{7,6},{8,9},{9,8},{10,11... | collective-permute-start | bytes 73736 | tf_op jit(solution)/shard_map/ppermute | solution.py:511
  24.5 8.1 %collective-permute-start.7 = (bf16[16,768]{1,0:T(8,128)(2,1)S(1)}, bf16[16,768]{1,0:T(8,128)(2,1)S(1)}, u32[]{:S(2)}, u32[]{:S(2)}) collective-permute-start(bf16[16,768]{1,0:T(8,128)(2,1)S(1)} %get-tuple-element.79), channel_id=1, source_target_pairs={{0,2},{1,3},{2,0},{3,1},{4,6},{5,7},{6,4},{7,5},{8,10},{9,11},{10,... | collective-permute-start | bytes 73736 | tf_op jit(solution)/shard_map/ppermute | solution.py:511
  25.8 7.5 %collective-permute-start.8 = (bf16[16,768]{1,0:T(8,128)(2,1)S(1)}, bf16[16,768]{1,0:T(8,128)(2,1)S(1)}, u32[]{:S(2)}, u32[]{:S(2)}) collective-permute-start(bf16[16,768]{1,0:T(8,128)(2,1)S(1)} %get-tuple-element.80), channel_id=1, source_target_pairs={{0,3},{1,2},{2,1},{3,0},{4,7},{5,6},{6,5},{7,4},{8,11},{9,10},{10,... | collective-permute-start | bytes 73736 | tf_op jit(solution)/shard_map/ppermute | solution.py:511
  26.6 10.9 %collective-permute-start.9 = (f32[16,16,256]{2,1,0:T(8,128)S(1)}, f32[16,16,256]{2,1,0:T(8,128)S(1)}, u32[]{:S(2)}, u32[]{:S(2)}) collective-permute-start(f32[16,16,256]{2,1,0:T(8,128)S(1)} %copy-done.6), channel_id=1, source_target_pairs={{0,1},{1,0},{2,3},{3,2},{4,5},{5,4},{6,7},{7,6},{8,9},{9,8},{10,11... | collective-permute-start | bytes 786440 | tf_op jit(solution)/shard_map/ppermute | solution.py:511
  33.3 5.2 %collective-permute-start.11 = (f32[16,16,256]{2,1,0:T(8,128)S(1)}, f32[16,16,256]{2,1,0:T(8,128)S(1)}, u32[]{:S(2)}, u32[]{:S(2)}) collective-permute-start(f32[16,16,256]{2,1,0:T(8,128)S(1)} %collective-permute-done.10.refs_3_), channel_id=1, source_target_pairs={{0,1},{1,0},{2,3},{3,2},{4,5},{5,4},{6,7},{7,6},{8,9},{9,8},{10,11... | collective-permute-start | bytes 786440 | tf_op jit(solution)/shard_map/ppermute | solution.py:511
  33.7 5.8 %collective-permute-start.12 = (bf16[64,768]{1,0:T(8,128)(2,1)S(1)}, bf16[64,768]{1,0:T(8,128)(2,1)S(1)}, u32[]{:S(2)}, u32[]{:S(2)}) collective-permute-start(bf16[64,768]{1,0:T(8,128)(2,1)S(1)} %shard_map.199.refs_0_), channel_id=1, source_target_pairs={{0,4},{4,8},{8,12},{12,0},{1,5},{5,9},{9,13},{13,1},{2,6},{6,10},{... | collective-permute-start | bytes 294920 | tf_op jit(solution)/shard_map/ppermute | solution.py:615
  35.0 8.4 %collective-permute-start.13 = (bf16[64,768]{1,0:T(8,128)(2,1)S(1)}, bf16[64,768]{1,0:T(8,128)(2,1)S(1)}, u32[]{:S(2)}, u32[]{:S(2)}) collective-permute-start(bf16[64,768]{1,0:T(8,128)(2,1)S(1)} %shard_map.199.refs_0_), channel_id=1, source_target_pairs={{0,8},{4,12},{8,0},{12,4},{1,9},{5,13},{9,1},{13,5},{2,10},{6,14},... | collective-permute-start | bytes 294920 | tf_op jit(solution)/shard_map/ppermute | solution.py:615
  36.1 9.6 %collective-permute-start.14 = (bf16[64,768]{1,0:T(8,128)(2,1)S(1)}, bf16[64,768]{1,0:T(8,128)(2,1)S(1)}, u32[]{:S(2)}, u32[]{:S(2)}) collective-permute-start(bf16[64,768]{1,0:T(8,128)(2,1)S(1)} %shard_map.199.refs_0_), channel_id=1, source_target_pairs={{0,12},{4,0},{8,4},{12,8},{1,13},{5,1},{9,5},{13,9},{2,14},{6,2},{... | collective-permute-start | bytes 294920 | tf_op jit(solution)/shard_map/ppermute | solution.py:615
  37.5 16.4 %collective-permute-start.20 = (f32[200,128]{1,0:T(8,128)S(1)}, f32[200,128]{1,0:T(8,128)S(1)}, u32[]{:S(2)}, u32[]{:S(2)}) collective-permute-start(f32[200,128]{1,0:T(8,128)S(1)} %get-tuple-element.91), channel_id=1, source_target_pairs={{0,1},{1,0},{2,3},{3,2},{4,5},{5,4},{6,7},{7,6},{8,9},{9,8},{10,11... | collective-permute-start | bytes 307208 | tf_op jit(solution)/shard_map/ppermute | solution.py:506
  38.5 15.4 %collective-permute-start.21 = (f32[200,128]{1,0:T(8,128)S(1)}, f32[200,128]{1,0:T(8,128)S(1)}, u32[]{:S(2)}, u32[]{:S(2)}) collective-permute-start(f32[200,128]{1,0:T(8,128)S(1)} %get-tuple-element.92), channel_id=1, source_target_pairs={{1,2},{3,4},{5,6},{7,8},{9,10},{11,12},{13,14},{2,1},{4,3},{6,5},{... | collective-permute-start | bytes 307208 | tf_op jit(solution)/shard_map/ppermute | solution.py:505
  39.5 12.3 %copy-start.1 = (bf16[768,768]{1,0:T(8,128)(2,1)S(1)}, bf16[768,768]{1,0:T(8,128)(2,1)}, u32[]{:S(2)}) copy-start(bf16[768,768]{1,0:T(8,128)(2,1)} %refs_5_.7) | copy-start | bytes 3538948
  39.5 12.3 %copy-start.2 = (bf16[768,128]{1,0:T(8,128)(2,1)S(1)}, bf16[768,128]{1,0:T(8,128)(2,1)}, u32[]{:S(2)}) copy-start(bf16[768,128]{1,0:T(8,128)(2,1)} %refs_6_.5) | copy-start | bytes 589828
  47.5 17.6 %copy-start.3 = (f32[4,3,128]{2,0,1:T(4,128)S(1)}, f32[4,3,128]{2,0,1:T(4,128)}, u32[]{:S(2)}) copy-start(f32[4,3,128]{2,0,1:T(4,128)} %param.20) | copy-start | bytes 18436
  47.5 17.6 %copy-start.4 = (f32[3,128]{1,0:T(4,128)S(1)}, f32[3,128]{1,0:T(4,128)}, u32[]{:S(2)}) copy-start(f32[3,128]{1,0:T(4,128)} %refs_11_.1) | copy-start | bytes 4612
  47.5 17.6 %copy-start.5 = (bf16[3,128]{1,0:T(4,128)(2,1)S(1)}, bf16[3,128]{1,0:T(4,128)(2,1)}, u32[]{:S(2)}) copy-start(bf16[3,128]{1,0:T(4,128)(2,1)} %refs_9_.3) | copy-start | bytes 2308
  47.5 2.3 %collective-permute-start.15 = (bf16[16,768]{1,0:T(8,128)(2,1)S(1)}, bf16[16,768]{1,0:T(8,128)(2,1)S(1)}, u32[]{:S(2)}, u32[]{:S(2)}) collective-permute-start(bf16[16,768]{1,0:T(8,128)(2,1)S(1)} %get-tuple-element.87), channel_id=1, source_target_pairs={{0,1},{1,0},{2,3},{3,2},{4,5},{5,4},{6,7},{7,6},{8,9},{9,8},{10,11... | collective-permute-start | bytes 73736 | tf_op jit(solution)/shard_map/ppermute | solution.py:511
  48.0 2.7 %collective-permute-start.16 = (bf16[16,768]{1,0:T(8,128)(2,1)S(1)}, bf16[16,768]{1,0:T(8,128)(2,1)S(1)}, u32[]{:S(2)}, u32[]{:S(2)}) collective-permute-start(bf16[16,768]{1,0:T(8,128)(2,1)S(1)} %get-tuple-element.88), channel_id=1, source_target_pairs={{0,2},{1,3},{2,0},{3,1},{4,6},{5,7},{6,4},{7,5},{8,10},{9,11},{10,... | collective-permute-start | bytes 73736 | tf_op jit(solution)/shard_map/ppermute | solution.py:511
  48.5 3.3 %collective-permute-start.17 = (bf16[16,768]{1,0:T(8,128)(2,1)S(1)}, bf16[16,768]{1,0:T(8,128)(2,1)S(1)}, u32[]{:S(2)}, u32[]{:S(2)}) collective-permute-start(bf16[16,768]{1,0:T(8,128)(2,1)S(1)} %get-tuple-element.89), channel_id=1, source_target_pairs={{0,3},{1,2},{2,1},{3,0},{4,7},{5,6},{6,5},{7,4},{8,11},{9,10},{10,... | collective-permute-start | bytes 73736 | tf_op jit(solution)/shard_map/ppermute | solution.py:511
  52.5 1.4 %collective-permute-start.18 = (bf16[64,128]{1,0:T(8,128)(2,1)S(1)}, bf16[64,128]{1,0:T(8,128)(2,1)S(1)}, u32[]{:S(2)}, u32[]{:S(2)}) collective-permute-start(bf16[64,128]{1,0:T(8,128)(2,1)S(1)} %get-tuple-element.90.refs_2_), channel_id=1, source_target_pairs={{0,1},{1,0},{2,3},{3,2},{4,5},{5,4},{6,7},{7,6},{8,9},{9,8},{10,11... | collective-permute-start | bytes 49160 | tf_op jit(solution)/shard_map/ppermute | solution.py:506
  53.0 3.5 %collective-permute-start.19 = (bf16[64,128]{1,0:T(8,128)(2,1)S(1)}, bf16[64,128]{1,0:T(8,128)(2,1)S(1)}, u32[]{:S(2)}, u32[]{:S(2)}) collective-permute-start(bf16[64,128]{1,0:T(8,128)(2,1)S(1)} %get-tuple-element.90.refs_2_), channel_id=1, source_target_pairs={{1,2},{3,4},{5,6},{7,8},{9,10},{11,12},{13,14},{2,1},{4,3},{6,5},{... | collective-permute-start | bytes 49160 | tf_op jit(solution)/shard_map/ppermute | solution.py:505
  59.2 2.0 %collective-permute-start.22 = (bf16[192,256]{1,0:T(8,128)(2,1)S(1)}, bf16[192,256]{1,0:T(8,128)(2,1)S(1)}, u32[]{:S(2)}, u32[]{:S(2)}) collective-permute-start(bf16[192,256]{1,0:T(8,128)(2,1)S(1)} %get-tuple-element.100), channel_id=1, source_target_pairs={{0,1},{1,0},{2,3},{3,2},{4,5},{5,4},{6,7},{7,6},{8,9},{9,8},{10,11... | collective-permute-start | bytes 294920 | tf_op jit(solution)/shard_map/ppermute | solution.py:506
  60.0 5.1 %collective-permute-start.23 = (bf16[192,256]{1,0:T(8,128)(2,1)S(1)}, bf16[192,256]{1,0:T(8,128)(2,1)S(1)}, u32[]{:S(2)}, u32[]{:S(2)}) collective-permute-start(bf16[192,256]{1,0:T(8,128)(2,1)S(1)} %get-tuple-element.101), channel_id=1, source_target_pairs={{1,2},{3,4},{5,6},{7,8},{9,10},{11,12},{13,14},{2,1},{4,3},{6,5},{... | collective-permute-start | bytes 294920 | tf_op jit(solution)/shard_map/ppermute | solution.py:505

commit v9 on v8

--- a/solution.py
+++ b/solution.py
@@ -194,7 +194,7 @@
         sems,
     )
     channels = single.shape[-1]
-    for copy in copies:
+    for copy in copies[:-1]:
         copy.wait()
     sigma, total = sigma_of(level, samples)
     inverse = lax.rsqrt(total)
@@ -203,7 +203,7 @@
         (x_true[c : c + 1] + sigma * noise[c]) * inverse for c in range(x_true.shape[0])
     ]
 
-    def place(s, _):
+    def place(s):
         coords = jnp.concatenate([one[s : s + 1] for one in scaled], 0)
         return base + lax.dot_general(
             coords, w_coord[...], (((0,), (0,)), ((), ())),
@@ -219,7 +219,11 @@
         q_ref[s * rows : (s + 1) * rows] = projected[:, :channels].astype(BF)
         kv_ref[s * rows : (s + 1) * rows] = projected[:, channels:].astype(BF)
 
-    in_stages([place, normalise, project], range(samples))
+    units = range(samples)
+    normals = [normalise(s, place(s)) for s in units]
+    copies[-1].wait()
+    for s in units:
+        project(s, normals[s])
     emit_rims(kv_ref, meta[0], samples, rows, first_ref, second_ref)
 
 
@@ -392,14 +396,15 @@
 
     def soften(h, scores):
         expo = jnp.exp2(scores - jnp.max(scores, -1, keepdims=True))
-        attend = expo * (1.0 / jnp.sum(expo, -1, keepdims=True))
-        upper = attend.astype(BF)
-        return upper, (attend - upper.astype(F32)).astype(BF)
+        upper = expo.astype(BF)
+        lower = (expo - upper.astype(F32)).astype(BF)
+        return upper, lower, 1.0 / jnp.sum(expo, -1, keepdims=True)
 
     def mix(h, attends):
         at, mask = lanes_of(h)
         values = kv_all[:, width + at.start : width + at.stop]
-        mixed_all[:, at] += (dot(attends[0], values) + dot(attends[1], values)) * mask
+        upper, lower, inverse = attends
+        mixed_all[:, at] += (dot(upper, values) + dot(lower, values)) * (mask * inverse)
 
     in_stages([score, soften, mix], range(heads))
     for k in range(samples):

time: 68 us -> 67.8 us (level)
  transfers between devices with their start and end apart: 24 -> 24, of which waited for: 11 -> 11; matrix products, arithmetic and copies ran while one was open for 0% -> 0% of each run, Pallas kernels for 8% -> 7%
where the time goes in v9:
time: 67.8 us; the launch traced here: 67.6 us
  waiting for transfers between devices  31.6 us (47%)
  starting transfers between devices  18.3 us (27%)
  Pallas kernels  16.8 us (25%)
  between operations  0.95 us (1%)
    pallas_call x12, Pallas kernels, call(): pl.pallas_call(body, out_shape=out_shape, in_specs=specs, out_specs=out_s...  16.8 us
    ppermute x6, waiting for transfers between devices, swap(): second = lax.ppermute(second, ('groups',) + SEQ, upper)  16.7 us
    ppermute x9, waiting for transfers between devices, toward(): return lax.ppermute(array, 'p', [(i, i ^ k) for i in range(count)])  8.67 us
    ppermute x3, waiting for transfers between devices, shards(): gathered.append(lax.ppermute(normal, 'z', shift))  6.13 us
    ppermute x6, starting transfers between devices, swap(): second = lax.ppermute(second, ('groups',) + SEQ, upper)  5.72 us
    ppermute x9, starting transfers between devices, toward(): return lax.ppermute(array, 'p', [(i, i ^ k) for i in range(count)])  5.31 us
    ppermute x3, starting transfers between devices, shards(): gathered.append(lax.ppermute(normal, 'z', shift))  3.78 us
    ppermute x6, starting transfers between devices, swap(): first = lax.ppermute(first, SEQ, lower)  3.47 us
  transfers between devices with their start and end apart: 24, of which 11 were waited for; matrix products, arithmetic and copies ran while one was open for 0% of the time, Pallas kernels for 7%

profile of v9, /device:TPU:9, one launch (start us, length us, event | category | flops | bytes accessed | tf_op | source)
XLA Modules:
  0.0 67.6 jit_solution(14213291037940545325)
XLA Ops:
  0.6 1.8 %shard_map.194 = (f32[512,128]{1,0:T(8,128)S(1)}, bf16[512,128]{1,0:T(8,128)(2,1)S(1)}, bf16[512,256]{1,0:T(8,128)(2,1)S(1)}, bf16[192,256]{1,0:T(8,128)(2,1)S(1)}, bf16[192,256]{1,0:T(8,128)(2,1)S(1)}) custom-call(s32[4]{0:T(128)} %refs_10_.1, f32[3,128]{1,0:T(4,128)} %refs_11_.1, f32[3,4,128]{2,1,0:T(4,128)} %bitcast.4, bf16[128,128]{1,0:T(8,128)(2,1)} %refs_3_.2, ...), custom_call_target="tpu_custom_call" | custom-call | tf_op jit(solution)/shard_map/pallas_call | solution.py:69
  2.4 0.7 %collective-permute-start = (bf16[192,256]{1,0:T(8,128)(2,1)S(1)}, bf16[192,256]{1,0:T(8,128)(2,1)S(1)}, u32[]{:S(2)}, u32[]{:S(2)}) collective-permute-start(bf16[192,256]{1,0:T(8,128)(2,1)S(1)} %get-tuple-element.56), channel_id=1, source_target_pairs={{0,1},{1,0},{2,3},{3,2},{4,5},{5,4},{6,7},{7,6},{8,9},{9,8},{10,11... | collective-permute-start | bytes 294920 | tf_op jit(solution)/shard_map/ppermute | solution.py:511
  3.2 1.2 %collective-permute-start.1 = (bf16[192,256]{1,0:T(8,128)(2,1)S(1)}, bf16[192,256]{1,0:T(8,128)(2,1)S(1)}, u32[]{:S(2)}, u32[]{:S(2)}) collective-permute-start(bf16[192,256]{1,0:T(8,128)(2,1)S(1)} %get-tuple-element.57), channel_id=1, source_target_pairs={{1,2},{3,4},{5,6},{7,8},{9,10},{11,12},{13,14},{2,1},{4,3},{6,5},{... | collective-permute-start | bytes 294920 | tf_op jit(solution)/shard_map/ppermute | solution.py:510
  4.4 1.7 %shard_map.195 = (f32[4,128,128]{2,1,0:T(8,128)S(1)}, bf16[4,128,128]{2,1,0:T(8,128)(2,1)S(1)}, bf16[4,128,512]{2,1,0:T(8,128)(2,1)S(1)}, bf16[4,256,128]{2,1,0:...) custom-call(s32[2,4]{1,0:T(2,128)} %bitcast.6, ...), custom_call_target="tpu_custom_call" | custom-call | tf_op jit(solution)/shard_map/pallas_call | solution.py:69
  6.1 2.1 %collective-permute-done.1.refs_3_ = bf16[192,256]{1,0:T(8,128)(2,1)S(1)} collective-permute-done((bf16[192,256]{1,0:T(8,128)(2,1)S(1)}, bf16[192,256]{1,0:T(8,128)(2,1)S(1)}, u32[]{:S(2)}, u32[]{:S(2)}) %collective-permute-start.1) | collective-permute-done | bytes 98336 | tf_op jit(solution)/shard_map/ppermute | solution.py:510
  8.3 2.0 %shard_map.196 = (f32[512,128]{1,0:T(8,128)S(1)}, bf16[512,128]{1,0:T(8,128)(2,1)S(1)}, bf16[512,256]{1,0:T(8,128)(2,1)S(1)}, bf16[192,256]{1,0:T(8,128)(2,1)S(1)}, bf16[192,256]{1,0:T(8,128)(2,1)S(1)}) custom-call(bf16[512,128]{1,0:T(8,128)(2,1)S(1)} %get-tuple-element.54.refs_0_, bf16[512,256]{1,0:T(8,128)(2,1)S(1)} %get-tuple-element.55.refs_1_, ...), custom_call_target="tpu_custom_call" | custom-call | tf_op jit(solution)/shard_map/pallas_call | solution.py:69
  10.3 0.1 collective-permute-start.2
  10.4 1.5 %collective-permute-start.3 = (bf16[192,256]{1,0:T(8,128)(2,1)S(1)}, bf16[192,256]{1,0:T(8,128)(2,1)S(1)}, u32[]{:S(2)}, u32[]{:S(2)}) collective-permute-start(bf16[192,256]{1,0:T(8,128)(2,1)S(1)} %get-tuple-element.67), channel_id=1, source_target_pairs={{1,2},{3,4},{5,6},{7,8},{9,10},{11,12},{13,14},{2,1},{4,3},{6,5},{... | collective-permute-start | bytes 294920 | tf_op jit(solution)/shard_map/ppermute | solution.py:510
  11.8 3.7 %collective-permute-done.3.refs_3_ = bf16[192,256]{1,0:T(8,128)(2,1)S(1)} collective-permute-done((bf16[192,256]{1,0:T(8,128)(2,1)S(1)}, bf16[192,256]{1,0:T(8,128)(2,1)S(1)}, u32[]{:S(2)}, u32[]{:S(2)}) %collective-permute-start.3) | collective-permute-done | bytes 98336 | tf_op jit(solution)/shard_map/ppermute | solution.py:510
  15.5 2.3 %shard_map.197 = (f32[512,128]{1,0:T(8,128)S(1)}, f32[80,896]{1,0:T(8,128)S(1)}, bf16[64,896]{1,0:T(8,128)(2,1)S(1)}, bf16[64,896]{1,0:T(8,128)(2,1)S(1)}, f32[2...) custom-call(bf16[512,128]{1,0:T(8,128)(2,1)S(1)} %get-tuple-element.64.refs_0_, ...), custom_call_target="tpu_custom_call" | custom-call | tf_op jit(solution)/shard_map/pallas_call | solution.py:69
  17.8 0.4 collective-permute-start.4
  18.3 0.9 %collective-permute-start.5 = (bf16[64,896]{1,0:T(8,128)(2,1)S(1)}, bf16[64,896]{1,0:T(8,128)(2,1)S(1)}, u32[]{:S(2)}, u32[]{:S(2)}) collective-permute-start(bf16[64,896]{1,0:T(8,128)(2,1)S(1)} %get-tuple-element.75), channel_id=1, source_target_pairs={{1,2},{3,4},{5,6},{7,8},{9,10},{11,12},{13,14},{2,1},{4,3},{6,5},{... | collective-permute-start | bytes 344072 | tf_op jit(solution)/shard_map/ppermute | solution.py:510
  19.2 0.0 collective-permute-done.4.refs_1_
  19.2 4.5 %collective-permute-done.5.refs_2_ = bf16[64,896]{1,0:T(8,128)(2,1)S(1)} collective-permute-done((bf16[64,896]{1,0:T(8,128)(2,1)S(1)}, bf16[64,896]{1,0:T(8,128)(2,1)S(1)}, u32[]{:S(2)}, u32[]{:S(2)}) %collective-permute-start.5) | collective-permute-done | bytes 114720 | tf_op jit(solution)/shard_map/ppermute | solution.py:510
  23.7 0.3 shard_map.198
  24.0 0.4 collective-permute-start.10
  24.4 1.3 %collective-permute-start.7 = (bf16[16,768]{1,0:T(8,128)(2,1)S(1)}, bf16[16,768]{1,0:T(8,128)(2,1)S(1)}, u32[]{:S(2)}, u32[]{:S(2)}) collective-permute-start(bf16[16,768]{1,0:T(8,128)(2,1)S(1)} %get-tuple-element.79), channel_id=1, source_target_pairs={{0,2},{1,3},{2,0},{3,1},{4,6},{5,7},{6,4},{7,5},{8,10},{9,11},{10,... | collective-permute-start | bytes 73736 | tf_op jit(solution)/shard_map/ppermute | solution.py:516
  25.7 0.9 %collective-permute-start.8 = (bf16[16,768]{1,0:T(8,128)(2,1)S(1)}, bf16[16,768]{1,0:T(8,128)(2,1)S(1)}, u32[]{:S(2)}, u32[]{:S(2)}) collective-permute-start(bf16[16,768]{1,0:T(8,128)(2,1)S(1)} %get-tuple-element.80), channel_id=1, source_target_pairs={{0,3},{1,2},{2,1},{3,0},{4,7},{5,6},{6,5},{7,4},{8,11},{9,10},{10,... | collective-permute-start | bytes 73736 | tf_op jit(solution)/shard_map/ppermute | solution.py:516
  26.6 6.0 %collective-permute-done.7.refs_2_ = bf16[16,768]{1,0:T(8,128)(2,1)S(1)} collective-permute-done((bf16[16,768]{1,0:T(8,128)(2,1)S(1)}, bf16[16,768]{1,0:T(8,128)(2,1)S(1)}, u32[]{:S(2)}, u32[]{:S(2)}) %collective-permute-start.7) | collective-permute-done | bytes 24608 | tf_op jit(solution)/shard_map/ppermute | solution.py:516
  32.5 0.6 collective-permute-done.8.refs_3_
  33.2 0.5 collective-permute-start.11
  33.7 1.3 %collective-permute-start.12 = (bf16[64,768]{1,0:T(8,128)(2,1)S(1)}, bf16[64,768]{1,0:T(8,128)(2,1)S(1)}, u32[]{:S(2)}, u32[]{:S(2)}) collective-permute-start(bf16[64,768]{1,0:T(8,128)(2,1)S(1)} %shard_map.199.refs_0_), channel_id=1, source_target_pairs={{0,4},{4,8},{8,12},{12,0},{1,5},{5,9},{9,13},{13,1},{2,6},{6,10},{... | collective-permute-start | bytes 294920 | tf_op jit(solution)/shard_map/ppermute | solution.py:620
  35.0 1.0 %collective-permute-start.13 = (bf16[64,768]{1,0:T(8,128)(2,1)S(1)}, bf16[64,768]{1,0:T(8,128)(2,1)S(1)}, u32[]{:S(2)}, u32[]{:S(2)}) collective-permute-start(bf16[64,768]{1,0:T(8,128)(2,1)S(1)} %shard_map.199.refs_0_), channel_id=1, source_target_pairs={{0,8},{4,12},{8,0},{12,4},{1,9},{5,13},{9,1},{13,5},{2,10},{6,14},... | collective-permute-start | bytes 294920 | tf_op jit(solution)/shard_map/ppermute | solution.py:620
  36.0 1.5 %collective-permute-start.14 = (bf16[64,768]{1,0:T(8,128)(2,1)S(1)}, bf16[64,768]{1,0:T(8,128)(2,1)S(1)}, u32[]{:S(2)}, u32[]{:S(2)}) collective-permute-start(bf16[64,768]{1,0:T(8,128)(2,1)S(1)} %shard_map.199.refs_0_), channel_id=1, source_target_pairs={{0,12},{4,0},{8,4},{12,8},{1,13},{5,1},{9,5},{13,9},{2,14},{6,2},{... | collective-permute-start | bytes 294920 | tf_op jit(solution)/shard_map/ppermute | solution.py:620
  37.5 0.9 %collective-permute-start.20 = (f32[200,128]{1,0:T(8,128)S(1)}, f32[200,128]{1,0:T(8,128)S(1)}, u32[]{:S(2)}, u32[]{:S(2)}) collective-permute-start(f32[200,128]{1,0:T(8,128)S(1)} %get-tuple-element.91), channel_id=1, source_target_pairs={{0,1},{1,0},{2,3},{3,2},{4,5},{5,4},{6,7},{7,6},{8,9},{9,8},{10,11... | collective-permute-start | bytes 307208 | tf_op jit(solution)/shard_map/ppermute | solution.py:511
  38.4 1.0 %shard_map.200 = (bf16[64,768]{1,0:T(8,128)(2,1)S(1)}, bf16[64,1536]{1,0:T(8,128)(2,1)S(1)}, f32[16,64,256]{2,1,0:T(8,128)S(1)}) custom-call(bf16[64,768]{1,0:T(8,128)(2,1)S(1)} %shard_map.199.refs_0_, f32[16,16,256]{2,1,0:T(8,128)} %refs_1_.5, f32[16,16,256]{2,1,0:T(8,128)S(1)} %collective-permute-done.9.refs_2_, ...), custom_call_target="tpu_custom_call" | custom-call | tf_op jit(solution)/shard_map/pallas_call | solution.py:69
  39.4 0.0 copy-start.1
  39.4 0.0 copy-start.2
  39.5 3.9 %collective-permute-done.13.refs_4_ = bf16[64,768]{1,0:T(8,128)(2,1)S(1)} collective-permute-done((bf16[64,768]{1,0:T(8,128)(2,1)S(1)}, bf16[64,768]{1,0:T(8,128)(2,1)S(1)}, u32[]{:S(2)}, u32[]{:S(2)}) %collective-permute-start.13) | collective-permute-done | bytes 98336 | tf_op jit(solution)/shard_map/ppermute | solution.py:620
  43.3 2.2 %collective-permute-done.14.refs_5_ = bf16[64,768]{1,0:T(8,128)(2,1)S(1)} collective-permute-done((bf16[64,768]{1,0:T(8,128)(2,1)S(1)}, bf16[64,768]{1,0:T(8,128)(2,1)S(1)}, u32[]{:S(2)}, u32[]{:S(2)}) %collective-permute-start.14) | collective-permute-done | bytes 98336 | tf_op jit(solution)/shard_map/ppermute | solution.py:620
  45.6 1.7 %shard_map.201 = (bf16[16,768]{1,0:T(8,128)(2,1)S(1)}, bf16[16,768]{1,0:T(8,128)(2,1)S(1)}, bf16[16,768]{1,0:T(8,128)(2,1)S(1)}, bf16[16,768]{1,0:T(8,128)(2,1)S(1)}) custom-call(bf16[64,768]{1,0:T(8,128)(2,1)S(1)} %get-tuple-element.83.refs_0_, bf16[64,1536]{1,0:T(8,128)(2,1)S(1)} %get-tuple-element.84.refs_1_, ...), custom_call_target="tpu_custom_call" | custom-call | tf_op jit(solution)/shard_map/pallas_call | solution.py:69
  47.3 0.0 copy-start.3
  47.3 0.0 copy-start.5
  47.3 0.5 collective-permute-start.15
  47.8 0.5 collective-permute-start.16
  48.3 1.2 %collective-permute-start.17 = (bf16[16,768]{1,0:T(8,128)(2,1)S(1)}, bf16[16,768]{1,0:T(8,128)(2,1)S(1)}, u32[]{:S(2)}, u32[]{:S(2)}) collective-permute-start(bf16[16,768]{1,0:T(8,128)(2,1)S(1)} %get-tuple-element.89), channel_id=1, source_target_pairs={{0,3},{1,2},{2,1},{3,0},{4,7},{5,6},{6,5},{7,4},{8,11},{9,10},{10,... | collective-permute-start | bytes 73736 | tf_op jit(solution)/shard_map/ppermute | solution.py:516
  49.6 1.0 %collective-permute-done.16.refs_3_ = bf16[16,768]{1,0:T(8,128)(2,1)S(1)} collective-permute-done((bf16[16,768]{1,0:T(8,128)(2,1)S(1)}, bf16[16,768]{1,0:T(8,128)(2,1)S(1)}, u32[]{:S(2)}, u32[]{:S(2)}) %collective-permute-start.16) | collective-permute-done | bytes 24608 | tf_op jit(solution)/shard_map/ppermute | solution.py:516
  50.5 1.1 %collective-permute-done.17.refs_4_ = bf16[16,768]{1,0:T(8,128)(2,1)S(1)} collective-permute-done((bf16[16,768]{1,0:T(8,128)(2,1)S(1)}, bf16[16,768]{1,0:T(8,128)(2,1)S(1)}, u32[]{:S(2)}, u32[]{:S(2)}) %collective-permute-start.17) | collective-permute-done | bytes 24608 | tf_op jit(solution)/shard_map/ppermute | solution.py:516
  51.6 0.7 shard_map.202
  52.3 0.5 collective-permute-start.18
  52.8 0.9 %collective-permute-start.19 = (bf16[64,128]{1,0:T(8,128)(2,1)S(1)}, bf16[64,128]{1,0:T(8,128)(2,1)S(1)}, u32[]{:S(2)}, u32[]{:S(2)}) collective-permute-start(bf16[64,128]{1,0:T(8,128)(2,1)S(1)} %get-tuple-element.90.refs_2_), channel_id=1, source_target_pairs={{1,2},{3,4},{5,6},{7,8},{9,10},{11,12},{13,14},{2,1},{4,3},{6,5},{... | collective-permute-start | bytes 49160 | tf_op jit(solution)/shard_map/ppermute | solution.py:510
  53.7 2.5 %collective-permute-done.19.refs_4_ = bf16[64,128]{1,0:T(8,128)(2,1)S(1)} collective-permute-done((bf16[64,128]{1,0:T(8,128)(2,1)S(1)}, bf16[64,128]{1,0:T(8,128)(2,1)S(1)}, u32[]{:S(2)}, u32[]{:S(2)}) %collective-permute-start.19) | collective-permute-done | bytes 16416 | tf_op jit(solution)/shard_map/ppermute | solution.py:510
  56.2 0.8 %shard_map.203 = (f32[512,128]{1,0:T(8,128)S(1)}, bf16[512,128]{1,0:T(8,128)(2,1)S(1)}, bf16[512,256]{1,0:T(8,128)(2,1)S(1)}, bf16[192,256]{1,0:T(8,128)(2,1)S(1)}, bf16[192,256]{1,0:T(8,128)(2,1)S(1)}) custom-call(f32[512,128]{1,0:T(8,128)S(1)} %get-tuple-element.72.refs_0_, s32[1,128]{1,0:T(1,128)S(1)} %get-tuple-element.70.refs_10_.refs_1_, ...), custom_call_target="tpu_custom_call" | custom-call | tf_op jit(solution)/shard_map/pallas_call | solution.py:69
  57.0 2.0 %shard_map.204 = (f32[512,128]{1,0:T(8,128)S(1)}, bf16[512,128]{1,0:T(8,128)(2,1)S(1)}, bf16[512,256]{1,0:T(8,128)(2,1)S(1)}, bf16[192,256]{1,0:T(8,128)(2,1)S(1)}, bf16[192,256]{1,0:T(8,128)(2,1)S(1)}) custom-call(bf16[512,128]{1,0:T(8,128)(2,1)S(1)} %get-tuple-element.93.refs_0_, bf16[512,256]{1,0:T(8,128)(2,1)S(1)} %get-tuple-element.94.refs_1_, ...), custom_call_target="tpu_custom_call" | custom-call | tf_op jit(solution)/shard_map/pallas_call | solution.py:69
  59.0 0.8 %collective-permute-start.22 = (bf16[192,256]{1,0:T(8,128)(2,1)S(1)}, bf16[192,256]{1,0:T(8,128)(2,1)S(1)}, u32[]{:S(2)}, u32[]{:S(2)}) collective-permute-start(bf16[192,256]{1,0:T(8,128)(2,1)S(1)} %get-tuple-element.100), channel_id=1, source_target_pairs={{0,1},{1,0},{2,3},{3,2},{4,5},{5,4},{6,7},{7,6},{8,9},{9,8},{10,11... | collective-permute-start | bytes 294920 | tf_op jit(solution)/shard_map/ppermute | solution.py:511
  59.8 1.2 %collective-permute-start.23 = (bf16[192,256]{1,0:T(8,128)(2,1)S(1)}, bf16[192,256]{1,0:T(8,128)(2,1)S(1)}, u32[]{:S(2)}, u32[]{:S(2)}) collective-permute-start(bf16[192,256]{1,0:T(8,128)(2,1)S(1)} %get-tuple-element.101), channel_id=1, source_target_pairs={{1,2},{3,4},{5,6},{7,8},{9,10},{11,12},{13,14},{2,1},{4,3},{6,5},{... | collective-permute-start | bytes 294920 | tf_op jit(solution)/shard_map/ppermute | solution.py:510
  61.0 3.9 %collective-permute-done.23.refs_3_ = bf16[192,256]{1,0:T(8,128)(2,1)S(1)} collective-permute-done((bf16[192,256]{1,0:T(8,128)(2,1)S(1)}, bf16[192,256]{1,0:T(8,128)(2,1)S(1)}, u32[]{:S(2)}, u32[]{:S(2)}) %collective-permute-start.23) | collective-permute-done | bytes 98336 | tf_op jit(solution)/shard_map/ppermute | solution.py:510
  64.9 2.6 %shard_map.205 = (f32[3,4,128]{2,1,0:T(4,128)}, f32[4,16,768]{2,1,0:T(8,128)}) custom-call(bf16[512,128]{1,0:T(8,128)(2,1)S(1)} %get-tuple-element.98.refs_0_, bf16[512,256]{1,0:T(8,128)(2,1)S(1)} %get-tuple-element.99.refs_1_, bf16[192,256]{1,0:T(8,128)(2,1)S(1)} %collective-permute-done.22.refs_2_, bf16[192,256]{1,0:T(8,128)(2,1)S(1)} %collective-permute-done.23.refs_3_, ...), custom_call_target="tpu_custom_call" | custom-call | tf_op jit(solution)/shard_map/pallas_call | solution.py:69
  (26 shorter events, 0.1 us)
Async XLA Ops:
  2.4 3.7 %collective-permute-start = (bf16[192,256]{1,0:T(8,128)(2,1)S(1)}, bf16[192,256]{1,0:T(8,128)(2,1)S(1)}, u32[]{:S(2)}, u32[]{:S(2)}) collective-permute-start(bf16[192,256]{1,0:T(8,128)(2,1)S(1)} %get-tuple-element.56), channel_id=1, source_target_pairs={{0,1},{1,0},{2,3},{3,2},{4,5},{5,4},{6,7},{7,6},{8,9},{9,8},{10,11... | collective-permute-start | bytes 294920 | tf_op jit(solution)/shard_map/ppermute | solution.py:511
  3.2 5.1 %collective-permute-start.1 = (bf16[192,256]{1,0:T(8,128)(2,1)S(1)}, bf16[192,256]{1,0:T(8,128)(2,1)S(1)}, u32[]{:S(2)}, u32[]{:S(2)}) collective-permute-start(bf16[192,256]{1,0:T(8,128)(2,1)S(1)} %get-tuple-element.57), channel_id=1, source_target_pairs={{1,2},{3,4},{5,6},{7,8},{9,10},{11,12},{13,14},{2,1},{4,3},{6,5},{... | collective-permute-start | bytes 294920 | tf_op jit(solution)/shard_map/ppermute | solution.py:510
  4.4 19.6 %copy-start.6 = (f32[16,16,256]{2,1,0:T(8,128)S(1)}, f32[16,16,256]{2,1,0:T(8,128)}, u32[]{:S(2)}) copy-start(f32[16,16,256]{2,1,0:T(8,128)} %refs_1_.5) | copy-start | bytes 786436
  4.4 34.0 %copy-start = (bf16[768,2304]{1,0:T(8,128)(2,1)S(1)}, bf16[768,2304]{1,0:T(8,128)(2,1)}, u32[]{:S(2)}) copy-start(bf16[768,2304]{1,0:T(8,128)(2,1)} %refs_6_.4) | copy-start | bytes 10616836
  10.3 1.5 %collective-permute-start.2 = (bf16[192,256]{1,0:T(8,128)(2,1)S(1)}, bf16[192,256]{1,0:T(8,128)(2,1)S(1)}, u32[]{:S(2)}, u32[]{:S(2)}) collective-permute-start(bf16[192,256]{1,0:T(8,128)(2,1)S(1)} %get-tuple-element.66), channel_id=1, source_target_pairs={{0,1},{1,0},{2,3},{3,2},{4,5},{5,4},{6,7},{7,6},{8,9},{9,8},{10,11... | collective-permute-start | bytes 294920 | tf_op jit(solution)/shard_map/ppermute | solution.py:511
  10.4 5.1 %collective-permute-start.3 = (bf16[192,256]{1,0:T(8,128)(2,1)S(1)}, bf16[192,256]{1,0:T(8,128)(2,1)S(1)}, u32[]{:S(2)}, u32[]{:S(2)}) collective-permute-start(bf16[192,256]{1,0:T(8,128)(2,1)S(1)} %get-tuple-element.67), channel_id=1, source_target_pairs={{1,2},{3,4},{5,6},{7,8},{9,10},{11,12},{13,14},{2,1},{4,3},{6,5},{... | collective-permute-start | bytes 294920 | tf_op jit(solution)/shard_map/ppermute | solution.py:510
  17.8 1.4 %collective-permute-start.4 = (bf16[64,896]{1,0:T(8,128)(2,1)S(1)}, bf16[64,896]{1,0:T(8,128)(2,1)S(1)}, u32[]{:S(2)}, u32[]{:S(2)}) collective-permute-start(bf16[64,896]{1,0:T(8,128)(2,1)S(1)} %get-tuple-element.74), channel_id=1, source_target_pairs={{0,1},{1,0},{2,3},{3,2},{4,5},{5,4},{6,7},{7,6},{8,9},{9,8},{10,11... | collective-permute-start | bytes 344072 | tf_op jit(solution)/shard_map/ppermute | solution.py:511
  18.3 5.4 %collective-permute-start.5 = (bf16[64,896]{1,0:T(8,128)(2,1)S(1)}, bf16[64,896]{1,0:T(8,128)(2,1)S(1)}, u32[]{:S(2)}, u32[]{:S(2)}) collective-permute-start(bf16[64,896]{1,0:T(8,128)(2,1)S(1)} %get-tuple-element.75), channel_id=1, source_target_pairs={{1,2},{3,4},{5,6},{7,8},{9,10},{11,12},{13,14},{2,1},{4,3},{6,5},{... | collective-permute-start | bytes 344072 | tf_op jit(solution)/shard_map/ppermute | solution.py:510
  24.0 9.2 %collective-permute-start.10 = (f32[16,16,256]{2,1,0:T(8,128)S(1)}, f32[16,16,256]{2,1,0:T(8,128)S(1)}, u32[]{:S(2)}, u32[]{:S(2)}) collective-permute-start(f32[16,16,256]{2,1,0:T(8,128)S(1)} %copy-done.6), channel_id=1, source_target_pairs={{0,2},{1,3},{2,0},{3,1},{4,6},{5,7},{6,4},{7,5},{8,10},{9,11},{10,... | collective-permute-start | bytes 786440 | tf_op jit(solution)/shard_map/ppermute | solution.py:516
  24.4 2.1 %collective-permute-start.6 = (bf16[16,768]{1,0:T(8,128)(2,1)S(1)}, bf16[16,768]{1,0:T(8,128)(2,1)S(1)}, u32[]{:S(2)}, u32[]{:S(2)}) collective-permute-start(bf16[16,768]{1,0:T(8,128)(2,1)S(1)} %get-tuple-element.78), channel_id=1, source_target_pairs={{0,1},{1,0},{2,3},{3,2},{4,5},{5,4},{6,7},{7,6},{8,9},{9,8},{10,11... | collective-permute-start | bytes 73736 | tf_op jit(solution)/shard_map/ppermute | solution.py:516
  24.4 8.1 %collective-permute-start.7 = (bf16[16,768]{1,0:T(8,128)(2,1)S(1)}, bf16[16,768]{1,0:T(8,128)(2,1)S(1)}, u32[]{:S(2)}, u32[]{:S(2)}) collective-permute-start(bf16[16,768]{1,0:T(8,128)(2,1)S(1)} %get-tuple-element.79), channel_id=1, source_target_pairs={{0,2},{1,3},{2,0},{3,1},{4,6},{5,7},{6,4},{7,5},{8,10},{9,11},{10,... | collective-permute-start | bytes 73736 | tf_op jit(solution)/shard_map/ppermute | solution.py:516
  25.7 7.5 %collective-permute-start.8 = (bf16[16,768]{1,0:T(8,128)(2,1)S(1)}, bf16[16,768]{1,0:T(8,128)(2,1)S(1)}, u32[]{:S(2)}, u32[]{:S(2)}) collective-permute-start(bf16[16,768]{1,0:T(8,128)(2,1)S(1)} %get-tuple-element.80), channel_id=1, source_target_pairs={{0,3},{1,2},{2,1},{3,0},{4,7},{5,6},{6,5},{7,4},{8,11},{9,10},{10,... | collective-permute-start | bytes 73736 | tf_op jit(solution)/shard_map/ppermute | solution.py:516
  26.6 10.9 %collective-permute-start.9 = (f32[16,16,256]{2,1,0:T(8,128)S(1)}, f32[16,16,256]{2,1,0:T(8,128)S(1)}, u32[]{:S(2)}, u32[]{:S(2)}) collective-permute-start(f32[16,16,256]{2,1,0:T(8,128)S(1)} %copy-done.6), channel_id=1, source_target_pairs={{0,1},{1,0},{2,3},{3,2},{4,5},{5,4},{6,7},{7,6},{8,9},{9,8},{10,11... | collective-permute-start | bytes 786440 | tf_op jit(solution)/shard_map/ppermute | solution.py:516
  33.2 5.2 %collective-permute-start.11 = (f32[16,16,256]{2,1,0:T(8,128)S(1)}, f32[16,16,256]{2,1,0:T(8,128)S(1)}, u32[]{:S(2)}, u32[]{:S(2)}) collective-permute-start(f32[16,16,256]{2,1,0:T(8,128)S(1)} %collective-permute-done.10.refs_3_), channel_id=1, source_target_pairs={{0,1},{1,0},{2,3},{3,2},{4,5},{5,4},{6,7},{7,6},{8,9},{9,8},{10,11... | collective-permute-start | bytes 786440 | tf_op jit(solution)/shard_map/ppermute | solution.py:516
  33.7 5.8 %collective-permute-start.12 = (bf16[64,768]{1,0:T(8,128)(2,1)S(1)}, bf16[64,768]{1,0:T(8,128)(2,1)S(1)}, u32[]{:S(2)}, u32[]{:S(2)}) collective-permute-start(bf16[64,768]{1,0:T(8,128)(2,1)S(1)} %shard_map.199.refs_0_), channel_id=1, source_target_pairs={{0,4},{4,8},{8,12},{12,0},{1,5},{5,9},{9,13},{13,1},{2,6},{6,10},{... | collective-permute-start | bytes 294920 | tf_op jit(solution)/shard_map/ppermute | solution.py:620
  35.0 8.4 %collective-permute-start.13 = (bf16[64,768]{1,0:T(8,128)(2,1)S(1)}, bf16[64,768]{1,0:T(8,128)(2,1)S(1)}, u32[]{:S(2)}, u32[]{:S(2)}) collective-permute-start(bf16[64,768]{1,0:T(8,128)(2,1)S(1)} %shard_map.199.refs_0_), channel_id=1, source_target_pairs={{0,8},{4,12},{8,0},{12,4},{1,9},{5,13},{9,1},{13,5},{2,10},{6,14},... | collective-permute-start | bytes 294920 | tf_op jit(solution)/shard_map/ppermute | solution.py:620
  36.0 9.6 %collective-permute-start.14 = (bf16[64,768]{1,0:T(8,128)(2,1)S(1)}, bf16[64,768]{1,0:T(8,128)(2,1)S(1)}, u32[]{:S(2)}, u32[]{:S(2)}) collective-permute-start(bf16[64,768]{1,0:T(8,128)(2,1)S(1)} %shard_map.199.refs_0_), channel_id=1, source_target_pairs={{0,12},{4,0},{8,4},{12,8},{1,13},{5,1},{9,5},{13,9},{2,14},{6,2},{... | collective-permute-start | bytes 294920 | tf_op jit(solution)/shard_map/ppermute | solution.py:620
  37.5 16.2 %collective-permute-start.20 = (f32[200,128]{1,0:T(8,128)S(1)}, f32[200,128]{1,0:T(8,128)S(1)}, u32[]{:S(2)}, u32[]{:S(2)}) collective-permute-start(f32[200,128]{1,0:T(8,128)S(1)} %get-tuple-element.91), channel_id=1, source_target_pairs={{0,1},{1,0},{2,3},{3,2},{4,5},{5,4},{6,7},{7,6},{8,9},{9,8},{10,11... | collective-permute-start | bytes 307208 | tf_op jit(solution)/shard_map/ppermute | solution.py:511
  38.4 15.3 %collective-permute-start.21 = (f32[200,128]{1,0:T(8,128)S(1)}, f32[200,128]{1,0:T(8,128)S(1)}, u32[]{:S(2)}, u32[]{:S(2)}) collective-permute-start(f32[200,128]{1,0:T(8,128)S(1)} %get-tuple-element.92), channel_id=1, source_target_pairs={{1,2},{3,4},{5,6},{7,8},{9,10},{11,12},{13,14},{2,1},{4,3},{6,5},{... | collective-permute-start | bytes 307208 | tf_op jit(solution)/shard_map/ppermute | solution.py:510
  39.4 12.2 %copy-start.1 = (bf16[768,768]{1,0:T(8,128)(2,1)S(1)}, bf16[768,768]{1,0:T(8,128)(2,1)}, u32[]{:S(2)}) copy-start(bf16[768,768]{1,0:T(8,128)(2,1)} %refs_5_.7) | copy-start | bytes 3538948
  39.4 12.2 %copy-start.2 = (bf16[768,128]{1,0:T(8,128)(2,1)S(1)}, bf16[768,128]{1,0:T(8,128)(2,1)}, u32[]{:S(2)}) copy-start(bf16[768,128]{1,0:T(8,128)(2,1)} %refs_6_.5) | copy-start | bytes 589828
  47.3 17.6 %copy-start.3 = (f32[4,3,128]{2,0,1:T(4,128)S(1)}, f32[4,3,128]{2,0,1:T(4,128)}, u32[]{:S(2)}) copy-start(f32[4,3,128]{2,0,1:T(4,128)} %param.20) | copy-start | bytes 18436
  47.3 17.6 %copy-start.4 = (f32[3,128]{1,0:T(4,128)S(1)}, f32[3,128]{1,0:T(4,128)}, u32[]{:S(2)}) copy-start(f32[3,128]{1,0:T(4,128)} %refs_11_.1) | copy-start | bytes 4612
  47.3 17.6 %copy-start.5 = (bf16[3,128]{1,0:T(4,128)(2,1)S(1)}, bf16[3,128]{1,0:T(4,128)(2,1)}, u32[]{:S(2)}) copy-start(bf16[3,128]{1,0:T(4,128)(2,1)} %refs_9_.3) | copy-start | bytes 2308
  47.3 2.3 %collective-permute-start.15 = (bf16[16,768]{1,0:T(8,128)(2,1)S(1)}, bf16[16,768]{1,0:T(8,128)(2,1)S(1)}, u32[]{:S(2)}, u32[]{:S(2)}) collective-permute-start(bf16[16,768]{1,0:T(8,128)(2,1)S(1)} %get-tuple-element.87), channel_id=1, source_target_pairs={{0,1},{1,0},{2,3},{3,2},{4,5},{5,4},{6,7},{7,6},{8,9},{9,8},{10,11... | collective-permute-start | bytes 73736 | tf_op jit(solution)/shard_map/ppermute | solution.py:516
  47.8 2.7 %collective-permute-start.16 = (bf16[16,768]{1,0:T(8,128)(2,1)S(1)}, bf16[16,768]{1,0:T(8,128)(2,1)S(1)}, u32[]{:S(2)}, u32[]{:S(2)}) collective-permute-start(bf16[16,768]{1,0:T(8,128)(2,1)S(1)} %get-tuple-element.88), channel_id=1, source_target_pairs={{0,2},{1,3},{2,0},{3,1},{4,6},{5,7},{6,4},{7,5},{8,10},{9,11},{10,... | collective-permute-start | bytes 73736 | tf_op jit(solution)/shard_map/ppermute | solution.py:516
  48.3 3.3 %collective-permute-start.17 = (bf16[16,768]{1,0:T(8,128)(2,1)S(1)}, bf16[16,768]{1,0:T(8,128)(2,1)S(1)}, u32[]{:S(2)}, u32[]{:S(2)}) collective-permute-start(bf16[16,768]{1,0:T(8,128)(2,1)S(1)} %get-tuple-element.89), channel_id=1, source_target_pairs={{0,3},{1,2},{2,1},{3,0},{4,7},{5,6},{6,5},{7,4},{8,11},{9,10},{10,... | collective-permute-start | bytes 73736 | tf_op jit(solution)/shard_map/ppermute | solution.py:516
  52.3 1.4 %collective-permute-start.18 = (bf16[64,128]{1,0:T(8,128)(2,1)S(1)}, bf16[64,128]{1,0:T(8,128)(2,1)S(1)}, u32[]{:S(2)}, u32[]{:S(2)}) collective-permute-start(bf16[64,128]{1,0:T(8,128)(2,1)S(1)} %get-tuple-element.90.refs_2_), channel_id=1, source_target_pairs={{0,1},{1,0},{2,3},{3,2},{4,5},{5,4},{6,7},{7,6},{8,9},{9,8},{10,11... | collective-permute-start | bytes 49160 | tf_op jit(solution)/shard_map/ppermute | solution.py:511
  52.8 3.5 %collective-permute-start.19 = (bf16[64,128]{1,0:T(8,128)(2,1)S(1)}, bf16[64,128]{1,0:T(8,128)(2,1)S(1)}, u32[]{:S(2)}, u32[]{:S(2)}) collective-permute-start(bf16[64,128]{1,0:T(8,128)(2,1)S(1)} %get-tuple-element.90.refs_2_), channel_id=1, source_target_pairs={{1,2},{3,4},{5,6},{7,8},{9,10},{11,12},{13,14},{2,1},{4,3},{6,5},{... | collective-permute-start | bytes 49160 | tf_op jit(solution)/shard_map/ppermute | solution.py:510
  59.0 2.0 %collective-permute-start.22 = (bf16[192,256]{1,0:T(8,128)(2,1)S(1)}, bf16[192,256]{1,0:T(8,128)(2,1)S(1)}, u32[]{:S(2)}, u32[]{:S(2)}) collective-permute-start(bf16[192,256]{1,0:T(8,128)(2,1)S(1)} %get-tuple-element.100), channel_id=1, source_target_pairs={{0,1},{1,0},{2,3},{3,2},{4,5},{5,4},{6,7},{7,6},{8,9},{9,8},{10,11... | collective-permute-start | bytes 294920 | tf_op jit(solution)/shard_map/ppermute | solution.py:511
  59.8 5.1 %collective-permute-start.23 = (bf16[192,256]{1,0:T(8,128)(2,1)S(1)}, bf16[192,256]{1,0:T(8,128)(2,1)S(1)}, u32[]{:S(2)}, u32[]{:S(2)}) collective-permute-start(bf16[192,256]{1,0:T(8,128)(2,1)S(1)} %get-tuple-element.101), channel_id=1, source_target_pairs={{1,2},{3,4},{5,6},{7,8},{9,10},{11,12},{13,14},{2,1},{4,3},{6,5},{... | collective-permute-start | bytes 294920 | tf_op jit(solution)/shard_map/ppermute | solution.py:510
